TPU v7x, 256 devices: a whole 4x4x8 slice. The times are simulated.
256 devices in a mesh: row: 32 (over z, y_lo, core), col: 8 (over x, y_hi).
Axes of the slice: x: 4, y: 4 (y_hi: 2, y_lo: 2; y = y_hi * 2 + y_lo), z: 8, core: 2. Of those that a mesh axis runs over, the one named last changes fastest.
Arguments:
- half_panel: bfloat16 [48, 2048, 2048], P(None, 'row', 'col'), may hold values from -6 to 6
- orbitals: bfloat16 [2048, 2048], replicated, may hold values from -0.125 to 0.125
Outputs:
- integrals: bfloat16 [48, 2048, 2048], P(None, 'row', 'col')
All inputs are finite; a program needn't handle non-finite values.
Results may differ from a plain program's by a relative error of at most 0.0049.
Values may be sent and summed in bfloat16 or wider, within the bound.
No kernel may reach another device: no remote copies, remote signals or barrier semaphores. Data moves between devices by JAX's collectives and lax.ppermute only.
A program may use at most 64 MiB of HBM per device.

v0:
```python
import functools

import jax
import jax.numpy as jnp
from jax import lax
from jax.experimental import pallas as pl
from jax.experimental.pallas import tpu as pltpu
from jax.sharding import Mesh, PartitionSpec as P

Z, YLO, CORE, X, YHI = 8, 2, 2, 4, 2
COLS = X * YHI
BLOCKS = 8
PLANE = ("x", "yhi", "ylo")
SIDE = ("x", "yhi")
AT_Z, AT_YLO, AT_CORE, AT_C = range(4)
F32 = jnp.float32
BF16 = jnp.bfloat16
PARAMS = pltpu.CompilerParams(vmem_limit_bytes=24 * 2**20)
SMALL = pltpu.CompilerParams(vmem_limit_bytes=8 * 2**20)


STEPS = 4
HBM = pl.BlockSpec(memory_space=pltpu.HBM)


def in_hbm(value):
    return pltpu.with_memory_space_constraint(value, pltpu.HBM)


def fetch_of(c_hbm, c_ref, sems, step):
    rows = c_ref.shape[1]
    return pltpu.make_async_copy(
        c_hbm.at[pl.ds(pl.multiple_of(step * rows, rows), rows)], c_ref.at[step], sems.at[step]
    )


def steps(c_hbm, c_ref, sems, body):
    def start(step, carry):
        fetch_of(c_hbm, c_ref, sems, step).start()
        return carry

    def run(step, carry):
        body(step)
        return carry

    lax.fori_loop(0, STEPS, start, 0)
    lax.fori_loop(0, STEPS, run, 0)


def fetch_scratch(value):
    size, width = value.shape
    return [pltpu.VMEM((STEPS, size // STEPS, width), BF16), pltpu.SemaphoreType.DMA((STEPS,))]


def transposed(block):
    size = block.shape[1]
    row = lax.broadcasted_iota(jnp.int32, (size, size), 0)
    column = lax.broadcasted_iota(jnp.int32, (size, size), 1)
    eye = (row == column).astype(F32).astype(BF16)
    return lax.dot_general(
        eye, block, (((1,), (1,)), ((), ())), preferred_element_type=F32
    ).astype(BF16)


def pick_kernel(place, c_hbm, out_hbm, c_ref, sems, chosen, out_sems):
    block = c_hbm.shape[1] // BLOCKS
    lanes = block // CORE
    half = lanes // 2
    rows = c_hbm.shape[0] // STEPS

    def store_of(step):
        return pltpu.make_async_copy(
            chosen.at[step], out_hbm.at[pl.ds(pl.multiple_of(step * rows, rows), rows)], out_sems.at[step]
        )

    def choose(step):
        fetch_of(c_hbm, c_ref, sems, step).wait()
        for core in range(CORE):
            @pl.when(place[AT_CORE] == core)
            def _():
                for b in range(BLOCKS):
                    pieces = []
                    for y in range(YLO):
                        tile = c_ref[step, :, b * block + y * lanes:b * block + (y + 1) * lanes]
                        pieces.append(tile[:, core * half:(core + 1) * half])
                    chosen[step, :, b * lanes:(b + 1) * lanes] = jnp.concatenate(pieces, axis=1)
        store_of(step).start()

    def finish_store(step, carry):
        store_of(step).wait()
        return carry

    steps(c_hbm, c_ref, sems, choose)
    lax.fori_loop(0, STEPS, finish_store, 0)


def pick_columns(place, orbitals):
    size = orbitals.shape[0]
    width = size // CORE
    return pl.pallas_call(
        pick_kernel,
        out_shape=pltpu.HBM((size, width), BF16),
        in_specs=[pl.BlockSpec(memory_space=pltpu.SMEM), HBM],
        out_specs=HBM,
        scratch_shapes=fetch_scratch(orbitals) + [
            pltpu.VMEM((STEPS, size // STEPS, width), BF16), pltpu.SemaphoreType.DMA((STEPS,))],
        compiler_params=PARAMS,
        name="pick_columns",
    )(place, in_hbm(orbitals))


def first_kernel(index, place, direct, direct_other, turned, turned_other, c_hbm, t_ref,
                 c_ref, sems, sym, turn, total):
    _, _, depth, rows, block = direct.shape
    mine, core = place[index], place[AT_CORE]
    per_step = BLOCKS // STEPS
    total[...] = jnp.zeros(total.shape, F32)

    def work(step):
        for u in range(per_step):
            b = step * per_step + u
            cols = slice(u * block, (u + 1) * block)

            @pl.when(b >= mine)
            def _():
                for k in range(depth):
                    for y in range(YLO):
                        at = k * block + y * CORE * rows
                        sym[pl.ds(pl.multiple_of(at + core * rows, rows), rows), cols] = direct[b, y, k]
                        sym[pl.ds(pl.multiple_of(at + (1 - core) * rows, rows), rows), cols] = direct_other[b, y, k]

            @pl.when(b == mine)
            def _():
                row = lax.broadcasted_iota(jnp.int32, (block, block), 0)
                column = lax.broadcasted_iota(jnp.int32, (block, block), 1)
                for k in range(depth):
                    upper = sym[k * block:(k + 1) * block, cols]
                    sym[k * block:(k + 1) * block, cols] = jnp.where(row <= column, upper, transposed(upper))

            @pl.when(b < mine)
            def _():
                for k in range(depth):
                    for y in range(YLO):
                        at = k * block + y * CORE * rows
                        turn[pl.ds(pl.multiple_of(at + core * rows, rows), rows), :] = turned[b, y, k]
                        turn[pl.ds(pl.multiple_of(at + (1 - core) * rows, rows), rows), :] = turned_other[b, y, k]
                for k in range(depth):
                    sym[k * block:(k + 1) * block, cols] = transposed(turn[k * block:(k + 1) * block])

        fetch_of(c_hbm, c_ref, sems, step).wait()
        total[...] += jnp.dot(sym[...], c_ref[step], preferred_element_type=F32)

    steps(c_hbm, c_ref, sems, work)
    lanes = t_ref.shape[3]
    for part in range(t_ref.shape[0]):
        for k in range(depth):
            t_ref[part, k] = total[k * block:(k + 1) * block, part * lanes:(part + 1) * lanes].astype(BF16)


def first_half(index, place, direct, direct_other, turned, turned_other, picked, name):
    _, _, depth, rows, block = direct.shape
    size, width = picked.shape
    vmem = pl.BlockSpec(memory_space=pltpu.VMEM)
    return pl.pallas_call(
        functools.partial(first_kernel, index),
        out_shape=jax.ShapeDtypeStruct((BLOCKS, depth, block, width // BLOCKS), BF16),
        in_specs=[pl.BlockSpec(memory_space=pltpu.SMEM), vmem, vmem, vmem, vmem, HBM],
        out_specs=vmem,
        scratch_shapes=fetch_scratch(picked) + [
            pltpu.VMEM((depth * block, size // STEPS), BF16),
            pltpu.VMEM((depth * block, block), BF16),
            pltpu.VMEM((depth * block, width), F32)],
        compiler_params=PARAMS,
        name=name,
    )(place, direct, direct_other, turned, turned_other, in_hbm(picked))


def second_kernel(t_ref, c_hbm, out_ref, c_ref, sems, left, total):
    count, depth, block, lanes = t_ref.shape
    rows = lanes // YLO
    per_step = count // STEPS
    total[...] = jnp.zeros(total.shape, F32)

    def work(step):
        for u in range(per_step):
            for k in range(depth):
                left[k * lanes:(k + 1) * lanes, u * block:(u + 1) * block] = transposed(t_ref[step * per_step + u, k])
        fetch_of(c_hbm, c_ref, sems, step).wait()
        total[...] += jnp.dot(left[...], c_ref[step], preferred_element_type=F32)

    steps(c_hbm, c_ref, sems, work)
    for c in range(COLS):
        for y in range(YLO):
            for k in range(depth):
                at = k * lanes + y * rows
                out_ref[c, y, k] = total[at:at + rows, c * block:(c + 1) * block].astype(BF16)


def second_half(partial_value, orbitals):
    _, depth, block, lanes = partial_value.shape
    size = orbitals.shape[0]
    vmem = pl.BlockSpec(memory_space=pltpu.VMEM)
    return pl.pallas_call(
        second_kernel,
        out_shape=jax.ShapeDtypeStruct((COLS, YLO, depth, lanes // YLO, block), BF16),
        in_specs=[vmem, HBM],
        out_specs=vmem,
        scratch_shapes=fetch_scratch(orbitals) + [
            pltpu.VMEM((depth * lanes, size // STEPS), BF16),
            pltpu.VMEM((depth * lanes, size), F32)],
        compiler_params=PARAMS,
        name="second_half",
    )(partial_value, in_hbm(orbitals))


def second_side_kernel(place, t_ref, other_ref, c_hbm, keep, send, c_ref, sems, left, total, final):
    count, _, block, lanes = t_ref.shape
    rows = lanes // YLO
    per_step = count // STEPS
    ylo, core = place[AT_YLO], place[AT_CORE]
    total[...] = jnp.zeros(total.shape, F32)

    def work(step):
        for u in range(per_step):
            cols = slice(u * block, (u + 1) * block)
            own = transposed(t_ref[step * per_step + u, 0])
            other = transposed(other_ref[step * per_step + u, 0])
            for y in range(YLO):
                at = y * CORE * rows
                left[pl.ds(pl.multiple_of(at + core * rows, rows), rows), cols] = own[y * rows:(y + 1) * rows]
                left[pl.ds(pl.multiple_of(at + (1 - core) * rows, rows), rows), cols] = other[y * rows:(y + 1) * rows]
        fetch_of(c_hbm, c_ref, sems, step).wait()
        total[...] += jnp.dot(left[...], c_ref[step], preferred_element_type=F32)

    steps(c_hbm, c_ref, sems, work)
    for part in range(total.shape[1] // block):
        cols = slice(part * block, (part + 1) * block)
        final[cols] = transposed(total[:, cols].astype(BF16))
    for z in range(Z):
        at = z * YLO * rows
        keep[z] = final[pl.ds(pl.multiple_of(at + ylo * rows, rows), rows)]
        send[z] = final[pl.ds(pl.multiple_of(at + (1 - ylo) * rows, rows), rows)]


def second_half_side(place, own, other, picked):
    _, _, block, lanes = own.shape
    size, width = picked.shape
    vmem = pl.BlockSpec(memory_space=pltpu.VMEM)
    out = jax.ShapeDtypeStruct((Z, lanes // YLO, block), BF16)
    return pl.pallas_call(
        second_side_kernel,
        out_shape=[out, out],
        in_specs=[pl.BlockSpec(memory_space=pltpu.SMEM), vmem, vmem, HBM],
        out_specs=[vmem, vmem],
        scratch_shapes=fetch_scratch(picked) + [
            pltpu.VMEM((block, size // STEPS), BF16),
            pltpu.VMEM((block, width), F32),
            pltpu.VMEM((width, block), BF16)],
        compiler_params=PARAMS,
        name="second_half_side",
    )(place, own, other, in_hbm(picked))


def spread_kernel(index, place, x_ref, *out_refs):
    for d in range(BLOCKS):
        out_refs[d][...] = x_ref[(place[index] + d) % BLOCKS]


def spread(index, place, value):
    vmem = pl.BlockSpec(memory_space=pltpu.VMEM)
    return pl.pallas_call(
        functools.partial(spread_kernel, index),
        out_shape=[jax.ShapeDtypeStruct(value.shape[1:], BF16)] * BLOCKS,
        in_specs=[pl.BlockSpec(memory_space=pltpu.SMEM), vmem],
        out_specs=[vmem] * BLOCKS,
        compiler_params=SMALL,
        name="spread",
    )(place, value)


def join_kernel(place, keep, got, *out_refs):
    z, ylo = place[AT_Z], place[AT_YLO]
    for d in range(BLOCKS):
        out_refs[d][ylo] = keep[(z + d) % BLOCKS]
        out_refs[d][1 - ylo] = got[(z + d) % BLOCKS]


def join_and_spread(place, keep, got):
    vmem = pl.BlockSpec(memory_space=pltpu.VMEM)
    return pl.pallas_call(
        join_kernel,
        out_shape=[jax.ShapeDtypeStruct((YLO,) + keep.shape[1:], BF16)] * BLOCKS,
        in_specs=[pl.BlockSpec(memory_space=pltpu.SMEM), vmem, vmem],
        out_specs=[vmem] * BLOCKS,
        compiler_params=SMALL,
        name="join_and_spread",
    )(place, keep, got)


def collect_kernel(index, place, *refs):
    out_ref = refs[BLOCKS]
    for d in range(BLOCKS):
        out_ref[(place[index] + BLOCKS - d) % BLOCKS] = refs[d][...]


def collect(index, place, parts):
    vmem = pl.BlockSpec(memory_space=pltpu.VMEM)
    return pl.pallas_call(
        functools.partial(collect_kernel, index),
        out_shape=jax.ShapeDtypeStruct((BLOCKS,) + parts[0].shape, BF16),
        in_specs=[pl.BlockSpec(memory_space=pltpu.SMEM)] + [vmem] * BLOCKS,
        out_specs=vmem,
        compiler_params=SMALL,
        name="collect",
    )(place, *parts)


def finish_kernel(place, *refs):
    main_ref, out_ref = refs[BLOCKS:]
    main = main_ref.shape[0]
    out_ref[:main] = main_ref[...]
    for d in range(BLOCKS):
        for y in range(YLO):
            out_ref[main + y * BLOCKS + (place[AT_Z] + BLOCKS - d) % BLOCKS] = refs[d][y]


def finish(place, parts, main):
    pairs, rows, block = main.shape
    vmem = pl.BlockSpec(memory_space=pltpu.VMEM)
    return pl.pallas_call(
        finish_kernel,
        out_shape=jax.ShapeDtypeStruct((pairs + YLO * BLOCKS, rows, block), BF16),
        in_specs=[pl.BlockSpec(memory_space=pltpu.SMEM)] + [vmem] * (BLOCKS + 1),
        out_specs=vmem,
        compiler_params=SMALL,
        name="finish",
    )(place, *parts, main)


def rotate(parts, axes):
    out = [parts[0]]
    for d in range(1, BLOCKS):
        out.append(lax.ppermute(parts[d], axes, [(i, (i + d) % BLOCKS) for i in range(BLOCKS)]))
    return out


def swap(value, axis):
    return lax.ppermute(value, axis, [(0, 1), (1, 0)])


def per_device(half_panel, orbitals):
    pairs, rows, block = half_panel.shape
    side_pairs = Z * YLO
    main_pairs = pairs - side_pairs
    depth = main_pairs // (COLS * YLO)
    z, ylo, core = lax.axis_index("z"), lax.axis_index("ylo"), lax.axis_index("core")
    c = lax.axis_index("x") * YHI + lax.axis_index("yhi")

    place = jnp.stack([z, ylo, core, c]).astype(jnp.int32)

    def deep(value):
        return value.reshape(BLOCKS, YLO, 1, rows, block)

    together = lax.optimization_barrier

    with jax.named_scope("side_in"):
        side = half_panel[main_pairs:].reshape(YLO, Z, rows, block)
        got = swap(lax.dynamic_index_in_dim(side, 1 - ylo, 0, keepdims=False), "ylo")
        keep = lax.dynamic_index_in_dim(side, ylo, 0, keepdims=False)
    picked = pick_columns(place, orbitals)
    own = half_panel[:main_pairs].reshape(COLS * YLO, depth, rows, block)
    own, got, keep, picked = together((own, got, keep, picked))

    with jax.named_scope("panels_in"):
        own = lax.all_to_all(own, PLANE, 0, 0, tiled=True)
        own = own.reshape(COLS, YLO, depth, rows, block)
    with jax.named_scope("side_in"):
        parts = rotate(join_and_spread(place, keep, got), "z")
        side_own = collect(AT_Z, place, parts)
    own, side_own, picked = together((own, side_own, picked))

    with jax.named_scope("mirror"):
        own_low = lax.all_to_all(own, "z", 0, 0, tiled=True)
    other = swap(own, "core")
    with jax.named_scope("side_mirror"):
        side_other = swap(side_own, "core")
        parts = rotate(spread(AT_C, place, side_own), SIDE)
        side_low = collect(AT_C, place, parts)
        side_other_low = swap(side_low, "core")
        side_partial = first_half(
            AT_C, place, deep(side_low), deep(side_other_low), deep(side_own), deep(side_other),
            picked, "first_half_side"
        )
    own_low, other, side_partial = together((own_low, other, side_partial))

    other_low = swap(own_low, "core")
    partial_value = first_half(AT_Z, place, own, other, own_low, other_low, picked, "first_half")
    with jax.named_scope("partial"):
        partial_value = lax.all_to_all(partial_value, "z", 0, 0, tiled=True)
    with jax.named_scope("side_partial"):
        parts = rotate(spread(AT_C, place, side_partial), SIDE)
        side_partial = collect(AT_C, place, parts)
        side_partial_other = swap(side_partial, "core")
        keep, send = second_half_side(place, side_partial, side_partial_other, picked)
    partial_value, keep, send = together((partial_value, keep, send))

    got = swap(send, "ylo")
    result = second_half(partial_value, orbitals)
    result, got, keep = together((result, got, keep))

    with jax.named_scope("panels_out"):
        result = result.reshape(COLS * YLO, depth, rows, block)
        result = lax.all_to_all(result, PLANE, 0, 0, tiled=True)
        result = result.reshape(main_pairs, rows, block)
    with jax.named_scope("side_out"):
        parts = rotate(join_and_spread(place, keep, got), "z")
    return finish(place, parts, result)


def solution(mesh):
    fine = Mesh(mesh.devices.reshape(Z, YLO, CORE, X, YHI), ("z", "ylo", "core", "x", "yhi"))
    spec = P(None, ("z", "ylo", "core"), ("x", "yhi"))
    return jax.shard_map(
        per_device, mesh=fine, in_specs=(spec, P()), out_specs=spec, check_vma=False
    )
```

profile of v0, /device:TPU:2, one launch (start us, length us, event | category | flops | bytes accessed | tf_op | source)
XLA Modules:
  0.0 158.0 jit_solution(6789309792426871774)
XLA Ops:
  0.0 1.1 slice.7
  1.1 1.7 %collective-permute-start = (bf16[8,64,256]{2,1,0:T(8,128)(2,1)S(1)}, bf16[8,64,256]{2,1,0:T(8,128)(2,1)S(1)}, u32[]{:S(2)}, u32[]{:S(2)}) collective-permute-start(bf16[8,64,256]{2,1,0:T(8,128)(2,1)S(1)} %get-tuple-element.106), channel_id=1, source_target_pairs={{0,16},{16,0},{1,17},{17,1},{2,18},{18,2},{3,19},{19,3},{4,20},{20... | collective-permute-start | bytes 786440 | tf_op jit(solution)/shard_map/side_in/ppermute | solution.py:348
  2.8 2.3 %slice.6 = bf16[32,64,256]{2,1,0:T(8,128)(2,1)} slice(bf16[48,64,256]{2,1,0:T(8,128)(2,1)} %param.2), slice={[0:32], [0:64], [0:256]} | slice | bytes 2097152 | tf_op jit(solution)/shard_map/slice | solution.py:371
  5.2 6.2 %pick_columns.1.c_hbm = bf16[2048,1024]{1,0:T(8,128)(2,1)} custom-call(s32[4]{0:T(128)S(1)} %pad_add_fusion.place, bf16[2048,2048]{1,0:T(8,128)(2,1)} %c_hbm.3), custom_call_target="tpu_custom_call" | custom-call | tf_op jit(solution)/shard_map/pick_columns/pallas_call | solution.py:100
  11.4 7.2 %all-to-all-start = ((bf16[16,2,64,256]{3,2,1,0:T(8,128)(2,1)}), bf16[16,2,64,256]{3,2,1,0:T(8,128)(2,1)}, u32[]{:S(2)}, u32[]{:S(2)}) async-start(bf16[16,2,64,256]{3,2,1,0:T(8,128)(2,1)} %bitcast.4), calls=%async_computation | async-start | bytes 2097152 | tf_op jit(solution)/shard_map/panels_in/all_to_all | solution.py:375
  18.6 0.6 join_and_spread.2
  19.2 2.0 %collective-permute-start.1 = (bf16[2,64,256]{2,1,0:T(8,128)(2,1)S(1)}, bf16[2,64,256]{2,1,0:T(8,128)(2,1)S(1)}, u32[]{:S(2)}, u32[]{:S(2)}) collective-permute-start(bf16[2,64,256]{2,1,0:T(8,128)(2,1)S(1)} %get-tuple-element.59), channel_id=1, source_target_pairs={{0,32},{32,64},{64,96},{96,128},{128,160},{160,192},{192,224},{224... | collective-permute-start | bytes 196616 | tf_op jit(solution)/shard_map/side_in/ppermute | solution.py:343
  21.2 3.3 %collective-permute-start.2 = (bf16[2,64,256]{2,1,0:T(8,128)(2,1)S(1)}, bf16[2,64,256]{2,1,0:T(8,128)(2,1)S(1)}, u32[]{:S(2)}, u32[]{:S(2)}) collective-permute-start(bf16[2,64,256]{2,1,0:T(8,128)(2,1)S(1)} %get-tuple-element.60), channel_id=1, source_target_pairs={{0,64},{32,96},{64,128},{96,160},{128,192},{160,224},{192,0},{224,... | collective-permute-start | bytes 196616 | tf_op jit(solution)/shard_map/side_in/ppermute | solution.py:343
  24.4 4.0 %collective-permute-start.3 = (bf16[2,64,256]{2,1,0:T(8,128)(2,1)S(1)}, bf16[2,64,256]{2,1,0:T(8,128)(2,1)S(1)}, u32[]{:S(2)}, u32[]{:S(2)}) collective-permute-start(bf16[2,64,256]{2,1,0:T(8,128)(2,1)S(1)} %get-tuple-element.61), channel_id=1, source_target_pairs={{0,96},{32,128},{64,160},{96,192},{128,224},{160,0},{192,32},{224,... | collective-permute-start | bytes 196616 | tf_op jit(solution)/shard_map/side_in/ppermute | solution.py:343
  29.0 4.9 %collective-permute-start.5 = (bf16[2,64,256]{2,1,0:T(8,128)(2,1)S(1)}, bf16[2,64,256]{2,1,0:T(8,128)(2,1)S(1)}, u32[]{:S(2)}, u32[]{:S(2)}) collective-permute-start(bf16[2,64,256]{2,1,0:T(8,128)(2,1)S(1)} %get-tuple-element.63), channel_id=1, source_target_pairs={{0,160},{32,192},{64,224},{96,0},{128,32},{160,64},{192,96},{224,1... | collective-permute-start | bytes 196616 | tf_op jit(solution)/shard_map/side_in/ppermute | solution.py:343
  34.0 2.7 %collective-permute-start.6 = (bf16[2,64,256]{2,1,0:T(8,128)(2,1)S(1)}, bf16[2,64,256]{2,1,0:T(8,128)(2,1)S(1)}, u32[]{:S(2)}, u32[]{:S(2)}) collective-permute-start(bf16[2,64,256]{2,1,0:T(8,128)(2,1)S(1)} %get-tuple-element.64), channel_id=1, source_target_pairs={{0,192},{32,224},{64,0},{96,32},{128,64},{160,96},{192,128},{224,1... | collective-permute-start | bytes 196616 | tf_op jit(solution)/shard_map/side_in/ppermute | solution.py:343
  36.6 1.0 collective-permute-start.7
  37.7 4.0 %collective-permute-done.5.refs_5_ = bf16[2,64,256]{2,1,0:T(8,128)(2,1)S(1)} collective-permute-done((bf16[2,64,256]{2,1,0:T(8,128)(2,1)S(1)}, bf16[2,64,256]{2,1,0:T(8,128)(2,1)S(1)}, u32[]{:S(2)}, u32[]{:S(2)}) %collective-permute-start.5) | collective-permute-done | bytes 65568 | tf_op jit(solution)/shard_map/side_in/ppermute | solution.py:343
  41.7 0.7 collective-permute-done.6.refs_6_
  42.4 0.6 collective-permute-done.7.refs_7_
  43.0 0.6 collect.3.x_ref
  43.6 4.5 %all-to-all-start.1 = ((bf16[8,2,2,64,256]{4,3,2,1,0:T(8,128)(2,1)}), bf16[8,2,2,64,256]{4,3,2,1,0:T(8,128)(2,1)S(1)}, u32[]{:S(2)}, u32[]{:S(2)}) async-start(bf16[8,2,2,64,256]{4,3,2,1,0:T(8,128)(2,1)} %bitcast.8.direct), calls=%async_computation.1 | async-start | bytes 2097152 | tf_op jit(solution)/shard_map/mirror/all_to_all | solution.py:383
  48.1 0.6 spread.2
  48.7 3.0 %collective-permute-start.9 = (bf16[2,64,256]{2,1,0:T(8,128)(2,1)S(1)}, bf16[2,64,256]{2,1,0:T(8,128)(2,1)S(1)}, u32[]{:S(2)}, u32[]{:S(2)}) collective-permute-start(bf16[2,64,256]{2,1,0:T(8,128)(2,1)S(1)} %get-tuple-element.70), channel_id=1, source_target_pairs={{0,1},{1,2},{2,3},{3,4},{4,5},{5,6},{6,7},{7,0},{8,9},{9,10},{10,1... | collective-permute-start | bytes 196616 | tf_op jit(solution)/shard_map/side_mirror/ppermute | solution.py:343
  51.8 1.5 collective-permute-start.10
  53.2 0.8 collective-permute-start.11
  54.0 2.8 %collective-permute-start.12 = (bf16[2,64,256]{2,1,0:T(8,128)(2,1)S(1)}, bf16[2,64,256]{2,1,0:T(8,128)(2,1)S(1)}, u32[]{:S(2)}, u32[]{:S(2)}) collective-permute-start(bf16[2,64,256]{2,1,0:T(8,128)(2,1)S(1)} %get-tuple-element.73), channel_id=1, source_target_pairs={{0,4},{1,5},{2,6},{3,7},{4,0},{5,1},{6,2},{7,3},{8,12},{9,13},{10,... | collective-permute-start | bytes 196616 | tf_op jit(solution)/shard_map/side_mirror/ppermute | solution.py:343
  56.8 3.6 %collective-permute-start.13 = (bf16[2,64,256]{2,1,0:T(8,128)(2,1)S(1)}, bf16[2,64,256]{2,1,0:T(8,128)(2,1)S(1)}, u32[]{:S(2)}, u32[]{:S(2)}) collective-permute-start(bf16[2,64,256]{2,1,0:T(8,128)(2,1)S(1)} %get-tuple-element.74), channel_id=1, source_target_pairs={{0,5},{1,6},{2,7},{3,0},{4,1},{5,2},{6,3},{7,4},{8,13},{9,14},{10,... | collective-permute-start | bytes 196616 | tf_op jit(solution)/shard_map/side_mirror/ppermute | solution.py:343
  60.4 2.1 %collective-permute-start.14 = (bf16[2,64,256]{2,1,0:T(8,128)(2,1)S(1)}, bf16[2,64,256]{2,1,0:T(8,128)(2,1)S(1)}, u32[]{:S(2)}, u32[]{:S(2)}) collective-permute-start(bf16[2,64,256]{2,1,0:T(8,128)(2,1)S(1)} %get-tuple-element.75), channel_id=1, source_target_pairs={{0,6},{1,7},{2,0},{3,1},{4,2},{5,3},{6,4},{7,5},{8,14},{9,15},{10,... | collective-permute-start | bytes 196616 | tf_op jit(solution)/shard_map/side_mirror/ppermute | solution.py:343
  62.4 0.7 collective-permute-start.15
  63.1 1.5 collective-permute-done.13.refs_5_
  64.6 0.7 collective-permute-done.14.refs_6_
  65.3 2.9 %collective-permute-done.15.refs_7_ = bf16[2,64,256]{2,1,0:T(8,128)(2,1)S(1)} collective-permute-done((bf16[2,64,256]{2,1,0:T(8,128)(2,1)S(1)}, bf16[2,64,256]{2,1,0:T(8,128)(2,1)S(1)}, u32[]{:S(2)}, u32[]{:S(2)}) %collective-permute-start.15) | collective-permute-done | bytes 65568 | tf_op jit(solution)/shard_map/side_mirror/ppermute | solution.py:343
  68.2 0.6 collect.4
  68.9 1.9 %collective-permute-done.16 = bf16[8,2,64,256]{3,2,1,0:T(8,128)(2,1)S(1)} collective-permute-done((bf16[8,2,64,256]{3,2,1,0:T(8,128)(2,1)S(1)}, bf16[8,2,64,256]{3,2,1,0:T(8,128)(2,1)S(1)}, u32[]{:S(2)}, u32[]{:S(2)}) %collective-permute-start.16) | collective-permute-done | bytes 524320 | tf_op jit(solution)/shard_map/side_mirror/ppermute | solution.py:348
  70.8 4.0 %first_half_side.1.x_ref = bf16[8,1,256,128]{3,2,1,0:T(8,128)(2,1)S(1)} custom-call(s32[4]{0:T(128)S(1)} %pad_add_fusion.place, bf16[8,2,1,64,256]{4,3,2,1,0:T(8,128)(2,1)S(1)} %bitcast.19, bf16[8,2,1,64,256]{4,3,2,1,0:T(8,128)(2,1)S(1)} %bitcast.21, bf16[8,2,1,64,256]{4,3,2,1,0:T(8,128)(2,1)S(1)} %bitcast.17, bf16[8,2,1,64,256]{4,3,2,1,0:T(8,128)(2,1)S(1)} %bitcast.20, ...), custom_call_target="tpu_custom_call" | custom-call | tf_op jit(solution)/shard_map/side_mirror/first_half_side/pallas_call | solution.py:164
  74.8 1.4 all-to-all-done.1.turned
  76.2 2.6 %collective-permute-done.18.turned_other = bf16[8,2,2,64,256]{4,3,2,1,0:T(8,128)(2,1)S(1)} collective-permute-done((bf16[8,2,2,64,256]{4,3,2,1,0:T(8,128)(2,1)S(1)}, bf16[8,2,2,64,256]{4,3,2,1,0:T(8,128)(2,1)S(1)}, u32[]{:S(2)}, u32[]{:S(2)}) %collective-permute-start.18) | collective-permute-done | bytes 1048608 | tf_op jit(solution)/shard_map/ppermute | solution.py:348
  78.9 6.8 %first_half.1 = bf16[8,2,256,128]{3,2,1,0:T(8,128)(2,1)} custom-call(s32[4]{0:T(128)S(1)} %pad_add_fusion.place, bf16[8,2,2,64,256]{4,3,2,1,0:T(8,128)(2,1)} %bitcast.8.direct, bf16[8,2,2,64,256]{4,3,2,1,0:T(8,128)(2,1)S(1)} %collective-permute-done.8.direct_other, bf16[8,2,2,64,256]{4,3,2,1,0:T(8,128)(2,1)S(1)} %all-to-all-done.1.turned, ...), custom_call_target="tpu_custom_call" | custom-call | tf_op jit(solution)/shard_map/first_half/pallas_call | solution.py:164
  85.7 6.7 %all-to-all-start.2 = ((bf16[8,2,256,128]{3,2,1,0:T(8,128)(2,1)}), bf16[8,2,256,128]{3,2,1,0:T(8,128)(2,1)S(1)}, u32[]{:S(2)}, u32[]{:S(2)}) async-start(bf16[8,2,256,128]{3,2,1,0:T(8,128)(2,1)} %first_half.1), calls=%async_computation.2 | async-start | bytes 2097152 | tf_op jit(solution)/shard_map/partial/all_to_all | solution.py:399
  92.4 0.6 spread.3
  93.0 1.3 collective-permute-start.19
  94.3 1.6 %collective-permute-start.20 = (bf16[1,256,128]{2,1,0:T(8,128)(2,1)S(1)}, bf16[1,256,128]{2,1,0:T(8,128)(2,1)S(1)}, u32[]{:S(2)}, u32[]{:S(2)}) collective-permute-start(bf16[1,256,128]{2,1,0:T(8,128)(2,1)S(1)} %get-tuple-element.83), channel_id=1, source_target_pairs={{0,2},{1,3},{2,4},{3,5},{4,6},{5,7},{6,0},{7,1},{8,10},{9,11},{10,... | collective-permute-start | bytes 196616 | tf_op jit(solution)/shard_map/side_partial/ppermute | solution.py:343
  95.9 3.4 %collective-permute-start.21 = (bf16[1,256,128]{2,1,0:T(8,128)(2,1)S(1)}, bf16[1,256,128]{2,1,0:T(8,128)(2,1)S(1)}, u32[]{:S(2)}, u32[]{:S(2)}) collective-permute-start(bf16[1,256,128]{2,1,0:T(8,128)(2,1)S(1)} %get-tuple-element.84), channel_id=1, source_target_pairs={{0,3},{1,4},{2,5},{3,6},{4,7},{5,0},{6,1},{7,2},{8,11},{9,12},{10,... | collective-permute-start | bytes 196616 | tf_op jit(solution)/shard_map/side_partial/ppermute | solution.py:343
  99.3 1.4 collective-permute-start.22
  100.7 3.1 %collective-permute-start.23 = (bf16[1,256,128]{2,1,0:T(8,128)(2,1)S(1)}, bf16[1,256,128]{2,1,0:T(8,128)(2,1)S(1)}, u32[]{:S(2)}, u32[]{:S(2)}) collective-permute-start(bf16[1,256,128]{2,1,0:T(8,128)(2,1)S(1)} %get-tuple-element.86), channel_id=1, source_target_pairs={{0,5},{1,6},{2,7},{3,0},{4,1},{5,2},{6,3},{7,4},{8,13},{9,14},{10,... | collective-permute-start | bytes 196616 | tf_op jit(solution)/shard_map/side_partial/ppermute | solution.py:343
  103.8 2.6 %collective-permute-start.24 = (bf16[1,256,128]{2,1,0:T(8,128)(2,1)S(1)}, bf16[1,256,128]{2,1,0:T(8,128)(2,1)S(1)}, u32[]{:S(2)}, u32[]{:S(2)}) collective-permute-start(bf16[1,256,128]{2,1,0:T(8,128)(2,1)S(1)} %get-tuple-element.87), channel_id=1, source_target_pairs={{0,6},{1,7},{2,0},{3,1},{4,2},{5,3},{6,4},{7,5},{8,14},{9,15},{10,... | collective-permute-start | bytes 196616 | tf_op jit(solution)/shard_map/side_partial/ppermute | solution.py:343
  106.5 1.1 collective-permute-done.23.refs_5_
  107.6 1.6 collective-permute-done.24.refs_6_
  109.2 3.0 %collective-permute-done.25.refs_7_ = bf16[1,256,128]{2,1,0:T(8,128)(2,1)S(1)} collective-permute-done((bf16[1,256,128]{2,1,0:T(8,128)(2,1)S(1)}, bf16[1,256,128]{2,1,0:T(8,128)(2,1)S(1)}, u32[]{:S(2)}, u32[]{:S(2)}) %collective-permute-start.25) | collective-permute-done | bytes 65568 | tf_op jit(solution)/shard_map/side_partial/ppermute | solution.py:343
  112.2 0.6 collect.5.t_ref
  112.9 1.9 %collective-permute-done.26.other_ref = bf16[8,1,256,128]{3,2,1,0:T(8,128)(2,1)S(1)} collective-permute-done((bf16[8,1,256,128]{3,2,1,0:T(8,128)(2,1)S(1)}, bf16[8,1,256,128]{3,2,1,0:T(8,128)(2,1)S(1)}, u32[]{:S(2)}, u32[]{:S(2)}) %collective-permute-start.26) | collective-permute-done | bytes 524320 | tf_op jit(solution)/shard_map/side_partial/ppermute | solution.py:348
  114.8 4.7 %second_half_side.1 = (bf16[8,64,256]{2,1,0:T(8,128)(2,1)S(1)}, bf16[8,64,256]{2,1,0:T(8,128)(2,1)S(1)}) custom-call(s32[4]{0:T(128)S(1)} %pad_add_fusion.place, bf16[8,1,256,128]{3,2,1,0:T(8,128)(2,1)S(1)} %collect.5.t_ref, bf16[8,1,256,128]{3,2,1,0:T(8,128)(2,1)S(1)} %collective-permute-done.26.other_ref, bf16[2048,1024]{1,0:T(8,128)(2,1)} %pick_columns.1.c_hbm), custom_call_target="tpu_custom_call" | custom-call | tf_op jit(solution)/shard_map/side_partial/second_half_side/pallas_call | solution.py:250
  119.5 2.0 %all-to-all-done.2.t_ref = bf16[8,2,256,128]{3,2,1,0:T(8,128)(2,1)S(1)} async-done(((bf16[8,2,256,128]{3,2,1,0:T(8,128)(2,1)}), bf16[8,2,256,128]{3,2,1,0:T(8,128)(2,1)S(1)}, u32[]{:S(2)}, u32[]{:S(2)}) %all-to-all-start.2) | async-done | bytes 1048608 | tf_op jit(solution)/shard_map/partial/all_to_all | solution.py:399
  121.5 0.6 collective-permute-start.27
  122.0 6.4 %second_half.1 = bf16[8,2,2,64,256]{4,3,2,1,0:T(8,128)(2,1)} custom-call(bf16[8,2,256,128]{3,2,1,0:T(8,128)(2,1)S(1)} %all-to-all-done.2.t_ref, bf16[2048,2048]{1,0:T(8,128)(2,1)} %c_hbm.3), custom_call_target="tpu_custom_call" | custom-call | tf_op jit(solution)/shard_map/second_half/pallas_call | solution.py:203
  128.4 1.3 collective-permute-done.27.got
  129.7 6.7 %all-to-all-start.3 = ((bf16[16,2,64,256]{3,2,1,0:T(8,128)(2,1)}), bf16[16,2,64,256]{3,2,1,0:T(8,128)(2,1)S(1)}, u32[]{:S(2)}, u32[]{:S(2)}) async-start(bf16[16,2,64,256]{3,2,1,0:T(8,128)(2,1)} %bitcast.13), calls=%async_computation.3 | async-start | bytes 2097152 | tf_op jit(solution)/shard_map/panels_out/all_to_all | solution.py:413
  136.4 0.6 join_and_spread.3
  137.1 0.9 collective-permute-start.29
  137.9 2.7 %collective-permute-start.30 = (bf16[2,64,256]{2,1,0:T(8,128)(2,1)S(1)}, bf16[2,64,256]{2,1,0:T(8,128)(2,1)S(1)}, u32[]{:S(2)}, u32[]{:S(2)}) collective-permute-start(bf16[2,64,256]{2,1,0:T(8,128)(2,1)S(1)} %get-tuple-element.99), channel_id=1, source_target_pairs={{0,96},{32,128},{64,160},{96,192},{128,224},{160,0},{192,32},{224,... | collective-permute-start | bytes 196616 | tf_op jit(solution)/shard_map/side_out/ppermute | solution.py:343
  140.6 2.9 %collective-permute-start.31 = (bf16[2,64,256]{2,1,0:T(8,128)(2,1)S(1)}, bf16[2,64,256]{2,1,0:T(8,128)(2,1)S(1)}, u32[]{:S(2)}, u32[]{:S(2)}) collective-permute-start(bf16[2,64,256]{2,1,0:T(8,128)(2,1)S(1)} %get-tuple-element.100), channel_id=1, source_target_pairs={{0,128},{32,160},{64,192},{96,224},{128,0},{160,32},{192,64},{224,... | collective-permute-start | bytes 196616 | tf_op jit(solution)/shard_map/side_out/ppermute | solution.py:343
  143.6 2.1 %collective-permute-start.32 = (bf16[2,64,256]{2,1,0:T(8,128)(2,1)S(1)}, bf16[2,64,256]{2,1,0:T(8,128)(2,1)S(1)}, u32[]{:S(2)}, u32[]{:S(2)}) collective-permute-start(bf16[2,64,256]{2,1,0:T(8,128)(2,1)S(1)} %get-tuple-element.101), channel_id=1, source_target_pairs={{0,160},{32,192},{64,224},{96,0},{128,32},{160,64},{192,96},{224,1... | collective-permute-start | bytes 196616 | tf_op jit(solution)/shard_map/side_out/ppermute | solution.py:343
  145.7 3.6 %collective-permute-start.33 = (bf16[2,64,256]{2,1,0:T(8,128)(2,1)S(1)}, bf16[2,64,256]{2,1,0:T(8,128)(2,1)S(1)}, u32[]{:S(2)}, u32[]{:S(2)}) collective-permute-start(bf16[2,64,256]{2,1,0:T(8,128)(2,1)S(1)} %get-tuple-element.102), channel_id=1, source_target_pairs={{0,192},{32,224},{64,0},{96,32},{128,64},{160,96},{192,128},{224,1... | collective-permute-start | bytes 196616 | tf_op jit(solution)/shard_map/side_out/ppermute | solution.py:343
  149.2 1.5 collective-permute-start.34
  150.7 1.4 collective-permute-done.32.refs_5_
  152.1 3.5 %collective-permute-done.33.refs_6_ = bf16[2,64,256]{2,1,0:T(8,128)(2,1)S(1)} collective-permute-done((bf16[2,64,256]{2,1,0:T(8,128)(2,1)S(1)}, bf16[2,64,256]{2,1,0:T(8,128)(2,1)S(1)}, u32[]{:S(2)}, u32[]{:S(2)}) %collective-permute-start.33) | collective-permute-done | bytes 65568 | tf_op jit(solution)/shard_map/side_out/ppermute | solution.py:343
  155.6 0.7 collective-permute-done.34.refs_7_
  156.3 1.8 %finish.1 = bf16[48,64,256]{2,1,0:T(8,128)(2,1)} custom-call(s32[4]{0:T(128)S(1)} %pad_add_fusion.place, bf16[2,64,256]{2,1,0:T(8,128)(2,1)S(1)} %get-tuple-element.96.refs_0_, bf16[2,64,256]{2,1,0:T(8,128)(2,1)S(1)} %collective-permute-done.28.refs_1_, bf16[2,64,256]{2,1,0:T(8,128)(2,1)S(1)} %collective-permute-done.29.refs_2_, ...), custom_call_target="tpu_custom_call" | custom-call | tf_op jit(solution)/shard_map/finish/pallas_call | solution.py:330
  (31 shorter events, 1.1 us)
Async XLA Ops:
  1.1 10.2 %collective-permute-start = (bf16[8,64,256]{2,1,0:T(8,128)(2,1)S(1)}, bf16[8,64,256]{2,1,0:T(8,128)(2,1)S(1)}, u32[]{:S(2)}, u32[]{:S(2)}) collective-permute-start(bf16[8,64,256]{2,1,0:T(8,128)(2,1)S(1)} %get-tuple-element.106), channel_id=1, source_target_pairs={{0,16},{16,0},{1,17},{17,1},{2,18},{18,2},{3,19},{19,3},{4,20},{20... | collective-permute-start | bytes 786440 | tf_op jit(solution)/shard_map/side_in/ppermute | solution.py:348
  11.4 32.2 %all-to-all-start = ((bf16[16,2,64,256]{3,2,1,0:T(8,128)(2,1)}), bf16[16,2,64,256]{3,2,1,0:T(8,128)(2,1)}, u32[]{:S(2)}, u32[]{:S(2)}) async-start(bf16[16,2,64,256]{3,2,1,0:T(8,128)(2,1)} %bitcast.4), calls=%async_computation | async-start | bytes 2097152 | tf_op jit(solution)/shard_map/panels_in/all_to_all | solution.py:375
  19.2 14.8 %collective-permute-start.1 = (bf16[2,64,256]{2,1,0:T(8,128)(2,1)S(1)}, bf16[2,64,256]{2,1,0:T(8,128)(2,1)S(1)}, u32[]{:S(2)}, u32[]{:S(2)}) collective-permute-start(bf16[2,64,256]{2,1,0:T(8,128)(2,1)S(1)} %get-tuple-element.59), channel_id=1, source_target_pairs={{0,32},{32,64},{64,96},{96,128},{128,160},{160,192},{192,224},{224... | collective-permute-start | bytes 196616 | tf_op jit(solution)/shard_map/side_in/ppermute | solution.py:343
  21.2 15.5 %collective-permute-start.2 = (bf16[2,64,256]{2,1,0:T(8,128)(2,1)S(1)}, bf16[2,64,256]{2,1,0:T(8,128)(2,1)S(1)}, u32[]{:S(2)}, u32[]{:S(2)}) collective-permute-start(bf16[2,64,256]{2,1,0:T(8,128)(2,1)S(1)} %get-tuple-element.60), channel_id=1, source_target_pairs={{0,64},{32,96},{64,128},{96,160},{128,192},{160,224},{192,0},{224,... | collective-permute-start | bytes 196616 | tf_op jit(solution)/shard_map/side_in/ppermute | solution.py:343
  24.4 13.2 %collective-permute-start.3 = (bf16[2,64,256]{2,1,0:T(8,128)(2,1)S(1)}, bf16[2,64,256]{2,1,0:T(8,128)(2,1)S(1)}, u32[]{:S(2)}, u32[]{:S(2)}) collective-permute-start(bf16[2,64,256]{2,1,0:T(8,128)(2,1)S(1)} %get-tuple-element.61), channel_id=1, source_target_pairs={{0,96},{32,128},{64,160},{96,192},{128,224},{160,0},{192,32},{224,... | collective-permute-start | bytes 196616 | tf_op jit(solution)/shard_map/side_in/ppermute | solution.py:343
  28.5 9.2 %collective-permute-start.4 = (bf16[2,64,256]{2,1,0:T(8,128)(2,1)S(1)}, bf16[2,64,256]{2,1,0:T(8,128)(2,1)S(1)}, u32[]{:S(2)}, u32[]{:S(2)}) collective-permute-start(bf16[2,64,256]{2,1,0:T(8,128)(2,1)S(1)} %get-tuple-element.62), channel_id=1, source_target_pairs={{0,128},{32,160},{64,192},{96,224},{128,0},{160,32},{192,64},{224,... | collective-permute-start | bytes 196616 | tf_op jit(solution)/shard_map/side_in/ppermute | solution.py:343
  29.0 12.7 %collective-permute-start.5 = (bf16[2,64,256]{2,1,0:T(8,128)(2,1)S(1)}, bf16[2,64,256]{2,1,0:T(8,128)(2,1)S(1)}, u32[]{:S(2)}, u32[]{:S(2)}) collective-permute-start(bf16[2,64,256]{2,1,0:T(8,128)(2,1)S(1)} %get-tuple-element.63), channel_id=1, source_target_pairs={{0,160},{32,192},{64,224},{96,0},{128,32},{160,64},{192,96},{224,1... | collective-permute-start | bytes 196616 | tf_op jit(solution)/shard_map/side_in/ppermute | solution.py:343
  34.0 8.4 %collective-permute-start.6 = (bf16[2,64,256]{2,1,0:T(8,128)(2,1)S(1)}, bf16[2,64,256]{2,1,0:T(8,128)(2,1)S(1)}, u32[]{:S(2)}, u32[]{:S(2)}) collective-permute-start(bf16[2,64,256]{2,1,0:T(8,128)(2,1)S(1)} %get-tuple-element.64), channel_id=1, source_target_pairs={{0,192},{32,224},{64,0},{96,32},{128,64},{160,96},{192,128},{224,1... | collective-permute-start | bytes 196616 | tf_op jit(solution)/shard_map/side_in/ppermute | solution.py:343
  36.6 6.4 %collective-permute-start.7 = (bf16[2,64,256]{2,1,0:T(8,128)(2,1)S(1)}, bf16[2,64,256]{2,1,0:T(8,128)(2,1)S(1)}, u32[]{:S(2)}, u32[]{:S(2)}) collective-permute-start(bf16[2,64,256]{2,1,0:T(8,128)(2,1)S(1)} %get-tuple-element.65), channel_id=1, source_target_pairs={{0,224},{32,0},{64,32},{96,64},{128,96},{160,128},{192,160},{224,1... | collective-permute-start | bytes 196616 | tf_op jit(solution)/shard_map/side_in/ppermute | solution.py:343
  43.6 32.6 %all-to-all-start.1 = ((bf16[8,2,2,64,256]{4,3,2,1,0:T(8,128)(2,1)}), bf16[8,2,2,64,256]{4,3,2,1,0:T(8,128)(2,1)S(1)}, u32[]{:S(2)}, u32[]{:S(2)}) async-start(bf16[8,2,2,64,256]{4,3,2,1,0:T(8,128)(2,1)} %bitcast.8.direct), calls=%async_computation.1 | async-start | bytes 2097152 | tf_op jit(solution)/shard_map/mirror/all_to_all | solution.py:383
  48.1 26.7 %collective-permute-start.8 = (bf16[8,2,2,64,256]{4,3,2,1,0:T(8,128)(2,1)}, bf16[8,2,2,64,256]{4,3,2,1,0:T(8,128)(2,1)S(1)}, u32[]{:S(2)}, u32[]{:S(2)}) collective-permute-start(bf16[8,2,2,64,256]{4,3,2,1,0:T(8,128)(2,1)} %bitcast.8.direct), channel_id=1, source_target_pairs={{0,8},{8,0},{1,9},{9,1},{2,10},{10,2},{3,11},{11,3},{4,12},{12,4},... | collective-permute-start | bytes 3145736 | tf_op jit(solution)/shard_map/ppermute | solution.py:348
  48.7 8.0 %collective-permute-start.9 = (bf16[2,64,256]{2,1,0:T(8,128)(2,1)S(1)}, bf16[2,64,256]{2,1,0:T(8,128)(2,1)S(1)}, u32[]{:S(2)}, u32[]{:S(2)}) collective-permute-start(bf16[2,64,256]{2,1,0:T(8,128)(2,1)S(1)} %get-tuple-element.70), channel_id=1, source_target_pairs={{0,1},{1,2},{2,3},{3,4},{4,5},{5,6},{6,7},{7,0},{8,9},{9,10},{10,1... | collective-permute-start | bytes 196616 | tf_op jit(solution)/shard_map/side_mirror/ppermute | solution.py:343
  51.8 8.6 %collective-permute-start.10 = (bf16[2,64,256]{2,1,0:T(8,128)(2,1)S(1)}, bf16[2,64,256]{2,1,0:T(8,128)(2,1)S(1)}, u32[]{:S(2)}, u32[]{:S(2)}) collective-permute-start(bf16[2,64,256]{2,1,0:T(8,128)(2,1)S(1)} %get-tuple-element.71), channel_id=1, source_target_pairs={{0,2},{1,3},{2,4},{3,5},{4,6},{5,7},{6,0},{7,1},{8,10},{9,11},{10,... | collective-permute-start | bytes 196616 | tf_op jit(solution)/shard_map/side_mirror/ppermute | solution.py:343
  53.2 9.2 %collective-permute-start.11 = (bf16[2,64,256]{2,1,0:T(8,128)(2,1)S(1)}, bf16[2,64,256]{2,1,0:T(8,128)(2,1)S(1)}, u32[]{:S(2)}, u32[]{:S(2)}) collective-permute-start(bf16[2,64,256]{2,1,0:T(8,128)(2,1)S(1)} %get-tuple-element.72), channel_id=1, source_target_pairs={{0,3},{1,4},{2,5},{3,6},{4,7},{5,0},{6,1},{7,2},{8,11},{9,12},{10,... | collective-permute-start | bytes 196616 | tf_op jit(solution)/shard_map/side_mirror/ppermute | solution.py:343
  54.0 9.1 %collective-permute-start.12 = (bf16[2,64,256]{2,1,0:T(8,128)(2,1)S(1)}, bf16[2,64,256]{2,1,0:T(8,128)(2,1)S(1)}, u32[]{:S(2)}, u32[]{:S(2)}) collective-permute-start(bf16[2,64,256]{2,1,0:T(8,128)(2,1)S(1)} %get-tuple-element.73), channel_id=1, source_target_pairs={{0,4},{1,5},{2,6},{3,7},{4,0},{5,1},{6,2},{7,3},{8,12},{9,13},{10,... | collective-permute-start | bytes 196616 | tf_op jit(solution)/shard_map/side_mirror/ppermute | solution.py:343
  56.8 7.8 %collective-permute-start.13 = (bf16[2,64,256]{2,1,0:T(8,128)(2,1)S(1)}, bf16[2,64,256]{2,1,0:T(8,128)(2,1)S(1)}, u32[]{:S(2)}, u32[]{:S(2)}) collective-permute-start(bf16[2,64,256]{2,1,0:T(8,128)(2,1)S(1)} %get-tuple-element.74), channel_id=1, source_target_pairs={{0,5},{1,6},{2,7},{3,0},{4,1},{5,2},{6,3},{7,4},{8,13},{9,14},{10,... | collective-permute-start | bytes 196616 | tf_op jit(solution)/shard_map/side_mirror/ppermute | solution.py:343
  60.4 5.0 %collective-permute-start.14 = (bf16[2,64,256]{2,1,0:T(8,128)(2,1)S(1)}, bf16[2,64,256]{2,1,0:T(8,128)(2,1)S(1)}, u32[]{:S(2)}, u32[]{:S(2)}) collective-permute-start(bf16[2,64,256]{2,1,0:T(8,128)(2,1)S(1)} %get-tuple-element.75), channel_id=1, source_target_pairs={{0,6},{1,7},{2,0},{3,1},{4,2},{5,3},{6,4},{7,5},{8,14},{9,15},{10,... | collective-permute-start | bytes 196616 | tf_op jit(solution)/shard_map/side_mirror/ppermute | solution.py:343
  62.4 5.8 %collective-permute-start.15 = (bf16[2,64,256]{2,1,0:T(8,128)(2,1)S(1)}, bf16[2,64,256]{2,1,0:T(8,128)(2,1)S(1)}, u32[]{:S(2)}, u32[]{:S(2)}) collective-permute-start(bf16[2,64,256]{2,1,0:T(8,128)(2,1)S(1)} %get-tuple-element.76), channel_id=1, source_target_pairs={{0,7},{1,0},{2,1},{3,2},{4,3},{5,4},{6,5},{7,6},{8,15},{9,8},{10,9... | collective-permute-start | bytes 196616 | tf_op jit(solution)/shard_map/side_mirror/ppermute | solution.py:343
  63.1 5.8 %collective-permute-start.17 = (bf16[8,2,64,256]{3,2,1,0:T(8,128)(2,1)S(1)}, bf16[8,2,64,256]{3,2,1,0:T(8,128)(2,1)S(1)}, u32[]{:S(2)}, u32[]{:S(2)}) collective-permute-start(bf16[8,2,64,256]{3,2,1,0:T(8,128)(2,1)S(1)} %collect.3.x_ref), channel_id=1, source_target_pairs={{0,8},{8,0},{1,9},{9,1},{2,10},{10,2},{3,11},{11,3},{4,12},{12,4},... | collective-permute-start | bytes 1572872 | tf_op jit(solution)/shard_map/side_mirror/ppermute | solution.py:348
  68.8 2.0 %collective-permute-start.16 = (bf16[8,2,64,256]{3,2,1,0:T(8,128)(2,1)S(1)}, bf16[8,2,64,256]{3,2,1,0:T(8,128)(2,1)S(1)}, u32[]{:S(2)}, u32[]{:S(2)}) collective-permute-start(bf16[8,2,64,256]{3,2,1,0:T(8,128)(2,1)S(1)} %collect.4), channel_id=1, source_target_pairs={{0,8},{8,0},{1,9},{9,1},{2,10},{10,2},{3,11},{11,3},{4,12},{12,4},... | collective-permute-start | bytes 1572872 | tf_op jit(solution)/shard_map/side_mirror/ppermute | solution.py:348
  76.2 2.7 %collective-permute-start.18 = (bf16[8,2,2,64,256]{4,3,2,1,0:T(8,128)(2,1)S(1)}, bf16[8,2,2,64,256]{4,3,2,1,0:T(8,128)(2,1)S(1)}, u32[]{:S(2)}, u32[]{:S(2)}) collective-permute-start(bf16[8,2,2,64,256]{4,3,2,1,0:T(8,128)(2,1)S(1)} %all-to-all-done.1.turned), channel_id=1, source_target_pairs={{0,8},{8,0},{1,9},{9,1},{2,10},{10,2},{3,11},{11,3},{4,12},{12,4},... | collective-permute-start | bytes 3145736 | tf_op jit(solution)/shard_map/ppermute | solution.py:348
  85.7 35.8 %all-to-all-start.2 = ((bf16[8,2,256,128]{3,2,1,0:T(8,128)(2,1)}), bf16[8,2,256,128]{3,2,1,0:T(8,128)(2,1)S(1)}, u32[]{:S(2)}, u32[]{:S(2)}) async-start(bf16[8,2,256,128]{3,2,1,0:T(8,128)(2,1)} %first_half.1), calls=%async_computation.2 | async-start | bytes 2097152 | tf_op jit(solution)/shard_map/partial/all_to_all | solution.py:399
  93.0 10.8 %collective-permute-start.19 = (bf16[1,256,128]{2,1,0:T(8,128)(2,1)S(1)}, bf16[1,256,128]{2,1,0:T(8,128)(2,1)S(1)}, u32[]{:S(2)}, u32[]{:S(2)}) collective-permute-start(bf16[1,256,128]{2,1,0:T(8,128)(2,1)S(1)} %get-tuple-element.82), channel_id=1, source_target_pairs={{0,1},{1,2},{2,3},{3,4},{4,5},{5,6},{6,7},{7,0},{8,9},{9,10},{10,1... | collective-permute-start | bytes 196616 | tf_op jit(solution)/shard_map/side_partial/ppermute | solution.py:343
  94.3 12.1 %collective-permute-start.20 = (bf16[1,256,128]{2,1,0:T(8,128)(2,1)S(1)}, bf16[1,256,128]{2,1,0:T(8,128)(2,1)S(1)}, u32[]{:S(2)}, u32[]{:S(2)}) collective-permute-start(bf16[1,256,128]{2,1,0:T(8,128)(2,1)S(1)} %get-tuple-element.83), channel_id=1, source_target_pairs={{0,2},{1,3},{2,4},{3,5},{4,6},{5,7},{6,0},{7,1},{8,10},{9,11},{10,... | collective-permute-start | bytes 196616 | tf_op jit(solution)/shard_map/side_partial/ppermute | solution.py:343
  95.9 10.6 %collective-permute-start.21 = (bf16[1,256,128]{2,1,0:T(8,128)(2,1)S(1)}, bf16[1,256,128]{2,1,0:T(8,128)(2,1)S(1)}, u32[]{:S(2)}, u32[]{:S(2)}) collective-permute-start(bf16[1,256,128]{2,1,0:T(8,128)(2,1)S(1)} %get-tuple-element.84), channel_id=1, source_target_pairs={{0,3},{1,4},{2,5},{3,6},{4,7},{5,0},{6,1},{7,2},{8,11},{9,12},{10,... | collective-permute-start | bytes 196616 | tf_op jit(solution)/shard_map/side_partial/ppermute | solution.py:343
  99.3 7.2 %collective-permute-start.22 = (bf16[1,256,128]{2,1,0:T(8,128)(2,1)S(1)}, bf16[1,256,128]{2,1,0:T(8,128)(2,1)S(1)}, u32[]{:S(2)}, u32[]{:S(2)}) collective-permute-start(bf16[1,256,128]{2,1,0:T(8,128)(2,1)S(1)} %get-tuple-element.85), channel_id=1, source_target_pairs={{0,4},{1,5},{2,6},{3,7},{4,0},{5,1},{6,2},{7,3},{8,12},{9,13},{10,... | collective-permute-start | bytes 196616 | tf_op jit(solution)/shard_map/side_partial/ppermute | solution.py:343
  100.7 6.9 %collective-permute-start.23 = (bf16[1,256,128]{2,1,0:T(8,128)(2,1)S(1)}, bf16[1,256,128]{2,1,0:T(8,128)(2,1)S(1)}, u32[]{:S(2)}, u32[]{:S(2)}) collective-permute-start(bf16[1,256,128]{2,1,0:T(8,128)(2,1)S(1)} %get-tuple-element.86), channel_id=1, source_target_pairs={{0,5},{1,6},{2,7},{3,0},{4,1},{5,2},{6,3},{7,4},{8,13},{9,14},{10,... | collective-permute-start | bytes 196616 | tf_op jit(solution)/shard_map/side_partial/ppermute | solution.py:343
  103.8 5.4 %collective-permute-start.24 = (bf16[1,256,128]{2,1,0:T(8,128)(2,1)S(1)}, bf16[1,256,128]{2,1,0:T(8,128)(2,1)S(1)}, u32[]{:S(2)}, u32[]{:S(2)}) collective-permute-start(bf16[1,256,128]{2,1,0:T(8,128)(2,1)S(1)} %get-tuple-element.87), channel_id=1, source_target_pairs={{0,6},{1,7},{2,0},{3,1},{4,2},{5,3},{6,4},{7,5},{8,14},{9,15},{10,... | collective-permute-start | bytes 196616 | tf_op jit(solution)/shard_map/side_partial/ppermute | solution.py:343
  106.4 5.8 %collective-permute-start.25 = (bf16[1,256,128]{2,1,0:T(8,128)(2,1)S(1)}, bf16[1,256,128]{2,1,0:T(8,128)(2,1)S(1)}, u32[]{:S(2)}, u32[]{:S(2)}) collective-permute-start(bf16[1,256,128]{2,1,0:T(8,128)(2,1)S(1)} %get-tuple-element.88), channel_id=1, source_target_pairs={{0,7},{1,0},{2,1},{3,2},{4,3},{5,4},{6,5},{7,6},{8,15},{9,8},{10,9... | collective-permute-start | bytes 196616 | tf_op jit(solution)/shard_map/side_partial/ppermute | solution.py:343
  112.8 2.0 %collective-permute-start.26 = (bf16[8,1,256,128]{3,2,1,0:T(8,128)(2,1)S(1)}, bf16[8,1,256,128]{3,2,1,0:T(8,128)(2,1)S(1)}, u32[]{:S(2)}, u32[]{:S(2)}) collective-permute-start(bf16[8,1,256,128]{3,2,1,0:T(8,128)(2,1)S(1)} %collect.5.t_ref), channel_id=1, source_target_pairs={{0,8},{8,0},{1,9},{9,1},{2,10},{10,2},{3,11},{11,3},{4,12},{12,4},... | collective-permute-start | bytes 1572872 | tf_op jit(solution)/shard_map/side_partial/ppermute | solution.py:348
  121.5 8.2 %collective-permute-start.27 = (bf16[8,64,256]{2,1,0:T(8,128)(2,1)S(1)}, bf16[8,64,256]{2,1,0:T(8,128)(2,1)S(1)}, u32[]{:S(2)}, u32[]{:S(2)}) collective-permute-start(bf16[8,64,256]{2,1,0:T(8,128)(2,1)S(1)} %get-tuple-element.92), channel_id=1, source_target_pairs={{0,16},{16,0},{1,17},{17,1},{2,18},{18,2},{3,19},{19,3},{4,20},{20... | collective-permute-start | bytes 786440 | tf_op jit(solution)/shard_map/ppermute | solution.py:348
  129.7 26.6 %all-to-all-start.3 = ((bf16[16,2,64,256]{3,2,1,0:T(8,128)(2,1)}), bf16[16,2,64,256]{3,2,1,0:T(8,128)(2,1)S(1)}, u32[]{:S(2)}, u32[]{:S(2)}) async-start(bf16[16,2,64,256]{3,2,1,0:T(8,128)(2,1)} %bitcast.13), calls=%async_computation.3 | async-start | bytes 2097152 | tf_op jit(solution)/shard_map/panels_out/all_to_all | solution.py:413
  137.0 8.7 %collective-permute-start.28 = (bf16[2,64,256]{2,1,0:T(8,128)(2,1)S(1)}, bf16[2,64,256]{2,1,0:T(8,128)(2,1)S(1)}, u32[]{:S(2)}, u32[]{:S(2)}) collective-permute-start(bf16[2,64,256]{2,1,0:T(8,128)(2,1)S(1)} %get-tuple-element.97), channel_id=1, source_target_pairs={{0,32},{32,64},{64,96},{96,128},{128,160},{160,192},{192,224},{224... | collective-permute-start | bytes 196616 | tf_op jit(solution)/shard_map/side_out/ppermute | solution.py:343
  137.1 12.2 %collective-permute-start.29 = (bf16[2,64,256]{2,1,0:T(8,128)(2,1)S(1)}, bf16[2,64,256]{2,1,0:T(8,128)(2,1)S(1)}, u32[]{:S(2)}, u32[]{:S(2)}) collective-permute-start(bf16[2,64,256]{2,1,0:T(8,128)(2,1)S(1)} %get-tuple-element.98), channel_id=1, source_target_pairs={{0,64},{32,96},{64,128},{96,160},{128,192},{160,224},{192,0},{224,... | collective-permute-start | bytes 196616 | tf_op jit(solution)/shard_map/side_out/ppermute | solution.py:343
  137.9 12.8 %collective-permute-start.30 = (bf16[2,64,256]{2,1,0:T(8,128)(2,1)S(1)}, bf16[2,64,256]{2,1,0:T(8,128)(2,1)S(1)}, u32[]{:S(2)}, u32[]{:S(2)}) collective-permute-start(bf16[2,64,256]{2,1,0:T(8,128)(2,1)S(1)} %get-tuple-element.99), channel_id=1, source_target_pairs={{0,96},{32,128},{64,160},{96,192},{128,224},{160,0},{192,32},{224,... | collective-permute-start | bytes 196616 | tf_op jit(solution)/shard_map/side_out/ppermute | solution.py:343
  140.6 10.1 %collective-permute-start.31 = (bf16[2,64,256]{2,1,0:T(8,128)(2,1)S(1)}, bf16[2,64,256]{2,1,0:T(8,128)(2,1)S(1)}, u32[]{:S(2)}, u32[]{:S(2)}) collective-permute-start(bf16[2,64,256]{2,1,0:T(8,128)(2,1)S(1)} %get-tuple-element.100), channel_id=1, source_target_pairs={{0,128},{32,160},{64,192},{96,224},{128,0},{160,32},{192,64},{224,... | collective-permute-start | bytes 196616 | tf_op jit(solution)/shard_map/side_out/ppermute | solution.py:343
  143.6 8.5 %collective-permute-start.32 = (bf16[2,64,256]{2,1,0:T(8,128)(2,1)S(1)}, bf16[2,64,256]{2,1,0:T(8,128)(2,1)S(1)}, u32[]{:S(2)}, u32[]{:S(2)}) collective-permute-start(bf16[2,64,256]{2,1,0:T(8,128)(2,1)S(1)} %get-tuple-element.101), channel_id=1, source_target_pairs={{0,160},{32,192},{64,224},{96,0},{128,32},{160,64},{192,96},{224,1... | collective-permute-start | bytes 196616 | tf_op jit(solution)/shard_map/side_out/ppermute | solution.py:343
  145.7 9.9 %collective-permute-start.33 = (bf16[2,64,256]{2,1,0:T(8,128)(2,1)S(1)}, bf16[2,64,256]{2,1,0:T(8,128)(2,1)S(1)}, u32[]{:S(2)}, u32[]{:S(2)}) collective-permute-start(bf16[2,64,256]{2,1,0:T(8,128)(2,1)S(1)} %get-tuple-element.102), channel_id=1, source_target_pairs={{0,192},{32,224},{64,0},{96,32},{128,64},{160,96},{192,128},{224,1... | collective-permute-start | bytes 196616 | tf_op jit(solution)/shard_map/side_out/ppermute | solution.py:343
  149.2 7.0 %collective-permute-start.34 = (bf16[2,64,256]{2,1,0:T(8,128)(2,1)S(1)}, bf16[2,64,256]{2,1,0:T(8,128)(2,1)S(1)}, u32[]{:S(2)}, u32[]{:S(2)}) collective-permute-start(bf16[2,64,256]{2,1,0:T(8,128)(2,1)S(1)} %get-tuple-element.103), channel_id=1, source_target_pairs={{0,224},{32,0},{64,32},{96,64},{128,96},{160,128},{192,160},{224,1... | collective-permute-start | bytes 196616 | tf_op jit(solution)/shard_map/side_out/ppermute | solution.py:343
where the time goes:
time: 159 us; the launch traced here: 158 us
  starting transfers between devices  87.7 us (55%)
  Pallas kernels  34 us (21%)
  waiting for transfers between devices  32.7 us (21%)
  local copies, waits for them, and re-layouts  3.43 us (2%)
    ppermute x28, starting transfers between devices, rotate(): lax.ppermute(parts[d], axes, [(i, (i + d) % BLOCKS) for i in range(BLOCKS)])  60.1 us
    ppermute x28, waiting for transfers between devices, rotate(): lax.ppermute(parts[d], axes, [(i, (i + d) % BLOCKS) for i in range(BLOCKS)])  21.7 us
    pallas_call x2, Pallas kernels, first_half(): pl.pallas_call(functools.partial(first_kernel, index), out_shape=jax.Shap...  10.8 us
    ppermute x7, waiting for transfers between devices, swap(): return lax.ppermute(value, axis, [(0, 1), (1, 0)])  7.71 us
    all_to_all x1, starting transfers between devices, per_device(): own = lax.all_to_all(own, PLANE, 0, 0, tiled=True)  7.2 us
    all_to_all x1, starting transfers between devices, per_device(): partial_value = lax.all_to_all(partial_value, 'z', 0, 0, tiled=True)  6.71 us
    all_to_all x1, starting transfers between devices, per_device(): result = lax.all_to_all(result, PLANE, 0, 0, tiled=True)  6.69 us
    pallas_call x1, Pallas kernels, second_half(): pl.pallas_call(second_kernel, out_shape=jax.ShapeDtypeStruct((COLS, YLO,...  6.38 us
  transfers between devices with their start and end apart: 39, of which 18 were waited for; matrix products, arithmetic and copies ran while one was open for 2% of the time, Pallas kernels for 16%

commit v1 on v0

--- a/solution.py
+++ b/solution.py
@@ -19,6 +19,7 @@
 SMALL = pltpu.CompilerParams(vmem_limit_bytes=8 * 2**20)
 
 
+ORDER = {AT_Z: (0, 4, 3, 5, 2, 6, 1, 7), AT_C: (0, 3, 5, 1, 7, 4, 2, 6)}
 STEPS = 4
 HBM = pl.BlockSpec(memory_space=pltpu.HBM)
 
@@ -109,8 +110,9 @@
     )(place, in_hbm(orbitals))
 
 
-def first_kernel(index, place, direct, direct_other, turned, turned_other, c_hbm, t_ref,
-                 c_ref, sems, sym, turn, total):
+def first_kernel(index, place, direct, direct_other, turned, turned_other, c_hbm, *rest):
+    t_refs = rest[:-5]
+    c_ref, sems, sym, turn, total = rest[-5:]
     _, _, depth, rows, block = direct.shape
     mine, core = place[index], place[AT_CORE]
     per_step = BLOCKS // STEPS
@@ -151,21 +153,27 @@
         total[...] += jnp.dot(sym[...], c_ref[step], preferred_element_type=F32)
 
     steps(c_hbm, c_ref, sems, work)
-    lanes = t_ref.shape[3]
-    for part in range(t_ref.shape[0]):
-        for k in range(depth):
-            t_ref[part, k] = total[k * block:(k + 1) * block, part * lanes:(part + 1) * lanes].astype(BF16)
-
-
-def first_half(index, place, direct, direct_other, turned, turned_other, picked, name):
+    if len(t_refs) == 1:
+        lanes = t_refs[0].shape[3]
+        for part in range(BLOCKS):
+            for k in range(depth):
+                t_refs[0][part, k] = total[k * block:(k + 1) * block, part * lanes:(part + 1) * lanes].astype(BF16)
+    else:
+        lanes = t_refs[0].shape[2]
+        for d in range(BLOCKS):
+            part = (mine + ORDER[index][d]) % BLOCKS
+            t_refs[d][0] = total[:, pl.ds(pl.multiple_of(part * lanes, lanes), lanes)].astype(BF16)
+
+
+def first_half(index, place, direct, direct_other, turned, turned_other, picked, outs, name):
     _, _, depth, rows, block = direct.shape
     size, width = picked.shape
     vmem = pl.BlockSpec(memory_space=pltpu.VMEM)
     return pl.pallas_call(
         functools.partial(first_kernel, index),
-        out_shape=jax.ShapeDtypeStruct((BLOCKS, depth, block, width // BLOCKS), BF16),
+        out_shape=[jax.ShapeDtypeStruct(out, BF16) for out in outs],
         in_specs=[pl.BlockSpec(memory_space=pltpu.SMEM), vmem, vmem, vmem, vmem, HBM],
-        out_specs=vmem,
+        out_specs=[vmem] * len(outs),
         scratch_shapes=fetch_scratch(picked) + [
             pltpu.VMEM((depth * block, size // STEPS), BF16),
             pltpu.VMEM((depth * block, block), BF16),
@@ -263,7 +271,7 @@
 
 def spread_kernel(index, place, x_ref, *out_refs):
     for d in range(BLOCKS):
-        out_refs[d][...] = x_ref[(place[index] + d) % BLOCKS]
+        out_refs[d][...] = x_ref[(place[index] + ORDER[index][d]) % BLOCKS]
 
 
 def spread(index, place, value):
@@ -281,8 +289,8 @@
 def join_kernel(place, keep, got, *out_refs):
     z, ylo = place[AT_Z], place[AT_YLO]
     for d in range(BLOCKS):
-        out_refs[d][ylo] = keep[(z + d) % BLOCKS]
-        out_refs[d][1 - ylo] = got[(z + d) % BLOCKS]
+        out_refs[d][ylo] = keep[(z + ORDER[AT_Z][d]) % BLOCKS]
+        out_refs[d][1 - ylo] = got[(z + ORDER[AT_Z][d]) % BLOCKS]
 
 
 def join_and_spread(place, keep, got):
@@ -300,7 +308,7 @@
 def collect_kernel(index, place, *refs):
     out_ref = refs[BLOCKS]
     for d in range(BLOCKS):
-        out_ref[(place[index] + BLOCKS - d) % BLOCKS] = refs[d][...]
+        out_ref[(place[index] + BLOCKS - ORDER[index][d]) % BLOCKS] = refs[d][...]
 
 
 def collect(index, place, parts):
@@ -316,12 +324,17 @@
 
 
 def finish_kernel(place, *refs):
-    main_ref, out_ref = refs[BLOCKS:]
+    main_ref, out_hbm, sems = refs[BLOCKS:]
     main = main_ref.shape[0]
-    out_ref[:main] = main_ref[...]
+    copies = [pltpu.make_async_copy(main_ref, out_hbm.at[pl.ds(0, main)], sems.at[BLOCKS * YLO])]
     for d in range(BLOCKS):
         for y in range(YLO):
-            out_ref[main + y * BLOCKS + (place[AT_Z] + BLOCKS - d) % BLOCKS] = refs[d][y]
+            to = main + y * BLOCKS + (place[AT_Z] + BLOCKS - ORDER[AT_Z][d]) % BLOCKS
+            copies.append(pltpu.make_async_copy(refs[d].at[y], out_hbm.at[to], sems.at[d * YLO + y]))
+    for copy in copies:
+        copy.start()
+    for copy in copies:
+        copy.wait()
 
 
 def finish(place, parts, main):
@@ -331,16 +344,17 @@
         finish_kernel,
         out_shape=jax.ShapeDtypeStruct((pairs + YLO * BLOCKS, rows, block), BF16),
         in_specs=[pl.BlockSpec(memory_space=pltpu.SMEM)] + [vmem] * (BLOCKS + 1),
-        out_specs=vmem,
+        out_specs=HBM,
+        scratch_shapes=[pltpu.SemaphoreType.DMA((BLOCKS * YLO + 1,))],
         compiler_params=SMALL,
         name="finish",
     )(place, *parts, main)
 
 
-def rotate(parts, axes):
+def rotate(index, parts, axes):
     out = [parts[0]]
-    for d in range(1, BLOCKS):
-        out.append(lax.ppermute(parts[d], axes, [(i, (i + d) % BLOCKS) for i in range(BLOCKS)]))
+    for part, d in zip(parts[1:], ORDER[index][1:]):
+        out.append(lax.ppermute(part, axes, [(i, (i + d) % BLOCKS) for i in range(BLOCKS)]))
     return out
 
 
@@ -375,7 +389,7 @@
         own = lax.all_to_all(own, PLANE, 0, 0, tiled=True)
         own = own.reshape(COLS, YLO, depth, rows, block)
     with jax.named_scope("side_in"):
-        parts = rotate(join_and_spread(place, keep, got), "z")
+        parts = rotate(AT_Z, join_and_spread(place, keep, got), "z")
         side_own = collect(AT_Z, place, parts)
     own, side_own, picked = together((own, side_own, picked))
 
@@ -384,27 +398,30 @@
     other = swap(own, "core")
     with jax.named_scope("side_mirror"):
         side_other = swap(side_own, "core")
-        parts = rotate(spread(AT_C, place, side_own), SIDE)
+        parts = rotate(AT_C, spread(AT_C, place, side_own), SIDE)
         side_low = collect(AT_C, place, parts)
         side_other_low = swap(side_low, "core")
         side_partial = first_half(
             AT_C, place, deep(side_low), deep(side_other_low), deep(side_own), deep(side_other),
-            picked, "first_half_side"
+            picked, [(1, block, block // CORE)] * BLOCKS, "first_half_side"
         )
     own_low, other, side_partial = together((own_low, other, side_partial))
 
     other_low = swap(own_low, "core")
-    partial_value = first_half(AT_Z, place, own, other, own_low, other_low, picked, "first_half")
+    partial_value, = first_half(
+        AT_Z, place, own, other, own_low, other_low, picked,
+        [(BLOCKS, depth, block, block // CORE)], "first_half"
+    )
     with jax.named_scope("partial"):
         partial_value = lax.all_to_all(partial_value, "z", 0, 0, tiled=True)
     with jax.named_scope("side_partial"):
-        parts = rotate(spread(AT_C, place, side_partial), SIDE)
+        parts = rotate(AT_C, side_partial, SIDE)
         side_partial = collect(AT_C, place, parts)
         side_partial_other = swap(side_partial, "core")
         keep, send = second_half_side(place, side_partial, side_partial_other, picked)
-    partial_value, keep, send = together((partial_value, keep, send))
-
     got = swap(send, "ylo")
+    partial_value, keep = together((partial_value, keep))
+
     result = second_half(partial_value, orbitals)
     result, got, keep = together((result, got, keep))
 
@@ -413,7 +430,7 @@
         result = lax.all_to_all(result, PLANE, 0, 0, tiled=True)
         result = result.reshape(main_pairs, rows, block)
     with jax.named_scope("side_out"):
-        parts = rotate(join_and_spread(place, keep, got), "z")
+        parts = rotate(AT_Z, join_and_spread(place, keep, got), "z")
     return finish(place, parts, result)
 
 

time: 159 us -> 156 us (0.981)
  waiting for transfers between devices: 32.7 us -> 20.9 us
  starting transfers between devices: 87.7 us -> 96.7 us
    ppermute x28, waiting for transfers between devices: 21.7 us -> 12.2 us  [rotate(): lax.ppermute(part, axes, [(i, (i + d) % BLOCKS) for i in range(BLOCKS)])]
    ppermute x28, starting transfers between devices: 60.1 us -> 66.7 us  [rotate(): lax.ppermute(part, axes, [(i, (i + d) % BLOCKS) for i in range(BLOCKS)])]
where the time goes in v1:
time: 156 us; the launch traced here: 155 us
  starting transfers between devices  96.7 us (62%)
  Pallas kernels  33.5 us (21%)
  waiting for transfers between devices  20.9 us (13%)
  local copies, waits for them, and re-layouts  3.43 us (2%)
    ppermute x28, starting transfers between devices, rotate(): lax.ppermute(part, axes, [(i, (i + d) % BLOCKS) for i in range(BLOCKS)])  66.7 us
    ppermute x28, waiting for transfers between devices, rotate(): lax.ppermute(part, axes, [(i, (i + d) % BLOCKS) for i in range(BLOCKS)])  12.2 us
    pallas_call x2, Pallas kernels, first_half(): pl.pallas_call(functools.partial(first_kernel, index), out_shape=[jax.Sha...  10.9 us
    all_to_all x1, starting transfers between devices, per_device(): result = lax.all_to_all(result, PLANE, 0, 0, tiled=True)  8.2 us
    all_to_all x1, starting transfers between devices, per_device(): own = lax.all_to_all(own, PLANE, 0, 0, tiled=True)  7.2 us
    ppermute x7, waiting for transfers between devices, swap(): return lax.ppermute(value, axis, [(0, 1), (1, 0)])  6.45 us
    all_to_all x1, starting transfers between devices, per_device(): partial_value = lax.all_to_all(partial_value, 'z', 0, 0, tiled=True)  6.44 us
    pallas_call x1, Pallas kernels, second_half(): pl.pallas_call(second_kernel, out_shape=jax.ShapeDtypeStruct((COLS, YLO,...  6.38 us
  transfers between devices with their start and end apart: 39, of which 18 were waited for; matrix products, arithmetic and copies ran while one was open for 2% of the time, Pallas kernels for 16%

profile of v1, /device:TPU:2, one launch (start us, length us, event | category | flops | bytes accessed | tf_op | source)
XLA Modules:
  0.0 155.0 jit_solution(3473517865658262472)
XLA Ops:
  0.0 1.1 slice.7
  1.1 1.7 %collective-permute-start = (bf16[8,64,256]{2,1,0:T(8,128)(2,1)S(1)}, bf16[8,64,256]{2,1,0:T(8,128)(2,1)S(1)}, u32[]{:S(2)}, u32[]{:S(2)}) collective-permute-start(bf16[8,64,256]{2,1,0:T(8,128)(2,1)S(1)} %get-tuple-element.118), channel_id=1, source_target_pairs={{0,16},{16,0},{1,17},{17,1},{2,18},{18,2},{3,19},{19,3},{4,20},{20... | collective-permute-start | bytes 786440 | tf_op jit(solution)/shard_map/side_in/ppermute | solution.py:362
  2.8 2.3 %slice.6 = bf16[32,64,256]{2,1,0:T(8,128)(2,1)} slice(bf16[48,64,256]{2,1,0:T(8,128)(2,1)} %param.2), slice={[0:32], [0:64], [0:256]} | slice | bytes 2097152 | tf_op jit(solution)/shard_map/slice | solution.py:385
  5.2 6.2 %pick_columns.1.c_hbm = bf16[2048,1024]{1,0:T(8,128)(2,1)} custom-call(s32[4]{0:T(128)S(1)} %pad_add_fusion.place, bf16[2048,2048]{1,0:T(8,128)(2,1)} %c_hbm.3), custom_call_target="tpu_custom_call" | custom-call | tf_op jit(solution)/shard_map/pick_columns/pallas_call | solution.py:101
  11.4 7.2 %all-to-all-start = ((bf16[16,2,64,256]{3,2,1,0:T(8,128)(2,1)}), bf16[16,2,64,256]{3,2,1,0:T(8,128)(2,1)}, u32[]{:S(2)}, u32[]{:S(2)}) async-start(bf16[16,2,64,256]{3,2,1,0:T(8,128)(2,1)} %bitcast.4), calls=%async_computation | async-start | bytes 2097152 | tf_op jit(solution)/shard_map/panels_in/all_to_all | solution.py:389
  18.6 0.6 join_and_spread.2
  19.2 7.3 %collective-permute-start.1 = (bf16[2,64,256]{2,1,0:T(8,128)(2,1)S(1)}, bf16[2,64,256]{2,1,0:T(8,128)(2,1)S(1)}, u32[]{:S(2)}, u32[]{:S(2)}) collective-permute-start(bf16[2,64,256]{2,1,0:T(8,128)(2,1)S(1)} %get-tuple-element.65), channel_id=1, source_target_pairs={{0,128},{32,160},{64,192},{96,224},{128,0},{160,32},{192,64},{224,... | collective-permute-start | bytes 196616 | tf_op jit(solution)/shard_map/side_in/ppermute | solution.py:357
  26.5 1.9 %collective-permute-start.2 = (bf16[2,64,256]{2,1,0:T(8,128)(2,1)S(1)}, bf16[2,64,256]{2,1,0:T(8,128)(2,1)S(1)}, u32[]{:S(2)}, u32[]{:S(2)}) collective-permute-start(bf16[2,64,256]{2,1,0:T(8,128)(2,1)S(1)} %get-tuple-element.66), channel_id=1, source_target_pairs={{0,96},{32,128},{64,160},{96,192},{128,224},{160,0},{192,32},{224,... | collective-permute-start | bytes 196616 | tf_op jit(solution)/shard_map/side_in/ppermute | solution.py:357
  28.4 3.1 %collective-permute-start.3 = (bf16[2,64,256]{2,1,0:T(8,128)(2,1)S(1)}, bf16[2,64,256]{2,1,0:T(8,128)(2,1)S(1)}, u32[]{:S(2)}, u32[]{:S(2)}) collective-permute-start(bf16[2,64,256]{2,1,0:T(8,128)(2,1)S(1)} %get-tuple-element.67), channel_id=1, source_target_pairs={{0,160},{32,192},{64,224},{96,0},{128,32},{160,64},{192,96},{224,1... | collective-permute-start | bytes 196616 | tf_op jit(solution)/shard_map/side_in/ppermute | solution.py:357
  31.5 1.5 collective-permute-start.4
  33.0 2.7 %collective-permute-start.5 = (bf16[2,64,256]{2,1,0:T(8,128)(2,1)S(1)}, bf16[2,64,256]{2,1,0:T(8,128)(2,1)S(1)}, u32[]{:S(2)}, u32[]{:S(2)}) collective-permute-start(bf16[2,64,256]{2,1,0:T(8,128)(2,1)S(1)} %get-tuple-element.69), channel_id=1, source_target_pairs={{0,192},{32,224},{64,0},{96,32},{128,64},{160,96},{192,128},{224,1... | collective-permute-start | bytes 196616 | tf_op jit(solution)/shard_map/side_in/ppermute | solution.py:357
  35.6 1.0 collective-permute-start.6
  36.7 0.1 collective-permute-done.2.refs_2_
  36.8 2.1 %collective-permute-start.7 = (bf16[2,64,256]{2,1,0:T(8,128)(2,1)S(1)}, bf16[2,64,256]{2,1,0:T(8,128)(2,1)S(1)}, u32[]{:S(2)}, u32[]{:S(2)}) collective-permute-start(bf16[2,64,256]{2,1,0:T(8,128)(2,1)S(1)} %get-tuple-element.71), channel_id=1, source_target_pairs={{0,224},{32,0},{64,32},{96,64},{128,96},{160,128},{192,160},{224,1... | collective-permute-start | bytes 196616 | tf_op jit(solution)/shard_map/side_in/ppermute | solution.py:357
  38.9 0.7 collective-permute-done.5.refs_5_
  39.6 1.5 collective-permute-done.6.refs_6_
  41.1 0.6 collect.3.x_ref
  41.7 4.5 %all-to-all-start.1 = ((bf16[8,2,2,64,256]{4,3,2,1,0:T(8,128)(2,1)}), bf16[8,2,2,64,256]{4,3,2,1,0:T(8,128)(2,1)S(1)}, u32[]{:S(2)}, u32[]{:S(2)}) async-start(bf16[8,2,2,64,256]{4,3,2,1,0:T(8,128)(2,1)} %bitcast.8.direct), calls=%async_computation.1 | async-start | bytes 2097152 | tf_op jit(solution)/shard_map/mirror/all_to_all | solution.py:397
  46.3 0.6 spread.1
  46.8 3.9 %collective-permute-start.9 = (bf16[2,64,256]{2,1,0:T(8,128)(2,1)S(1)}, bf16[2,64,256]{2,1,0:T(8,128)(2,1)S(1)}, u32[]{:S(2)}, u32[]{:S(2)}) collective-permute-start(bf16[2,64,256]{2,1,0:T(8,128)(2,1)S(1)} %get-tuple-element.76), channel_id=1, source_target_pairs={{0,3},{1,4},{2,5},{3,6},{4,7},{5,0},{6,1},{7,2},{8,11},{9,12},{10,... | collective-permute-start | bytes 196616 | tf_op jit(solution)/shard_map/side_mirror/ppermute | solution.py:357
  50.8 2.1 %collective-permute-start.10 = (bf16[2,64,256]{2,1,0:T(8,128)(2,1)S(1)}, bf16[2,64,256]{2,1,0:T(8,128)(2,1)S(1)}, u32[]{:S(2)}, u32[]{:S(2)}) collective-permute-start(bf16[2,64,256]{2,1,0:T(8,128)(2,1)S(1)} %get-tuple-element.77), channel_id=1, source_target_pairs={{0,5},{1,6},{2,7},{3,0},{4,1},{5,2},{6,3},{7,4},{8,13},{9,14},{10,... | collective-permute-start | bytes 196616 | tf_op jit(solution)/shard_map/side_mirror/ppermute | solution.py:357
  52.9 1.5 collective-permute-start.11
  54.3 3.0 %collective-permute-start.12 = (bf16[2,64,256]{2,1,0:T(8,128)(2,1)S(1)}, bf16[2,64,256]{2,1,0:T(8,128)(2,1)S(1)}, u32[]{:S(2)}, u32[]{:S(2)}) collective-permute-start(bf16[2,64,256]{2,1,0:T(8,128)(2,1)S(1)} %get-tuple-element.79), channel_id=1, source_target_pairs={{0,7},{1,0},{2,1},{3,2},{4,3},{5,4},{6,5},{7,6},{8,15},{9,8},{10,9... | collective-permute-start | bytes 196616 | tf_op jit(solution)/shard_map/side_mirror/ppermute | solution.py:357
  57.3 2.1 %collective-permute-start.13 = (bf16[2,64,256]{2,1,0:T(8,128)(2,1)S(1)}, bf16[2,64,256]{2,1,0:T(8,128)(2,1)S(1)}, u32[]{:S(2)}, u32[]{:S(2)}) collective-permute-start(bf16[2,64,256]{2,1,0:T(8,128)(2,1)S(1)} %get-tuple-element.80), channel_id=1, source_target_pairs={{0,4},{1,5},{2,6},{3,7},{4,0},{5,1},{6,2},{7,3},{8,12},{9,13},{10,... | collective-permute-start | bytes 196616 | tf_op jit(solution)/shard_map/side_mirror/ppermute | solution.py:357
  59.4 1.0 collective-permute-start.14
  60.4 1.0 collective-permute-start.15
  61.4 2.1 %collective-permute-done.13.refs_5_ = bf16[2,64,256]{2,1,0:T(8,128)(2,1)S(1)} collective-permute-done((bf16[2,64,256]{2,1,0:T(8,128)(2,1)S(1)}, bf16[2,64,256]{2,1,0:T(8,128)(2,1)S(1)}, u32[]{:S(2)}, u32[]{:S(2)}) %collective-permute-start.13) | collective-permute-done | bytes 65568 | tf_op jit(solution)/shard_map/side_mirror/ppermute | solution.py:357
  63.5 0.2 collective-permute-done.14.refs_6_
  63.8 0.9 collective-permute-done.15.refs_7_
  64.6 0.6 collect.4
  65.3 1.9 %collective-permute-done.16 = bf16[8,2,64,256]{3,2,1,0:T(8,128)(2,1)S(1)} collective-permute-done((bf16[8,2,64,256]{3,2,1,0:T(8,128)(2,1)S(1)}, bf16[8,2,64,256]{3,2,1,0:T(8,128)(2,1)S(1)}, u32[]{:S(2)}, u32[]{:S(2)}) %collective-permute-start.16) | collective-permute-done | bytes 524320 | tf_op jit(solution)/shard_map/side_mirror/ppermute | solution.py:362
  67.2 4.1 %first_half_side.1 = (bf16[1,256,128]{2,1,0:T(8,128)(2,1)S(1)}, bf16[1,256,128]{2,1,0:T(8,128)(2,1)S(1)}, bf16[1,256,128]{2,1,0:T(8,128)(2,1)S(1)}, bf16[1,256,1...) custom-call(s32[4]{0:T(128)S(1)} %pad_add_fusion.place, ...), custom_call_target="tpu_custom_call" | custom-call | tf_op jit(solution)/shard_map/side_mirror/first_half_side/pallas_call | solution.py:172
  71.4 1.6 %all-to-all-done.1.turned = bf16[8,2,2,64,256]{4,3,2,1,0:T(8,128)(2,1)S(1)} async-done(((bf16[8,2,2,64,256]{4,3,2,1,0:T(8,128)(2,1)}), bf16[8,2,2,64,256]{4,3,2,1,0:T(8,128)(2,1)S(1)}, u32[]{:S(2)}, u32[]{:S(2)}) %all-to-all-start.1) | async-done | bytes 1048608 | tf_op jit(solution)/shard_map/mirror/all_to_all | solution.py:397
  73.0 2.7 %collective-permute-done.18.turned_other = bf16[8,2,2,64,256]{4,3,2,1,0:T(8,128)(2,1)S(1)} collective-permute-done((bf16[8,2,2,64,256]{4,3,2,1,0:T(8,128)(2,1)S(1)}, bf16[8,2,2,64,256]{4,3,2,1,0:T(8,128)(2,1)S(1)}, u32[]{:S(2)}, u32[]{:S(2)}) %collective-permute-start.18) | collective-permute-done | bytes 1048608 | tf_op jit(solution)/shard_map/ppermute | solution.py:362
  75.7 6.8 %first_half.1 = bf16[8,2,256,128]{3,2,1,0:T(8,128)(2,1)} custom-call(s32[4]{0:T(128)S(1)} %pad_add_fusion.place, bf16[8,2,2,64,256]{4,3,2,1,0:T(8,128)(2,1)} %bitcast.8.direct, bf16[8,2,2,64,256]{4,3,2,1,0:T(8,128)(2,1)S(1)} %collective-permute-done.8.direct_other, bf16[8,2,2,64,256]{4,3,2,1,0:T(8,128)(2,1)S(1)} %all-to-all-done.1.turned, ...), custom_call_target="tpu_custom_call" | custom-call | tf_op jit(solution)/shard_map/first_half/pallas_call | solution.py:172
  82.4 6.4 %all-to-all-start.2 = ((bf16[8,2,256,128]{3,2,1,0:T(8,128)(2,1)}), bf16[8,2,256,128]{3,2,1,0:T(8,128)(2,1)S(1)}, u32[]{:S(2)}, u32[]{:S(2)}) async-start(bf16[8,2,256,128]{3,2,1,0:T(8,128)(2,1)} %first_half.1), calls=%async_computation.2 | async-start | bytes 2097152 | tf_op jit(solution)/shard_map/partial/all_to_all | solution.py:416
  88.9 2.0 %collective-permute-start.19 = (bf16[1,256,128]{2,1,0:T(8,128)(2,1)S(1)}, bf16[1,256,128]{2,1,0:T(8,128)(2,1)S(1)}, u32[]{:S(2)}, u32[]{:S(2)}) collective-permute-start(bf16[1,256,128]{2,1,0:T(8,128)(2,1)S(1)} %get-tuple-element.95), channel_id=1, source_target_pairs={{0,3},{1,4},{2,5},{3,6},{4,7},{5,0},{6,1},{7,2},{8,11},{9,12},{10,... | collective-permute-start | bytes 196616 | tf_op jit(solution)/shard_map/side_partial/ppermute | solution.py:357
  90.9 3.9 %collective-permute-start.20 = (bf16[1,256,128]{2,1,0:T(8,128)(2,1)S(1)}, bf16[1,256,128]{2,1,0:T(8,128)(2,1)S(1)}, u32[]{:S(2)}, u32[]{:S(2)}) collective-permute-start(bf16[1,256,128]{2,1,0:T(8,128)(2,1)S(1)} %get-tuple-element.96), channel_id=1, source_target_pairs={{0,5},{1,6},{2,7},{3,0},{4,1},{5,2},{6,3},{7,4},{8,13},{9,14},{10,... | collective-permute-start | bytes 196616 | tf_op jit(solution)/shard_map/side_partial/ppermute | solution.py:357
  94.8 1.7 %collective-permute-start.21 = (bf16[1,256,128]{2,1,0:T(8,128)(2,1)S(1)}, bf16[1,256,128]{2,1,0:T(8,128)(2,1)S(1)}, u32[]{:S(2)}, u32[]{:S(2)}) collective-permute-start(bf16[1,256,128]{2,1,0:T(8,128)(2,1)S(1)} %get-tuple-element.97), channel_id=1, source_target_pairs={{0,1},{1,2},{2,3},{3,4},{4,5},{5,6},{6,7},{7,0},{8,9},{9,10},{10,1... | collective-permute-start | bytes 196616 | tf_op jit(solution)/shard_map/side_partial/ppermute | solution.py:357
  96.5 2.8 %collective-permute-start.22 = (bf16[1,256,128]{2,1,0:T(8,128)(2,1)S(1)}, bf16[1,256,128]{2,1,0:T(8,128)(2,1)S(1)}, u32[]{:S(2)}, u32[]{:S(2)}) collective-permute-start(bf16[1,256,128]{2,1,0:T(8,128)(2,1)S(1)} %get-tuple-element.98), channel_id=1, source_target_pairs={{0,7},{1,0},{2,1},{3,2},{4,3},{5,4},{6,5},{7,6},{8,15},{9,8},{10,9... | collective-permute-start | bytes 196616 | tf_op jit(solution)/shard_map/side_partial/ppermute | solution.py:357
  99.3 4.6 %collective-permute-start.23 = (bf16[1,256,128]{2,1,0:T(8,128)(2,1)S(1)}, bf16[1,256,128]{2,1,0:T(8,128)(2,1)S(1)}, u32[]{:S(2)}, u32[]{:S(2)}) collective-permute-start(bf16[1,256,128]{2,1,0:T(8,128)(2,1)S(1)} %get-tuple-element.99), channel_id=1, source_target_pairs={{0,4},{1,5},{2,6},{3,7},{4,0},{5,1},{6,2},{7,3},{8,12},{9,13},{10,... | collective-permute-start | bytes 196616 | tf_op jit(solution)/shard_map/side_partial/ppermute | solution.py:357
  103.9 2.0 %collective-permute-start.25 = (bf16[1,256,128]{2,1,0:T(8,128)(2,1)S(1)}, bf16[1,256,128]{2,1,0:T(8,128)(2,1)S(1)}, u32[]{:S(2)}, u32[]{:S(2)}) collective-permute-start(bf16[1,256,128]{2,1,0:T(8,128)(2,1)S(1)} %get-tuple-element.101), channel_id=1, source_target_pairs={{0,6},{1,7},{2,0},{3,1},{4,2},{5,3},{6,4},{7,5},{8,14},{9,15},{10,... | collective-permute-start | bytes 196616 | tf_op jit(solution)/shard_map/side_partial/ppermute | solution.py:357
  105.9 1.1 collective-permute-done.23.refs_5_
  107.1 1.1 collective-permute-done.24.refs_6_
  108.2 0.6 collect.5.t_ref
  108.9 1.9 %collective-permute-done.26.other_ref = bf16[8,1,256,128]{3,2,1,0:T(8,128)(2,1)S(1)} collective-permute-done((bf16[8,1,256,128]{3,2,1,0:T(8,128)(2,1)S(1)}, bf16[8,1,256,128]{3,2,1,0:T(8,128)(2,1)S(1)}, u32[]{:S(2)}, u32[]{:S(2)}) %collective-permute-start.26) | collective-permute-done | bytes 524320 | tf_op jit(solution)/shard_map/side_partial/ppermute | solution.py:362
  110.8 4.7 %second_half_side.1 = (bf16[8,64,256]{2,1,0:T(8,128)(2,1)S(1)}, bf16[8,64,256]{2,1,0:T(8,128)(2,1)S(1)}) custom-call(s32[4]{0:T(128)S(1)} %pad_add_fusion.place, bf16[8,1,256,128]{3,2,1,0:T(8,128)(2,1)S(1)} %collect.5.t_ref, bf16[8,1,256,128]{3,2,1,0:T(8,128)(2,1)S(1)} %collective-permute-done.26.other_ref, bf16[2048,1024]{1,0:T(8,128)(2,1)} %pick_columns.1.c_hbm), custom_call_target="tpu_custom_call" | custom-call | tf_op jit(solution)/shard_map/side_partial/second_half_side/pallas_call | solution.py:258
  115.5 1.8 %collective-permute-start.27 = (bf16[8,64,256]{2,1,0:T(8,128)(2,1)S(1)}, bf16[8,64,256]{2,1,0:T(8,128)(2,1)S(1)}, u32[]{:S(2)}, u32[]{:S(2)}) collective-permute-start(bf16[8,64,256]{2,1,0:T(8,128)(2,1)S(1)} %get-tuple-element.104), channel_id=1, source_target_pairs={{0,16},{16,0},{1,17},{17,1},{2,18},{18,2},{3,19},{19,3},{4,20},{20... | collective-permute-start | bytes 786440 | tf_op jit(solution)/shard_map/ppermute | solution.py:362
  117.3 0.7 all-to-all-done.2.t_ref
  118.0 6.4 %second_half.1 = bf16[8,2,2,64,256]{4,3,2,1,0:T(8,128)(2,1)} custom-call(bf16[8,2,256,128]{3,2,1,0:T(8,128)(2,1)S(1)} %all-to-all-done.2.t_ref, bf16[2048,2048]{1,0:T(8,128)(2,1)} %c_hbm.3), custom_call_target="tpu_custom_call" | custom-call | tf_op jit(solution)/shard_map/second_half/pallas_call | solution.py:211
  124.4 8.2 %all-to-all-start.3 = ((bf16[16,2,64,256]{3,2,1,0:T(8,128)(2,1)}), bf16[16,2,64,256]{3,2,1,0:T(8,128)(2,1)S(1)}, u32[]{:S(2)}, u32[]{:S(2)}) async-start(bf16[16,2,64,256]{3,2,1,0:T(8,128)(2,1)} %bitcast.13), calls=%async_computation.3 | async-start | bytes 2097152 | tf_op jit(solution)/shard_map/panels_out/all_to_all | solution.py:430
  132.6 0.6 join_and_spread.3
  133.2 4.5 %collective-permute-start.28 = (bf16[2,64,256]{2,1,0:T(8,128)(2,1)S(1)}, bf16[2,64,256]{2,1,0:T(8,128)(2,1)S(1)}, u32[]{:S(2)}, u32[]{:S(2)}) collective-permute-start(bf16[2,64,256]{2,1,0:T(8,128)(2,1)S(1)} %get-tuple-element.109), channel_id=1, source_target_pairs={{0,128},{32,160},{64,192},{96,224},{128,0},{160,32},{192,64},{224,... | collective-permute-start | bytes 196616 | tf_op jit(solution)/shard_map/side_out/ppermute | solution.py:357
  137.7 0.6 collective-permute-start.29
  138.2 4.5 %collective-permute-start.30 = (bf16[2,64,256]{2,1,0:T(8,128)(2,1)S(1)}, bf16[2,64,256]{2,1,0:T(8,128)(2,1)S(1)}, u32[]{:S(2)}, u32[]{:S(2)}) collective-permute-start(bf16[2,64,256]{2,1,0:T(8,128)(2,1)S(1)} %get-tuple-element.111), channel_id=1, source_target_pairs={{0,160},{32,192},{64,224},{96,0},{128,32},{160,64},{192,96},{224,1... | collective-permute-start | bytes 196616 | tf_op jit(solution)/shard_map/side_out/ppermute | solution.py:357
  142.7 0.6 collective-permute-start.31
  143.3 3.6 %collective-permute-start.32 = (bf16[2,64,256]{2,1,0:T(8,128)(2,1)S(1)}, bf16[2,64,256]{2,1,0:T(8,128)(2,1)S(1)}, u32[]{:S(2)}, u32[]{:S(2)}) collective-permute-start(bf16[2,64,256]{2,1,0:T(8,128)(2,1)S(1)} %get-tuple-element.113), channel_id=1, source_target_pairs={{0,192},{32,224},{64,0},{96,32},{128,64},{160,96},{192,128},{224,1... | collective-permute-start | bytes 196616 | tf_op jit(solution)/shard_map/side_out/ppermute | solution.py:357
  146.9 0.6 collective-permute-start.33
  147.4 1.4 collective-permute-done.29.refs_2_
  148.8 1.3 collective-permute-start.34
  150.1 0.1 collective-permute-done.32.refs_5_
  150.2 2.1 %collective-permute-done.33.refs_6_ = bf16[2,64,256]{2,1,0:T(8,128)(2,1)S(1)} collective-permute-done((bf16[2,64,256]{2,1,0:T(8,128)(2,1)S(1)}, bf16[2,64,256]{2,1,0:T(8,128)(2,1)S(1)}, u32[]{:S(2)}, u32[]{:S(2)}) %collective-permute-start.33) | collective-permute-done | bytes 65568 | tf_op jit(solution)/shard_map/side_out/ppermute | solution.py:357
  152.3 0.7 collective-permute-done.34.refs_7_
  153.1 1.8 %finish.1 = bf16[48,64,256]{2,1,0:T(8,128)(2,1)} custom-call(s32[4]{0:T(128)S(1)} %pad_add_fusion.place, bf16[2,64,256]{2,1,0:T(8,128)(2,1)S(1)} %get-tuple-element.108.refs_0_, bf16[2,64,256]{2,1,0:T(8,128)(2,1)S(1)} %collective-permute-done.28.refs_1_, bf16[2,64,256]{2,1,0:T(8,128)(2,1)S(1)} %collective-permute-done.29.refs_2_, ...), custom_call_target="tpu_custom_call" | custom-call | tf_op jit(solution)/shard_map/finish/pallas_call | solution.py:343
  (30 shorter events, 0.5 us)
Async XLA Ops:
  1.1 10.2 %collective-permute-start = (bf16[8,64,256]{2,1,0:T(8,128)(2,1)S(1)}, bf16[8,64,256]{2,1,0:T(8,128)(2,1)S(1)}, u32[]{:S(2)}, u32[]{:S(2)}) collective-permute-start(bf16[8,64,256]{2,1,0:T(8,128)(2,1)S(1)} %get-tuple-element.118), channel_id=1, source_target_pairs={{0,16},{16,0},{1,17},{17,1},{2,18},{18,2},{3,19},{19,3},{4,20},{20... | collective-permute-start | bytes 786440 | tf_op jit(solution)/shard_map/side_in/ppermute | solution.py:362
  11.4 30.3 %all-to-all-start = ((bf16[16,2,64,256]{3,2,1,0:T(8,128)(2,1)}), bf16[16,2,64,256]{3,2,1,0:T(8,128)(2,1)}, u32[]{:S(2)}, u32[]{:S(2)}) async-start(bf16[16,2,64,256]{3,2,1,0:T(8,128)(2,1)} %bitcast.4), calls=%async_computation | async-start | bytes 2097152 | tf_op jit(solution)/shard_map/panels_in/all_to_all | solution.py:389
  19.2 16.5 %collective-permute-start.1 = (bf16[2,64,256]{2,1,0:T(8,128)(2,1)S(1)}, bf16[2,64,256]{2,1,0:T(8,128)(2,1)S(1)}, u32[]{:S(2)}, u32[]{:S(2)}) collective-permute-start(bf16[2,64,256]{2,1,0:T(8,128)(2,1)S(1)} %get-tuple-element.65), channel_id=1, source_target_pairs={{0,128},{32,160},{64,192},{96,224},{128,0},{160,32},{192,64},{224,... | collective-permute-start | bytes 196616 | tf_op jit(solution)/shard_map/side_in/ppermute | solution.py:357
  26.5 10.3 %collective-permute-start.2 = (bf16[2,64,256]{2,1,0:T(8,128)(2,1)S(1)}, bf16[2,64,256]{2,1,0:T(8,128)(2,1)S(1)}, u32[]{:S(2)}, u32[]{:S(2)}) collective-permute-start(bf16[2,64,256]{2,1,0:T(8,128)(2,1)S(1)} %get-tuple-element.66), channel_id=1, source_target_pairs={{0,96},{32,128},{64,160},{96,192},{128,224},{160,0},{192,32},{224,... | collective-permute-start | bytes 196616 | tf_op jit(solution)/shard_map/side_in/ppermute | solution.py:357
  28.4 10.5 %collective-permute-start.3 = (bf16[2,64,256]{2,1,0:T(8,128)(2,1)S(1)}, bf16[2,64,256]{2,1,0:T(8,128)(2,1)S(1)}, u32[]{:S(2)}, u32[]{:S(2)}) collective-permute-start(bf16[2,64,256]{2,1,0:T(8,128)(2,1)S(1)} %get-tuple-element.67), channel_id=1, source_target_pairs={{0,160},{32,192},{64,224},{96,0},{128,32},{160,64},{192,96},{224,1... | collective-permute-start | bytes 196616 | tf_op jit(solution)/shard_map/side_in/ppermute | solution.py:357
  31.5 7.4 %collective-permute-start.4 = (bf16[2,64,256]{2,1,0:T(8,128)(2,1)S(1)}, bf16[2,64,256]{2,1,0:T(8,128)(2,1)S(1)}, u32[]{:S(2)}, u32[]{:S(2)}) collective-permute-start(bf16[2,64,256]{2,1,0:T(8,128)(2,1)S(1)} %get-tuple-element.68), channel_id=1, source_target_pairs={{0,64},{32,96},{64,128},{96,160},{128,192},{160,224},{192,0},{224,... | collective-permute-start | bytes 196616 | tf_op jit(solution)/shard_map/side_in/ppermute | solution.py:357
  33.0 6.6 %collective-permute-start.5 = (bf16[2,64,256]{2,1,0:T(8,128)(2,1)S(1)}, bf16[2,64,256]{2,1,0:T(8,128)(2,1)S(1)}, u32[]{:S(2)}, u32[]{:S(2)}) collective-permute-start(bf16[2,64,256]{2,1,0:T(8,128)(2,1)S(1)} %get-tuple-element.69), channel_id=1, source_target_pairs={{0,192},{32,224},{64,0},{96,32},{128,64},{160,96},{192,128},{224,1... | collective-permute-start | bytes 196616 | tf_op jit(solution)/shard_map/side_in/ppermute | solution.py:357
  35.6 5.5 %collective-permute-start.6 = (bf16[2,64,256]{2,1,0:T(8,128)(2,1)S(1)}, bf16[2,64,256]{2,1,0:T(8,128)(2,1)S(1)}, u32[]{:S(2)}, u32[]{:S(2)}) collective-permute-start(bf16[2,64,256]{2,1,0:T(8,128)(2,1)S(1)} %get-tuple-element.70), channel_id=1, source_target_pairs={{0,32},{32,64},{64,96},{96,128},{128,160},{160,192},{192,224},{224... | collective-permute-start | bytes 196616 | tf_op jit(solution)/shard_map/side_in/ppermute | solution.py:357
  36.8 4.4 %collective-permute-start.7 = (bf16[2,64,256]{2,1,0:T(8,128)(2,1)S(1)}, bf16[2,64,256]{2,1,0:T(8,128)(2,1)S(1)}, u32[]{:S(2)}, u32[]{:S(2)}) collective-permute-start(bf16[2,64,256]{2,1,0:T(8,128)(2,1)S(1)} %get-tuple-element.71), channel_id=1, source_target_pairs={{0,224},{32,0},{64,32},{96,64},{128,96},{160,128},{192,160},{224,1... | collective-permute-start | bytes 196616 | tf_op jit(solution)/shard_map/side_in/ppermute | solution.py:357
  41.7 31.3 %all-to-all-start.1 = ((bf16[8,2,2,64,256]{4,3,2,1,0:T(8,128)(2,1)}), bf16[8,2,2,64,256]{4,3,2,1,0:T(8,128)(2,1)S(1)}, u32[]{:S(2)}, u32[]{:S(2)}) async-start(bf16[8,2,2,64,256]{4,3,2,1,0:T(8,128)(2,1)} %bitcast.8.direct), calls=%async_computation.1 | async-start | bytes 2097152 | tf_op jit(solution)/shard_map/mirror/all_to_all | solution.py:397
  46.2 25.1 %collective-permute-start.8 = (bf16[8,2,2,64,256]{4,3,2,1,0:T(8,128)(2,1)}, bf16[8,2,2,64,256]{4,3,2,1,0:T(8,128)(2,1)S(1)}, u32[]{:S(2)}, u32[]{:S(2)}) collective-permute-start(bf16[8,2,2,64,256]{4,3,2,1,0:T(8,128)(2,1)} %bitcast.8.direct), channel_id=1, source_target_pairs={{0,8},{8,0},{1,9},{9,1},{2,10},{10,2},{3,11},{11,3},{4,12},{12,4},... | collective-permute-start | bytes 3145736 | tf_op jit(solution)/shard_map/ppermute | solution.py:362
  46.8 10.4 %collective-permute-start.9 = (bf16[2,64,256]{2,1,0:T(8,128)(2,1)S(1)}, bf16[2,64,256]{2,1,0:T(8,128)(2,1)S(1)}, u32[]{:S(2)}, u32[]{:S(2)}) collective-permute-start(bf16[2,64,256]{2,1,0:T(8,128)(2,1)S(1)} %get-tuple-element.76), channel_id=1, source_target_pairs={{0,3},{1,4},{2,5},{3,6},{4,7},{5,0},{6,1},{7,2},{8,11},{9,12},{10,... | collective-permute-start | bytes 196616 | tf_op jit(solution)/shard_map/side_mirror/ppermute | solution.py:357
  50.8 8.6 %collective-permute-start.10 = (bf16[2,64,256]{2,1,0:T(8,128)(2,1)S(1)}, bf16[2,64,256]{2,1,0:T(8,128)(2,1)S(1)}, u32[]{:S(2)}, u32[]{:S(2)}) collective-permute-start(bf16[2,64,256]{2,1,0:T(8,128)(2,1)S(1)} %get-tuple-element.77), channel_id=1, source_target_pairs={{0,5},{1,6},{2,7},{3,0},{4,1},{5,2},{6,3},{7,4},{8,13},{9,14},{10,... | collective-permute-start | bytes 196616 | tf_op jit(solution)/shard_map/side_mirror/ppermute | solution.py:357
  52.9 7.5 %collective-permute-start.11 = (bf16[2,64,256]{2,1,0:T(8,128)(2,1)S(1)}, bf16[2,64,256]{2,1,0:T(8,128)(2,1)S(1)}, u32[]{:S(2)}, u32[]{:S(2)}) collective-permute-start(bf16[2,64,256]{2,1,0:T(8,128)(2,1)S(1)} %get-tuple-element.78), channel_id=1, source_target_pairs={{0,1},{1,2},{2,3},{3,4},{4,5},{5,6},{6,7},{7,0},{8,9},{9,10},{10,1... | collective-permute-start | bytes 196616 | tf_op jit(solution)/shard_map/side_mirror/ppermute | solution.py:357
  54.3 7.1 %collective-permute-start.12 = (bf16[2,64,256]{2,1,0:T(8,128)(2,1)S(1)}, bf16[2,64,256]{2,1,0:T(8,128)(2,1)S(1)}, u32[]{:S(2)}, u32[]{:S(2)}) collective-permute-start(bf16[2,64,256]{2,1,0:T(8,128)(2,1)S(1)} %get-tuple-element.79), channel_id=1, source_target_pairs={{0,7},{1,0},{2,1},{3,2},{4,3},{5,4},{6,5},{7,6},{8,15},{9,8},{10,9... | collective-permute-start | bytes 196616 | tf_op jit(solution)/shard_map/side_mirror/ppermute | solution.py:357
  57.3 6.3 %collective-permute-start.13 = (bf16[2,64,256]{2,1,0:T(8,128)(2,1)S(1)}, bf16[2,64,256]{2,1,0:T(8,128)(2,1)S(1)}, u32[]{:S(2)}, u32[]{:S(2)}) collective-permute-start(bf16[2,64,256]{2,1,0:T(8,128)(2,1)S(1)} %get-tuple-element.80), channel_id=1, source_target_pairs={{0,4},{1,5},{2,6},{3,7},{4,0},{5,1},{6,2},{7,3},{8,12},{9,13},{10,... | collective-permute-start | bytes 196616 | tf_op jit(solution)/shard_map/side_mirror/ppermute | solution.py:357
  59.4 4.4 %collective-permute-start.14 = (bf16[2,64,256]{2,1,0:T(8,128)(2,1)S(1)}, bf16[2,64,256]{2,1,0:T(8,128)(2,1)S(1)}, u32[]{:S(2)}, u32[]{:S(2)}) collective-permute-start(bf16[2,64,256]{2,1,0:T(8,128)(2,1)S(1)} %get-tuple-element.81), channel_id=1, source_target_pairs={{0,2},{1,3},{2,4},{3,5},{4,6},{5,7},{6,0},{7,1},{8,10},{9,11},{10,... | collective-permute-start | bytes 196616 | tf_op jit(solution)/shard_map/side_mirror/ppermute | solution.py:357
  60.4 4.3 %collective-permute-start.15 = (bf16[2,64,256]{2,1,0:T(8,128)(2,1)S(1)}, bf16[2,64,256]{2,1,0:T(8,128)(2,1)S(1)}, u32[]{:S(2)}, u32[]{:S(2)}) collective-permute-start(bf16[2,64,256]{2,1,0:T(8,128)(2,1)S(1)} %get-tuple-element.82), channel_id=1, source_target_pairs={{0,6},{1,7},{2,0},{3,1},{4,2},{5,3},{6,4},{7,5},{8,14},{9,15},{10,... | collective-permute-start | bytes 196616 | tf_op jit(solution)/shard_map/side_mirror/ppermute | solution.py:357
  61.4 3.9 %collective-permute-start.17 = (bf16[8,2,64,256]{3,2,1,0:T(8,128)(2,1)S(1)}, bf16[8,2,64,256]{3,2,1,0:T(8,128)(2,1)S(1)}, u32[]{:S(2)}, u32[]{:S(2)}) collective-permute-start(bf16[8,2,64,256]{3,2,1,0:T(8,128)(2,1)S(1)} %collect.3.x_ref), channel_id=1, source_target_pairs={{0,8},{8,0},{1,9},{9,1},{2,10},{10,2},{3,11},{11,3},{4,12},{12,4},... | collective-permute-start | bytes 1572872 | tf_op jit(solution)/shard_map/side_mirror/ppermute | solution.py:362
  65.2 2.0 %collective-permute-start.16 = (bf16[8,2,64,256]{3,2,1,0:T(8,128)(2,1)S(1)}, bf16[8,2,64,256]{3,2,1,0:T(8,128)(2,1)S(1)}, u32[]{:S(2)}, u32[]{:S(2)}) collective-permute-start(bf16[8,2,64,256]{3,2,1,0:T(8,128)(2,1)S(1)} %collect.4), channel_id=1, source_target_pairs={{0,8},{8,0},{1,9},{9,1},{2,10},{10,2},{3,11},{11,3},{4,12},{12,4},... | collective-permute-start | bytes 1572872 | tf_op jit(solution)/shard_map/side_mirror/ppermute | solution.py:362
  73.0 2.7 %collective-permute-start.18 = (bf16[8,2,2,64,256]{4,3,2,1,0:T(8,128)(2,1)S(1)}, bf16[8,2,2,64,256]{4,3,2,1,0:T(8,128)(2,1)S(1)}, u32[]{:S(2)}, u32[]{:S(2)}) collective-permute-start(bf16[8,2,2,64,256]{4,3,2,1,0:T(8,128)(2,1)S(1)} %all-to-all-done.1.turned), channel_id=1, source_target_pairs={{0,8},{8,0},{1,9},{9,1},{2,10},{10,2},{3,11},{11,3},{4,12},{12,4},... | collective-permute-start | bytes 3145736 | tf_op jit(solution)/shard_map/ppermute | solution.py:362
  82.4 35.5 %all-to-all-start.2 = ((bf16[8,2,256,128]{3,2,1,0:T(8,128)(2,1)}), bf16[8,2,256,128]{3,2,1,0:T(8,128)(2,1)S(1)}, u32[]{:S(2)}, u32[]{:S(2)}) async-start(bf16[8,2,256,128]{3,2,1,0:T(8,128)(2,1)} %first_half.1), calls=%async_computation.2 | async-start | bytes 2097152 | tf_op jit(solution)/shard_map/partial/all_to_all | solution.py:416
  88.9 15.0 %collective-permute-start.19 = (bf16[1,256,128]{2,1,0:T(8,128)(2,1)S(1)}, bf16[1,256,128]{2,1,0:T(8,128)(2,1)S(1)}, u32[]{:S(2)}, u32[]{:S(2)}) collective-permute-start(bf16[1,256,128]{2,1,0:T(8,128)(2,1)S(1)} %get-tuple-element.95), channel_id=1, source_target_pairs={{0,3},{1,4},{2,5},{3,6},{4,7},{5,0},{6,1},{7,2},{8,11},{9,12},{10,... | collective-permute-start | bytes 196616 | tf_op jit(solution)/shard_map/side_partial/ppermute | solution.py:357
  90.9 13.0 %collective-permute-start.20 = (bf16[1,256,128]{2,1,0:T(8,128)(2,1)S(1)}, bf16[1,256,128]{2,1,0:T(8,128)(2,1)S(1)}, u32[]{:S(2)}, u32[]{:S(2)}) collective-permute-start(bf16[1,256,128]{2,1,0:T(8,128)(2,1)S(1)} %get-tuple-element.96), channel_id=1, source_target_pairs={{0,5},{1,6},{2,7},{3,0},{4,1},{5,2},{6,3},{7,4},{8,13},{9,14},{10,... | collective-permute-start | bytes 196616 | tf_op jit(solution)/shard_map/side_partial/ppermute | solution.py:357
  94.8 11.1 %collective-permute-start.21 = (bf16[1,256,128]{2,1,0:T(8,128)(2,1)S(1)}, bf16[1,256,128]{2,1,0:T(8,128)(2,1)S(1)}, u32[]{:S(2)}, u32[]{:S(2)}) collective-permute-start(bf16[1,256,128]{2,1,0:T(8,128)(2,1)S(1)} %get-tuple-element.97), channel_id=1, source_target_pairs={{0,1},{1,2},{2,3},{3,4},{4,5},{5,6},{6,7},{7,0},{8,9},{9,10},{10,1... | collective-permute-start | bytes 196616 | tf_op jit(solution)/shard_map/side_partial/ppermute | solution.py:357
  96.5 9.4 %collective-permute-start.22 = (bf16[1,256,128]{2,1,0:T(8,128)(2,1)S(1)}, bf16[1,256,128]{2,1,0:T(8,128)(2,1)S(1)}, u32[]{:S(2)}, u32[]{:S(2)}) collective-permute-start(bf16[1,256,128]{2,1,0:T(8,128)(2,1)S(1)} %get-tuple-element.98), channel_id=1, source_target_pairs={{0,7},{1,0},{2,1},{3,2},{4,3},{5,4},{6,5},{7,6},{8,15},{9,8},{10,9... | collective-permute-start | bytes 196616 | tf_op jit(solution)/shard_map/side_partial/ppermute | solution.py:357
  99.3 7.8 %collective-permute-start.23 = (bf16[1,256,128]{2,1,0:T(8,128)(2,1)S(1)}, bf16[1,256,128]{2,1,0:T(8,128)(2,1)S(1)}, u32[]{:S(2)}, u32[]{:S(2)}) collective-permute-start(bf16[1,256,128]{2,1,0:T(8,128)(2,1)S(1)} %get-tuple-element.99), channel_id=1, source_target_pairs={{0,4},{1,5},{2,6},{3,7},{4,0},{5,1},{6,2},{7,3},{8,12},{9,13},{10,... | collective-permute-start | bytes 196616 | tf_op jit(solution)/shard_map/side_partial/ppermute | solution.py:357
  103.9 4.3 %collective-permute-start.24 = (bf16[1,256,128]{2,1,0:T(8,128)(2,1)S(1)}, bf16[1,256,128]{2,1,0:T(8,128)(2,1)S(1)}, u32[]{:S(2)}, u32[]{:S(2)}) collective-permute-start(bf16[1,256,128]{2,1,0:T(8,128)(2,1)S(1)} %get-tuple-element.100), channel_id=1, source_target_pairs={{0,2},{1,3},{2,4},{3,5},{4,6},{5,7},{6,0},{7,1},{8,10},{9,11},{10,... | collective-permute-start | bytes 196616 | tf_op jit(solution)/shard_map/side_partial/ppermute | solution.py:357
  103.9 4.3 %collective-permute-start.25 = (bf16[1,256,128]{2,1,0:T(8,128)(2,1)S(1)}, bf16[1,256,128]{2,1,0:T(8,128)(2,1)S(1)}, u32[]{:S(2)}, u32[]{:S(2)}) collective-permute-start(bf16[1,256,128]{2,1,0:T(8,128)(2,1)S(1)} %get-tuple-element.101), channel_id=1, source_target_pairs={{0,6},{1,7},{2,0},{3,1},{4,2},{5,3},{6,4},{7,5},{8,14},{9,15},{10,... | collective-permute-start | bytes 196616 | tf_op jit(solution)/shard_map/side_partial/ppermute | solution.py:357
  108.8 2.0 %collective-permute-start.26 = (bf16[8,1,256,128]{3,2,1,0:T(8,128)(2,1)S(1)}, bf16[8,1,256,128]{3,2,1,0:T(8,128)(2,1)S(1)}, u32[]{:S(2)}, u32[]{:S(2)}) collective-permute-start(bf16[8,1,256,128]{3,2,1,0:T(8,128)(2,1)S(1)} %collect.5.t_ref), channel_id=1, source_target_pairs={{0,8},{8,0},{1,9},{9,1},{2,10},{10,2},{3,11},{11,3},{4,12},{12,4},... | collective-permute-start | bytes 1572872 | tf_op jit(solution)/shard_map/side_partial/ppermute | solution.py:362
  115.5 8.8 %collective-permute-start.27 = (bf16[8,64,256]{2,1,0:T(8,128)(2,1)S(1)}, bf16[8,64,256]{2,1,0:T(8,128)(2,1)S(1)}, u32[]{:S(2)}, u32[]{:S(2)}) collective-permute-start(bf16[8,64,256]{2,1,0:T(8,128)(2,1)S(1)} %get-tuple-element.104), channel_id=1, source_target_pairs={{0,16},{16,0},{1,17},{17,1},{2,18},{18,2},{3,19},{19,3},{4,20},{20... | collective-permute-start | bytes 786440 | tf_op jit(solution)/shard_map/ppermute | solution.py:362
  124.4 28.7 %all-to-all-start.3 = ((bf16[16,2,64,256]{3,2,1,0:T(8,128)(2,1)}), bf16[16,2,64,256]{3,2,1,0:T(8,128)(2,1)S(1)}, u32[]{:S(2)}, u32[]{:S(2)}) async-start(bf16[16,2,64,256]{3,2,1,0:T(8,128)(2,1)} %bitcast.13), calls=%async_computation.3 | async-start | bytes 2097152 | tf_op jit(solution)/shard_map/panels_out/all_to_all | solution.py:430
  133.2 13.7 %collective-permute-start.28 = (bf16[2,64,256]{2,1,0:T(8,128)(2,1)S(1)}, bf16[2,64,256]{2,1,0:T(8,128)(2,1)S(1)}, u32[]{:S(2)}, u32[]{:S(2)}) collective-permute-start(bf16[2,64,256]{2,1,0:T(8,128)(2,1)S(1)} %get-tuple-element.109), channel_id=1, source_target_pairs={{0,128},{32,160},{64,192},{96,224},{128,0},{160,32},{192,64},{224,... | collective-permute-start | bytes 196616 | tf_op jit(solution)/shard_map/side_out/ppermute | solution.py:357
  137.7 11.1 %collective-permute-start.29 = (bf16[2,64,256]{2,1,0:T(8,128)(2,1)S(1)}, bf16[2,64,256]{2,1,0:T(8,128)(2,1)S(1)}, u32[]{:S(2)}, u32[]{:S(2)}) collective-permute-start(bf16[2,64,256]{2,1,0:T(8,128)(2,1)S(1)} %get-tuple-element.110), channel_id=1, source_target_pairs={{0,96},{32,128},{64,160},{96,192},{128,224},{160,0},{192,32},{224,... | collective-permute-start | bytes 196616 | tf_op jit(solution)/shard_map/side_out/ppermute | solution.py:357
  138.2 11.9 %collective-permute-start.30 = (bf16[2,64,256]{2,1,0:T(8,128)(2,1)S(1)}, bf16[2,64,256]{2,1,0:T(8,128)(2,1)S(1)}, u32[]{:S(2)}, u32[]{:S(2)}) collective-permute-start(bf16[2,64,256]{2,1,0:T(8,128)(2,1)S(1)} %get-tuple-element.111), channel_id=1, source_target_pairs={{0,160},{32,192},{64,224},{96,0},{128,32},{160,64},{192,96},{224,1... | collective-permute-start | bytes 196616 | tf_op jit(solution)/shard_map/side_out/ppermute | solution.py:357
  142.7 7.4 %collective-permute-start.31 = (bf16[2,64,256]{2,1,0:T(8,128)(2,1)S(1)}, bf16[2,64,256]{2,1,0:T(8,128)(2,1)S(1)}, u32[]{:S(2)}, u32[]{:S(2)}) collective-permute-start(bf16[2,64,256]{2,1,0:T(8,128)(2,1)S(1)} %get-tuple-element.112), channel_id=1, source_target_pairs={{0,64},{32,96},{64,128},{96,160},{128,192},{160,224},{192,0},{224,... | collective-permute-start | bytes 196616 | tf_op jit(solution)/shard_map/side_out/ppermute | solution.py:357
  143.3 6.9 %collective-permute-start.32 = (bf16[2,64,256]{2,1,0:T(8,128)(2,1)S(1)}, bf16[2,64,256]{2,1,0:T(8,128)(2,1)S(1)}, u32[]{:S(2)}, u32[]{:S(2)}) collective-permute-start(bf16[2,64,256]{2,1,0:T(8,128)(2,1)S(1)} %get-tuple-element.113), channel_id=1, source_target_pairs={{0,192},{32,224},{64,0},{96,32},{128,64},{160,96},{192,128},{224,1... | collective-permute-start | bytes 196616 | tf_op jit(solution)/shard_map/side_out/ppermute | solution.py:357
  146.9 5.5 %collective-permute-start.33 = (bf16[2,64,256]{2,1,0:T(8,128)(2,1)S(1)}, bf16[2,64,256]{2,1,0:T(8,128)(2,1)S(1)}, u32[]{:S(2)}, u32[]{:S(2)}) collective-permute-start(bf16[2,64,256]{2,1,0:T(8,128)(2,1)S(1)} %get-tuple-element.114), channel_id=1, source_target_pairs={{0,32},{32,64},{64,96},{96,128},{128,160},{160,192},{192,224},{224... | collective-permute-start | bytes 196616 | tf_op jit(solution)/shard_map/side_out/ppermute | solution.py:357
  148.8 4.3 %collective-permute-start.34 = (bf16[2,64,256]{2,1,0:T(8,128)(2,1)S(1)}, bf16[2,64,256]{2,1,0:T(8,128)(2,1)S(1)}, u32[]{:S(2)}, u32[]{:S(2)}) collective-permute-start(bf16[2,64,256]{2,1,0:T(8,128)(2,1)S(1)} %get-tuple-element.115), channel_id=1, source_target_pairs={{0,224},{32,0},{64,32},{96,64},{128,96},{160,128},{192,160},{224,1... | collective-permute-start | bytes 196616 | tf_op jit(solution)/shard_map/side_out/ppermute | solution.py:357

commit v2 on v1

--- a/solution.py
+++ b/solution.py
@@ -53,17 +53,22 @@
     return [pltpu.VMEM((STEPS, size // STEPS, width), BF16), pltpu.SemaphoreType.DMA((STEPS,))]
 
 
-def transposed(block):
+def set_identity(eye):
+    row = lax.broadcasted_iota(jnp.int32, eye.shape, 0)
+    column = lax.broadcasted_iota(jnp.int32, eye.shape, 1)
+    eye[...] = (row == column).astype(F32).astype(BF16)
+
+
+def transposed(block, eye):
     size = block.shape[1]
-    row = lax.broadcasted_iota(jnp.int32, (size, size), 0)
-    column = lax.broadcasted_iota(jnp.int32, (size, size), 1)
-    eye = (row == column).astype(F32).astype(BF16)
     return lax.dot_general(
-        eye, block, (((1,), (1,)), ((), ())), preferred_element_type=F32
+        eye[:size, :size], block, (((1,), (1,)), ((), ())), preferred_element_type=F32
     ).astype(BF16)
 
 
-def pick_kernel(place, c_hbm, out_hbm, c_ref, sems, chosen, out_sems):
+def pick_kernel(place, c_hbm, panel_hbm, out_hbm, main_hbm, c_ref, sems, chosen, out_sems, main_sem):
+    main = pltpu.make_async_copy(panel_hbm.at[pl.ds(0, main_hbm.shape[0])], main_hbm, main_sem)
+    main.start()
     block = c_hbm.shape[1] // BLOCKS
     lanes = block // CORE
     half = lanes // 2
@@ -93,26 +98,29 @@
 
     steps(c_hbm, c_ref, sems, choose)
     lax.fori_loop(0, STEPS, finish_store, 0)
-
-
-def pick_columns(place, orbitals):
+    main.wait()
+
+
+def pick_columns(place, orbitals, half_panel, main_pairs):
     size = orbitals.shape[0]
     width = size // CORE
     return pl.pallas_call(
         pick_kernel,
-        out_shape=pltpu.HBM((size, width), BF16),
-        in_specs=[pl.BlockSpec(memory_space=pltpu.SMEM), HBM],
-        out_specs=HBM,
+        out_shape=[pltpu.HBM((size, width), BF16), pltpu.HBM((main_pairs,) + half_panel.shape[1:], BF16)],
+        in_specs=[pl.BlockSpec(memory_space=pltpu.SMEM), HBM, HBM],
+        out_specs=[HBM, HBM],
         scratch_shapes=fetch_scratch(orbitals) + [
-            pltpu.VMEM((STEPS, size // STEPS, width), BF16), pltpu.SemaphoreType.DMA((STEPS,))],
+            pltpu.VMEM((STEPS, size // STEPS, width), BF16), pltpu.SemaphoreType.DMA((STEPS,)),
+            pltpu.SemaphoreType.DMA(())],
         compiler_params=PARAMS,
         name="pick_columns",
-    )(place, in_hbm(orbitals))
+    )(place, in_hbm(orbitals), in_hbm(half_panel))
 
 
 def first_kernel(index, place, direct, direct_other, turned, turned_other, c_hbm, *rest):
-    t_refs = rest[:-5]
-    c_ref, sems, sym, turn, total = rest[-5:]
+    t_refs = rest[:-6]
+    c_ref, sems, sym, turn, total, eye = rest[-6:]
+    set_identity(eye)
     _, _, depth, rows, block = direct.shape
     mine, core = place[index], place[AT_CORE]
     per_step = BLOCKS // STEPS
@@ -137,7 +145,7 @@
                 column = lax.broadcasted_iota(jnp.int32, (block, block), 1)
                 for k in range(depth):
                     upper = sym[k * block:(k + 1) * block, cols]
-                    sym[k * block:(k + 1) * block, cols] = jnp.where(row <= column, upper, transposed(upper))
+                    sym[k * block:(k + 1) * block, cols] = jnp.where(row <= column, upper, transposed(upper, eye))
 
             @pl.when(b < mine)
             def _():
@@ -147,7 +155,7 @@
                         turn[pl.ds(pl.multiple_of(at + core * rows, rows), rows), :] = turned[b, y, k]
                         turn[pl.ds(pl.multiple_of(at + (1 - core) * rows, rows), rows), :] = turned_other[b, y, k]
                 for k in range(depth):
-                    sym[k * block:(k + 1) * block, cols] = transposed(turn[k * block:(k + 1) * block])
+                    sym[k * block:(k + 1) * block, cols] = transposed(turn[k * block:(k + 1) * block], eye)
 
         fetch_of(c_hbm, c_ref, sems, step).wait()
         total[...] += jnp.dot(sym[...], c_ref[step], preferred_element_type=F32)
@@ -177,13 +185,15 @@
         scratch_shapes=fetch_scratch(picked) + [
             pltpu.VMEM((depth * block, size // STEPS), BF16),
             pltpu.VMEM((depth * block, block), BF16),
-            pltpu.VMEM((depth * block, width), F32)],
+            pltpu.VMEM((depth * block, width), F32),
+            pltpu.VMEM((block, block), BF16)],
         compiler_params=PARAMS,
         name=name,
     )(place, direct, direct_other, turned, turned_other, in_hbm(picked))
 
 
-def second_kernel(t_ref, c_hbm, out_ref, c_ref, sems, left, total):
+def second_kernel(t_ref, c_hbm, out_ref, c_ref, sems, left, total, eye):
+    set_identity(eye)
     count, depth, block, lanes = t_ref.shape
     rows = lanes // YLO
     per_step = count // STEPS
@@ -192,7 +202,7 @@
     def work(step):
         for u in range(per_step):
             for k in range(depth):
-                left[k * lanes:(k + 1) * lanes, u * block:(u + 1) * block] = transposed(t_ref[step * per_step + u, k])
+                left[k * lanes:(k + 1) * lanes, u * block:(u + 1) * block] = transposed(t_ref[step * per_step + u, k], eye)
         fetch_of(c_hbm, c_ref, sems, step).wait()
         total[...] += jnp.dot(left[...], c_ref[step], preferred_element_type=F32)
 
@@ -215,13 +225,15 @@
         out_specs=vmem,
         scratch_shapes=fetch_scratch(orbitals) + [
             pltpu.VMEM((depth * lanes, size // STEPS), BF16),
-            pltpu.VMEM((depth * lanes, size), F32)],
+            pltpu.VMEM((depth * lanes, size), F32),
+            pltpu.VMEM((lanes, lanes), BF16)],
         compiler_params=PARAMS,
         name="second_half",
     )(partial_value, in_hbm(orbitals))
 
 
-def second_side_kernel(place, t_ref, other_ref, c_hbm, keep, send, c_ref, sems, left, total, final):
+def second_side_kernel(place, t_ref, other_ref, c_hbm, keep, send, c_ref, sems, left, total, final, eye):
+    set_identity(eye)
     count, _, block, lanes = t_ref.shape
     rows = lanes // YLO
     per_step = count // STEPS
@@ -231,8 +243,8 @@
     def work(step):
         for u in range(per_step):
             cols = slice(u * block, (u + 1) * block)
-            own = transposed(t_ref[step * per_step + u, 0])
-            other = transposed(other_ref[step * per_step + u, 0])
+            own = transposed(t_ref[step * per_step + u, 0], eye)
+            other = transposed(other_ref[step * per_step + u, 0], eye)
             for y in range(YLO):
                 at = y * CORE * rows
                 left[pl.ds(pl.multiple_of(at + core * rows, rows), rows), cols] = own[y * rows:(y + 1) * rows]
@@ -243,7 +255,7 @@
     steps(c_hbm, c_ref, sems, work)
     for part in range(total.shape[1] // block):
         cols = slice(part * block, (part + 1) * block)
-        final[cols] = transposed(total[:, cols].astype(BF16))
+        final[cols] = transposed(total[:, cols].astype(BF16), eye)
     for z in range(Z):
         at = z * YLO * rows
         keep[z] = final[pl.ds(pl.multiple_of(at + ylo * rows, rows), rows)]
@@ -263,7 +275,8 @@
         scratch_shapes=fetch_scratch(picked) + [
             pltpu.VMEM((block, size // STEPS), BF16),
             pltpu.VMEM((block, width), F32),
-            pltpu.VMEM((width, block), BF16)],
+            pltpu.VMEM((width, block), BF16),
+            pltpu.VMEM((block, block), BF16)],
         compiler_params=PARAMS,
         name="second_half_side",
     )(place, own, other, in_hbm(picked))
@@ -381,8 +394,8 @@
         side = half_panel[main_pairs:].reshape(YLO, Z, rows, block)
         got = swap(lax.dynamic_index_in_dim(side, 1 - ylo, 0, keepdims=False), "ylo")
         keep = lax.dynamic_index_in_dim(side, ylo, 0, keepdims=False)
-    picked = pick_columns(place, orbitals)
-    own = half_panel[:main_pairs].reshape(COLS * YLO, depth, rows, block)
+    picked, own = pick_columns(place, orbitals, half_panel, main_pairs)
+    own = own.reshape(COLS * YLO, depth, rows, block)
     own, got, keep, picked = together((own, got, keep, picked))
 
     with jax.named_scope("panels_in"):

time: 156 us -> 181 us (1.16)
  Pallas kernels: 33.5 us -> 61 us
  local copies, waits for them, and re-layouts: 3.43 us -> 1.13 us
    pallas_call x1, Pallas kernels: 6.19 us -> 33.5 us  [pick_columns(): pl.pallas_call(pick_kernel, out_shape=[pltpu.HBM((size, width), BF16), pl...]
    slice x1 -> x0, local copies, waits for them, and re-layouts: 2.3 us -> none  [per_device(): own = half_panel[:main_pairs].reshape(COLS * YLO, depth, rows, block)]
  transfers between devices with their start and end apart: 39 -> 39, of which waited for: 18 -> 18; matrix products, arithmetic and copies ran while one was open for 2% -> 0% of each run, Pallas kernels for 16% -> 29%
where the time goes in v2:
time: 181 us; the launch traced here: 180 us
  starting transfers between devices  96.6 us (53%)
  Pallas kernels  61 us (34%)
  waiting for transfers between devices  21 us (12%)
    ppermute x28, starting transfers between devices, rotate(): lax.ppermute(part, axes, [(i, (i + d) % BLOCKS) for i in range(BLOCKS)])  66.6 us
    pallas_call x1, Pallas kernels, pick_columns(): pl.pallas_call(pick_kernel, out_shape=[pltpu.HBM((size, width), BF16), pl...  33.5 us
    ppermute x28, waiting for transfers between devices, rotate(): lax.ppermute(part, axes, [(i, (i + d) % BLOCKS) for i in range(BLOCKS)])  12.3 us
    pallas_call x2, Pallas kernels, first_half(): pl.pallas_call(functools.partial(first_kernel, index), out_shape=[jax.Sha...  11 us
    all_to_all x1, starting transfers between devices, per_device(): result = lax.all_to_all(result, PLANE, 0, 0, tiled=True)  8.18 us
    all_to_all x1, starting transfers between devices, per_device(): own = lax.all_to_all(own, PLANE, 0, 0, tiled=True)  7.2 us
    all_to_all x1, starting transfers between devices, per_device(): partial_value = lax.all_to_all(partial_value, 'z', 0, 0, tiled=True)  6.49 us
    pallas_call x1, Pallas kernels, second_half(): pl.pallas_call(second_kernel, out_shape=jax.ShapeDtypeStruct((COLS, YLO,...  6.46 us
  transfers between devices with their start and end apart: 39, of which 18 were waited for; matrix products, arithmetic and copies ran while one was open for 0% of the time, Pallas kernels for 29%

profile of v2, /device:TPU:2, one launch (start us, length us, event | category | flops | bytes accessed | tf_op | source)
XLA Modules:
  0.0 180.2 jit_solution(6000520473631225666)
XLA Ops:
  0.0 1.1 slice.3
  1.1 1.7 collective-permute-start
  2.9 33.5 %pick_columns.1 = (bf16[2048,1024]{1,0:T(8,128)(2,1)}, bf16[32,64,256]{2,1,0:T(8,128)(2,1)}) custom-call(s32[4]{0:T(128)S(1)} %pad_add_fusion.place, bf16[2048,2048]{1,0:T(8,128)(2,1)} %c_hbm.3, bf16[48,64,256]{2,1,0:T(8,128)(2,1)} %panel_hbm.1), custom_call_target="tpu_custom_call" | custom-call | tf_op jit(solution)/shard_map/pick_columns/pallas_call | solution.py:107
  36.4 7.2 %all-to-all-start = ((bf16[16,2,64,256]{3,2,1,0:T(8,128)(2,1)}), bf16[16,2,64,256]{3,2,1,0:T(8,128)(2,1)}, u32[]{:S(2)}, u32[]{:S(2)}) async-start(bf16[16,2,64,256]{3,2,1,0:T(8,128)(2,1)} %bitcast.23), calls=%async_computation | async-start | bytes 2097152 | tf_op jit(solution)/shard_map/panels_in/all_to_all | solution.py:402
  43.6 0.6 join_and_spread.2
  44.2 7.3 %collective-permute-start.1 = (bf16[2,64,256]{2,1,0:T(8,128)(2,1)S(1)}, bf16[2,64,256]{2,1,0:T(8,128)(2,1)S(1)}, u32[]{:S(2)}, u32[]{:S(2)}) collective-permute-start(bf16[2,64,256]{2,1,0:T(8,128)(2,1)S(1)} %get-tuple-element.69), channel_id=1, source_target_pairs={{0,128},{32,160},{64,192},{96,224},{128,0},{160,32},{192,64},{224,... | collective-permute-start | bytes 196616 | tf_op jit(solution)/shard_map/side_in/ppermute | solution.py:370
  51.5 1.9 %collective-permute-start.2 = (bf16[2,64,256]{2,1,0:T(8,128)(2,1)S(1)}, bf16[2,64,256]{2,1,0:T(8,128)(2,1)S(1)}, u32[]{:S(2)}, u32[]{:S(2)}) collective-permute-start(bf16[2,64,256]{2,1,0:T(8,128)(2,1)S(1)} %get-tuple-element.70), channel_id=1, source_target_pairs={{0,96},{32,128},{64,160},{96,192},{128,224},{160,0},{192,32},{224,... | collective-permute-start | bytes 196616 | tf_op jit(solution)/shard_map/side_in/ppermute | solution.py:370
  53.4 3.1 %collective-permute-start.3 = (bf16[2,64,256]{2,1,0:T(8,128)(2,1)S(1)}, bf16[2,64,256]{2,1,0:T(8,128)(2,1)S(1)}, u32[]{:S(2)}, u32[]{:S(2)}) collective-permute-start(bf16[2,64,256]{2,1,0:T(8,128)(2,1)S(1)} %get-tuple-element.71), channel_id=1, source_target_pairs={{0,160},{32,192},{64,224},{96,0},{128,32},{160,64},{192,96},{224,1... | collective-permute-start | bytes 196616 | tf_op jit(solution)/shard_map/side_in/ppermute | solution.py:370
  56.5 1.5 collective-permute-start.4
  58.0 2.7 %collective-permute-start.5 = (bf16[2,64,256]{2,1,0:T(8,128)(2,1)S(1)}, bf16[2,64,256]{2,1,0:T(8,128)(2,1)S(1)}, u32[]{:S(2)}, u32[]{:S(2)}) collective-permute-start(bf16[2,64,256]{2,1,0:T(8,128)(2,1)S(1)} %get-tuple-element.73), channel_id=1, source_target_pairs={{0,192},{32,224},{64,0},{96,32},{128,64},{160,96},{192,128},{224,1... | collective-permute-start | bytes 196616 | tf_op jit(solution)/shard_map/side_in/ppermute | solution.py:370
  60.6 1.0 collective-permute-start.6
  61.6 0.1 collective-permute-done.2.refs_2_
  61.8 2.1 %collective-permute-start.7 = (bf16[2,64,256]{2,1,0:T(8,128)(2,1)S(1)}, bf16[2,64,256]{2,1,0:T(8,128)(2,1)S(1)}, u32[]{:S(2)}, u32[]{:S(2)}) collective-permute-start(bf16[2,64,256]{2,1,0:T(8,128)(2,1)S(1)} %get-tuple-element.75), channel_id=1, source_target_pairs={{0,224},{32,0},{64,32},{96,64},{128,96},{160,128},{192,160},{224,1... | collective-permute-start | bytes 196616 | tf_op jit(solution)/shard_map/side_in/ppermute | solution.py:370
  63.9 0.7 collective-permute-done.5.refs_5_
  64.6 1.5 collective-permute-done.6.refs_6_
  66.1 0.6 collect.3.x_ref
  66.7 4.5 %all-to-all-start.1 = ((bf16[8,2,2,64,256]{4,3,2,1,0:T(8,128)(2,1)}), bf16[8,2,2,64,256]{4,3,2,1,0:T(8,128)(2,1)S(1)}, u32[]{:S(2)}, u32[]{:S(2)}) async-start(bf16[8,2,2,64,256]{4,3,2,1,0:T(8,128)(2,1)} %bitcast.8.direct), calls=%async_computation.1 | async-start | bytes 2097152 | tf_op jit(solution)/shard_map/mirror/all_to_all | solution.py:410
  71.2 0.6 spread.1
  71.8 3.9 %collective-permute-start.9 = (bf16[2,64,256]{2,1,0:T(8,128)(2,1)S(1)}, bf16[2,64,256]{2,1,0:T(8,128)(2,1)S(1)}, u32[]{:S(2)}, u32[]{:S(2)}) collective-permute-start(bf16[2,64,256]{2,1,0:T(8,128)(2,1)S(1)} %get-tuple-element.80), channel_id=1, source_target_pairs={{0,3},{1,4},{2,5},{3,6},{4,7},{5,0},{6,1},{7,2},{8,11},{9,12},{10,... | collective-permute-start | bytes 196616 | tf_op jit(solution)/shard_map/side_mirror/ppermute | solution.py:370
  75.8 2.1 %collective-permute-start.10 = (bf16[2,64,256]{2,1,0:T(8,128)(2,1)S(1)}, bf16[2,64,256]{2,1,0:T(8,128)(2,1)S(1)}, u32[]{:S(2)}, u32[]{:S(2)}) collective-permute-start(bf16[2,64,256]{2,1,0:T(8,128)(2,1)S(1)} %get-tuple-element.81), channel_id=1, source_target_pairs={{0,5},{1,6},{2,7},{3,0},{4,1},{5,2},{6,3},{7,4},{8,13},{9,14},{10,... | collective-permute-start | bytes 196616 | tf_op jit(solution)/shard_map/side_mirror/ppermute | solution.py:370
  77.9 1.5 collective-permute-start.11
  79.3 3.0 %collective-permute-start.12 = (bf16[2,64,256]{2,1,0:T(8,128)(2,1)S(1)}, bf16[2,64,256]{2,1,0:T(8,128)(2,1)S(1)}, u32[]{:S(2)}, u32[]{:S(2)}) collective-permute-start(bf16[2,64,256]{2,1,0:T(8,128)(2,1)S(1)} %get-tuple-element.83), channel_id=1, source_target_pairs={{0,7},{1,0},{2,1},{3,2},{4,3},{5,4},{6,5},{7,6},{8,15},{9,8},{10,9... | collective-permute-start | bytes 196616 | tf_op jit(solution)/shard_map/side_mirror/ppermute | solution.py:370
  82.3 2.1 %collective-permute-start.13 = (bf16[2,64,256]{2,1,0:T(8,128)(2,1)S(1)}, bf16[2,64,256]{2,1,0:T(8,128)(2,1)S(1)}, u32[]{:S(2)}, u32[]{:S(2)}) collective-permute-start(bf16[2,64,256]{2,1,0:T(8,128)(2,1)S(1)} %get-tuple-element.84), channel_id=1, source_target_pairs={{0,4},{1,5},{2,6},{3,7},{4,0},{5,1},{6,2},{7,3},{8,12},{9,13},{10,... | collective-permute-start | bytes 196616 | tf_op jit(solution)/shard_map/side_mirror/ppermute | solution.py:370
  84.4 1.0 collective-permute-start.14
  85.4 1.0 collective-permute-start.15
  86.4 2.1 %collective-permute-done.13.refs_5_ = bf16[2,64,256]{2,1,0:T(8,128)(2,1)S(1)} collective-permute-done((bf16[2,64,256]{2,1,0:T(8,128)(2,1)S(1)}, bf16[2,64,256]{2,1,0:T(8,128)(2,1)S(1)}, u32[]{:S(2)}, u32[]{:S(2)}) %collective-permute-start.13) | collective-permute-done | bytes 65568 | tf_op jit(solution)/shard_map/side_mirror/ppermute | solution.py:370
  88.5 0.2 collective-permute-done.14.refs_6_
  88.8 0.9 collective-permute-done.15.refs_7_
  89.6 0.6 collect.4
  90.2 0.1 collective-permute-start.16
  90.3 1.9 %collective-permute-done.16 = bf16[8,2,64,256]{3,2,1,0:T(8,128)(2,1)S(1)} collective-permute-done((bf16[8,2,64,256]{3,2,1,0:T(8,128)(2,1)S(1)}, bf16[8,2,64,256]{3,2,1,0:T(8,128)(2,1)S(1)}, u32[]{:S(2)}, u32[]{:S(2)}) %collective-permute-start.16) | collective-permute-done | bytes 524320 | tf_op jit(solution)/shard_map/side_mirror/ppermute | solution.py:375
  92.2 4.2 %first_half_side.1 = (bf16[1,256,128]{2,1,0:T(8,128)(2,1)S(1)}, bf16[1,256,128]{2,1,0:T(8,128)(2,1)S(1)}, bf16[1,256,128]{2,1,0:T(8,128)(2,1)S(1)}, bf16[1,256,1...) custom-call(s32[4]{0:T(128)S(1)} %pad_add_fusion.place, ...), custom_call_target="tpu_custom_call" | custom-call | tf_op jit(solution)/shard_map/side_mirror/first_half_side/pallas_call | solution.py:180
  96.4 1.6 all-to-all-done.1.turned
  98.0 2.7 %collective-permute-done.18.turned_other = bf16[8,2,2,64,256]{4,3,2,1,0:T(8,128)(2,1)S(1)} collective-permute-done((bf16[8,2,2,64,256]{4,3,2,1,0:T(8,128)(2,1)S(1)}, bf16[8,2,2,64,256]{4,3,2,1,0:T(8,128)(2,1)S(1)}, u32[]{:S(2)}, u32[]{:S(2)}) %collective-permute-start.18) | collective-permute-done | bytes 1048608 | tf_op jit(solution)/shard_map/ppermute | solution.py:375
  100.7 6.8 %first_half.1 = bf16[8,2,256,128]{3,2,1,0:T(8,128)(2,1)} custom-call(s32[4]{0:T(128)S(1)} %pad_add_fusion.place, bf16[8,2,2,64,256]{4,3,2,1,0:T(8,128)(2,1)} %bitcast.8.direct, bf16[8,2,2,64,256]{4,3,2,1,0:T(8,128)(2,1)S(1)} %collective-permute-done.8.direct_other, bf16[8,2,2,64,256]{4,3,2,1,0:T(8,128)(2,1)S(1)} %all-to-all-done.1.turned, ...), custom_call_target="tpu_custom_call" | custom-call | tf_op jit(solution)/shard_map/first_half/pallas_call | solution.py:180
  107.5 6.5 %all-to-all-start.2 = ((bf16[8,2,256,128]{3,2,1,0:T(8,128)(2,1)}), bf16[8,2,256,128]{3,2,1,0:T(8,128)(2,1)S(1)}, u32[]{:S(2)}, u32[]{:S(2)}) async-start(bf16[8,2,256,128]{3,2,1,0:T(8,128)(2,1)} %first_half.1), calls=%async_computation.2 | async-start | bytes 2097152 | tf_op jit(solution)/shard_map/partial/all_to_all | solution.py:429
  114.0 2.0 %collective-permute-start.19 = (bf16[1,256,128]{2,1,0:T(8,128)(2,1)S(1)}, bf16[1,256,128]{2,1,0:T(8,128)(2,1)S(1)}, u32[]{:S(2)}, u32[]{:S(2)}) collective-permute-start(bf16[1,256,128]{2,1,0:T(8,128)(2,1)S(1)} %get-tuple-element.99), channel_id=1, source_target_pairs={{0,3},{1,4},{2,5},{3,6},{4,7},{5,0},{6,1},{7,2},{8,11},{9,12},{10,... | collective-permute-start | bytes 196616 | tf_op jit(solution)/shard_map/side_partial/ppermute | solution.py:370
  116.0 3.9 %collective-permute-start.20 = (bf16[1,256,128]{2,1,0:T(8,128)(2,1)S(1)}, bf16[1,256,128]{2,1,0:T(8,128)(2,1)S(1)}, u32[]{:S(2)}, u32[]{:S(2)}) collective-permute-start(bf16[1,256,128]{2,1,0:T(8,128)(2,1)S(1)} %get-tuple-element.100), channel_id=1, source_target_pairs={{0,5},{1,6},{2,7},{3,0},{4,1},{5,2},{6,3},{7,4},{8,13},{9,14},{10,... | collective-permute-start | bytes 196616 | tf_op jit(solution)/shard_map/side_partial/ppermute | solution.py:370
  119.9 1.7 collective-permute-start.21
  121.6 2.8 %collective-permute-start.22 = (bf16[1,256,128]{2,1,0:T(8,128)(2,1)S(1)}, bf16[1,256,128]{2,1,0:T(8,128)(2,1)S(1)}, u32[]{:S(2)}, u32[]{:S(2)}) collective-permute-start(bf16[1,256,128]{2,1,0:T(8,128)(2,1)S(1)} %get-tuple-element.102), channel_id=1, source_target_pairs={{0,7},{1,0},{2,1},{3,2},{4,3},{5,4},{6,5},{7,6},{8,15},{9,8},{10,9... | collective-permute-start | bytes 196616 | tf_op jit(solution)/shard_map/side_partial/ppermute | solution.py:370
  124.3 4.6 %collective-permute-start.23 = (bf16[1,256,128]{2,1,0:T(8,128)(2,1)S(1)}, bf16[1,256,128]{2,1,0:T(8,128)(2,1)S(1)}, u32[]{:S(2)}, u32[]{:S(2)}) collective-permute-start(bf16[1,256,128]{2,1,0:T(8,128)(2,1)S(1)} %get-tuple-element.103), channel_id=1, source_target_pairs={{0,4},{1,5},{2,6},{3,7},{4,0},{5,1},{6,2},{7,3},{8,12},{9,13},{10,... | collective-permute-start | bytes 196616 | tf_op jit(solution)/shard_map/side_partial/ppermute | solution.py:370
  129.0 2.0 %collective-permute-start.25 = (bf16[1,256,128]{2,1,0:T(8,128)(2,1)S(1)}, bf16[1,256,128]{2,1,0:T(8,128)(2,1)S(1)}, u32[]{:S(2)}, u32[]{:S(2)}) collective-permute-start(bf16[1,256,128]{2,1,0:T(8,128)(2,1)S(1)} %get-tuple-element.105), channel_id=1, source_target_pairs={{0,6},{1,7},{2,0},{3,1},{4,2},{5,3},{6,4},{7,5},{8,14},{9,15},{10,... | collective-permute-start | bytes 196616 | tf_op jit(solution)/shard_map/side_partial/ppermute | solution.py:370
  131.0 1.1 collective-permute-done.23.refs_5_
  132.1 1.1 collective-permute-done.24.refs_6_
  133.3 0.6 collect.5.t_ref
  134.0 1.9 %collective-permute-done.26.other_ref = bf16[8,1,256,128]{3,2,1,0:T(8,128)(2,1)S(1)} collective-permute-done((bf16[8,1,256,128]{3,2,1,0:T(8,128)(2,1)S(1)}, bf16[8,1,256,128]{3,2,1,0:T(8,128)(2,1)S(1)}, u32[]{:S(2)}, u32[]{:S(2)}) %collective-permute-start.26) | collective-permute-done | bytes 524320 | tf_op jit(solution)/shard_map/side_partial/ppermute | solution.py:375
  135.9 4.8 %second_half_side.1 = (bf16[8,64,256]{2,1,0:T(8,128)(2,1)S(1)}, bf16[8,64,256]{2,1,0:T(8,128)(2,1)S(1)}) custom-call(s32[4]{0:T(128)S(1)} %pad_add_fusion.place, bf16[8,1,256,128]{3,2,1,0:T(8,128)(2,1)S(1)} %collect.5.t_ref, bf16[8,1,256,128]{3,2,1,0:T(8,128)(2,1)S(1)} %collective-permute-done.26.other_ref, bf16[2048,1024]{1,0:T(8,128)(2,1)} %get-tuple-element.87.c_hbm), custom_call_target="tpu_custom_call" | custom-call | tf_op jit(solution)/shard_map/side_partial/second_half_side/pallas_call | solution.py:270
  140.7 1.8 collective-permute-start.27
  142.4 0.6 all-to-all-done.2.t_ref
  143.0 6.5 %second_half.1 = bf16[8,2,2,64,256]{4,3,2,1,0:T(8,128)(2,1)} custom-call(bf16[8,2,256,128]{3,2,1,0:T(8,128)(2,1)S(1)} %all-to-all-done.2.t_ref, bf16[2048,2048]{1,0:T(8,128)(2,1)} %c_hbm.3), custom_call_target="tpu_custom_call" | custom-call | tf_op jit(solution)/shard_map/second_half/pallas_call | solution.py:221
  149.5 8.2 %all-to-all-start.3 = ((bf16[16,2,64,256]{3,2,1,0:T(8,128)(2,1)}), bf16[16,2,64,256]{3,2,1,0:T(8,128)(2,1)S(1)}, u32[]{:S(2)}, u32[]{:S(2)}) async-start(bf16[16,2,64,256]{3,2,1,0:T(8,128)(2,1)} %bitcast.13), calls=%async_computation.3 | async-start | bytes 2097152 | tf_op jit(solution)/shard_map/panels_out/all_to_all | solution.py:443
  157.7 0.6 join_and_spread.3
  158.3 4.5 %collective-permute-start.28 = (bf16[2,64,256]{2,1,0:T(8,128)(2,1)S(1)}, bf16[2,64,256]{2,1,0:T(8,128)(2,1)S(1)}, u32[]{:S(2)}, u32[]{:S(2)}) collective-permute-start(bf16[2,64,256]{2,1,0:T(8,128)(2,1)S(1)} %get-tuple-element.113), channel_id=1, source_target_pairs={{0,128},{32,160},{64,192},{96,224},{128,0},{160,32},{192,64},{224,... | collective-permute-start | bytes 196616 | tf_op jit(solution)/shard_map/side_out/ppermute | solution.py:370
  162.8 0.6 collective-permute-start.29
  163.4 4.5 %collective-permute-start.30 = (bf16[2,64,256]{2,1,0:T(8,128)(2,1)S(1)}, bf16[2,64,256]{2,1,0:T(8,128)(2,1)S(1)}, u32[]{:S(2)}, u32[]{:S(2)}) collective-permute-start(bf16[2,64,256]{2,1,0:T(8,128)(2,1)S(1)} %get-tuple-element.115), channel_id=1, source_target_pairs={{0,160},{32,192},{64,224},{96,0},{128,32},{160,64},{192,96},{224,1... | collective-permute-start | bytes 196616 | tf_op jit(solution)/shard_map/side_out/ppermute | solution.py:370
  167.8 0.6 collective-permute-start.31
  168.4 3.5 %collective-permute-start.32 = (bf16[2,64,256]{2,1,0:T(8,128)(2,1)S(1)}, bf16[2,64,256]{2,1,0:T(8,128)(2,1)S(1)}, u32[]{:S(2)}, u32[]{:S(2)}) collective-permute-start(bf16[2,64,256]{2,1,0:T(8,128)(2,1)S(1)} %get-tuple-element.117), channel_id=1, source_target_pairs={{0,192},{32,224},{64,0},{96,32},{128,64},{160,96},{192,128},{224,1... | collective-permute-start | bytes 196616 | tf_op jit(solution)/shard_map/side_out/ppermute | solution.py:370
  172.0 0.6 collective-permute-start.33
  172.5 1.4 collective-permute-done.29.refs_2_
  174.0 1.2 collective-permute-start.34
  175.2 0.2 collective-permute-done.32.refs_5_
  175.4 2.1 %collective-permute-done.33.refs_6_ = bf16[2,64,256]{2,1,0:T(8,128)(2,1)S(1)} collective-permute-done((bf16[2,64,256]{2,1,0:T(8,128)(2,1)S(1)}, bf16[2,64,256]{2,1,0:T(8,128)(2,1)S(1)}, u32[]{:S(2)}, u32[]{:S(2)}) %collective-permute-start.33) | collective-permute-done | bytes 65568 | tf_op jit(solution)/shard_map/side_out/ppermute | solution.py:370
  177.4 0.8 collective-permute-done.34.refs_7_
  178.2 1.8 %finish.1 = bf16[48,64,256]{2,1,0:T(8,128)(2,1)} custom-call(s32[4]{0:T(128)S(1)} %pad_add_fusion.place, bf16[2,64,256]{2,1,0:T(8,128)(2,1)S(1)} %get-tuple-element.112.refs_0_, bf16[2,64,256]{2,1,0:T(8,128)(2,1)S(1)} %collective-permute-done.28.refs_1_, bf16[2,64,256]{2,1,0:T(8,128)(2,1)S(1)} %collective-permute-done.29.refs_2_, ...), custom_call_target="tpu_custom_call" | custom-call | tf_op jit(solution)/shard_map/finish/pallas_call | solution.py:356
  (29 shorter events, 0.4 us)
Async XLA Ops:
  1.1 35.2 %collective-permute-start = (bf16[8,64,256]{2,1,0:T(8,128)(2,1)S(1)}, bf16[8,64,256]{2,1,0:T(8,128)(2,1)S(1)}, u32[]{:S(2)}, u32[]{:S(2)}) collective-permute-start(bf16[8,64,256]{2,1,0:T(8,128)(2,1)S(1)} %get-tuple-element.122), channel_id=1, source_target_pairs={{0,16},{16,0},{1,17},{17,1},{2,18},{18,2},{3,19},{19,3},{4,20},{20... | collective-permute-start | bytes 786440 | tf_op jit(solution)/shard_map/side_in/ppermute | solution.py:375
  36.4 30.3 %all-to-all-start = ((bf16[16,2,64,256]{3,2,1,0:T(8,128)(2,1)}), bf16[16,2,64,256]{3,2,1,0:T(8,128)(2,1)}, u32[]{:S(2)}, u32[]{:S(2)}) async-start(bf16[16,2,64,256]{3,2,1,0:T(8,128)(2,1)} %bitcast.23), calls=%async_computation | async-start | bytes 2097152 | tf_op jit(solution)/shard_map/panels_in/all_to_all | solution.py:402
  44.2 16.5 %collective-permute-start.1 = (bf16[2,64,256]{2,1,0:T(8,128)(2,1)S(1)}, bf16[2,64,256]{2,1,0:T(8,128)(2,1)S(1)}, u32[]{:S(2)}, u32[]{:S(2)}) collective-permute-start(bf16[2,64,256]{2,1,0:T(8,128)(2,1)S(1)} %get-tuple-element.69), channel_id=1, source_target_pairs={{0,128},{32,160},{64,192},{96,224},{128,0},{160,32},{192,64},{224,... | collective-permute-start | bytes 196616 | tf_op jit(solution)/shard_map/side_in/ppermute | solution.py:370
  51.5 10.3 %collective-permute-start.2 = (bf16[2,64,256]{2,1,0:T(8,128)(2,1)S(1)}, bf16[2,64,256]{2,1,0:T(8,128)(2,1)S(1)}, u32[]{:S(2)}, u32[]{:S(2)}) collective-permute-start(bf16[2,64,256]{2,1,0:T(8,128)(2,1)S(1)} %get-tuple-element.70), channel_id=1, source_target_pairs={{0,96},{32,128},{64,160},{96,192},{128,224},{160,0},{192,32},{224,... | collective-permute-start | bytes 196616 | tf_op jit(solution)/shard_map/side_in/ppermute | solution.py:370
  53.4 10.5 %collective-permute-start.3 = (bf16[2,64,256]{2,1,0:T(8,128)(2,1)S(1)}, bf16[2,64,256]{2,1,0:T(8,128)(2,1)S(1)}, u32[]{:S(2)}, u32[]{:S(2)}) collective-permute-start(bf16[2,64,256]{2,1,0:T(8,128)(2,1)S(1)} %get-tuple-element.71), channel_id=1, source_target_pairs={{0,160},{32,192},{64,224},{96,0},{128,32},{160,64},{192,96},{224,1... | collective-permute-start | bytes 196616 | tf_op jit(solution)/shard_map/side_in/ppermute | solution.py:370
  56.5 7.4 %collective-permute-start.4 = (bf16[2,64,256]{2,1,0:T(8,128)(2,1)S(1)}, bf16[2,64,256]{2,1,0:T(8,128)(2,1)S(1)}, u32[]{:S(2)}, u32[]{:S(2)}) collective-permute-start(bf16[2,64,256]{2,1,0:T(8,128)(2,1)S(1)} %get-tuple-element.72), channel_id=1, source_target_pairs={{0,64},{32,96},{64,128},{96,160},{128,192},{160,224},{192,0},{224,... | collective-permute-start | bytes 196616 | tf_op jit(solution)/shard_map/side_in/ppermute | solution.py:370
  58.0 6.6 %collective-permute-start.5 = (bf16[2,64,256]{2,1,0:T(8,128)(2,1)S(1)}, bf16[2,64,256]{2,1,0:T(8,128)(2,1)S(1)}, u32[]{:S(2)}, u32[]{:S(2)}) collective-permute-start(bf16[2,64,256]{2,1,0:T(8,128)(2,1)S(1)} %get-tuple-element.73), channel_id=1, source_target_pairs={{0,192},{32,224},{64,0},{96,32},{128,64},{160,96},{192,128},{224,1... | collective-permute-start | bytes 196616 | tf_op jit(solution)/shard_map/side_in/ppermute | solution.py:370
  60.6 5.5 %collective-permute-start.6 = (bf16[2,64,256]{2,1,0:T(8,128)(2,1)S(1)}, bf16[2,64,256]{2,1,0:T(8,128)(2,1)S(1)}, u32[]{:S(2)}, u32[]{:S(2)}) collective-permute-start(bf16[2,64,256]{2,1,0:T(8,128)(2,1)S(1)} %get-tuple-element.74), channel_id=1, source_target_pairs={{0,32},{32,64},{64,96},{96,128},{128,160},{160,192},{192,224},{224... | collective-permute-start | bytes 196616 | tf_op jit(solution)/shard_map/side_in/ppermute | solution.py:370
  61.8 4.4 %collective-permute-start.7 = (bf16[2,64,256]{2,1,0:T(8,128)(2,1)S(1)}, bf16[2,64,256]{2,1,0:T(8,128)(2,1)S(1)}, u32[]{:S(2)}, u32[]{:S(2)}) collective-permute-start(bf16[2,64,256]{2,1,0:T(8,128)(2,1)S(1)} %get-tuple-element.75), channel_id=1, source_target_pairs={{0,224},{32,0},{64,32},{96,64},{128,96},{160,128},{192,160},{224,1... | collective-permute-start | bytes 196616 | tf_op jit(solution)/shard_map/side_in/ppermute | solution.py:370
  66.7 31.3 %all-to-all-start.1 = ((bf16[8,2,2,64,256]{4,3,2,1,0:T(8,128)(2,1)}), bf16[8,2,2,64,256]{4,3,2,1,0:T(8,128)(2,1)S(1)}, u32[]{:S(2)}, u32[]{:S(2)}) async-start(bf16[8,2,2,64,256]{4,3,2,1,0:T(8,128)(2,1)} %bitcast.8.direct), calls=%async_computation.1 | async-start | bytes 2097152 | tf_op jit(solution)/shard_map/mirror/all_to_all | solution.py:410
  71.2 25.2 %collective-permute-start.8 = (bf16[8,2,2,64,256]{4,3,2,1,0:T(8,128)(2,1)}, bf16[8,2,2,64,256]{4,3,2,1,0:T(8,128)(2,1)S(1)}, u32[]{:S(2)}, u32[]{:S(2)}) collective-permute-start(bf16[8,2,2,64,256]{4,3,2,1,0:T(8,128)(2,1)} %bitcast.8.direct), channel_id=1, source_target_pairs={{0,8},{8,0},{1,9},{9,1},{2,10},{10,2},{3,11},{11,3},{4,12},{12,4},... | collective-permute-start | bytes 3145736 | tf_op jit(solution)/shard_map/ppermute | solution.py:375
  71.8 10.4 %collective-permute-start.9 = (bf16[2,64,256]{2,1,0:T(8,128)(2,1)S(1)}, bf16[2,64,256]{2,1,0:T(8,128)(2,1)S(1)}, u32[]{:S(2)}, u32[]{:S(2)}) collective-permute-start(bf16[2,64,256]{2,1,0:T(8,128)(2,1)S(1)} %get-tuple-element.80), channel_id=1, source_target_pairs={{0,3},{1,4},{2,5},{3,6},{4,7},{5,0},{6,1},{7,2},{8,11},{9,12},{10,... | collective-permute-start | bytes 196616 | tf_op jit(solution)/shard_map/side_mirror/ppermute | solution.py:370
  75.8 8.6 %collective-permute-start.10 = (bf16[2,64,256]{2,1,0:T(8,128)(2,1)S(1)}, bf16[2,64,256]{2,1,0:T(8,128)(2,1)S(1)}, u32[]{:S(2)}, u32[]{:S(2)}) collective-permute-start(bf16[2,64,256]{2,1,0:T(8,128)(2,1)S(1)} %get-tuple-element.81), channel_id=1, source_target_pairs={{0,5},{1,6},{2,7},{3,0},{4,1},{5,2},{6,3},{7,4},{8,13},{9,14},{10,... | collective-permute-start | bytes 196616 | tf_op jit(solution)/shard_map/side_mirror/ppermute | solution.py:370
  77.9 7.5 %collective-permute-start.11 = (bf16[2,64,256]{2,1,0:T(8,128)(2,1)S(1)}, bf16[2,64,256]{2,1,0:T(8,128)(2,1)S(1)}, u32[]{:S(2)}, u32[]{:S(2)}) collective-permute-start(bf16[2,64,256]{2,1,0:T(8,128)(2,1)S(1)} %get-tuple-element.82), channel_id=1, source_target_pairs={{0,1},{1,2},{2,3},{3,4},{4,5},{5,6},{6,7},{7,0},{8,9},{9,10},{10,1... | collective-permute-start | bytes 196616 | tf_op jit(solution)/shard_map/side_mirror/ppermute | solution.py:370
  79.3 7.1 %collective-permute-start.12 = (bf16[2,64,256]{2,1,0:T(8,128)(2,1)S(1)}, bf16[2,64,256]{2,1,0:T(8,128)(2,1)S(1)}, u32[]{:S(2)}, u32[]{:S(2)}) collective-permute-start(bf16[2,64,256]{2,1,0:T(8,128)(2,1)S(1)} %get-tuple-element.83), channel_id=1, source_target_pairs={{0,7},{1,0},{2,1},{3,2},{4,3},{5,4},{6,5},{7,6},{8,15},{9,8},{10,9... | collective-permute-start | bytes 196616 | tf_op jit(solution)/shard_map/side_mirror/ppermute | solution.py:370
  82.3 6.3 %collective-permute-start.13 = (bf16[2,64,256]{2,1,0:T(8,128)(2,1)S(1)}, bf16[2,64,256]{2,1,0:T(8,128)(2,1)S(1)}, u32[]{:S(2)}, u32[]{:S(2)}) collective-permute-start(bf16[2,64,256]{2,1,0:T(8,128)(2,1)S(1)} %get-tuple-element.84), channel_id=1, source_target_pairs={{0,4},{1,5},{2,6},{3,7},{4,0},{5,1},{6,2},{7,3},{8,12},{9,13},{10,... | collective-permute-start | bytes 196616 | tf_op jit(solution)/shard_map/side_mirror/ppermute | solution.py:370
  84.4 4.4 %collective-permute-start.14 = (bf16[2,64,256]{2,1,0:T(8,128)(2,1)S(1)}, bf16[2,64,256]{2,1,0:T(8,128)(2,1)S(1)}, u32[]{:S(2)}, u32[]{:S(2)}) collective-permute-start(bf16[2,64,256]{2,1,0:T(8,128)(2,1)S(1)} %get-tuple-element.85), channel_id=1, source_target_pairs={{0,2},{1,3},{2,4},{3,5},{4,6},{5,7},{6,0},{7,1},{8,10},{9,11},{10,... | collective-permute-start | bytes 196616 | tf_op jit(solution)/shard_map/side_mirror/ppermute | solution.py:370
  85.4 4.3 %collective-permute-start.15 = (bf16[2,64,256]{2,1,0:T(8,128)(2,1)S(1)}, bf16[2,64,256]{2,1,0:T(8,128)(2,1)S(1)}, u32[]{:S(2)}, u32[]{:S(2)}) collective-permute-start(bf16[2,64,256]{2,1,0:T(8,128)(2,1)S(1)} %get-tuple-element.86), channel_id=1, source_target_pairs={{0,6},{1,7},{2,0},{3,1},{4,2},{5,3},{6,4},{7,5},{8,14},{9,15},{10,... | collective-permute-start | bytes 196616 | tf_op jit(solution)/shard_map/side_mirror/ppermute | solution.py:370
  86.4 3.9 %collective-permute-start.17 = (bf16[8,2,64,256]{3,2,1,0:T(8,128)(2,1)S(1)}, bf16[8,2,64,256]{3,2,1,0:T(8,128)(2,1)S(1)}, u32[]{:S(2)}, u32[]{:S(2)}) collective-permute-start(bf16[8,2,64,256]{3,2,1,0:T(8,128)(2,1)S(1)} %collect.3.x_ref), channel_id=1, source_target_pairs={{0,8},{8,0},{1,9},{9,1},{2,10},{10,2},{3,11},{11,3},{4,12},{12,4},... | collective-permute-start | bytes 1572872 | tf_op jit(solution)/shard_map/side_mirror/ppermute | solution.py:375
  90.2 2.0 %collective-permute-start.16 = (bf16[8,2,64,256]{3,2,1,0:T(8,128)(2,1)S(1)}, bf16[8,2,64,256]{3,2,1,0:T(8,128)(2,1)S(1)}, u32[]{:S(2)}, u32[]{:S(2)}) collective-permute-start(bf16[8,2,64,256]{3,2,1,0:T(8,128)(2,1)S(1)} %collect.4), channel_id=1, source_target_pairs={{0,8},{8,0},{1,9},{9,1},{2,10},{10,2},{3,11},{11,3},{4,12},{12,4},... | collective-permute-start | bytes 1572872 | tf_op jit(solution)/shard_map/side_mirror/ppermute | solution.py:375
  98.0 2.7 %collective-permute-start.18 = (bf16[8,2,2,64,256]{4,3,2,1,0:T(8,128)(2,1)S(1)}, bf16[8,2,2,64,256]{4,3,2,1,0:T(8,128)(2,1)S(1)}, u32[]{:S(2)}, u32[]{:S(2)}) collective-permute-start(bf16[8,2,2,64,256]{4,3,2,1,0:T(8,128)(2,1)S(1)} %all-to-all-done.1.turned), channel_id=1, source_target_pairs={{0,8},{8,0},{1,9},{9,1},{2,10},{10,2},{3,11},{11,3},{4,12},{12,4},... | collective-permute-start | bytes 3145736 | tf_op jit(solution)/shard_map/ppermute | solution.py:375
  107.5 35.6 %all-to-all-start.2 = ((bf16[8,2,256,128]{3,2,1,0:T(8,128)(2,1)}), bf16[8,2,256,128]{3,2,1,0:T(8,128)(2,1)S(1)}, u32[]{:S(2)}, u32[]{:S(2)}) async-start(bf16[8,2,256,128]{3,2,1,0:T(8,128)(2,1)} %first_half.1), calls=%async_computation.2 | async-start | bytes 2097152 | tf_op jit(solution)/shard_map/partial/all_to_all | solution.py:429
  114.0 15.0 %collective-permute-start.19 = (bf16[1,256,128]{2,1,0:T(8,128)(2,1)S(1)}, bf16[1,256,128]{2,1,0:T(8,128)(2,1)S(1)}, u32[]{:S(2)}, u32[]{:S(2)}) collective-permute-start(bf16[1,256,128]{2,1,0:T(8,128)(2,1)S(1)} %get-tuple-element.99), channel_id=1, source_target_pairs={{0,3},{1,4},{2,5},{3,6},{4,7},{5,0},{6,1},{7,2},{8,11},{9,12},{10,... | collective-permute-start | bytes 196616 | tf_op jit(solution)/shard_map/side_partial/ppermute | solution.py:370
  116.0 13.0 %collective-permute-start.20 = (bf16[1,256,128]{2,1,0:T(8,128)(2,1)S(1)}, bf16[1,256,128]{2,1,0:T(8,128)(2,1)S(1)}, u32[]{:S(2)}, u32[]{:S(2)}) collective-permute-start(bf16[1,256,128]{2,1,0:T(8,128)(2,1)S(1)} %get-tuple-element.100), channel_id=1, source_target_pairs={{0,5},{1,6},{2,7},{3,0},{4,1},{5,2},{6,3},{7,4},{8,13},{9,14},{10,... | collective-permute-start | bytes 196616 | tf_op jit(solution)/shard_map/side_partial/ppermute | solution.py:370
  119.9 11.1 %collective-permute-start.21 = (bf16[1,256,128]{2,1,0:T(8,128)(2,1)S(1)}, bf16[1,256,128]{2,1,0:T(8,128)(2,1)S(1)}, u32[]{:S(2)}, u32[]{:S(2)}) collective-permute-start(bf16[1,256,128]{2,1,0:T(8,128)(2,1)S(1)} %get-tuple-element.101), channel_id=1, source_target_pairs={{0,1},{1,2},{2,3},{3,4},{4,5},{5,6},{6,7},{7,0},{8,9},{9,10},{10,1... | collective-permute-start | bytes 196616 | tf_op jit(solution)/shard_map/side_partial/ppermute | solution.py:370
  121.6 9.4 %collective-permute-start.22 = (bf16[1,256,128]{2,1,0:T(8,128)(2,1)S(1)}, bf16[1,256,128]{2,1,0:T(8,128)(2,1)S(1)}, u32[]{:S(2)}, u32[]{:S(2)}) collective-permute-start(bf16[1,256,128]{2,1,0:T(8,128)(2,1)S(1)} %get-tuple-element.102), channel_id=1, source_target_pairs={{0,7},{1,0},{2,1},{3,2},{4,3},{5,4},{6,5},{7,6},{8,15},{9,8},{10,9... | collective-permute-start | bytes 196616 | tf_op jit(solution)/shard_map/side_partial/ppermute | solution.py:370
  124.3 7.8 %collective-permute-start.23 = (bf16[1,256,128]{2,1,0:T(8,128)(2,1)S(1)}, bf16[1,256,128]{2,1,0:T(8,128)(2,1)S(1)}, u32[]{:S(2)}, u32[]{:S(2)}) collective-permute-start(bf16[1,256,128]{2,1,0:T(8,128)(2,1)S(1)} %get-tuple-element.103), channel_id=1, source_target_pairs={{0,4},{1,5},{2,6},{3,7},{4,0},{5,1},{6,2},{7,3},{8,12},{9,13},{10,... | collective-permute-start | bytes 196616 | tf_op jit(solution)/shard_map/side_partial/ppermute | solution.py:370
  129.0 4.3 %collective-permute-start.24 = (bf16[1,256,128]{2,1,0:T(8,128)(2,1)S(1)}, bf16[1,256,128]{2,1,0:T(8,128)(2,1)S(1)}, u32[]{:S(2)}, u32[]{:S(2)}) collective-permute-start(bf16[1,256,128]{2,1,0:T(8,128)(2,1)S(1)} %get-tuple-element.104), channel_id=1, source_target_pairs={{0,2},{1,3},{2,4},{3,5},{4,6},{5,7},{6,0},{7,1},{8,10},{9,11},{10,... | collective-permute-start | bytes 196616 | tf_op jit(solution)/shard_map/side_partial/ppermute | solution.py:370
  129.0 4.3 %collective-permute-start.25 = (bf16[1,256,128]{2,1,0:T(8,128)(2,1)S(1)}, bf16[1,256,128]{2,1,0:T(8,128)(2,1)S(1)}, u32[]{:S(2)}, u32[]{:S(2)}) collective-permute-start(bf16[1,256,128]{2,1,0:T(8,128)(2,1)S(1)} %get-tuple-element.105), channel_id=1, source_target_pairs={{0,6},{1,7},{2,0},{3,1},{4,2},{5,3},{6,4},{7,5},{8,14},{9,15},{10,... | collective-permute-start | bytes 196616 | tf_op jit(solution)/shard_map/side_partial/ppermute | solution.py:370
  133.9 2.0 %collective-permute-start.26 = (bf16[8,1,256,128]{3,2,1,0:T(8,128)(2,1)S(1)}, bf16[8,1,256,128]{3,2,1,0:T(8,128)(2,1)S(1)}, u32[]{:S(2)}, u32[]{:S(2)}) collective-permute-start(bf16[8,1,256,128]{3,2,1,0:T(8,128)(2,1)S(1)} %collect.5.t_ref), channel_id=1, source_target_pairs={{0,8},{8,0},{1,9},{9,1},{2,10},{10,2},{3,11},{11,3},{4,12},{12,4},... | collective-permute-start | bytes 1572872 | tf_op jit(solution)/shard_map/side_partial/ppermute | solution.py:375
  140.7 8.8 %collective-permute-start.27 = (bf16[8,64,256]{2,1,0:T(8,128)(2,1)S(1)}, bf16[8,64,256]{2,1,0:T(8,128)(2,1)S(1)}, u32[]{:S(2)}, u32[]{:S(2)}) collective-permute-start(bf16[8,64,256]{2,1,0:T(8,128)(2,1)S(1)} %get-tuple-element.108), channel_id=1, source_target_pairs={{0,16},{16,0},{1,17},{17,1},{2,18},{18,2},{3,19},{19,3},{4,20},{20... | collective-permute-start | bytes 786440 | tf_op jit(solution)/shard_map/ppermute | solution.py:375
  149.5 28.7 %all-to-all-start.3 = ((bf16[16,2,64,256]{3,2,1,0:T(8,128)(2,1)}), bf16[16,2,64,256]{3,2,1,0:T(8,128)(2,1)S(1)}, u32[]{:S(2)}, u32[]{:S(2)}) async-start(bf16[16,2,64,256]{3,2,1,0:T(8,128)(2,1)} %bitcast.13), calls=%async_computation.3 | async-start | bytes 2097152 | tf_op jit(solution)/shard_map/panels_out/all_to_all | solution.py:443
  158.3 13.7 %collective-permute-start.28 = (bf16[2,64,256]{2,1,0:T(8,128)(2,1)S(1)}, bf16[2,64,256]{2,1,0:T(8,128)(2,1)S(1)}, u32[]{:S(2)}, u32[]{:S(2)}) collective-permute-start(bf16[2,64,256]{2,1,0:T(8,128)(2,1)S(1)} %get-tuple-element.113), channel_id=1, source_target_pairs={{0,128},{32,160},{64,192},{96,224},{128,0},{160,32},{192,64},{224,... | collective-permute-start | bytes 196616 | tf_op jit(solution)/shard_map/side_out/ppermute | solution.py:370
  162.8 11.2 %collective-permute-start.29 = (bf16[2,64,256]{2,1,0:T(8,128)(2,1)S(1)}, bf16[2,64,256]{2,1,0:T(8,128)(2,1)S(1)}, u32[]{:S(2)}, u32[]{:S(2)}) collective-permute-start(bf16[2,64,256]{2,1,0:T(8,128)(2,1)S(1)} %get-tuple-element.114), channel_id=1, source_target_pairs={{0,96},{32,128},{64,160},{96,192},{128,224},{160,0},{192,32},{224,... | collective-permute-start | bytes 196616 | tf_op jit(solution)/shard_map/side_out/ppermute | solution.py:370
  163.4 11.8 %collective-permute-start.30 = (bf16[2,64,256]{2,1,0:T(8,128)(2,1)S(1)}, bf16[2,64,256]{2,1,0:T(8,128)(2,1)S(1)}, u32[]{:S(2)}, u32[]{:S(2)}) collective-permute-start(bf16[2,64,256]{2,1,0:T(8,128)(2,1)S(1)} %get-tuple-element.115), channel_id=1, source_target_pairs={{0,160},{32,192},{64,224},{96,0},{128,32},{160,64},{192,96},{224,1... | collective-permute-start | bytes 196616 | tf_op jit(solution)/shard_map/side_out/ppermute | solution.py:370
  167.8 7.4 %collective-permute-start.31 = (bf16[2,64,256]{2,1,0:T(8,128)(2,1)S(1)}, bf16[2,64,256]{2,1,0:T(8,128)(2,1)S(1)}, u32[]{:S(2)}, u32[]{:S(2)}) collective-permute-start(bf16[2,64,256]{2,1,0:T(8,128)(2,1)S(1)} %get-tuple-element.116), channel_id=1, source_target_pairs={{0,64},{32,96},{64,128},{96,160},{128,192},{160,224},{192,0},{224,... | collective-permute-start | bytes 196616 | tf_op jit(solution)/shard_map/side_out/ppermute | solution.py:370
  168.4 7.0 %collective-permute-start.32 = (bf16[2,64,256]{2,1,0:T(8,128)(2,1)S(1)}, bf16[2,64,256]{2,1,0:T(8,128)(2,1)S(1)}, u32[]{:S(2)}, u32[]{:S(2)}) collective-permute-start(bf16[2,64,256]{2,1,0:T(8,128)(2,1)S(1)} %get-tuple-element.117), channel_id=1, source_target_pairs={{0,192},{32,224},{64,0},{96,32},{128,64},{160,96},{192,128},{224,1... | collective-permute-start | bytes 196616 | tf_op jit(solution)/shard_map/side_out/ppermute | solution.py:370
  172.0 5.5 %collective-permute-start.33 = (bf16[2,64,256]{2,1,0:T(8,128)(2,1)S(1)}, bf16[2,64,256]{2,1,0:T(8,128)(2,1)S(1)}, u32[]{:S(2)}, u32[]{:S(2)}) collective-permute-start(bf16[2,64,256]{2,1,0:T(8,128)(2,1)S(1)} %get-tuple-element.118), channel_id=1, source_target_pairs={{0,32},{32,64},{64,96},{96,128},{128,160},{160,192},{192,224},{224... | collective-permute-start | bytes 196616 | tf_op jit(solution)/shard_map/side_out/ppermute | solution.py:370
  174.0 4.3 %collective-permute-start.34 = (bf16[2,64,256]{2,1,0:T(8,128)(2,1)S(1)}, bf16[2,64,256]{2,1,0:T(8,128)(2,1)S(1)}, u32[]{:S(2)}, u32[]{:S(2)}) collective-permute-start(bf16[2,64,256]{2,1,0:T(8,128)(2,1)S(1)} %get-tuple-element.119), channel_id=1, source_target_pairs={{0,224},{32,0},{64,32},{96,64},{128,96},{160,128},{192,160},{224,1... | collective-permute-start | bytes 196616 | tf_op jit(solution)/shard_map/side_out/ppermute | solution.py:370

commit v3 on v2

--- a/solution.py
+++ b/solution.py
@@ -53,6 +53,35 @@
     return [pltpu.VMEM((STEPS, size // STEPS, width), BF16), pltpu.SemaphoreType.DMA((STEPS,))]
 
 
+def columns_of(c_hbm, c_ref, sems, step):
+    width = c_ref.shape[2]
+    return pltpu.make_async_copy(
+        c_hbm.at[:, pl.ds(pl.multiple_of(step * width, width), width)], c_ref.at[step], sems.at[step]
+    )
+
+
+def fetch_columns(c_hbm, c_ref, sems):
+    def start(step, carry):
+        columns_of(c_hbm, c_ref, sems, step).start()
+        return carry
+
+    lax.fori_loop(0, STEPS, start, 0)
+
+
+def products(left, c_hbm, c_ref, sems, store):
+    def run(step, carry):
+        columns_of(c_hbm, c_ref, sems, step).wait()
+        store(step, jnp.dot(left[...], c_ref[step], preferred_element_type=F32).astype(BF16))
+        return carry
+
+    lax.fori_loop(0, STEPS, run, 0)
+
+
+def column_scratch(value):
+    size, width = value.shape
+    return [pltpu.VMEM((STEPS, size, width // STEPS), BF16), pltpu.SemaphoreType.DMA((STEPS,))]
+
+
 def set_identity(eye):
     row = lax.broadcasted_iota(jnp.int32, eye.shape, 0)
     column = lax.broadcasted_iota(jnp.int32, eye.shape, 1)
@@ -66,9 +95,10 @@
     ).astype(BF16)
 
 
-def pick_kernel(place, c_hbm, panel_hbm, out_hbm, main_hbm, c_ref, sems, chosen, out_sems, main_sem):
-    main = pltpu.make_async_copy(panel_hbm.at[pl.ds(0, main_hbm.shape[0])], main_hbm, main_sem)
-    main.start()
+def pick_kernel(place, c_hbm, panel_hbm, out_hbm, main_hbm, c_ref, sems, chosen, out_sems, panel, main_sems):
+    main_in = pltpu.make_async_copy(panel_hbm.at[pl.ds(0, main_hbm.shape[0])], panel, main_sems.at[0])
+    main_out = pltpu.make_async_copy(panel, main_hbm, main_sems.at[1])
+    main_in.start()
     block = c_hbm.shape[1] // BLOCKS
     lanes = block // CORE
     half = lanes // 2
@@ -97,8 +127,10 @@
         return carry
 
     steps(c_hbm, c_ref, sems, choose)
+    main_in.wait()
+    main_out.start()
     lax.fori_loop(0, STEPS, finish_store, 0)
-    main.wait()
+    main_out.wait()
 
 
 def pick_columns(place, orbitals, half_panel, main_pairs):
@@ -111,7 +143,7 @@
         out_specs=[HBM, HBM],
         scratch_shapes=fetch_scratch(orbitals) + [
             pltpu.VMEM((STEPS, size // STEPS, width), BF16), pltpu.SemaphoreType.DMA((STEPS,)),
-            pltpu.SemaphoreType.DMA(())],
+            pltpu.VMEM((main_pairs,) + half_panel.shape[1:], BF16), pltpu.SemaphoreType.DMA((2,))],
         compiler_params=PARAMS,
         name="pick_columns",
     )(place, in_hbm(orbitals), in_hbm(half_panel))
@@ -119,58 +151,59 @@
 
 def first_kernel(index, place, direct, direct_other, turned, turned_other, c_hbm, *rest):
     t_refs = rest[:-6]
-    c_ref, sems, sym, turn, total, eye = rest[-6:]
-    set_identity(eye)
+    c_ref, sems, sym, turn, final, eye = rest[-6:]
     _, _, depth, rows, block = direct.shape
     mine, core = place[index], place[AT_CORE]
-    per_step = BLOCKS // STEPS
-    total[...] = jnp.zeros(total.shape, F32)
-
-    def work(step):
-        for u in range(per_step):
-            b = step * per_step + u
-            cols = slice(u * block, (u + 1) * block)
-
-            @pl.when(b >= mine)
-            def _():
-                for k in range(depth):
-                    for y in range(YLO):
-                        at = k * block + y * CORE * rows
-                        sym[pl.ds(pl.multiple_of(at + core * rows, rows), rows), cols] = direct[b, y, k]
-                        sym[pl.ds(pl.multiple_of(at + (1 - core) * rows, rows), rows), cols] = direct_other[b, y, k]
-
-            @pl.when(b == mine)
-            def _():
-                row = lax.broadcasted_iota(jnp.int32, (block, block), 0)
-                column = lax.broadcasted_iota(jnp.int32, (block, block), 1)
-                for k in range(depth):
-                    upper = sym[k * block:(k + 1) * block, cols]
-                    sym[k * block:(k + 1) * block, cols] = jnp.where(row <= column, upper, transposed(upper, eye))
-
-            @pl.when(b < mine)
-            def _():
-                for k in range(depth):
-                    for y in range(YLO):
-                        at = k * block + y * CORE * rows
-                        turn[pl.ds(pl.multiple_of(at + core * rows, rows), rows), :] = turned[b, y, k]
-                        turn[pl.ds(pl.multiple_of(at + (1 - core) * rows, rows), rows), :] = turned_other[b, y, k]
-                for k in range(depth):
-                    sym[k * block:(k + 1) * block, cols] = transposed(turn[k * block:(k + 1) * block], eye)
-
-        fetch_of(c_hbm, c_ref, sems, step).wait()
-        total[...] += jnp.dot(sym[...], c_ref[step], preferred_element_type=F32)
-
-    steps(c_hbm, c_ref, sems, work)
+    fetch_columns(c_hbm, c_ref, sems)
+    set_identity(eye)
+
+    def build(b, carry):
+        cols = pl.ds(pl.multiple_of(b * block, block), block)
+
+        @pl.when(b >= mine)
+        def _():
+            for k in range(depth):
+                for y in range(YLO):
+                    at = k * block + y * CORE * rows
+                    sym[pl.ds(pl.multiple_of(at + core * rows, rows), rows), cols] = direct[b, y, k]
+                    sym[pl.ds(pl.multiple_of(at + (1 - core) * rows, rows), rows), cols] = direct_other[b, y, k]
+
+        @pl.when(b == mine)
+        def _():
+            row = lax.broadcasted_iota(jnp.int32, (block, block), 0)
+            column = lax.broadcasted_iota(jnp.int32, (block, block), 1)
+            for k in range(depth):
+                upper = sym[k * block:(k + 1) * block, cols]
+                sym[k * block:(k + 1) * block, cols] = jnp.where(row <= column, upper, transposed(upper, eye))
+
+        @pl.when(b < mine)
+        def _():
+            for k in range(depth):
+                for y in range(YLO):
+                    at = k * block + y * CORE * rows
+                    turn[pl.ds(pl.multiple_of(at + core * rows, rows), rows), :] = turned[b, y, k]
+                    turn[pl.ds(pl.multiple_of(at + (1 - core) * rows, rows), rows), :] = turned_other[b, y, k]
+            for k in range(depth):
+                sym[k * block:(k + 1) * block, cols] = transposed(turn[k * block:(k + 1) * block], eye)
+
+        return carry
+
+    def store(step, product):
+        width = product.shape[1]
+        final[:, pl.ds(pl.multiple_of(step * width, width), width)] = product
+
+    lax.fori_loop(0, BLOCKS, build, 0)
+    products(sym, c_hbm, c_ref, sems, store)
     if len(t_refs) == 1:
         lanes = t_refs[0].shape[3]
         for part in range(BLOCKS):
             for k in range(depth):
-                t_refs[0][part, k] = total[k * block:(k + 1) * block, part * lanes:(part + 1) * lanes].astype(BF16)
+                t_refs[0][part, k] = final[k * block:(k + 1) * block, part * lanes:(part + 1) * lanes]
     else:
         lanes = t_refs[0].shape[2]
         for d in range(BLOCKS):
             part = (mine + ORDER[index][d]) % BLOCKS
-            t_refs[d][0] = total[:, pl.ds(pl.multiple_of(part * lanes, lanes), lanes)].astype(BF16)
+            t_refs[d][0] = final[:, pl.ds(pl.multiple_of(part * lanes, lanes), lanes)]
 
 
 def first_half(index, place, direct, direct_other, turned, turned_other, picked, outs, name):
@@ -182,36 +215,37 @@
         out_shape=[jax.ShapeDtypeStruct(out, BF16) for out in outs],
         in_specs=[pl.BlockSpec(memory_space=pltpu.SMEM), vmem, vmem, vmem, vmem, HBM],
         out_specs=[vmem] * len(outs),
-        scratch_shapes=fetch_scratch(picked) + [
-            pltpu.VMEM((depth * block, size // STEPS), BF16),
+        scratch_shapes=column_scratch(picked) + [
+            pltpu.VMEM((depth * block, size), BF16),
             pltpu.VMEM((depth * block, block), BF16),
-            pltpu.VMEM((depth * block, width), F32),
+            pltpu.VMEM((depth * block, width), BF16),
             pltpu.VMEM((block, block), BF16)],
         compiler_params=PARAMS,
         name=name,
     )(place, direct, direct_other, turned, turned_other, in_hbm(picked))
 
 
-def second_kernel(t_ref, c_hbm, out_ref, c_ref, sems, left, total, eye):
-    set_identity(eye)
+def second_kernel(t_ref, c_hbm, out_ref, c_ref, sems, left, eye):
     count, depth, block, lanes = t_ref.shape
     rows = lanes // YLO
-    per_step = count // STEPS
-    total[...] = jnp.zeros(total.shape, F32)
-
-    def work(step):
+    fetch_columns(c_hbm, c_ref, sems)
+    set_identity(eye)
+
+    def build(b, carry):
+        for k in range(depth):
+            left[k * lanes:(k + 1) * lanes, pl.ds(pl.multiple_of(b * block, block), block)] = transposed(t_ref[b, k], eye)
+        return carry
+
+    def store(step, product):
+        per_step = COLS // STEPS
         for u in range(per_step):
-            for k in range(depth):
-                left[k * lanes:(k + 1) * lanes, u * block:(u + 1) * block] = transposed(t_ref[step * per_step + u, k], eye)
-        fetch_of(c_hbm, c_ref, sems, step).wait()
-        total[...] += jnp.dot(left[...], c_ref[step], preferred_element_type=F32)
-
-    steps(c_hbm, c_ref, sems, work)
-    for c in range(COLS):
-        for y in range(YLO):
-            for k in range(depth):
-                at = k * lanes + y * rows
-                out_ref[c, y, k] = total[at:at + rows, c * block:(c + 1) * block].astype(BF16)
+            for y in range(YLO):
+                for k in range(depth):
+                    at = k * lanes + y * rows
+                    out_ref[step * per_step + u, y, k] = product[at:at + rows, u * block:(u + 1) * block]
+
+    lax.fori_loop(0, count, build, 0)
+    products(left, c_hbm, c_ref, sems, store)
 
 
 def second_half(partial_value, orbitals):
@@ -223,39 +257,37 @@
         out_shape=jax.ShapeDtypeStruct((COLS, YLO, depth, lanes // YLO, block), BF16),
         in_specs=[vmem, HBM],
         out_specs=vmem,
-        scratch_shapes=fetch_scratch(orbitals) + [
-            pltpu.VMEM((depth * lanes, size // STEPS), BF16),
-            pltpu.VMEM((depth * lanes, size), F32),
+        scratch_shapes=column_scratch(orbitals) + [
+            pltpu.VMEM((depth * lanes, size), BF16),
             pltpu.VMEM((lanes, lanes), BF16)],
         compiler_params=PARAMS,
         name="second_half",
     )(partial_value, in_hbm(orbitals))
 
 
-def second_side_kernel(place, t_ref, other_ref, c_hbm, keep, send, c_ref, sems, left, total, final, eye):
-    set_identity(eye)
+def second_side_kernel(place, t_ref, other_ref, c_hbm, keep, send, c_ref, sems, left, final, eye):
     count, _, block, lanes = t_ref.shape
     rows = lanes // YLO
-    per_step = count // STEPS
     ylo, core = place[AT_YLO], place[AT_CORE]
-    total[...] = jnp.zeros(total.shape, F32)
-
-    def work(step):
-        for u in range(per_step):
-            cols = slice(u * block, (u + 1) * block)
-            own = transposed(t_ref[step * per_step + u, 0], eye)
-            other = transposed(other_ref[step * per_step + u, 0], eye)
-            for y in range(YLO):
-                at = y * CORE * rows
-                left[pl.ds(pl.multiple_of(at + core * rows, rows), rows), cols] = own[y * rows:(y + 1) * rows]
-                left[pl.ds(pl.multiple_of(at + (1 - core) * rows, rows), rows), cols] = other[y * rows:(y + 1) * rows]
-        fetch_of(c_hbm, c_ref, sems, step).wait()
-        total[...] += jnp.dot(left[...], c_ref[step], preferred_element_type=F32)
-
-    steps(c_hbm, c_ref, sems, work)
-    for part in range(total.shape[1] // block):
-        cols = slice(part * block, (part + 1) * block)
-        final[cols] = transposed(total[:, cols].astype(BF16), eye)
+    fetch_columns(c_hbm, c_ref, sems)
+    set_identity(eye)
+
+    def build(b, carry):
+        cols = pl.ds(pl.multiple_of(b * block, block), block)
+        own = transposed(t_ref[b, 0], eye)
+        other = transposed(other_ref[b, 0], eye)
+        for y in range(YLO):
+            at = y * CORE * rows
+            left[pl.ds(pl.multiple_of(at + core * rows, rows), rows), cols] = own[y * rows:(y + 1) * rows]
+            left[pl.ds(pl.multiple_of(at + (1 - core) * rows, rows), rows), cols] = other[y * rows:(y + 1) * rows]
+        return carry
+
+    def store(step, product):
+        width = product.shape[1]
+        final[pl.ds(pl.multiple_of(step * width, width), width)] = transposed(product, eye)
+
+    lax.fori_loop(0, count, build, 0)
+    products(left, c_hbm, c_ref, sems, store)
     for z in range(Z):
         at = z * YLO * rows
         keep[z] = final[pl.ds(pl.multiple_of(at + ylo * rows, rows), rows)]
@@ -272,9 +304,8 @@
         out_shape=[out, out],
         in_specs=[pl.BlockSpec(memory_space=pltpu.SMEM), vmem, vmem, HBM],
         out_specs=[vmem, vmem],
-        scratch_shapes=fetch_scratch(picked) + [
-            pltpu.VMEM((block, size // STEPS), BF16),
-            pltpu.VMEM((block, width), F32),
+        scratch_shapes=column_scratch(picked) + [
+            pltpu.VMEM((block, size), BF16),
             pltpu.VMEM((width, block), BF16),
             pltpu.VMEM((block, block), BF16)],
         compiler_params=PARAMS,

time: 181 us -> 152 us (0.84)
  Pallas kernels: 61 us -> 33 us
    pallas_call x1, Pallas kernels: 33.5 us -> 6.85 us  [pick_columns(): pl.pallas_call(pick_kernel, out_shape=[pltpu.HBM((size, width), BF16), pl...]
    ppermute x28, starting transfers between devices: 66.6 us -> 69 us  [rotate(): lax.ppermute(part, axes, [(i, (i + d) % BLOCKS) for i in range(BLOCKS)])]
    ppermute x28, waiting for transfers between devices: 12.3 us -> 10.1 us  [rotate(): lax.ppermute(part, axes, [(i, (i + d) % BLOCKS) for i in range(BLOCKS)])]
  transfers between devices with their start and end apart: 39 -> 39, of which waited for: 18 -> 16; matrix products, arithmetic and copies ran while one was open for 0% -> 0% of each run, Pallas kernels for 29% -> 16%
where the time goes in v3:
time: 152 us
  starting transfers between devices  97.2 us (64%)
  Pallas kernels  33 us (22%)
  waiting for transfers between devices  20 us (13%)
    ppermute x28, starting transfers between devices, rotate(): lax.ppermute(part, axes, [(i, (i + d) % BLOCKS) for i in range(BLOCKS)])  69 us
    pallas_call x2, Pallas kernels, first_half(): pl.pallas_call(functools.partial(first_kernel, index), out_shape=[jax.Sha...  10.3 us
    ppermute x28, waiting for transfers between devices, rotate(): lax.ppermute(part, axes, [(i, (i + d) % BLOCKS) for i in range(BLOCKS)])  10.1 us
    all_to_all x1, starting transfers between devices, per_device(): result = lax.all_to_all(result, PLANE, 0, 0, tiled=True)  7.34 us
    all_to_all x1, starting transfers between devices, per_device(): own = lax.all_to_all(own, PLANE, 0, 0, tiled=True)  7.2 us
    ppermute x7, waiting for transfers between devices, swap(): return lax.ppermute(value, axis, [(0, 1), (1, 0)])  6.98 us
    pallas_call x1, Pallas kernels, pick_columns(): pl.pallas_call(pick_kernel, out_shape=[pltpu.HBM((size, width), BF16), pl...  6.85 us
    all_to_all x1, starting transfers between devices, per_device(): partial_value = lax.all_to_all(partial_value, 'z', 0, 0, tiled=True)  5.75 us
  transfers between devices with their start and end apart: 39, of which 16 were waited for; matrix products, arithmetic and copies ran while one was open for 0% of the time, Pallas kernels for 16%

profile of v3, /device:TPU:2, one launch (start us, length us, event | category | flops | bytes accessed | tf_op | source)
XLA Modules:
  0.0 151.8 jit_solution(525461377491366701)
XLA Ops:
  0.0 1.1 slice.3
  1.1 1.7 %collective-permute-start = (bf16[8,64,256]{2,1,0:T(8,128)(2,1)S(1)}, bf16[8,64,256]{2,1,0:T(8,128)(2,1)S(1)}, u32[]{:S(2)}, u32[]{:S(2)}) collective-permute-start(bf16[8,64,256]{2,1,0:T(8,128)(2,1)S(1)} %get-tuple-element.122), channel_id=1, source_target_pairs={{0,16},{16,0},{1,17},{17,1},{2,18},{18,2},{3,19},{19,3},{4,20},{20... | collective-permute-start | bytes 786440 | tf_op jit(solution)/shard_map/side_in/ppermute | solution.py:406
  2.9 6.9 %pick_columns.1 = (bf16[2048,1024]{1,0:T(8,128)(2,1)}, bf16[32,64,256]{2,1,0:T(8,128)(2,1)}) custom-call(s32[4]{0:T(128)S(1)} %pad_add_fusion.place, bf16[2048,2048]{1,0:T(8,128)(2,1)} %c_hbm.3, bf16[48,64,256]{2,1,0:T(8,128)(2,1)} %panel_hbm.1), custom_call_target="tpu_custom_call" | custom-call | tf_op jit(solution)/shard_map/pick_columns/pallas_call | solution.py:139
  9.8 7.2 %all-to-all-start = ((bf16[16,2,64,256]{3,2,1,0:T(8,128)(2,1)}), bf16[16,2,64,256]{3,2,1,0:T(8,128)(2,1)}, u32[]{:S(2)}, u32[]{:S(2)}) async-start(bf16[16,2,64,256]{3,2,1,0:T(8,128)(2,1)} %bitcast.23), calls=%async_computation | async-start | bytes 2097152 | tf_op jit(solution)/shard_map/panels_in/all_to_all | solution.py:433
  16.9 0.6 join_and_spread.2
  17.5 7.3 %collective-permute-start.1 = (bf16[2,64,256]{2,1,0:T(8,128)(2,1)S(1)}, bf16[2,64,256]{2,1,0:T(8,128)(2,1)S(1)}, u32[]{:S(2)}, u32[]{:S(2)}) collective-permute-start(bf16[2,64,256]{2,1,0:T(8,128)(2,1)S(1)} %get-tuple-element.69), channel_id=1, source_target_pairs={{0,128},{32,160},{64,192},{96,224},{128,0},{160,32},{192,64},{224,... | collective-permute-start | bytes 196616 | tf_op jit(solution)/shard_map/side_in/ppermute | solution.py:401
  24.8 1.9 %collective-permute-start.2 = (bf16[2,64,256]{2,1,0:T(8,128)(2,1)S(1)}, bf16[2,64,256]{2,1,0:T(8,128)(2,1)S(1)}, u32[]{:S(2)}, u32[]{:S(2)}) collective-permute-start(bf16[2,64,256]{2,1,0:T(8,128)(2,1)S(1)} %get-tuple-element.70), channel_id=1, source_target_pairs={{0,96},{32,128},{64,160},{96,192},{128,224},{160,0},{192,32},{224,... | collective-permute-start | bytes 196616 | tf_op jit(solution)/shard_map/side_in/ppermute | solution.py:401
  26.8 3.1 %collective-permute-start.3 = (bf16[2,64,256]{2,1,0:T(8,128)(2,1)S(1)}, bf16[2,64,256]{2,1,0:T(8,128)(2,1)S(1)}, u32[]{:S(2)}, u32[]{:S(2)}) collective-permute-start(bf16[2,64,256]{2,1,0:T(8,128)(2,1)S(1)} %get-tuple-element.71), channel_id=1, source_target_pairs={{0,160},{32,192},{64,224},{96,0},{128,32},{160,64},{192,96},{224,1... | collective-permute-start | bytes 196616 | tf_op jit(solution)/shard_map/side_in/ppermute | solution.py:401
  29.9 1.5 collective-permute-start.4
  31.3 2.7 %collective-permute-start.5 = (bf16[2,64,256]{2,1,0:T(8,128)(2,1)S(1)}, bf16[2,64,256]{2,1,0:T(8,128)(2,1)S(1)}, u32[]{:S(2)}, u32[]{:S(2)}) collective-permute-start(bf16[2,64,256]{2,1,0:T(8,128)(2,1)S(1)} %get-tuple-element.73), channel_id=1, source_target_pairs={{0,192},{32,224},{64,0},{96,32},{128,64},{160,96},{192,128},{224,1... | collective-permute-start | bytes 196616 | tf_op jit(solution)/shard_map/side_in/ppermute | solution.py:401
  34.0 1.0 collective-permute-start.6
  35.0 0.1 collective-permute-done.2.refs_2_
  35.1 2.1 %collective-permute-start.7 = (bf16[2,64,256]{2,1,0:T(8,128)(2,1)S(1)}, bf16[2,64,256]{2,1,0:T(8,128)(2,1)S(1)}, u32[]{:S(2)}, u32[]{:S(2)}) collective-permute-start(bf16[2,64,256]{2,1,0:T(8,128)(2,1)S(1)} %get-tuple-element.75), channel_id=1, source_target_pairs={{0,224},{32,0},{64,32},{96,64},{128,96},{160,128},{192,160},{224,1... | collective-permute-start | bytes 196616 | tf_op jit(solution)/shard_map/side_in/ppermute | solution.py:401
  37.2 0.7 collective-permute-done.5.refs_5_
  38.0 1.5 %collective-permute-done.6.refs_6_ = bf16[2,64,256]{2,1,0:T(8,128)(2,1)S(1)} collective-permute-done((bf16[2,64,256]{2,1,0:T(8,128)(2,1)S(1)}, bf16[2,64,256]{2,1,0:T(8,128)(2,1)S(1)}, u32[]{:S(2)}, u32[]{:S(2)}) %collective-permute-start.6) | collective-permute-done | bytes 65568 | tf_op jit(solution)/shard_map/side_in/ppermute | solution.py:401
  39.5 0.6 collect.3.x_ref
  40.1 4.5 %all-to-all-start.1 = ((bf16[8,2,2,64,256]{4,3,2,1,0:T(8,128)(2,1)}), bf16[8,2,2,64,256]{4,3,2,1,0:T(8,128)(2,1)S(1)}, u32[]{:S(2)}, u32[]{:S(2)}) async-start(bf16[8,2,2,64,256]{4,3,2,1,0:T(8,128)(2,1)} %bitcast.8.direct), calls=%async_computation.1 | async-start | bytes 2097152 | tf_op jit(solution)/shard_map/mirror/all_to_all | solution.py:441
  44.6 0.6 spread.1
  45.2 3.9 %collective-permute-start.9 = (bf16[2,64,256]{2,1,0:T(8,128)(2,1)S(1)}, bf16[2,64,256]{2,1,0:T(8,128)(2,1)S(1)}, u32[]{:S(2)}, u32[]{:S(2)}) collective-permute-start(bf16[2,64,256]{2,1,0:T(8,128)(2,1)S(1)} %get-tuple-element.80), channel_id=1, source_target_pairs={{0,3},{1,4},{2,5},{3,6},{4,7},{5,0},{6,1},{7,2},{8,11},{9,12},{10,... | collective-permute-start | bytes 196616 | tf_op jit(solution)/shard_map/side_mirror/ppermute | solution.py:401
  49.2 2.1 %collective-permute-start.10 = (bf16[2,64,256]{2,1,0:T(8,128)(2,1)S(1)}, bf16[2,64,256]{2,1,0:T(8,128)(2,1)S(1)}, u32[]{:S(2)}, u32[]{:S(2)}) collective-permute-start(bf16[2,64,256]{2,1,0:T(8,128)(2,1)S(1)} %get-tuple-element.81), channel_id=1, source_target_pairs={{0,5},{1,6},{2,7},{3,0},{4,1},{5,2},{6,3},{7,4},{8,13},{9,14},{10,... | collective-permute-start | bytes 196616 | tf_op jit(solution)/shard_map/side_mirror/ppermute | solution.py:401
  51.2 1.5 collective-permute-start.11
  52.7 3.0 %collective-permute-start.12 = (bf16[2,64,256]{2,1,0:T(8,128)(2,1)S(1)}, bf16[2,64,256]{2,1,0:T(8,128)(2,1)S(1)}, u32[]{:S(2)}, u32[]{:S(2)}) collective-permute-start(bf16[2,64,256]{2,1,0:T(8,128)(2,1)S(1)} %get-tuple-element.83), channel_id=1, source_target_pairs={{0,7},{1,0},{2,1},{3,2},{4,3},{5,4},{6,5},{7,6},{8,15},{9,8},{10,9... | collective-permute-start | bytes 196616 | tf_op jit(solution)/shard_map/side_mirror/ppermute | solution.py:401
  55.7 2.1 %collective-permute-start.13 = (bf16[2,64,256]{2,1,0:T(8,128)(2,1)S(1)}, bf16[2,64,256]{2,1,0:T(8,128)(2,1)S(1)}, u32[]{:S(2)}, u32[]{:S(2)}) collective-permute-start(bf16[2,64,256]{2,1,0:T(8,128)(2,1)S(1)} %get-tuple-element.84), channel_id=1, source_target_pairs={{0,4},{1,5},{2,6},{3,7},{4,0},{5,1},{6,2},{7,3},{8,12},{9,13},{10,... | collective-permute-start | bytes 196616 | tf_op jit(solution)/shard_map/side_mirror/ppermute | solution.py:401
  57.7 1.0 collective-permute-start.14
  58.7 1.0 collective-permute-start.15
  59.8 2.1 %collective-permute-done.13.refs_5_ = bf16[2,64,256]{2,1,0:T(8,128)(2,1)S(1)} collective-permute-done((bf16[2,64,256]{2,1,0:T(8,128)(2,1)S(1)}, bf16[2,64,256]{2,1,0:T(8,128)(2,1)S(1)}, u32[]{:S(2)}, u32[]{:S(2)}) %collective-permute-start.13) | collective-permute-done | bytes 65568 | tf_op jit(solution)/shard_map/side_mirror/ppermute | solution.py:401
  61.9 0.2 collective-permute-done.14.refs_6_
  62.1 0.9 collective-permute-done.15.refs_7_
  63.0 0.6 collect.4
  63.6 0.1 collective-permute-start.16
  63.7 1.9 %collective-permute-done.16 = bf16[8,2,64,256]{3,2,1,0:T(8,128)(2,1)S(1)} collective-permute-done((bf16[8,2,64,256]{3,2,1,0:T(8,128)(2,1)S(1)}, bf16[8,2,64,256]{3,2,1,0:T(8,128)(2,1)S(1)}, u32[]{:S(2)}, u32[]{:S(2)}) %collective-permute-start.16) | collective-permute-done | bytes 524320 | tf_op jit(solution)/shard_map/side_mirror/ppermute | solution.py:406
  65.6 3.7 %first_half_side.1 = (bf16[1,256,128]{2,1,0:T(8,128)(2,1)S(1)}, bf16[1,256,128]{2,1,0:T(8,128)(2,1)S(1)}, bf16[1,256,128]{2,1,0:T(8,128)(2,1)S(1)}, bf16[1,256,1...) custom-call(s32[4]{0:T(128)S(1)} %pad_add_fusion.place, ...), custom_call_target="tpu_custom_call" | custom-call | tf_op jit(solution)/shard_map/side_mirror/first_half_side/pallas_call | solution.py:213
  69.3 2.0 %all-to-all-done.1.turned = bf16[8,2,2,64,256]{4,3,2,1,0:T(8,128)(2,1)S(1)} async-done(((bf16[8,2,2,64,256]{4,3,2,1,0:T(8,128)(2,1)}), bf16[8,2,2,64,256]{4,3,2,1,0:T(8,128)(2,1)S(1)}, u32[]{:S(2)}, u32[]{:S(2)}) %all-to-all-start.1) | async-done | bytes 1048608 | tf_op jit(solution)/shard_map/mirror/all_to_all | solution.py:441
  71.4 2.7 %collective-permute-done.18.turned_other = bf16[8,2,2,64,256]{4,3,2,1,0:T(8,128)(2,1)S(1)} collective-permute-done((bf16[8,2,2,64,256]{4,3,2,1,0:T(8,128)(2,1)S(1)}, bf16[8,2,2,64,256]{4,3,2,1,0:T(8,128)(2,1)S(1)}, u32[]{:S(2)}, u32[]{:S(2)}) %collective-permute-start.18) | collective-permute-done | bytes 1048608 | tf_op jit(solution)/shard_map/ppermute | solution.py:406
  74.0 6.5 %first_half.1 = bf16[8,2,256,128]{3,2,1,0:T(8,128)(2,1)} custom-call(s32[4]{0:T(128)S(1)} %pad_add_fusion.place, bf16[8,2,2,64,256]{4,3,2,1,0:T(8,128)(2,1)} %bitcast.8.direct, bf16[8,2,2,64,256]{4,3,2,1,0:T(8,128)(2,1)S(1)} %collective-permute-done.8.direct_other, bf16[8,2,2,64,256]{4,3,2,1,0:T(8,128)(2,1)S(1)} %all-to-all-done.1.turned, ...), custom_call_target="tpu_custom_call" | custom-call | tf_op jit(solution)/shard_map/first_half/pallas_call | solution.py:213
  80.6 5.7 %all-to-all-start.2 = ((bf16[8,2,256,128]{3,2,1,0:T(8,128)(2,1)}), bf16[8,2,256,128]{3,2,1,0:T(8,128)(2,1)S(1)}, u32[]{:S(2)}, u32[]{:S(2)}) async-start(bf16[8,2,256,128]{3,2,1,0:T(8,128)(2,1)} %first_half.1), calls=%async_computation.2 | async-start | bytes 2097152 | tf_op jit(solution)/shard_map/partial/all_to_all | solution.py:460
  86.3 1.8 %collective-permute-start.19 = (bf16[1,256,128]{2,1,0:T(8,128)(2,1)S(1)}, bf16[1,256,128]{2,1,0:T(8,128)(2,1)S(1)}, u32[]{:S(2)}, u32[]{:S(2)}) collective-permute-start(bf16[1,256,128]{2,1,0:T(8,128)(2,1)S(1)} %get-tuple-element.99), channel_id=1, source_target_pairs={{0,3},{1,4},{2,5},{3,6},{4,7},{5,0},{6,1},{7,2},{8,11},{9,12},{10,... | collective-permute-start | bytes 196616 | tf_op jit(solution)/shard_map/side_partial/ppermute | solution.py:401
  88.1 4.1 %collective-permute-start.20 = (bf16[1,256,128]{2,1,0:T(8,128)(2,1)S(1)}, bf16[1,256,128]{2,1,0:T(8,128)(2,1)S(1)}, u32[]{:S(2)}, u32[]{:S(2)}) collective-permute-start(bf16[1,256,128]{2,1,0:T(8,128)(2,1)S(1)} %get-tuple-element.100), channel_id=1, source_target_pairs={{0,5},{1,6},{2,7},{3,0},{4,1},{5,2},{6,3},{7,4},{8,13},{9,14},{10,... | collective-permute-start | bytes 196616 | tf_op jit(solution)/shard_map/side_partial/ppermute | solution.py:401
  92.2 1.4 collective-permute-start.21
  93.6 3.1 %collective-permute-start.22 = (bf16[1,256,128]{2,1,0:T(8,128)(2,1)S(1)}, bf16[1,256,128]{2,1,0:T(8,128)(2,1)S(1)}, u32[]{:S(2)}, u32[]{:S(2)}) collective-permute-start(bf16[1,256,128]{2,1,0:T(8,128)(2,1)S(1)} %get-tuple-element.102), channel_id=1, source_target_pairs={{0,7},{1,0},{2,1},{3,2},{4,3},{5,4},{6,5},{7,6},{8,15},{9,8},{10,9... | collective-permute-start | bytes 196616 | tf_op jit(solution)/shard_map/side_partial/ppermute | solution.py:401
  96.7 4.3 %collective-permute-start.23 = (bf16[1,256,128]{2,1,0:T(8,128)(2,1)S(1)}, bf16[1,256,128]{2,1,0:T(8,128)(2,1)S(1)}, u32[]{:S(2)}, u32[]{:S(2)}) collective-permute-start(bf16[1,256,128]{2,1,0:T(8,128)(2,1)S(1)} %get-tuple-element.103), channel_id=1, source_target_pairs={{0,4},{1,5},{2,6},{3,7},{4,0},{5,1},{6,2},{7,3},{8,12},{9,13},{10,... | collective-permute-start | bytes 196616 | tf_op jit(solution)/shard_map/side_partial/ppermute | solution.py:401
  101.0 2.0 %collective-permute-start.25 = (bf16[1,256,128]{2,1,0:T(8,128)(2,1)S(1)}, bf16[1,256,128]{2,1,0:T(8,128)(2,1)S(1)}, u32[]{:S(2)}, u32[]{:S(2)}) collective-permute-start(bf16[1,256,128]{2,1,0:T(8,128)(2,1)S(1)} %get-tuple-element.105), channel_id=1, source_target_pairs={{0,6},{1,7},{2,0},{3,1},{4,2},{5,3},{6,4},{7,5},{8,14},{9,15},{10,... | collective-permute-start | bytes 196616 | tf_op jit(solution)/shard_map/side_partial/ppermute | solution.py:401
  103.0 1.1 collective-permute-done.23.refs_5_
  104.2 1.1 collective-permute-done.24.refs_6_
  105.3 0.1 collective-permute-done.25.refs_7_
  105.4 0.6 collect.5.t_ref
  106.0 0.1 collective-permute-start.26
  106.1 1.9 %collective-permute-done.26.other_ref = bf16[8,1,256,128]{3,2,1,0:T(8,128)(2,1)S(1)} collective-permute-done((bf16[8,1,256,128]{3,2,1,0:T(8,128)(2,1)S(1)}, bf16[8,1,256,128]{3,2,1,0:T(8,128)(2,1)S(1)}, u32[]{:S(2)}, u32[]{:S(2)}) %collective-permute-start.26) | collective-permute-done | bytes 524320 | tf_op jit(solution)/shard_map/side_partial/ppermute | solution.py:406
  108.0 5.0 %second_half_side.1 = (bf16[8,64,256]{2,1,0:T(8,128)(2,1)S(1)}, bf16[8,64,256]{2,1,0:T(8,128)(2,1)S(1)}) custom-call(s32[4]{0:T(128)S(1)} %pad_add_fusion.place, bf16[8,1,256,128]{3,2,1,0:T(8,128)(2,1)S(1)} %collect.5.t_ref, bf16[8,1,256,128]{3,2,1,0:T(8,128)(2,1)S(1)} %collective-permute-done.26.other_ref, bf16[2048,1024]{1,0:T(8,128)(2,1)} %get-tuple-element.87.c_hbm), custom_call_target="tpu_custom_call" | custom-call | tf_op jit(solution)/shard_map/side_partial/second_half_side/pallas_call | solution.py:302
  113.0 1.5 %collective-permute-start.27 = (bf16[8,64,256]{2,1,0:T(8,128)(2,1)S(1)}, bf16[8,64,256]{2,1,0:T(8,128)(2,1)S(1)}, u32[]{:S(2)}, u32[]{:S(2)}) collective-permute-start(bf16[8,64,256]{2,1,0:T(8,128)(2,1)S(1)} %get-tuple-element.108), channel_id=1, source_target_pairs={{0,16},{16,0},{1,17},{17,1},{2,18},{18,2},{3,19},{19,3},{4,20},{20... | collective-permute-start | bytes 786440 | tf_op jit(solution)/shard_map/ppermute | solution.py:406
  114.5 0.9 all-to-all-done.2.t_ref
  115.4 5.5 %second_half.1 = bf16[8,2,2,64,256]{4,3,2,1,0:T(8,128)(2,1)} custom-call(bf16[8,2,256,128]{3,2,1,0:T(8,128)(2,1)S(1)} %all-to-all-done.2.t_ref, bf16[2048,2048]{1,0:T(8,128)(2,1)} %c_hbm.3), custom_call_target="tpu_custom_call" | custom-call | tf_op jit(solution)/shard_map/second_half/pallas_call | solution.py:255
  120.9 0.5 collective-permute-done.27.got
  121.4 7.3 %all-to-all-start.3 = ((bf16[16,2,64,256]{3,2,1,0:T(8,128)(2,1)}), bf16[16,2,64,256]{3,2,1,0:T(8,128)(2,1)S(1)}, u32[]{:S(2)}, u32[]{:S(2)}) async-start(bf16[16,2,64,256]{3,2,1,0:T(8,128)(2,1)} %bitcast.13), calls=%async_computation.3 | async-start | bytes 2097152 | tf_op jit(solution)/shard_map/panels_out/all_to_all | solution.py:474
  128.8 0.6 join_and_spread.3
  129.4 5.8 %collective-permute-start.28 = (bf16[2,64,256]{2,1,0:T(8,128)(2,1)S(1)}, bf16[2,64,256]{2,1,0:T(8,128)(2,1)S(1)}, u32[]{:S(2)}, u32[]{:S(2)}) collective-permute-start(bf16[2,64,256]{2,1,0:T(8,128)(2,1)S(1)} %get-tuple-element.113), channel_id=1, source_target_pairs={{0,128},{32,160},{64,192},{96,224},{128,0},{160,32},{192,64},{224,... | collective-permute-start | bytes 196616 | tf_op jit(solution)/shard_map/side_out/ppermute | solution.py:401
  135.1 0.6 collective-permute-start.29
  135.7 4.5 %collective-permute-start.30 = (bf16[2,64,256]{2,1,0:T(8,128)(2,1)S(1)}, bf16[2,64,256]{2,1,0:T(8,128)(2,1)S(1)}, u32[]{:S(2)}, u32[]{:S(2)}) collective-permute-start(bf16[2,64,256]{2,1,0:T(8,128)(2,1)S(1)} %get-tuple-element.115), channel_id=1, source_target_pairs={{0,160},{32,192},{64,224},{96,0},{128,32},{160,64},{192,96},{224,1... | collective-permute-start | bytes 196616 | tf_op jit(solution)/shard_map/side_out/ppermute | solution.py:401
  140.2 0.6 collective-permute-start.31
  140.7 3.6 %collective-permute-start.32 = (bf16[2,64,256]{2,1,0:T(8,128)(2,1)S(1)}, bf16[2,64,256]{2,1,0:T(8,128)(2,1)S(1)}, u32[]{:S(2)}, u32[]{:S(2)}) collective-permute-start(bf16[2,64,256]{2,1,0:T(8,128)(2,1)S(1)} %get-tuple-element.117), channel_id=1, source_target_pairs={{0,192},{32,224},{64,0},{96,32},{128,64},{160,96},{192,128},{224,1... | collective-permute-start | bytes 196616 | tf_op jit(solution)/shard_map/side_out/ppermute | solution.py:401
  144.3 0.6 collective-permute-start.33
  144.9 2.7 %collective-permute-start.34 = (bf16[2,64,256]{2,1,0:T(8,128)(2,1)S(1)}, bf16[2,64,256]{2,1,0:T(8,128)(2,1)S(1)}, u32[]{:S(2)}, u32[]{:S(2)}) collective-permute-start(bf16[2,64,256]{2,1,0:T(8,128)(2,1)S(1)} %get-tuple-element.119), channel_id=1, source_target_pairs={{0,224},{32,0},{64,32},{96,64},{128,96},{160,128},{192,160},{224,1... | collective-permute-start | bytes 196616 | tf_op jit(solution)/shard_map/side_out/ppermute | solution.py:401
  147.6 2.2 %collective-permute-done.33.refs_6_ = bf16[2,64,256]{2,1,0:T(8,128)(2,1)S(1)} collective-permute-done((bf16[2,64,256]{2,1,0:T(8,128)(2,1)S(1)}, bf16[2,64,256]{2,1,0:T(8,128)(2,1)S(1)}, u32[]{:S(2)}, u32[]{:S(2)}) %collective-permute-start.33) | collective-permute-done | bytes 65568 | tf_op jit(solution)/shard_map/side_out/ppermute | solution.py:401
  149.8 1.8 %finish.1 = bf16[48,64,256]{2,1,0:T(8,128)(2,1)} custom-call(s32[4]{0:T(128)S(1)} %pad_add_fusion.place, bf16[2,64,256]{2,1,0:T(8,128)(2,1)S(1)} %get-tuple-element.112.refs_0_, bf16[2,64,256]{2,1,0:T(8,128)(2,1)S(1)} %collective-permute-done.28.refs_1_, bf16[2,64,256]{2,1,0:T(8,128)(2,1)S(1)} %collective-permute-done.29.refs_2_, ...), custom_call_target="tpu_custom_call" | custom-call | tf_op jit(solution)/shard_map/finish/pallas_call | solution.py:387
  (29 shorter events, 0.2 us)
Async XLA Ops:
  1.1 8.6 %collective-permute-start = (bf16[8,64,256]{2,1,0:T(8,128)(2,1)S(1)}, bf16[8,64,256]{2,1,0:T(8,128)(2,1)S(1)}, u32[]{:S(2)}, u32[]{:S(2)}) collective-permute-start(bf16[8,64,256]{2,1,0:T(8,128)(2,1)S(1)} %get-tuple-element.122), channel_id=1, source_target_pairs={{0,16},{16,0},{1,17},{17,1},{2,18},{18,2},{3,19},{19,3},{4,20},{20... | collective-permute-start | bytes 786440 | tf_op jit(solution)/shard_map/side_in/ppermute | solution.py:406
  9.8 30.3 %all-to-all-start = ((bf16[16,2,64,256]{3,2,1,0:T(8,128)(2,1)}), bf16[16,2,64,256]{3,2,1,0:T(8,128)(2,1)}, u32[]{:S(2)}, u32[]{:S(2)}) async-start(bf16[16,2,64,256]{3,2,1,0:T(8,128)(2,1)} %bitcast.23), calls=%async_computation | async-start | bytes 2097152 | tf_op jit(solution)/shard_map/panels_in/all_to_all | solution.py:433
  17.5 16.5 %collective-permute-start.1 = (bf16[2,64,256]{2,1,0:T(8,128)(2,1)S(1)}, bf16[2,64,256]{2,1,0:T(8,128)(2,1)S(1)}, u32[]{:S(2)}, u32[]{:S(2)}) collective-permute-start(bf16[2,64,256]{2,1,0:T(8,128)(2,1)S(1)} %get-tuple-element.69), channel_id=1, source_target_pairs={{0,128},{32,160},{64,192},{96,224},{128,0},{160,32},{192,64},{224,... | collective-permute-start | bytes 196616 | tf_op jit(solution)/shard_map/side_in/ppermute | solution.py:401
  24.8 10.3 %collective-permute-start.2 = (bf16[2,64,256]{2,1,0:T(8,128)(2,1)S(1)}, bf16[2,64,256]{2,1,0:T(8,128)(2,1)S(1)}, u32[]{:S(2)}, u32[]{:S(2)}) collective-permute-start(bf16[2,64,256]{2,1,0:T(8,128)(2,1)S(1)} %get-tuple-element.70), channel_id=1, source_target_pairs={{0,96},{32,128},{64,160},{96,192},{128,224},{160,0},{192,32},{224,... | collective-permute-start | bytes 196616 | tf_op jit(solution)/shard_map/side_in/ppermute | solution.py:401
  26.8 10.5 %collective-permute-start.3 = (bf16[2,64,256]{2,1,0:T(8,128)(2,1)S(1)}, bf16[2,64,256]{2,1,0:T(8,128)(2,1)S(1)}, u32[]{:S(2)}, u32[]{:S(2)}) collective-permute-start(bf16[2,64,256]{2,1,0:T(8,128)(2,1)S(1)} %get-tuple-element.71), channel_id=1, source_target_pairs={{0,160},{32,192},{64,224},{96,0},{128,32},{160,64},{192,96},{224,1... | collective-permute-start | bytes 196616 | tf_op jit(solution)/shard_map/side_in/ppermute | solution.py:401
  29.9 7.4 %collective-permute-start.4 = (bf16[2,64,256]{2,1,0:T(8,128)(2,1)S(1)}, bf16[2,64,256]{2,1,0:T(8,128)(2,1)S(1)}, u32[]{:S(2)}, u32[]{:S(2)}) collective-permute-start(bf16[2,64,256]{2,1,0:T(8,128)(2,1)S(1)} %get-tuple-element.72), channel_id=1, source_target_pairs={{0,64},{32,96},{64,128},{96,160},{128,192},{160,224},{192,0},{224,... | collective-permute-start | bytes 196616 | tf_op jit(solution)/shard_map/side_in/ppermute | solution.py:401
  31.3 6.6 %collective-permute-start.5 = (bf16[2,64,256]{2,1,0:T(8,128)(2,1)S(1)}, bf16[2,64,256]{2,1,0:T(8,128)(2,1)S(1)}, u32[]{:S(2)}, u32[]{:S(2)}) collective-permute-start(bf16[2,64,256]{2,1,0:T(8,128)(2,1)S(1)} %get-tuple-element.73), channel_id=1, source_target_pairs={{0,192},{32,224},{64,0},{96,32},{128,64},{160,96},{192,128},{224,1... | collective-permute-start | bytes 196616 | tf_op jit(solution)/shard_map/side_in/ppermute | solution.py:401
  34.0 5.5 %collective-permute-start.6 = (bf16[2,64,256]{2,1,0:T(8,128)(2,1)S(1)}, bf16[2,64,256]{2,1,0:T(8,128)(2,1)S(1)}, u32[]{:S(2)}, u32[]{:S(2)}) collective-permute-start(bf16[2,64,256]{2,1,0:T(8,128)(2,1)S(1)} %get-tuple-element.74), channel_id=1, source_target_pairs={{0,32},{32,64},{64,96},{96,128},{128,160},{160,192},{192,224},{224... | collective-permute-start | bytes 196616 | tf_op jit(solution)/shard_map/side_in/ppermute | solution.py:401
  35.1 4.4 %collective-permute-start.7 = (bf16[2,64,256]{2,1,0:T(8,128)(2,1)S(1)}, bf16[2,64,256]{2,1,0:T(8,128)(2,1)S(1)}, u32[]{:S(2)}, u32[]{:S(2)}) collective-permute-start(bf16[2,64,256]{2,1,0:T(8,128)(2,1)S(1)} %get-tuple-element.75), channel_id=1, source_target_pairs={{0,224},{32,0},{64,32},{96,64},{128,96},{160,128},{192,160},{224,1... | collective-permute-start | bytes 196616 | tf_op jit(solution)/shard_map/side_in/ppermute | solution.py:401
  40.1 31.3 %all-to-all-start.1 = ((bf16[8,2,2,64,256]{4,3,2,1,0:T(8,128)(2,1)}), bf16[8,2,2,64,256]{4,3,2,1,0:T(8,128)(2,1)S(1)}, u32[]{:S(2)}, u32[]{:S(2)}) async-start(bf16[8,2,2,64,256]{4,3,2,1,0:T(8,128)(2,1)} %bitcast.8.direct), calls=%async_computation.1 | async-start | bytes 2097152 | tf_op jit(solution)/shard_map/mirror/all_to_all | solution.py:441
  44.6 24.7 %collective-permute-start.8 = (bf16[8,2,2,64,256]{4,3,2,1,0:T(8,128)(2,1)}, bf16[8,2,2,64,256]{4,3,2,1,0:T(8,128)(2,1)S(1)}, u32[]{:S(2)}, u32[]{:S(2)}) collective-permute-start(bf16[8,2,2,64,256]{4,3,2,1,0:T(8,128)(2,1)} %bitcast.8.direct), channel_id=1, source_target_pairs={{0,8},{8,0},{1,9},{9,1},{2,10},{10,2},{3,11},{11,3},{4,12},{12,4},... | collective-permute-start | bytes 3145736 | tf_op jit(solution)/shard_map/ppermute | solution.py:406
  45.2 10.4 %collective-permute-start.9 = (bf16[2,64,256]{2,1,0:T(8,128)(2,1)S(1)}, bf16[2,64,256]{2,1,0:T(8,128)(2,1)S(1)}, u32[]{:S(2)}, u32[]{:S(2)}) collective-permute-start(bf16[2,64,256]{2,1,0:T(8,128)(2,1)S(1)} %get-tuple-element.80), channel_id=1, source_target_pairs={{0,3},{1,4},{2,5},{3,6},{4,7},{5,0},{6,1},{7,2},{8,11},{9,12},{10,... | collective-permute-start | bytes 196616 | tf_op jit(solution)/shard_map/side_mirror/ppermute | solution.py:401
  49.2 8.6 %collective-permute-start.10 = (bf16[2,64,256]{2,1,0:T(8,128)(2,1)S(1)}, bf16[2,64,256]{2,1,0:T(8,128)(2,1)S(1)}, u32[]{:S(2)}, u32[]{:S(2)}) collective-permute-start(bf16[2,64,256]{2,1,0:T(8,128)(2,1)S(1)} %get-tuple-element.81), channel_id=1, source_target_pairs={{0,5},{1,6},{2,7},{3,0},{4,1},{5,2},{6,3},{7,4},{8,13},{9,14},{10,... | collective-permute-start | bytes 196616 | tf_op jit(solution)/shard_map/side_mirror/ppermute | solution.py:401
  51.2 7.5 %collective-permute-start.11 = (bf16[2,64,256]{2,1,0:T(8,128)(2,1)S(1)}, bf16[2,64,256]{2,1,0:T(8,128)(2,1)S(1)}, u32[]{:S(2)}, u32[]{:S(2)}) collective-permute-start(bf16[2,64,256]{2,1,0:T(8,128)(2,1)S(1)} %get-tuple-element.82), channel_id=1, source_target_pairs={{0,1},{1,2},{2,3},{3,4},{4,5},{5,6},{6,7},{7,0},{8,9},{9,10},{10,1... | collective-permute-start | bytes 196616 | tf_op jit(solution)/shard_map/side_mirror/ppermute | solution.py:401
  52.7 7.1 %collective-permute-start.12 = (bf16[2,64,256]{2,1,0:T(8,128)(2,1)S(1)}, bf16[2,64,256]{2,1,0:T(8,128)(2,1)S(1)}, u32[]{:S(2)}, u32[]{:S(2)}) collective-permute-start(bf16[2,64,256]{2,1,0:T(8,128)(2,1)S(1)} %get-tuple-element.83), channel_id=1, source_target_pairs={{0,7},{1,0},{2,1},{3,2},{4,3},{5,4},{6,5},{7,6},{8,15},{9,8},{10,9... | collective-permute-start | bytes 196616 | tf_op jit(solution)/shard_map/side_mirror/ppermute | solution.py:401
  55.7 6.3 %collective-permute-start.13 = (bf16[2,64,256]{2,1,0:T(8,128)(2,1)S(1)}, bf16[2,64,256]{2,1,0:T(8,128)(2,1)S(1)}, u32[]{:S(2)}, u32[]{:S(2)}) collective-permute-start(bf16[2,64,256]{2,1,0:T(8,128)(2,1)S(1)} %get-tuple-element.84), channel_id=1, source_target_pairs={{0,4},{1,5},{2,6},{3,7},{4,0},{5,1},{6,2},{7,3},{8,12},{9,13},{10,... | collective-permute-start | bytes 196616 | tf_op jit(solution)/shard_map/side_mirror/ppermute | solution.py:401
  57.7 4.4 %collective-permute-start.14 = (bf16[2,64,256]{2,1,0:T(8,128)(2,1)S(1)}, bf16[2,64,256]{2,1,0:T(8,128)(2,1)S(1)}, u32[]{:S(2)}, u32[]{:S(2)}) collective-permute-start(bf16[2,64,256]{2,1,0:T(8,128)(2,1)S(1)} %get-tuple-element.85), channel_id=1, source_target_pairs={{0,2},{1,3},{2,4},{3,5},{4,6},{5,7},{6,0},{7,1},{8,10},{9,11},{10,... | collective-permute-start | bytes 196616 | tf_op jit(solution)/shard_map/side_mirror/ppermute | solution.py:401
  58.7 4.3 %collective-permute-start.15 = (bf16[2,64,256]{2,1,0:T(8,128)(2,1)S(1)}, bf16[2,64,256]{2,1,0:T(8,128)(2,1)S(1)}, u32[]{:S(2)}, u32[]{:S(2)}) collective-permute-start(bf16[2,64,256]{2,1,0:T(8,128)(2,1)S(1)} %get-tuple-element.86), channel_id=1, source_target_pairs={{0,6},{1,7},{2,0},{3,1},{4,2},{5,3},{6,4},{7,5},{8,14},{9,15},{10,... | collective-permute-start | bytes 196616 | tf_op jit(solution)/shard_map/side_mirror/ppermute | solution.py:401
  59.8 3.9 %collective-permute-start.17 = (bf16[8,2,64,256]{3,2,1,0:T(8,128)(2,1)S(1)}, bf16[8,2,64,256]{3,2,1,0:T(8,128)(2,1)S(1)}, u32[]{:S(2)}, u32[]{:S(2)}) collective-permute-start(bf16[8,2,64,256]{3,2,1,0:T(8,128)(2,1)S(1)} %collect.3.x_ref), channel_id=1, source_target_pairs={{0,8},{8,0},{1,9},{9,1},{2,10},{10,2},{3,11},{11,3},{4,12},{12,4},... | collective-permute-start | bytes 1572872 | tf_op jit(solution)/shard_map/side_mirror/ppermute | solution.py:406
  63.6 2.0 %collective-permute-start.16 = (bf16[8,2,64,256]{3,2,1,0:T(8,128)(2,1)S(1)}, bf16[8,2,64,256]{3,2,1,0:T(8,128)(2,1)S(1)}, u32[]{:S(2)}, u32[]{:S(2)}) collective-permute-start(bf16[8,2,64,256]{3,2,1,0:T(8,128)(2,1)S(1)} %collect.4), channel_id=1, source_target_pairs={{0,8},{8,0},{1,9},{9,1},{2,10},{10,2},{3,11},{11,3},{4,12},{12,4},... | collective-permute-start | bytes 1572872 | tf_op jit(solution)/shard_map/side_mirror/ppermute | solution.py:406
  71.4 2.7 %collective-permute-start.18 = (bf16[8,2,2,64,256]{4,3,2,1,0:T(8,128)(2,1)S(1)}, bf16[8,2,2,64,256]{4,3,2,1,0:T(8,128)(2,1)S(1)}, u32[]{:S(2)}, u32[]{:S(2)}) collective-permute-start(bf16[8,2,2,64,256]{4,3,2,1,0:T(8,128)(2,1)S(1)} %all-to-all-done.1.turned), channel_id=1, source_target_pairs={{0,8},{8,0},{1,9},{9,1},{2,10},{10,2},{3,11},{11,3},{4,12},{12,4},... | collective-permute-start | bytes 3145736 | tf_op jit(solution)/shard_map/ppermute | solution.py:406
  80.6 34.8 %all-to-all-start.2 = ((bf16[8,2,256,128]{3,2,1,0:T(8,128)(2,1)}), bf16[8,2,256,128]{3,2,1,0:T(8,128)(2,1)S(1)}, u32[]{:S(2)}, u32[]{:S(2)}) async-start(bf16[8,2,256,128]{3,2,1,0:T(8,128)(2,1)} %first_half.1), calls=%async_computation.2 | async-start | bytes 2097152 | tf_op jit(solution)/shard_map/partial/all_to_all | solution.py:460
  86.3 14.7 %collective-permute-start.19 = (bf16[1,256,128]{2,1,0:T(8,128)(2,1)S(1)}, bf16[1,256,128]{2,1,0:T(8,128)(2,1)S(1)}, u32[]{:S(2)}, u32[]{:S(2)}) collective-permute-start(bf16[1,256,128]{2,1,0:T(8,128)(2,1)S(1)} %get-tuple-element.99), channel_id=1, source_target_pairs={{0,3},{1,4},{2,5},{3,6},{4,7},{5,0},{6,1},{7,2},{8,11},{9,12},{10,... | collective-permute-start | bytes 196616 | tf_op jit(solution)/shard_map/side_partial/ppermute | solution.py:401
  88.1 12.9 %collective-permute-start.20 = (bf16[1,256,128]{2,1,0:T(8,128)(2,1)S(1)}, bf16[1,256,128]{2,1,0:T(8,128)(2,1)S(1)}, u32[]{:S(2)}, u32[]{:S(2)}) collective-permute-start(bf16[1,256,128]{2,1,0:T(8,128)(2,1)S(1)} %get-tuple-element.100), channel_id=1, source_target_pairs={{0,5},{1,6},{2,7},{3,0},{4,1},{5,2},{6,3},{7,4},{8,13},{9,14},{10,... | collective-permute-start | bytes 196616 | tf_op jit(solution)/shard_map/side_partial/ppermute | solution.py:401
  92.2 10.8 %collective-permute-start.21 = (bf16[1,256,128]{2,1,0:T(8,128)(2,1)S(1)}, bf16[1,256,128]{2,1,0:T(8,128)(2,1)S(1)}, u32[]{:S(2)}, u32[]{:S(2)}) collective-permute-start(bf16[1,256,128]{2,1,0:T(8,128)(2,1)S(1)} %get-tuple-element.101), channel_id=1, source_target_pairs={{0,1},{1,2},{2,3},{3,4},{4,5},{5,6},{6,7},{7,0},{8,9},{9,10},{10,1... | collective-permute-start | bytes 196616 | tf_op jit(solution)/shard_map/side_partial/ppermute | solution.py:401
  93.6 9.4 %collective-permute-start.22 = (bf16[1,256,128]{2,1,0:T(8,128)(2,1)S(1)}, bf16[1,256,128]{2,1,0:T(8,128)(2,1)S(1)}, u32[]{:S(2)}, u32[]{:S(2)}) collective-permute-start(bf16[1,256,128]{2,1,0:T(8,128)(2,1)S(1)} %get-tuple-element.102), channel_id=1, source_target_pairs={{0,7},{1,0},{2,1},{3,2},{4,3},{5,4},{6,5},{7,6},{8,15},{9,8},{10,9... | collective-permute-start | bytes 196616 | tf_op jit(solution)/shard_map/side_partial/ppermute | solution.py:401
  96.7 7.5 %collective-permute-start.23 = (bf16[1,256,128]{2,1,0:T(8,128)(2,1)S(1)}, bf16[1,256,128]{2,1,0:T(8,128)(2,1)S(1)}, u32[]{:S(2)}, u32[]{:S(2)}) collective-permute-start(bf16[1,256,128]{2,1,0:T(8,128)(2,1)S(1)} %get-tuple-element.103), channel_id=1, source_target_pairs={{0,4},{1,5},{2,6},{3,7},{4,0},{5,1},{6,2},{7,3},{8,12},{9,13},{10,... | collective-permute-start | bytes 196616 | tf_op jit(solution)/shard_map/side_partial/ppermute | solution.py:401
  101.0 4.3 %collective-permute-start.24 = (bf16[1,256,128]{2,1,0:T(8,128)(2,1)S(1)}, bf16[1,256,128]{2,1,0:T(8,128)(2,1)S(1)}, u32[]{:S(2)}, u32[]{:S(2)}) collective-permute-start(bf16[1,256,128]{2,1,0:T(8,128)(2,1)S(1)} %get-tuple-element.104), channel_id=1, source_target_pairs={{0,2},{1,3},{2,4},{3,5},{4,6},{5,7},{6,0},{7,1},{8,10},{9,11},{10,... | collective-permute-start | bytes 196616 | tf_op jit(solution)/shard_map/side_partial/ppermute | solution.py:401
  101.0 4.3 %collective-permute-start.25 = (bf16[1,256,128]{2,1,0:T(8,128)(2,1)S(1)}, bf16[1,256,128]{2,1,0:T(8,128)(2,1)S(1)}, u32[]{:S(2)}, u32[]{:S(2)}) collective-permute-start(bf16[1,256,128]{2,1,0:T(8,128)(2,1)S(1)} %get-tuple-element.105), channel_id=1, source_target_pairs={{0,6},{1,7},{2,0},{3,1},{4,2},{5,3},{6,4},{7,5},{8,14},{9,15},{10,... | collective-permute-start | bytes 196616 | tf_op jit(solution)/shard_map/side_partial/ppermute | solution.py:401
  106.0 2.0 %collective-permute-start.26 = (bf16[8,1,256,128]{3,2,1,0:T(8,128)(2,1)S(1)}, bf16[8,1,256,128]{3,2,1,0:T(8,128)(2,1)S(1)}, u32[]{:S(2)}, u32[]{:S(2)}) collective-permute-start(bf16[8,1,256,128]{3,2,1,0:T(8,128)(2,1)S(1)} %collect.5.t_ref), channel_id=1, source_target_pairs={{0,8},{8,0},{1,9},{9,1},{2,10},{10,2},{3,11},{11,3},{4,12},{12,4},... | collective-permute-start | bytes 1572872 | tf_op jit(solution)/shard_map/side_partial/ppermute | solution.py:406
  113.0 8.4 %collective-permute-start.27 = (bf16[8,64,256]{2,1,0:T(8,128)(2,1)S(1)}, bf16[8,64,256]{2,1,0:T(8,128)(2,1)S(1)}, u32[]{:S(2)}, u32[]{:S(2)}) collective-permute-start(bf16[8,64,256]{2,1,0:T(8,128)(2,1)S(1)} %get-tuple-element.108), channel_id=1, source_target_pairs={{0,16},{16,0},{1,17},{17,1},{2,18},{18,2},{3,19},{19,3},{4,20},{20... | collective-permute-start | bytes 786440 | tf_op jit(solution)/shard_map/ppermute | solution.py:406
  121.4 28.4 %all-to-all-start.3 = ((bf16[16,2,64,256]{3,2,1,0:T(8,128)(2,1)}), bf16[16,2,64,256]{3,2,1,0:T(8,128)(2,1)S(1)}, u32[]{:S(2)}, u32[]{:S(2)}) async-start(bf16[16,2,64,256]{3,2,1,0:T(8,128)(2,1)} %bitcast.13), calls=%async_computation.3 | async-start | bytes 2097152 | tf_op jit(solution)/shard_map/panels_out/all_to_all | solution.py:474
  129.4 14.9 %collective-permute-start.28 = (bf16[2,64,256]{2,1,0:T(8,128)(2,1)S(1)}, bf16[2,64,256]{2,1,0:T(8,128)(2,1)S(1)}, u32[]{:S(2)}, u32[]{:S(2)}) collective-permute-start(bf16[2,64,256]{2,1,0:T(8,128)(2,1)S(1)} %get-tuple-element.113), channel_id=1, source_target_pairs={{0,128},{32,160},{64,192},{96,224},{128,0},{160,32},{192,64},{224,... | collective-permute-start | bytes 196616 | tf_op jit(solution)/shard_map/side_out/ppermute | solution.py:401
  135.1 9.7 %collective-permute-start.29 = (bf16[2,64,256]{2,1,0:T(8,128)(2,1)S(1)}, bf16[2,64,256]{2,1,0:T(8,128)(2,1)S(1)}, u32[]{:S(2)}, u32[]{:S(2)}) collective-permute-start(bf16[2,64,256]{2,1,0:T(8,128)(2,1)S(1)} %get-tuple-element.114), channel_id=1, source_target_pairs={{0,96},{32,128},{64,160},{96,192},{128,224},{160,0},{192,32},{224,... | collective-permute-start | bytes 196616 | tf_op jit(solution)/shard_map/side_out/ppermute | solution.py:401
  135.7 11.9 %collective-permute-start.30 = (bf16[2,64,256]{2,1,0:T(8,128)(2,1)S(1)}, bf16[2,64,256]{2,1,0:T(8,128)(2,1)S(1)}, u32[]{:S(2)}, u32[]{:S(2)}) collective-permute-start(bf16[2,64,256]{2,1,0:T(8,128)(2,1)S(1)} %get-tuple-element.115), channel_id=1, source_target_pairs={{0,160},{32,192},{64,224},{96,0},{128,32},{160,64},{192,96},{224,1... | collective-permute-start | bytes 196616 | tf_op jit(solution)/shard_map/side_out/ppermute | solution.py:401
  140.2 7.4 %collective-permute-start.31 = (bf16[2,64,256]{2,1,0:T(8,128)(2,1)S(1)}, bf16[2,64,256]{2,1,0:T(8,128)(2,1)S(1)}, u32[]{:S(2)}, u32[]{:S(2)}) collective-permute-start(bf16[2,64,256]{2,1,0:T(8,128)(2,1)S(1)} %get-tuple-element.116), channel_id=1, source_target_pairs={{0,64},{32,96},{64,128},{96,160},{128,192},{160,224},{192,0},{224,... | collective-permute-start | bytes 196616 | tf_op jit(solution)/shard_map/side_out/ppermute | solution.py:401
  140.7 6.8 %collective-permute-start.32 = (bf16[2,64,256]{2,1,0:T(8,128)(2,1)S(1)}, bf16[2,64,256]{2,1,0:T(8,128)(2,1)S(1)}, u32[]{:S(2)}, u32[]{:S(2)}) collective-permute-start(bf16[2,64,256]{2,1,0:T(8,128)(2,1)S(1)} %get-tuple-element.117), channel_id=1, source_target_pairs={{0,192},{32,224},{64,0},{96,32},{128,64},{160,96},{192,128},{224,1... | collective-permute-start | bytes 196616 | tf_op jit(solution)/shard_map/side_out/ppermute | solution.py:401
  144.3 5.5 %collective-permute-start.33 = (bf16[2,64,256]{2,1,0:T(8,128)(2,1)S(1)}, bf16[2,64,256]{2,1,0:T(8,128)(2,1)S(1)}, u32[]{:S(2)}, u32[]{:S(2)}) collective-permute-start(bf16[2,64,256]{2,1,0:T(8,128)(2,1)S(1)} %get-tuple-element.118), channel_id=1, source_target_pairs={{0,32},{32,64},{64,96},{96,128},{128,160},{160,192},{192,224},{224... | collective-permute-start | bytes 196616 | tf_op jit(solution)/shard_map/side_out/ppermute | solution.py:401
  144.9 4.9 %collective-permute-start.34 = (bf16[2,64,256]{2,1,0:T(8,128)(2,1)S(1)}, bf16[2,64,256]{2,1,0:T(8,128)(2,1)S(1)}, u32[]{:S(2)}, u32[]{:S(2)}) collective-permute-start(bf16[2,64,256]{2,1,0:T(8,128)(2,1)S(1)} %get-tuple-element.119), channel_id=1, source_target_pairs={{0,224},{32,0},{64,32},{96,64},{128,96},{160,128},{192,160},{224,1... | collective-permute-start | bytes 196616 | tf_op jit(solution)/shard_map/side_out/ppermute | solution.py:401

commit v4 on v3

--- a/solution.py
+++ b/solution.py
@@ -20,6 +20,7 @@
 
 
 ORDER = {AT_Z: (0, 4, 3, 5, 2, 6, 1, 7), AT_C: (0, 3, 5, 1, 7, 4, 2, 6)}
+EARLY = 6
 STEPS = 4
 HBM = pl.BlockSpec(memory_space=pltpu.HBM)
 
@@ -190,16 +191,18 @@
 
     def store(step, product):
         width = product.shape[1]
-        final[:, pl.ds(pl.multiple_of(step * width, width), width)] = product
+        if len(t_refs) > 1:
+            final[:, pl.ds(pl.multiple_of(step * width, width), width)] = product
+        else:
+            lanes = t_refs[0].shape[3]
+            per_step = width // lanes
+            for u in range(per_step):
+                for k in range(depth):
+                    t_refs[0][step * per_step + u, k] = product[k * block:(k + 1) * block, u * lanes:(u + 1) * lanes]
 
     lax.fori_loop(0, BLOCKS, build, 0)
     products(sym, c_hbm, c_ref, sems, store)
-    if len(t_refs) == 1:
-        lanes = t_refs[0].shape[3]
-        for part in range(BLOCKS):
-            for k in range(depth):
-                t_refs[0][part, k] = final[k * block:(k + 1) * block, part * lanes:(part + 1) * lanes]
-    else:
+    if len(t_refs) > 1:
         lanes = t_refs[0].shape[2]
         for d in range(BLOCKS):
             part = (mine + ORDER[index][d]) % BLOCKS
@@ -434,8 +437,8 @@
         own = own.reshape(COLS, YLO, depth, rows, block)
     with jax.named_scope("side_in"):
         parts = rotate(AT_Z, join_and_spread(place, keep, got), "z")
-        side_own = collect(AT_Z, place, parts)
-    own, side_own, picked = together((own, side_own, picked))
+    own, early, picked = together((own, parts[:EARLY], picked))
+    side_own = collect(AT_Z, place, list(early) + parts[EARLY:])
 
     with jax.named_scope("mirror"):
         own_low = lax.all_to_all(own, "z", 0, 0, tiled=True)

time: 152 us -> 173 us (1.14)
  waiting for transfers between devices: 20 us -> 39.7 us
    ppermute x28, waiting for transfers between devices: 10.1 us -> 32 us  [rotate(): lax.ppermute(part, axes, [(i, (i + d) % BLOCKS) for i in range(BLOCKS)])]
    all_to_all x1, waiting for transfers between devices: 2.01 us -> 0.01 us  [per_device(): own_low = lax.all_to_all(own, 'z', 0, 0, tiled=True)]
  transfers between devices with their start and end apart: 39 -> 39, of which waited for: 16 -> 18; matrix products, arithmetic and copies ran while one was open for 0% -> 0% of each run, Pallas kernels for 16% -> 14%
where the time goes in v4:
time: 173 us; the launch traced here: 172 us
  starting transfers between devices  98.3 us (57%)
  waiting for transfers between devices  39.7 us (23%)
  Pallas kernels  32.8 us (19%)
    ppermute x28, starting transfers between devices, rotate(): lax.ppermute(part, axes, [(i, (i + d) % BLOCKS) for i in range(BLOCKS)])  69.1 us
    ppermute x28, waiting for transfers between devices, rotate(): lax.ppermute(part, axes, [(i, (i + d) % BLOCKS) for i in range(BLOCKS)])  32 us
    pallas_call x2, Pallas kernels, first_half(): pl.pallas_call(functools.partial(first_kernel, index), out_shape=[jax.Sha...  10.1 us
    all_to_all x1, starting transfers between devices, per_device(): result = lax.all_to_all(result, PLANE, 0, 0, tiled=True)  7.29 us
    all_to_all x1, starting transfers between devices, per_device(): own = lax.all_to_all(own, PLANE, 0, 0, tiled=True)  7.2 us
    pallas_call x1, Pallas kernels, pick_columns(): pl.pallas_call(pick_kernel, out_shape=[pltpu.HBM((size, width), BF16), pl...  6.85 us
    all_to_all x1, starting transfers between devices, per_device(): partial_value = lax.all_to_all(partial_value, 'z', 0, 0, tiled=True)  6.53 us
    ppermute x7, waiting for transfers between devices, swap(): return lax.ppermute(value, axis, [(0, 1), (1, 0)])  6.49 us
  transfers between devices with their start and end apart: 39, of which 18 were waited for; matrix products, arithmetic and copies ran while one was open for 0% of the time, Pallas kernels for 14%

profile of v4, /device:TPU:2, one launch (start us, length us, event | category | flops | bytes accessed | tf_op | source)
XLA Modules:
  0.0 172.3 jit_solution(4286426556546760375)
XLA Ops:
  0.0 1.1 slice.3
  1.1 1.7 collective-permute-start
  2.9 6.9 %pick_columns.1 = (bf16[2048,1024]{1,0:T(8,128)(2,1)}, bf16[32,64,256]{2,1,0:T(8,128)(2,1)}) custom-call(s32[4]{0:T(128)S(1)} %pad_add_fusion.place, bf16[2048,2048]{1,0:T(8,128)(2,1)} %c_hbm.3, bf16[48,64,256]{2,1,0:T(8,128)(2,1)} %panel_hbm.1), custom_call_target="tpu_custom_call" | custom-call | tf_op jit(solution)/shard_map/pick_columns/pallas_call | solution.py:140
  9.8 7.2 %all-to-all-start = ((bf16[16,2,64,256]{3,2,1,0:T(8,128)(2,1)}), bf16[16,2,64,256]{3,2,1,0:T(8,128)(2,1)}, u32[]{:S(2)}, u32[]{:S(2)}) async-start(bf16[16,2,64,256]{3,2,1,0:T(8,128)(2,1)} %bitcast.23), calls=%async_computation | async-start | bytes 2097152 | tf_op jit(solution)/shard_map/panels_in/all_to_all | solution.py:436
  16.9 0.6 join_and_spread.2
  17.5 7.3 %collective-permute-start.1 = (bf16[2,64,256]{2,1,0:T(8,128)(2,1)S(1)}, bf16[2,64,256]{2,1,0:T(8,128)(2,1)S(1)}, u32[]{:S(2)}, u32[]{:S(2)}) collective-permute-start(bf16[2,64,256]{2,1,0:T(8,128)(2,1)S(1)} %get-tuple-element.74), channel_id=1, source_target_pairs={{0,128},{32,160},{64,192},{96,224},{128,0},{160,32},{192,64},{224,... | collective-permute-start | bytes 196616 | tf_op jit(solution)/shard_map/side_in/ppermute | solution.py:404
  24.8 1.9 %collective-permute-start.2 = (bf16[2,64,256]{2,1,0:T(8,128)(2,1)S(1)}, bf16[2,64,256]{2,1,0:T(8,128)(2,1)S(1)}, u32[]{:S(2)}, u32[]{:S(2)}) collective-permute-start(bf16[2,64,256]{2,1,0:T(8,128)(2,1)S(1)} %get-tuple-element.75), channel_id=1, source_target_pairs={{0,96},{32,128},{64,160},{96,192},{128,224},{160,0},{192,32},{224,... | collective-permute-start | bytes 196616 | tf_op jit(solution)/shard_map/side_in/ppermute | solution.py:404
  26.8 3.1 %collective-permute-start.3 = (bf16[2,64,256]{2,1,0:T(8,128)(2,1)S(1)}, bf16[2,64,256]{2,1,0:T(8,128)(2,1)S(1)}, u32[]{:S(2)}, u32[]{:S(2)}) collective-permute-start(bf16[2,64,256]{2,1,0:T(8,128)(2,1)S(1)} %get-tuple-element.76), channel_id=1, source_target_pairs={{0,160},{32,192},{64,224},{96,0},{128,32},{160,64},{192,96},{224,1... | collective-permute-start | bytes 196616 | tf_op jit(solution)/shard_map/side_in/ppermute | solution.py:404
  29.9 1.5 collective-permute-start.4
  31.3 2.7 %collective-permute-start.5 = (bf16[2,64,256]{2,1,0:T(8,128)(2,1)S(1)}, bf16[2,64,256]{2,1,0:T(8,128)(2,1)S(1)}, u32[]{:S(2)}, u32[]{:S(2)}) collective-permute-start(bf16[2,64,256]{2,1,0:T(8,128)(2,1)S(1)} %get-tuple-element.78), channel_id=1, source_target_pairs={{0,192},{32,224},{64,0},{96,32},{128,64},{160,96},{192,128},{224,1... | collective-permute-start | bytes 196616 | tf_op jit(solution)/shard_map/side_in/ppermute | solution.py:404
  34.0 1.3 collective-permute-done.2.refs_2_
  35.3 1.5 collective-permute-done.4.refs_4_
  36.8 0.5 collective-permute-done.5.refs_5_
  37.3 4.6 %all-to-all-start.1 = ((bf16[8,2,2,64,256]{4,3,2,1,0:T(8,128)(2,1)}), bf16[8,2,2,64,256]{4,3,2,1,0:T(8,128)(2,1)S(1)}, u32[]{:S(2)}, u32[]{:S(2)}) async-start(bf16[8,2,2,64,256]{4,3,2,1,0:T(8,128)(2,1)} %bitcast.8.direct), calls=%async_computation.1 | async-start | bytes 2097152 | tf_op jit(solution)/shard_map/mirror/all_to_all | solution.py:444
  41.9 2.0 %collective-permute-start.7 = (bf16[2,64,256]{2,1,0:T(8,128)(2,1)S(1)}, bf16[2,64,256]{2,1,0:T(8,128)(2,1)S(1)}, u32[]{:S(2)}, u32[]{:S(2)}) collective-permute-start(bf16[2,64,256]{2,1,0:T(8,128)(2,1)S(1)} %get-tuple-element.87), channel_id=1, source_target_pairs={{0,32},{32,64},{64,96},{96,128},{128,160},{160,192},{192,224},{224... | collective-permute-start | bytes 196616 | tf_op jit(solution)/shard_map/side_in/ppermute | solution.py:404
  43.9 1.3 collective-permute-start.8
  45.2 18.2 %collective-permute-done.7.refs_6_ = bf16[2,64,256]{2,1,0:T(8,128)(2,1)S(1)} collective-permute-done((bf16[2,64,256]{2,1,0:T(8,128)(2,1)S(1)}, bf16[2,64,256]{2,1,0:T(8,128)(2,1)S(1)}, u32[]{:S(2)}, u32[]{:S(2)}) %collective-permute-start.7) | collective-permute-done | bytes 65568 | tf_op jit(solution)/shard_map/side_in/ppermute | solution.py:404
  63.5 2.7 %collective-permute-done.8.refs_7_ = bf16[2,64,256]{2,1,0:T(8,128)(2,1)S(1)} collective-permute-done((bf16[2,64,256]{2,1,0:T(8,128)(2,1)S(1)}, bf16[2,64,256]{2,1,0:T(8,128)(2,1)S(1)}, u32[]{:S(2)}, u32[]{:S(2)}) %collective-permute-start.8) | collective-permute-done | bytes 65568 | tf_op jit(solution)/shard_map/side_in/ppermute | solution.py:404
  66.1 0.6 collect.3.x_ref
  66.7 0.6 spread.1
  67.3 3.9 %collective-permute-start.9 = (bf16[2,64,256]{2,1,0:T(8,128)(2,1)S(1)}, bf16[2,64,256]{2,1,0:T(8,128)(2,1)S(1)}, u32[]{:S(2)}, u32[]{:S(2)}) collective-permute-start(bf16[2,64,256]{2,1,0:T(8,128)(2,1)S(1)} %get-tuple-element.90), channel_id=1, source_target_pairs={{0,3},{1,4},{2,5},{3,6},{4,7},{5,0},{6,1},{7,2},{8,11},{9,12},{10,... | collective-permute-start | bytes 196616 | tf_op jit(solution)/shard_map/side_mirror/ppermute | solution.py:404
  71.3 2.1 %collective-permute-start.10 = (bf16[2,64,256]{2,1,0:T(8,128)(2,1)S(1)}, bf16[2,64,256]{2,1,0:T(8,128)(2,1)S(1)}, u32[]{:S(2)}, u32[]{:S(2)}) collective-permute-start(bf16[2,64,256]{2,1,0:T(8,128)(2,1)S(1)} %get-tuple-element.91), channel_id=1, source_target_pairs={{0,5},{1,6},{2,7},{3,0},{4,1},{5,2},{6,3},{7,4},{8,13},{9,14},{10,... | collective-permute-start | bytes 196616 | tf_op jit(solution)/shard_map/side_mirror/ppermute | solution.py:404
  73.3 1.5 collective-permute-start.11
  74.8 3.0 %collective-permute-start.12 = (bf16[2,64,256]{2,1,0:T(8,128)(2,1)S(1)}, bf16[2,64,256]{2,1,0:T(8,128)(2,1)S(1)}, u32[]{:S(2)}, u32[]{:S(2)}) collective-permute-start(bf16[2,64,256]{2,1,0:T(8,128)(2,1)S(1)} %get-tuple-element.93), channel_id=1, source_target_pairs={{0,7},{1,0},{2,1},{3,2},{4,3},{5,4},{6,5},{7,6},{8,15},{9,8},{10,9... | collective-permute-start | bytes 196616 | tf_op jit(solution)/shard_map/side_mirror/ppermute | solution.py:404
  77.8 2.1 %collective-permute-start.13 = (bf16[2,64,256]{2,1,0:T(8,128)(2,1)S(1)}, bf16[2,64,256]{2,1,0:T(8,128)(2,1)S(1)}, u32[]{:S(2)}, u32[]{:S(2)}) collective-permute-start(bf16[2,64,256]{2,1,0:T(8,128)(2,1)S(1)} %get-tuple-element.94), channel_id=1, source_target_pairs={{0,4},{1,5},{2,6},{3,7},{4,0},{5,1},{6,2},{7,3},{8,12},{9,13},{10,... | collective-permute-start | bytes 196616 | tf_op jit(solution)/shard_map/side_mirror/ppermute | solution.py:404
  79.8 1.4 collective-permute-start.14
  81.2 1.1 collective-permute-start.15
  82.3 1.2 collective-permute-done.13.refs_5_
  83.5 0.7 collective-permute-done.14.refs_6_
  84.2 1.2 collective-permute-done.15.refs_7_
  85.5 0.6 collect.4
  86.1 0.1 collective-permute-start.16
  86.2 1.9 %collective-permute-done.16 = bf16[8,2,64,256]{3,2,1,0:T(8,128)(2,1)S(1)} collective-permute-done((bf16[8,2,64,256]{3,2,1,0:T(8,128)(2,1)S(1)}, bf16[8,2,64,256]{3,2,1,0:T(8,128)(2,1)S(1)}, u32[]{:S(2)}, u32[]{:S(2)}) %collective-permute-start.16) | collective-permute-done | bytes 524320 | tf_op jit(solution)/shard_map/side_mirror/ppermute | solution.py:409
  88.1 3.8 %first_half_side.1 = (bf16[1,256,128]{2,1,0:T(8,128)(2,1)S(1)}, bf16[1,256,128]{2,1,0:T(8,128)(2,1)S(1)}, bf16[1,256,128]{2,1,0:T(8,128)(2,1)S(1)}, bf16[1,256,1...) custom-call(s32[4]{0:T(128)S(1)} %pad_add_fusion.place, ...), custom_call_target="tpu_custom_call" | custom-call | tf_op jit(solution)/shard_map/side_mirror/first_half_side/pallas_call | solution.py:216
  91.8 0.2 collective-permute-start.18
  92.1 2.5 %collective-permute-done.18.turned_other = bf16[8,2,2,64,256]{4,3,2,1,0:T(8,128)(2,1)S(1)} collective-permute-done((bf16[8,2,2,64,256]{4,3,2,1,0:T(8,128)(2,1)S(1)}, bf16[8,2,2,64,256]{4,3,2,1,0:T(8,128)(2,1)S(1)}, u32[]{:S(2)}, u32[]{:S(2)}) %collective-permute-start.18) | collective-permute-done | bytes 1048608 | tf_op jit(solution)/shard_map/ppermute | solution.py:409
  94.6 6.3 %first_half.1 = bf16[8,2,256,128]{3,2,1,0:T(8,128)(2,1)} custom-call(s32[4]{0:T(128)S(1)} %pad_add_fusion.place, bf16[8,2,2,64,256]{4,3,2,1,0:T(8,128)(2,1)} %bitcast.8.direct, bf16[8,2,2,64,256]{4,3,2,1,0:T(8,128)(2,1)S(1)} %collective-permute-done.6.direct_other, bf16[8,2,2,64,256]{4,3,2,1,0:T(8,128)(2,1)S(1)} %all-to-all-done.1.turned, ...), custom_call_target="tpu_custom_call" | custom-call | tf_op jit(solution)/shard_map/first_half/pallas_call | solution.py:216
  100.9 6.5 %all-to-all-start.2 = ((bf16[8,2,256,128]{3,2,1,0:T(8,128)(2,1)}), bf16[8,2,256,128]{3,2,1,0:T(8,128)(2,1)S(1)}, u32[]{:S(2)}, u32[]{:S(2)}) async-start(bf16[8,2,256,128]{3,2,1,0:T(8,128)(2,1)} %first_half.1), calls=%async_computation.2 | async-start | bytes 2097152 | tf_op jit(solution)/shard_map/partial/all_to_all | solution.py:463
  107.5 1.6 collective-permute-start.19
  109.0 4.4 %collective-permute-start.20 = (bf16[1,256,128]{2,1,0:T(8,128)(2,1)S(1)}, bf16[1,256,128]{2,1,0:T(8,128)(2,1)S(1)}, u32[]{:S(2)}, u32[]{:S(2)}) collective-permute-start(bf16[1,256,128]{2,1,0:T(8,128)(2,1)S(1)} %get-tuple-element.110), channel_id=1, source_target_pairs={{0,5},{1,6},{2,7},{3,0},{4,1},{5,2},{6,3},{7,4},{8,13},{9,14},{10,... | collective-permute-start | bytes 196616 | tf_op jit(solution)/shard_map/side_partial/ppermute | solution.py:404
  113.4 1.0 collective-permute-start.21
  114.4 3.4 %collective-permute-start.22 = (bf16[1,256,128]{2,1,0:T(8,128)(2,1)S(1)}, bf16[1,256,128]{2,1,0:T(8,128)(2,1)S(1)}, u32[]{:S(2)}, u32[]{:S(2)}) collective-permute-start(bf16[1,256,128]{2,1,0:T(8,128)(2,1)S(1)} %get-tuple-element.112), channel_id=1, source_target_pairs={{0,7},{1,0},{2,1},{3,2},{4,3},{5,4},{6,5},{7,6},{8,15},{9,8},{10,9... | collective-permute-start | bytes 196616 | tf_op jit(solution)/shard_map/side_partial/ppermute | solution.py:404
  117.8 4.0 %collective-permute-start.23 = (bf16[1,256,128]{2,1,0:T(8,128)(2,1)S(1)}, bf16[1,256,128]{2,1,0:T(8,128)(2,1)S(1)}, u32[]{:S(2)}, u32[]{:S(2)}) collective-permute-start(bf16[1,256,128]{2,1,0:T(8,128)(2,1)S(1)} %get-tuple-element.113), channel_id=1, source_target_pairs={{0,4},{1,5},{2,6},{3,7},{4,0},{5,1},{6,2},{7,3},{8,12},{9,13},{10,... | collective-permute-start | bytes 196616 | tf_op jit(solution)/shard_map/side_partial/ppermute | solution.py:404
  121.8 2.0 %collective-permute-start.25 = (bf16[1,256,128]{2,1,0:T(8,128)(2,1)S(1)}, bf16[1,256,128]{2,1,0:T(8,128)(2,1)S(1)}, u32[]{:S(2)}, u32[]{:S(2)}) collective-permute-start(bf16[1,256,128]{2,1,0:T(8,128)(2,1)S(1)} %get-tuple-element.115), channel_id=1, source_target_pairs={{0,6},{1,7},{2,0},{3,1},{4,2},{5,3},{6,4},{7,5},{8,14},{9,15},{10,... | collective-permute-start | bytes 196616 | tf_op jit(solution)/shard_map/side_partial/ppermute | solution.py:404
  123.8 1.1 collective-permute-done.23.refs_5_
  125.0 1.1 collective-permute-done.24.refs_6_
  126.1 0.6 collect.5.t_ref
  126.8 1.9 %collective-permute-done.26.other_ref = bf16[8,1,256,128]{3,2,1,0:T(8,128)(2,1)S(1)} collective-permute-done((bf16[8,1,256,128]{3,2,1,0:T(8,128)(2,1)S(1)}, bf16[8,1,256,128]{3,2,1,0:T(8,128)(2,1)S(1)}, u32[]{:S(2)}, u32[]{:S(2)}) %collective-permute-start.26) | collective-permute-done | bytes 524320 | tf_op jit(solution)/shard_map/side_partial/ppermute | solution.py:409
  128.7 5.0 %second_half_side.1 = (bf16[8,64,256]{2,1,0:T(8,128)(2,1)S(1)}, bf16[8,64,256]{2,1,0:T(8,128)(2,1)S(1)}) custom-call(s32[4]{0:T(128)S(1)} %pad_add_fusion.place, bf16[8,1,256,128]{3,2,1,0:T(8,128)(2,1)S(1)} %collect.5.t_ref, bf16[8,1,256,128]{3,2,1,0:T(8,128)(2,1)S(1)} %collective-permute-done.26.other_ref, bf16[2048,1024]{1,0:T(8,128)(2,1)} %get-tuple-element.97.c_hbm), custom_call_target="tpu_custom_call" | custom-call | tf_op jit(solution)/shard_map/side_partial/second_half_side/pallas_call | solution.py:305
  133.8 1.5 collective-permute-start.27
  135.3 1.2 all-to-all-done.2.t_ref
  136.6 5.5 %second_half.1 = bf16[8,2,2,64,256]{4,3,2,1,0:T(8,128)(2,1)} custom-call(bf16[8,2,256,128]{3,2,1,0:T(8,128)(2,1)S(1)} %all-to-all-done.2.t_ref, bf16[2048,2048]{1,0:T(8,128)(2,1)} %c_hbm.3), custom_call_target="tpu_custom_call" | custom-call | tf_op jit(solution)/shard_map/second_half/pallas_call | solution.py:258
  142.0 0.2 collective-permute-done.27.got
  142.2 7.3 %all-to-all-start.3 = ((bf16[16,2,64,256]{3,2,1,0:T(8,128)(2,1)}), bf16[16,2,64,256]{3,2,1,0:T(8,128)(2,1)S(1)}, u32[]{:S(2)}, u32[]{:S(2)}) async-start(bf16[16,2,64,256]{3,2,1,0:T(8,128)(2,1)} %bitcast.13), calls=%async_computation.3 | async-start | bytes 2097152 | tf_op jit(solution)/shard_map/panels_out/all_to_all | solution.py:477
  149.5 0.6 join_and_spread.3
  150.1 5.6 %collective-permute-start.28 = (bf16[2,64,256]{2,1,0:T(8,128)(2,1)S(1)}, bf16[2,64,256]{2,1,0:T(8,128)(2,1)S(1)}, u32[]{:S(2)}, u32[]{:S(2)}) collective-permute-start(bf16[2,64,256]{2,1,0:T(8,128)(2,1)S(1)} %get-tuple-element.123), channel_id=1, source_target_pairs={{0,128},{32,160},{64,192},{96,224},{128,0},{160,32},{192,64},{224,... | collective-permute-start | bytes 196616 | tf_op jit(solution)/shard_map/side_out/ppermute | solution.py:404
  155.7 0.6 collective-permute-start.29
  156.2 4.5 %collective-permute-start.30 = (bf16[2,64,256]{2,1,0:T(8,128)(2,1)S(1)}, bf16[2,64,256]{2,1,0:T(8,128)(2,1)S(1)}, u32[]{:S(2)}, u32[]{:S(2)}) collective-permute-start(bf16[2,64,256]{2,1,0:T(8,128)(2,1)S(1)} %get-tuple-element.125), channel_id=1, source_target_pairs={{0,160},{32,192},{64,224},{96,0},{128,32},{160,64},{192,96},{224,1... | collective-permute-start | bytes 196616 | tf_op jit(solution)/shard_map/side_out/ppermute | solution.py:404
  160.7 0.6 collective-permute-start.31
  161.3 3.6 %collective-permute-start.32 = (bf16[2,64,256]{2,1,0:T(8,128)(2,1)S(1)}, bf16[2,64,256]{2,1,0:T(8,128)(2,1)S(1)}, u32[]{:S(2)}, u32[]{:S(2)}) collective-permute-start(bf16[2,64,256]{2,1,0:T(8,128)(2,1)S(1)} %get-tuple-element.127), channel_id=1, source_target_pairs={{0,192},{32,224},{64,0},{96,32},{128,64},{160,96},{192,128},{224,1... | collective-permute-start | bytes 196616 | tf_op jit(solution)/shard_map/side_out/ppermute | solution.py:404
  164.9 0.6 collective-permute-start.33
  165.4 2.7 %collective-permute-start.34 = (bf16[2,64,256]{2,1,0:T(8,128)(2,1)S(1)}, bf16[2,64,256]{2,1,0:T(8,128)(2,1)S(1)}, u32[]{:S(2)}, u32[]{:S(2)}) collective-permute-start(bf16[2,64,256]{2,1,0:T(8,128)(2,1)S(1)} %get-tuple-element.129), channel_id=1, source_target_pairs={{0,224},{32,0},{64,32},{96,64},{128,96},{160,128},{192,160},{224,1... | collective-permute-start | bytes 196616 | tf_op jit(solution)/shard_map/side_out/ppermute | solution.py:404
  168.2 2.2 %collective-permute-done.33.refs_6_ = bf16[2,64,256]{2,1,0:T(8,128)(2,1)S(1)} collective-permute-done((bf16[2,64,256]{2,1,0:T(8,128)(2,1)S(1)}, bf16[2,64,256]{2,1,0:T(8,128)(2,1)S(1)}, u32[]{:S(2)}, u32[]{:S(2)}) %collective-permute-start.33) | collective-permute-done | bytes 65568 | tf_op jit(solution)/shard_map/side_out/ppermute | solution.py:404
  170.3 1.8 %finish.1 = bf16[48,64,256]{2,1,0:T(8,128)(2,1)} custom-call(s32[4]{0:T(128)S(1)} %pad_add_fusion.place, bf16[2,64,256]{2,1,0:T(8,128)(2,1)S(1)} %get-tuple-element.122.refs_0_, bf16[2,64,256]{2,1,0:T(8,128)(2,1)S(1)} %collective-permute-done.28.refs_1_, bf16[2,64,256]{2,1,0:T(8,128)(2,1)S(1)} %collective-permute-done.29.refs_2_, ...), custom_call_target="tpu_custom_call" | custom-call | tf_op jit(solution)/shard_map/finish/pallas_call | solution.py:390
  (29 shorter events, 0.4 us)
Async XLA Ops:
  1.1 8.6 %collective-permute-start = (bf16[8,64,256]{2,1,0:T(8,128)(2,1)S(1)}, bf16[8,64,256]{2,1,0:T(8,128)(2,1)S(1)}, u32[]{:S(2)}, u32[]{:S(2)}) collective-permute-start(bf16[8,64,256]{2,1,0:T(8,128)(2,1)S(1)} %get-tuple-element.132), channel_id=1, source_target_pairs={{0,16},{16,0},{1,17},{17,1},{2,18},{18,2},{3,19},{19,3},{4,20},{20... | collective-permute-start | bytes 786440 | tf_op jit(solution)/shard_map/side_in/ppermute | solution.py:409
  9.8 27.6 %all-to-all-start = ((bf16[16,2,64,256]{3,2,1,0:T(8,128)(2,1)}), bf16[16,2,64,256]{3,2,1,0:T(8,128)(2,1)}, u32[]{:S(2)}, u32[]{:S(2)}) async-start(bf16[16,2,64,256]{3,2,1,0:T(8,128)(2,1)} %bitcast.23), calls=%async_computation | async-start | bytes 2097152 | tf_op jit(solution)/shard_map/panels_in/all_to_all | solution.py:436
  17.5 16.5 %collective-permute-start.1 = (bf16[2,64,256]{2,1,0:T(8,128)(2,1)S(1)}, bf16[2,64,256]{2,1,0:T(8,128)(2,1)S(1)}, u32[]{:S(2)}, u32[]{:S(2)}) collective-permute-start(bf16[2,64,256]{2,1,0:T(8,128)(2,1)S(1)} %get-tuple-element.74), channel_id=1, source_target_pairs={{0,128},{32,160},{64,192},{96,224},{128,0},{160,32},{192,64},{224,... | collective-permute-start | bytes 196616 | tf_op jit(solution)/shard_map/side_in/ppermute | solution.py:404
  24.8 10.5 %collective-permute-start.2 = (bf16[2,64,256]{2,1,0:T(8,128)(2,1)S(1)}, bf16[2,64,256]{2,1,0:T(8,128)(2,1)S(1)}, u32[]{:S(2)}, u32[]{:S(2)}) collective-permute-start(bf16[2,64,256]{2,1,0:T(8,128)(2,1)S(1)} %get-tuple-element.75), channel_id=1, source_target_pairs={{0,96},{32,128},{64,160},{96,192},{128,224},{160,0},{192,32},{224,... | collective-permute-start | bytes 196616 | tf_op jit(solution)/shard_map/side_in/ppermute | solution.py:404
  26.8 8.5 %collective-permute-start.3 = (bf16[2,64,256]{2,1,0:T(8,128)(2,1)S(1)}, bf16[2,64,256]{2,1,0:T(8,128)(2,1)S(1)}, u32[]{:S(2)}, u32[]{:S(2)}) collective-permute-start(bf16[2,64,256]{2,1,0:T(8,128)(2,1)S(1)} %get-tuple-element.76), channel_id=1, source_target_pairs={{0,160},{32,192},{64,224},{96,0},{128,32},{160,64},{192,96},{224,1... | collective-permute-start | bytes 196616 | tf_op jit(solution)/shard_map/side_in/ppermute | solution.py:404
  29.9 7.0 %collective-permute-start.4 = (bf16[2,64,256]{2,1,0:T(8,128)(2,1)S(1)}, bf16[2,64,256]{2,1,0:T(8,128)(2,1)S(1)}, u32[]{:S(2)}, u32[]{:S(2)}) collective-permute-start(bf16[2,64,256]{2,1,0:T(8,128)(2,1)S(1)} %get-tuple-element.77), channel_id=1, source_target_pairs={{0,64},{32,96},{64,128},{96,160},{128,192},{160,224},{192,0},{224,... | collective-permute-start | bytes 196616 | tf_op jit(solution)/shard_map/side_in/ppermute | solution.py:404
  31.3 6.0 %collective-permute-start.5 = (bf16[2,64,256]{2,1,0:T(8,128)(2,1)S(1)}, bf16[2,64,256]{2,1,0:T(8,128)(2,1)S(1)}, u32[]{:S(2)}, u32[]{:S(2)}) collective-permute-start(bf16[2,64,256]{2,1,0:T(8,128)(2,1)S(1)} %get-tuple-element.78), channel_id=1, source_target_pairs={{0,192},{32,224},{64,0},{96,32},{128,64},{160,96},{192,128},{224,1... | collective-permute-start | bytes 196616 | tf_op jit(solution)/shard_map/side_in/ppermute | solution.py:404
  37.3 54.5 %all-to-all-start.1 = ((bf16[8,2,2,64,256]{4,3,2,1,0:T(8,128)(2,1)}), bf16[8,2,2,64,256]{4,3,2,1,0:T(8,128)(2,1)S(1)}, u32[]{:S(2)}, u32[]{:S(2)}) async-start(bf16[8,2,2,64,256]{4,3,2,1,0:T(8,128)(2,1)} %bitcast.8.direct), calls=%async_computation.1 | async-start | bytes 2097152 | tf_op jit(solution)/shard_map/mirror/all_to_all | solution.py:444
  41.9 49.9 %collective-permute-start.6 = (bf16[8,2,2,64,256]{4,3,2,1,0:T(8,128)(2,1)}, bf16[8,2,2,64,256]{4,3,2,1,0:T(8,128)(2,1)S(1)}, u32[]{:S(2)}, u32[]{:S(2)}) collective-permute-start(bf16[8,2,2,64,256]{4,3,2,1,0:T(8,128)(2,1)} %bitcast.8.direct), channel_id=1, source_target_pairs={{0,8},{8,0},{1,9},{9,1},{2,10},{10,2},{3,11},{11,3},{4,12},{12,4},... | collective-permute-start | bytes 3145736 | tf_op jit(solution)/shard_map/ppermute | solution.py:409
  41.9 21.5 %collective-permute-start.7 = (bf16[2,64,256]{2,1,0:T(8,128)(2,1)S(1)}, bf16[2,64,256]{2,1,0:T(8,128)(2,1)S(1)}, u32[]{:S(2)}, u32[]{:S(2)}) collective-permute-start(bf16[2,64,256]{2,1,0:T(8,128)(2,1)S(1)} %get-tuple-element.87), channel_id=1, source_target_pairs={{0,32},{32,64},{64,96},{96,128},{128,160},{160,192},{192,224},{224... | collective-permute-start | bytes 196616 | tf_op jit(solution)/shard_map/side_in/ppermute | solution.py:404
  43.9 22.2 %collective-permute-start.8 = (bf16[2,64,256]{2,1,0:T(8,128)(2,1)S(1)}, bf16[2,64,256]{2,1,0:T(8,128)(2,1)S(1)}, u32[]{:S(2)}, u32[]{:S(2)}) collective-permute-start(bf16[2,64,256]{2,1,0:T(8,128)(2,1)S(1)} %get-tuple-element.88), channel_id=1, source_target_pairs={{0,224},{32,0},{64,32},{96,64},{128,96},{160,128},{192,160},{224,1... | collective-permute-start | bytes 196616 | tf_op jit(solution)/shard_map/side_in/ppermute | solution.py:404
  67.3 10.4 %collective-permute-start.9 = (bf16[2,64,256]{2,1,0:T(8,128)(2,1)S(1)}, bf16[2,64,256]{2,1,0:T(8,128)(2,1)S(1)}, u32[]{:S(2)}, u32[]{:S(2)}) collective-permute-start(bf16[2,64,256]{2,1,0:T(8,128)(2,1)S(1)} %get-tuple-element.90), channel_id=1, source_target_pairs={{0,3},{1,4},{2,5},{3,6},{4,7},{5,0},{6,1},{7,2},{8,11},{9,12},{10,... | collective-permute-start | bytes 196616 | tf_op jit(solution)/shard_map/side_mirror/ppermute | solution.py:404
  71.3 8.6 %collective-permute-start.10 = (bf16[2,64,256]{2,1,0:T(8,128)(2,1)S(1)}, bf16[2,64,256]{2,1,0:T(8,128)(2,1)S(1)}, u32[]{:S(2)}, u32[]{:S(2)}) collective-permute-start(bf16[2,64,256]{2,1,0:T(8,128)(2,1)S(1)} %get-tuple-element.91), channel_id=1, source_target_pairs={{0,5},{1,6},{2,7},{3,0},{4,1},{5,2},{6,3},{7,4},{8,13},{9,14},{10,... | collective-permute-start | bytes 196616 | tf_op jit(solution)/shard_map/side_mirror/ppermute | solution.py:404
  73.3 7.9 %collective-permute-start.11 = (bf16[2,64,256]{2,1,0:T(8,128)(2,1)S(1)}, bf16[2,64,256]{2,1,0:T(8,128)(2,1)S(1)}, u32[]{:S(2)}, u32[]{:S(2)}) collective-permute-start(bf16[2,64,256]{2,1,0:T(8,128)(2,1)S(1)} %get-tuple-element.92), channel_id=1, source_target_pairs={{0,1},{1,2},{2,3},{3,4},{4,5},{5,6},{6,7},{7,0},{8,9},{9,10},{10,1... | collective-permute-start | bytes 196616 | tf_op jit(solution)/shard_map/side_mirror/ppermute | solution.py:404
  74.8 7.5 %collective-permute-start.12 = (bf16[2,64,256]{2,1,0:T(8,128)(2,1)S(1)}, bf16[2,64,256]{2,1,0:T(8,128)(2,1)S(1)}, u32[]{:S(2)}, u32[]{:S(2)}) collective-permute-start(bf16[2,64,256]{2,1,0:T(8,128)(2,1)S(1)} %get-tuple-element.93), channel_id=1, source_target_pairs={{0,7},{1,0},{2,1},{3,2},{4,3},{5,4},{6,5},{7,6},{8,15},{9,8},{10,9... | collective-permute-start | bytes 196616 | tf_op jit(solution)/shard_map/side_mirror/ppermute | solution.py:404
  77.8 5.8 %collective-permute-start.13 = (bf16[2,64,256]{2,1,0:T(8,128)(2,1)S(1)}, bf16[2,64,256]{2,1,0:T(8,128)(2,1)S(1)}, u32[]{:S(2)}, u32[]{:S(2)}) collective-permute-start(bf16[2,64,256]{2,1,0:T(8,128)(2,1)S(1)} %get-tuple-element.94), channel_id=1, source_target_pairs={{0,4},{1,5},{2,6},{3,7},{4,0},{5,1},{6,2},{7,3},{8,12},{9,13},{10,... | collective-permute-start | bytes 196616 | tf_op jit(solution)/shard_map/side_mirror/ppermute | solution.py:404
  79.8 4.4 %collective-permute-start.14 = (bf16[2,64,256]{2,1,0:T(8,128)(2,1)S(1)}, bf16[2,64,256]{2,1,0:T(8,128)(2,1)S(1)}, u32[]{:S(2)}, u32[]{:S(2)}) collective-permute-start(bf16[2,64,256]{2,1,0:T(8,128)(2,1)S(1)} %get-tuple-element.95), channel_id=1, source_target_pairs={{0,2},{1,3},{2,4},{3,5},{4,6},{5,7},{6,0},{7,1},{8,10},{9,11},{10,... | collective-permute-start | bytes 196616 | tf_op jit(solution)/shard_map/side_mirror/ppermute | solution.py:404
  81.2 4.3 %collective-permute-start.15 = (bf16[2,64,256]{2,1,0:T(8,128)(2,1)S(1)}, bf16[2,64,256]{2,1,0:T(8,128)(2,1)S(1)}, u32[]{:S(2)}, u32[]{:S(2)}) collective-permute-start(bf16[2,64,256]{2,1,0:T(8,128)(2,1)S(1)} %get-tuple-element.96), channel_id=1, source_target_pairs={{0,6},{1,7},{2,0},{3,1},{4,2},{5,3},{6,4},{7,5},{8,14},{9,15},{10,... | collective-permute-start | bytes 196616 | tf_op jit(solution)/shard_map/side_mirror/ppermute | solution.py:404
  82.3 3.9 %collective-permute-start.17 = (bf16[8,2,64,256]{3,2,1,0:T(8,128)(2,1)S(1)}, bf16[8,2,64,256]{3,2,1,0:T(8,128)(2,1)S(1)}, u32[]{:S(2)}, u32[]{:S(2)}) collective-permute-start(bf16[8,2,64,256]{3,2,1,0:T(8,128)(2,1)S(1)} %collect.3.x_ref), channel_id=1, source_target_pairs={{0,8},{8,0},{1,9},{9,1},{2,10},{10,2},{3,11},{11,3},{4,12},{12,4},... | collective-permute-start | bytes 1572872 | tf_op jit(solution)/shard_map/side_mirror/ppermute | solution.py:409
  86.1 2.0 %collective-permute-start.16 = (bf16[8,2,64,256]{3,2,1,0:T(8,128)(2,1)S(1)}, bf16[8,2,64,256]{3,2,1,0:T(8,128)(2,1)S(1)}, u32[]{:S(2)}, u32[]{:S(2)}) collective-permute-start(bf16[8,2,64,256]{3,2,1,0:T(8,128)(2,1)S(1)} %collect.4), channel_id=1, source_target_pairs={{0,8},{8,0},{1,9},{9,1},{2,10},{10,2},{3,11},{11,3},{4,12},{12,4},... | collective-permute-start | bytes 1572872 | tf_op jit(solution)/shard_map/side_mirror/ppermute | solution.py:409
  91.8 2.7 %collective-permute-start.18 = (bf16[8,2,2,64,256]{4,3,2,1,0:T(8,128)(2,1)S(1)}, bf16[8,2,2,64,256]{4,3,2,1,0:T(8,128)(2,1)S(1)}, u32[]{:S(2)}, u32[]{:S(2)}) collective-permute-start(bf16[8,2,2,64,256]{4,3,2,1,0:T(8,128)(2,1)S(1)} %all-to-all-done.1.turned), channel_id=1, source_target_pairs={{0,8},{8,0},{1,9},{9,1},{2,10},{10,2},{3,11},{11,3},{4,12},{12,4},... | collective-permute-start | bytes 3145736 | tf_op jit(solution)/shard_map/ppermute | solution.py:409
  100.9 35.6 %all-to-all-start.2 = ((bf16[8,2,256,128]{3,2,1,0:T(8,128)(2,1)}), bf16[8,2,256,128]{3,2,1,0:T(8,128)(2,1)S(1)}, u32[]{:S(2)}, u32[]{:S(2)}) async-start(bf16[8,2,256,128]{3,2,1,0:T(8,128)(2,1)} %first_half.1), calls=%async_computation.2 | async-start | bytes 2097152 | tf_op jit(solution)/shard_map/partial/all_to_all | solution.py:463
  107.5 14.3 %collective-permute-start.19 = (bf16[1,256,128]{2,1,0:T(8,128)(2,1)S(1)}, bf16[1,256,128]{2,1,0:T(8,128)(2,1)S(1)}, u32[]{:S(2)}, u32[]{:S(2)}) collective-permute-start(bf16[1,256,128]{2,1,0:T(8,128)(2,1)S(1)} %get-tuple-element.109), channel_id=1, source_target_pairs={{0,3},{1,4},{2,5},{3,6},{4,7},{5,0},{6,1},{7,2},{8,11},{9,12},{10,... | collective-permute-start | bytes 196616 | tf_op jit(solution)/shard_map/side_partial/ppermute | solution.py:404
  109.0 12.8 %collective-permute-start.20 = (bf16[1,256,128]{2,1,0:T(8,128)(2,1)S(1)}, bf16[1,256,128]{2,1,0:T(8,128)(2,1)S(1)}, u32[]{:S(2)}, u32[]{:S(2)}) collective-permute-start(bf16[1,256,128]{2,1,0:T(8,128)(2,1)S(1)} %get-tuple-element.110), channel_id=1, source_target_pairs={{0,5},{1,6},{2,7},{3,0},{4,1},{5,2},{6,3},{7,4},{8,13},{9,14},{10,... | collective-permute-start | bytes 196616 | tf_op jit(solution)/shard_map/side_partial/ppermute | solution.py:404
  113.4 10.4 %collective-permute-start.21 = (bf16[1,256,128]{2,1,0:T(8,128)(2,1)S(1)}, bf16[1,256,128]{2,1,0:T(8,128)(2,1)S(1)}, u32[]{:S(2)}, u32[]{:S(2)}) collective-permute-start(bf16[1,256,128]{2,1,0:T(8,128)(2,1)S(1)} %get-tuple-element.111), channel_id=1, source_target_pairs={{0,1},{1,2},{2,3},{3,4},{4,5},{5,6},{6,7},{7,0},{8,9},{9,10},{10,1... | collective-permute-start | bytes 196616 | tf_op jit(solution)/shard_map/side_partial/ppermute | solution.py:404
  114.4 9.4 %collective-permute-start.22 = (bf16[1,256,128]{2,1,0:T(8,128)(2,1)S(1)}, bf16[1,256,128]{2,1,0:T(8,128)(2,1)S(1)}, u32[]{:S(2)}, u32[]{:S(2)}) collective-permute-start(bf16[1,256,128]{2,1,0:T(8,128)(2,1)S(1)} %get-tuple-element.112), channel_id=1, source_target_pairs={{0,7},{1,0},{2,1},{3,2},{4,3},{5,4},{6,5},{7,6},{8,15},{9,8},{10,9... | collective-permute-start | bytes 196616 | tf_op jit(solution)/shard_map/side_partial/ppermute | solution.py:404
  117.8 7.1 %collective-permute-start.23 = (bf16[1,256,128]{2,1,0:T(8,128)(2,1)S(1)}, bf16[1,256,128]{2,1,0:T(8,128)(2,1)S(1)}, u32[]{:S(2)}, u32[]{:S(2)}) collective-permute-start(bf16[1,256,128]{2,1,0:T(8,128)(2,1)S(1)} %get-tuple-element.113), channel_id=1, source_target_pairs={{0,4},{1,5},{2,6},{3,7},{4,0},{5,1},{6,2},{7,3},{8,12},{9,13},{10,... | collective-permute-start | bytes 196616 | tf_op jit(solution)/shard_map/side_partial/ppermute | solution.py:404
  121.8 4.3 %collective-permute-start.24 = (bf16[1,256,128]{2,1,0:T(8,128)(2,1)S(1)}, bf16[1,256,128]{2,1,0:T(8,128)(2,1)S(1)}, u32[]{:S(2)}, u32[]{:S(2)}) collective-permute-start(bf16[1,256,128]{2,1,0:T(8,128)(2,1)S(1)} %get-tuple-element.114), channel_id=1, source_target_pairs={{0,2},{1,3},{2,4},{3,5},{4,6},{5,7},{6,0},{7,1},{8,10},{9,11},{10,... | collective-permute-start | bytes 196616 | tf_op jit(solution)/shard_map/side_partial/ppermute | solution.py:404
  121.8 4.3 %collective-permute-start.25 = (bf16[1,256,128]{2,1,0:T(8,128)(2,1)S(1)}, bf16[1,256,128]{2,1,0:T(8,128)(2,1)S(1)}, u32[]{:S(2)}, u32[]{:S(2)}) collective-permute-start(bf16[1,256,128]{2,1,0:T(8,128)(2,1)S(1)} %get-tuple-element.115), channel_id=1, source_target_pairs={{0,6},{1,7},{2,0},{3,1},{4,2},{5,3},{6,4},{7,5},{8,14},{9,15},{10,... | collective-permute-start | bytes 196616 | tf_op jit(solution)/shard_map/side_partial/ppermute | solution.py:404
  126.7 2.0 %collective-permute-start.26 = (bf16[8,1,256,128]{3,2,1,0:T(8,128)(2,1)S(1)}, bf16[8,1,256,128]{3,2,1,0:T(8,128)(2,1)S(1)}, u32[]{:S(2)}, u32[]{:S(2)}) collective-permute-start(bf16[8,1,256,128]{3,2,1,0:T(8,128)(2,1)S(1)} %collect.5.t_ref), channel_id=1, source_target_pairs={{0,8},{8,0},{1,9},{9,1},{2,10},{10,2},{3,11},{11,3},{4,12},{12,4},... | collective-permute-start | bytes 1572872 | tf_op jit(solution)/shard_map/side_partial/ppermute | solution.py:409
  133.8 8.4 %collective-permute-start.27 = (bf16[8,64,256]{2,1,0:T(8,128)(2,1)S(1)}, bf16[8,64,256]{2,1,0:T(8,128)(2,1)S(1)}, u32[]{:S(2)}, u32[]{:S(2)}) collective-permute-start(bf16[8,64,256]{2,1,0:T(8,128)(2,1)S(1)} %get-tuple-element.118), channel_id=1, source_target_pairs={{0,16},{16,0},{1,17},{17,1},{2,18},{18,2},{3,19},{19,3},{4,20},{20... | collective-permute-start | bytes 786440 | tf_op jit(solution)/shard_map/ppermute | solution.py:409
  142.2 28.1 %all-to-all-start.3 = ((bf16[16,2,64,256]{3,2,1,0:T(8,128)(2,1)}), bf16[16,2,64,256]{3,2,1,0:T(8,128)(2,1)S(1)}, u32[]{:S(2)}, u32[]{:S(2)}) async-start(bf16[16,2,64,256]{3,2,1,0:T(8,128)(2,1)} %bitcast.13), calls=%async_computation.3 | async-start | bytes 2097152 | tf_op jit(solution)/shard_map/panels_out/all_to_all | solution.py:477
  150.1 14.8 %collective-permute-start.28 = (bf16[2,64,256]{2,1,0:T(8,128)(2,1)S(1)}, bf16[2,64,256]{2,1,0:T(8,128)(2,1)S(1)}, u32[]{:S(2)}, u32[]{:S(2)}) collective-permute-start(bf16[2,64,256]{2,1,0:T(8,128)(2,1)S(1)} %get-tuple-element.123), channel_id=1, source_target_pairs={{0,128},{32,160},{64,192},{96,224},{128,0},{160,32},{192,64},{224,... | collective-permute-start | bytes 196616 | tf_op jit(solution)/shard_map/side_out/ppermute | solution.py:404
  155.7 9.7 %collective-permute-start.29 = (bf16[2,64,256]{2,1,0:T(8,128)(2,1)S(1)}, bf16[2,64,256]{2,1,0:T(8,128)(2,1)S(1)}, u32[]{:S(2)}, u32[]{:S(2)}) collective-permute-start(bf16[2,64,256]{2,1,0:T(8,128)(2,1)S(1)} %get-tuple-element.124), channel_id=1, source_target_pairs={{0,96},{32,128},{64,160},{96,192},{128,224},{160,0},{192,32},{224,... | collective-permute-start | bytes 196616 | tf_op jit(solution)/shard_map/side_out/ppermute | solution.py:404
  156.2 11.9 %collective-permute-start.30 = (bf16[2,64,256]{2,1,0:T(8,128)(2,1)S(1)}, bf16[2,64,256]{2,1,0:T(8,128)(2,1)S(1)}, u32[]{:S(2)}, u32[]{:S(2)}) collective-permute-start(bf16[2,64,256]{2,1,0:T(8,128)(2,1)S(1)} %get-tuple-element.125), channel_id=1, source_target_pairs={{0,160},{32,192},{64,224},{96,0},{128,32},{160,64},{192,96},{224,1... | collective-permute-start | bytes 196616 | tf_op jit(solution)/shard_map/side_out/ppermute | solution.py:404
  160.7 7.4 %collective-permute-start.31 = (bf16[2,64,256]{2,1,0:T(8,128)(2,1)S(1)}, bf16[2,64,256]{2,1,0:T(8,128)(2,1)S(1)}, u32[]{:S(2)}, u32[]{:S(2)}) collective-permute-start(bf16[2,64,256]{2,1,0:T(8,128)(2,1)S(1)} %get-tuple-element.126), channel_id=1, source_target_pairs={{0,64},{32,96},{64,128},{96,160},{128,192},{160,224},{192,0},{224,... | collective-permute-start | bytes 196616 | tf_op jit(solution)/shard_map/side_out/ppermute | solution.py:404
  161.3 6.9 %collective-permute-start.32 = (bf16[2,64,256]{2,1,0:T(8,128)(2,1)S(1)}, bf16[2,64,256]{2,1,0:T(8,128)(2,1)S(1)}, u32[]{:S(2)}, u32[]{:S(2)}) collective-permute-start(bf16[2,64,256]{2,1,0:T(8,128)(2,1)S(1)} %get-tuple-element.127), channel_id=1, source_target_pairs={{0,192},{32,224},{64,0},{96,32},{128,64},{160,96},{192,128},{224,1... | collective-permute-start | bytes 196616 | tf_op jit(solution)/shard_map/side_out/ppermute | solution.py:404
  164.9 5.5 %collective-permute-start.33 = (bf16[2,64,256]{2,1,0:T(8,128)(2,1)S(1)}, bf16[2,64,256]{2,1,0:T(8,128)(2,1)S(1)}, u32[]{:S(2)}, u32[]{:S(2)}) collective-permute-start(bf16[2,64,256]{2,1,0:T(8,128)(2,1)S(1)} %get-tuple-element.128), channel_id=1, source_target_pairs={{0,32},{32,64},{64,96},{96,128},{128,160},{160,192},{192,224},{224... | collective-permute-start | bytes 196616 | tf_op jit(solution)/shard_map/side_out/ppermute | solution.py:404
  165.4 4.9 %collective-permute-start.34 = (bf16[2,64,256]{2,1,0:T(8,128)(2,1)S(1)}, bf16[2,64,256]{2,1,0:T(8,128)(2,1)S(1)}, u32[]{:S(2)}, u32[]{:S(2)}) collective-permute-start(bf16[2,64,256]{2,1,0:T(8,128)(2,1)S(1)} %get-tuple-element.129), channel_id=1, source_target_pairs={{0,224},{32,0},{64,32},{96,64},{128,96},{160,128},{192,160},{224,1... | collective-permute-start | bytes 196616 | tf_op jit(solution)/shard_map/side_out/ppermute | solution.py:404

commit v5 on v4

--- a/solution.py
+++ b/solution.py
@@ -20,7 +20,6 @@
 
 
 ORDER = {AT_Z: (0, 4, 3, 5, 2, 6, 1, 7), AT_C: (0, 3, 5, 1, 7, 4, 2, 6)}
-EARLY = 6
 STEPS = 4
 HBM = pl.BlockSpec(memory_space=pltpu.HBM)
 
@@ -373,7 +372,11 @@
 def finish_kernel(place, *refs):
     main_ref, out_hbm, sems = refs[BLOCKS:]
     main = main_ref.shape[0]
-    copies = [pltpu.make_async_copy(main_ref, out_hbm.at[pl.ds(0, main)], sems.at[BLOCKS * YLO])]
+    share = main // STEPS
+    copies = []
+    for g in range(STEPS):
+        part = pl.ds(g * share, share)
+        copies.append(pltpu.make_async_copy(main_ref.at[part], out_hbm.at[part], sems.at[BLOCKS * YLO + g]))
     for d in range(BLOCKS):
         for y in range(YLO):
             to = main + y * BLOCKS + (place[AT_Z] + BLOCKS - ORDER[AT_Z][d]) % BLOCKS
@@ -392,7 +395,7 @@
         out_shape=jax.ShapeDtypeStruct((pairs + YLO * BLOCKS, rows, block), BF16),
         in_specs=[pl.BlockSpec(memory_space=pltpu.SMEM)] + [vmem] * (BLOCKS + 1),
         out_specs=HBM,
-        scratch_shapes=[pltpu.SemaphoreType.DMA((BLOCKS * YLO + 1,))],
+        scratch_shapes=[pltpu.SemaphoreType.DMA((BLOCKS * YLO + STEPS,))],
         compiler_params=SMALL,
         name="finish",
     )(place, *parts, main)
@@ -437,8 +440,8 @@
         own = own.reshape(COLS, YLO, depth, rows, block)
     with jax.named_scope("side_in"):
         parts = rotate(AT_Z, join_and_spread(place, keep, got), "z")
-    own, early, picked = together((own, parts[:EARLY], picked))
-    side_own = collect(AT_Z, place, list(early) + parts[EARLY:])
+        side_own = collect(AT_Z, place, parts)
+    own, side_own, picked = together((own, side_own, picked))
 
     with jax.named_scope("mirror"):
         own_low = lax.all_to_all(own, "z", 0, 0, tiled=True)

time: 173 us -> 152 us (0.88)
  waiting for transfers between devices: 39.7 us -> 20.1 us
    ppermute x28, waiting for transfers between devices: 32 us -> 10.2 us  [rotate(): lax.ppermute(part, axes, [(i, (i + d) % BLOCKS) for i in range(BLOCKS)])]
    all_to_all x1, waiting for transfers between devices: 0.01 us -> 2.01 us  [per_device(): own_low = lax.all_to_all(own, 'z', 0, 0, tiled=True)]
  transfers between devices with their start and end apart: 39 -> 39, of which waited for: 18 -> 18; matrix products, arithmetic and copies ran while one was open for 0% -> 0% of each run, Pallas kernels for 14% -> 16%
where the time goes in v5:
time: 152 us; the launch traced here: 151 us
  starting transfers between devices  97 us (64%)
  Pallas kernels  32.8 us (22%)
  waiting for transfers between devices  20.1 us (13%)
    ppermute x28, starting transfers between devices, rotate(): lax.ppermute(part, axes, [(i, (i + d) % BLOCKS) for i in range(BLOCKS)])  68.7 us
    ppermute x28, waiting for transfers between devices, rotate(): lax.ppermute(part, axes, [(i, (i + d) % BLOCKS) for i in range(BLOCKS)])  10.2 us
    pallas_call x2, Pallas kernels, first_half(): pl.pallas_call(functools.partial(first_kernel, index), out_shape=[jax.Sha...  10.1 us
    all_to_all x1, starting transfers between devices, per_device(): result = lax.all_to_all(result, PLANE, 0, 0, tiled=True)  7.34 us
    all_to_all x1, starting transfers between devices, per_device(): own = lax.all_to_all(own, PLANE, 0, 0, tiled=True)  7.2 us
    ppermute x7, waiting for transfers between devices, swap(): return lax.ppermute(value, axis, [(0, 1), (1, 0)])  6.99 us
    pallas_call x1, Pallas kernels, pick_columns(): pl.pallas_call(pick_kernel, out_shape=[pltpu.HBM((size, width), BF16), pl...  6.85 us
    all_to_all x1, starting transfers between devices, per_device(): partial_value = lax.all_to_all(partial_value, 'z', 0, 0, tiled=True)  5.75 us
  transfers between devices with their start and end apart: 39, of which 18 were waited for; matrix products, arithmetic and copies ran while one was open for 0% of the time, Pallas kernels for 16%

profile of v5, /device:TPU:2, one launch (start us, length us, event | category | flops | bytes accessed | tf_op | source)
XLA Modules:
  0.0 151.4 jit_solution(7073053655214128395)
XLA Ops:
  0.0 1.1 slice.3
  1.1 1.7 %collective-permute-start = (bf16[8,64,256]{2,1,0:T(8,128)(2,1)S(1)}, bf16[8,64,256]{2,1,0:T(8,128)(2,1)S(1)}, u32[]{:S(2)}, u32[]{:S(2)}) collective-permute-start(bf16[8,64,256]{2,1,0:T(8,128)(2,1)S(1)} %get-tuple-element.122), channel_id=1, source_target_pairs={{0,16},{16,0},{1,17},{17,1},{2,18},{18,2},{3,19},{19,3},{4,20},{20... | collective-permute-start | bytes 786440 | tf_op jit(solution)/shard_map/side_in/ppermute | solution.py:412
  2.9 6.9 %pick_columns.1 = (bf16[2048,1024]{1,0:T(8,128)(2,1)}, bf16[32,64,256]{2,1,0:T(8,128)(2,1)}) custom-call(s32[4]{0:T(128)S(1)} %pad_add_fusion.place, bf16[2048,2048]{1,0:T(8,128)(2,1)} %c_hbm.3, bf16[48,64,256]{2,1,0:T(8,128)(2,1)} %panel_hbm.1), custom_call_target="tpu_custom_call" | custom-call | tf_op jit(solution)/shard_map/pick_columns/pallas_call | solution.py:139
  9.8 7.2 %all-to-all-start = ((bf16[16,2,64,256]{3,2,1,0:T(8,128)(2,1)}), bf16[16,2,64,256]{3,2,1,0:T(8,128)(2,1)}, u32[]{:S(2)}, u32[]{:S(2)}) async-start(bf16[16,2,64,256]{3,2,1,0:T(8,128)(2,1)} %bitcast.23), calls=%async_computation | async-start | bytes 2097152 | tf_op jit(solution)/shard_map/panels_in/all_to_all | solution.py:439
  16.9 0.6 join_and_spread.2
  17.5 7.3 %collective-permute-start.1 = (bf16[2,64,256]{2,1,0:T(8,128)(2,1)S(1)}, bf16[2,64,256]{2,1,0:T(8,128)(2,1)S(1)}, u32[]{:S(2)}, u32[]{:S(2)}) collective-permute-start(bf16[2,64,256]{2,1,0:T(8,128)(2,1)S(1)} %get-tuple-element.69), channel_id=1, source_target_pairs={{0,128},{32,160},{64,192},{96,224},{128,0},{160,32},{192,64},{224,... | collective-permute-start | bytes 196616 | tf_op jit(solution)/shard_map/side_in/ppermute | solution.py:407
  24.8 1.9 %collective-permute-start.2 = (bf16[2,64,256]{2,1,0:T(8,128)(2,1)S(1)}, bf16[2,64,256]{2,1,0:T(8,128)(2,1)S(1)}, u32[]{:S(2)}, u32[]{:S(2)}) collective-permute-start(bf16[2,64,256]{2,1,0:T(8,128)(2,1)S(1)} %get-tuple-element.70), channel_id=1, source_target_pairs={{0,96},{32,128},{64,160},{96,192},{128,224},{160,0},{192,32},{224,... | collective-permute-start | bytes 196616 | tf_op jit(solution)/shard_map/side_in/ppermute | solution.py:407
  26.8 3.1 %collective-permute-start.3 = (bf16[2,64,256]{2,1,0:T(8,128)(2,1)S(1)}, bf16[2,64,256]{2,1,0:T(8,128)(2,1)S(1)}, u32[]{:S(2)}, u32[]{:S(2)}) collective-permute-start(bf16[2,64,256]{2,1,0:T(8,128)(2,1)S(1)} %get-tuple-element.71), channel_id=1, source_target_pairs={{0,160},{32,192},{64,224},{96,0},{128,32},{160,64},{192,96},{224,1... | collective-permute-start | bytes 196616 | tf_op jit(solution)/shard_map/side_in/ppermute | solution.py:407
  29.9 1.5 collective-permute-start.4
  31.3 2.7 %collective-permute-start.5 = (bf16[2,64,256]{2,1,0:T(8,128)(2,1)S(1)}, bf16[2,64,256]{2,1,0:T(8,128)(2,1)S(1)}, u32[]{:S(2)}, u32[]{:S(2)}) collective-permute-start(bf16[2,64,256]{2,1,0:T(8,128)(2,1)S(1)} %get-tuple-element.73), channel_id=1, source_target_pairs={{0,192},{32,224},{64,0},{96,32},{128,64},{160,96},{192,128},{224,1... | collective-permute-start | bytes 196616 | tf_op jit(solution)/shard_map/side_in/ppermute | solution.py:407
  34.0 1.0 collective-permute-start.6
  35.0 0.1 collective-permute-done.2.refs_2_
  35.1 2.1 %collective-permute-start.7 = (bf16[2,64,256]{2,1,0:T(8,128)(2,1)S(1)}, bf16[2,64,256]{2,1,0:T(8,128)(2,1)S(1)}, u32[]{:S(2)}, u32[]{:S(2)}) collective-permute-start(bf16[2,64,256]{2,1,0:T(8,128)(2,1)S(1)} %get-tuple-element.75), channel_id=1, source_target_pairs={{0,224},{32,0},{64,32},{96,64},{128,96},{160,128},{192,160},{224,1... | collective-permute-start | bytes 196616 | tf_op jit(solution)/shard_map/side_in/ppermute | solution.py:407
  37.2 0.7 collective-permute-done.5.refs_5_
  38.0 1.5 %collective-permute-done.6.refs_6_ = bf16[2,64,256]{2,1,0:T(8,128)(2,1)S(1)} collective-permute-done((bf16[2,64,256]{2,1,0:T(8,128)(2,1)S(1)}, bf16[2,64,256]{2,1,0:T(8,128)(2,1)S(1)}, u32[]{:S(2)}, u32[]{:S(2)}) %collective-permute-start.6) | collective-permute-done | bytes 65568 | tf_op jit(solution)/shard_map/side_in/ppermute | solution.py:407
  39.5 0.6 collect.3.x_ref
  40.1 4.5 %all-to-all-start.1 = ((bf16[8,2,2,64,256]{4,3,2,1,0:T(8,128)(2,1)}), bf16[8,2,2,64,256]{4,3,2,1,0:T(8,128)(2,1)S(1)}, u32[]{:S(2)}, u32[]{:S(2)}) async-start(bf16[8,2,2,64,256]{4,3,2,1,0:T(8,128)(2,1)} %bitcast.8.direct), calls=%async_computation.1 | async-start | bytes 2097152 | tf_op jit(solution)/shard_map/mirror/all_to_all | solution.py:447
  44.6 0.6 spread.1
  45.2 3.9 %collective-permute-start.9 = (bf16[2,64,256]{2,1,0:T(8,128)(2,1)S(1)}, bf16[2,64,256]{2,1,0:T(8,128)(2,1)S(1)}, u32[]{:S(2)}, u32[]{:S(2)}) collective-permute-start(bf16[2,64,256]{2,1,0:T(8,128)(2,1)S(1)} %get-tuple-element.80), channel_id=1, source_target_pairs={{0,3},{1,4},{2,5},{3,6},{4,7},{5,0},{6,1},{7,2},{8,11},{9,12},{10,... | collective-permute-start | bytes 196616 | tf_op jit(solution)/shard_map/side_mirror/ppermute | solution.py:407
  49.2 2.1 %collective-permute-start.10 = (bf16[2,64,256]{2,1,0:T(8,128)(2,1)S(1)}, bf16[2,64,256]{2,1,0:T(8,128)(2,1)S(1)}, u32[]{:S(2)}, u32[]{:S(2)}) collective-permute-start(bf16[2,64,256]{2,1,0:T(8,128)(2,1)S(1)} %get-tuple-element.81), channel_id=1, source_target_pairs={{0,5},{1,6},{2,7},{3,0},{4,1},{5,2},{6,3},{7,4},{8,13},{9,14},{10,... | collective-permute-start | bytes 196616 | tf_op jit(solution)/shard_map/side_mirror/ppermute | solution.py:407
  51.2 1.5 collective-permute-start.11
  52.7 3.0 %collective-permute-start.12 = (bf16[2,64,256]{2,1,0:T(8,128)(2,1)S(1)}, bf16[2,64,256]{2,1,0:T(8,128)(2,1)S(1)}, u32[]{:S(2)}, u32[]{:S(2)}) collective-permute-start(bf16[2,64,256]{2,1,0:T(8,128)(2,1)S(1)} %get-tuple-element.83), channel_id=1, source_target_pairs={{0,7},{1,0},{2,1},{3,2},{4,3},{5,4},{6,5},{7,6},{8,15},{9,8},{10,9... | collective-permute-start | bytes 196616 | tf_op jit(solution)/shard_map/side_mirror/ppermute | solution.py:407
  55.7 2.1 %collective-permute-start.13 = (bf16[2,64,256]{2,1,0:T(8,128)(2,1)S(1)}, bf16[2,64,256]{2,1,0:T(8,128)(2,1)S(1)}, u32[]{:S(2)}, u32[]{:S(2)}) collective-permute-start(bf16[2,64,256]{2,1,0:T(8,128)(2,1)S(1)} %get-tuple-element.84), channel_id=1, source_target_pairs={{0,4},{1,5},{2,6},{3,7},{4,0},{5,1},{6,2},{7,3},{8,12},{9,13},{10,... | collective-permute-start | bytes 196616 | tf_op jit(solution)/shard_map/side_mirror/ppermute | solution.py:407
  57.7 1.0 collective-permute-start.14
  58.7 1.0 collective-permute-start.15
  59.8 2.1 %collective-permute-done.13.refs_5_ = bf16[2,64,256]{2,1,0:T(8,128)(2,1)S(1)} collective-permute-done((bf16[2,64,256]{2,1,0:T(8,128)(2,1)S(1)}, bf16[2,64,256]{2,1,0:T(8,128)(2,1)S(1)}, u32[]{:S(2)}, u32[]{:S(2)}) %collective-permute-start.13) | collective-permute-done | bytes 65568 | tf_op jit(solution)/shard_map/side_mirror/ppermute | solution.py:407
  61.9 0.2 collective-permute-done.14.refs_6_
  62.1 0.9 collective-permute-done.15.refs_7_
  63.0 0.6 collect.4
  63.6 0.1 collective-permute-start.16
  63.7 1.9 %collective-permute-done.16 = bf16[8,2,64,256]{3,2,1,0:T(8,128)(2,1)S(1)} collective-permute-done((bf16[8,2,64,256]{3,2,1,0:T(8,128)(2,1)S(1)}, bf16[8,2,64,256]{3,2,1,0:T(8,128)(2,1)S(1)}, u32[]{:S(2)}, u32[]{:S(2)}) %collective-permute-start.16) | collective-permute-done | bytes 524320 | tf_op jit(solution)/shard_map/side_mirror/ppermute | solution.py:412
  65.6 3.7 %first_half_side.1 = (bf16[1,256,128]{2,1,0:T(8,128)(2,1)S(1)}, bf16[1,256,128]{2,1,0:T(8,128)(2,1)S(1)}, bf16[1,256,128]{2,1,0:T(8,128)(2,1)S(1)}, bf16[1,256,1...) custom-call(s32[4]{0:T(128)S(1)} %pad_add_fusion.place, ...), custom_call_target="tpu_custom_call" | custom-call | tf_op jit(solution)/shard_map/side_mirror/first_half_side/pallas_call | solution.py:215
  69.3 2.0 %all-to-all-done.1.turned = bf16[8,2,2,64,256]{4,3,2,1,0:T(8,128)(2,1)S(1)} async-done(((bf16[8,2,2,64,256]{4,3,2,1,0:T(8,128)(2,1)}), bf16[8,2,2,64,256]{4,3,2,1,0:T(8,128)(2,1)S(1)}, u32[]{:S(2)}, u32[]{:S(2)}) %all-to-all-start.1) | async-done | bytes 1048608 | tf_op jit(solution)/shard_map/mirror/all_to_all | solution.py:447
  71.4 2.7 %collective-permute-done.18.turned_other = bf16[8,2,2,64,256]{4,3,2,1,0:T(8,128)(2,1)S(1)} collective-permute-done((bf16[8,2,2,64,256]{4,3,2,1,0:T(8,128)(2,1)S(1)}, bf16[8,2,2,64,256]{4,3,2,1,0:T(8,128)(2,1)S(1)}, u32[]{:S(2)}, u32[]{:S(2)}) %collective-permute-start.18) | collective-permute-done | bytes 1048608 | tf_op jit(solution)/shard_map/ppermute | solution.py:412
  74.0 6.3 %first_half.1 = bf16[8,2,256,128]{3,2,1,0:T(8,128)(2,1)} custom-call(s32[4]{0:T(128)S(1)} %pad_add_fusion.place, bf16[8,2,2,64,256]{4,3,2,1,0:T(8,128)(2,1)} %bitcast.8.direct, bf16[8,2,2,64,256]{4,3,2,1,0:T(8,128)(2,1)S(1)} %collective-permute-done.8.direct_other, bf16[8,2,2,64,256]{4,3,2,1,0:T(8,128)(2,1)S(1)} %all-to-all-done.1.turned, ...), custom_call_target="tpu_custom_call" | custom-call | tf_op jit(solution)/shard_map/first_half/pallas_call | solution.py:215
  80.4 5.7 %all-to-all-start.2 = ((bf16[8,2,256,128]{3,2,1,0:T(8,128)(2,1)}), bf16[8,2,256,128]{3,2,1,0:T(8,128)(2,1)S(1)}, u32[]{:S(2)}, u32[]{:S(2)}) async-start(bf16[8,2,256,128]{3,2,1,0:T(8,128)(2,1)} %first_half.1), calls=%async_computation.2 | async-start | bytes 2097152 | tf_op jit(solution)/shard_map/partial/all_to_all | solution.py:466
  86.1 1.8 %collective-permute-start.19 = (bf16[1,256,128]{2,1,0:T(8,128)(2,1)S(1)}, bf16[1,256,128]{2,1,0:T(8,128)(2,1)S(1)}, u32[]{:S(2)}, u32[]{:S(2)}) collective-permute-start(bf16[1,256,128]{2,1,0:T(8,128)(2,1)S(1)} %get-tuple-element.99), channel_id=1, source_target_pairs={{0,3},{1,4},{2,5},{3,6},{4,7},{5,0},{6,1},{7,2},{8,11},{9,12},{10,... | collective-permute-start | bytes 196616 | tf_op jit(solution)/shard_map/side_partial/ppermute | solution.py:407
  87.9 4.1 %collective-permute-start.20 = (bf16[1,256,128]{2,1,0:T(8,128)(2,1)S(1)}, bf16[1,256,128]{2,1,0:T(8,128)(2,1)S(1)}, u32[]{:S(2)}, u32[]{:S(2)}) collective-permute-start(bf16[1,256,128]{2,1,0:T(8,128)(2,1)S(1)} %get-tuple-element.100), channel_id=1, source_target_pairs={{0,5},{1,6},{2,7},{3,0},{4,1},{5,2},{6,3},{7,4},{8,13},{9,14},{10,... | collective-permute-start | bytes 196616 | tf_op jit(solution)/shard_map/side_partial/ppermute | solution.py:407
  92.0 1.4 collective-permute-start.21
  93.4 3.1 %collective-permute-start.22 = (bf16[1,256,128]{2,1,0:T(8,128)(2,1)S(1)}, bf16[1,256,128]{2,1,0:T(8,128)(2,1)S(1)}, u32[]{:S(2)}, u32[]{:S(2)}) collective-permute-start(bf16[1,256,128]{2,1,0:T(8,128)(2,1)S(1)} %get-tuple-element.102), channel_id=1, source_target_pairs={{0,7},{1,0},{2,1},{3,2},{4,3},{5,4},{6,5},{7,6},{8,15},{9,8},{10,9... | collective-permute-start | bytes 196616 | tf_op jit(solution)/shard_map/side_partial/ppermute | solution.py:407
  96.5 4.3 %collective-permute-start.23 = (bf16[1,256,128]{2,1,0:T(8,128)(2,1)S(1)}, bf16[1,256,128]{2,1,0:T(8,128)(2,1)S(1)}, u32[]{:S(2)}, u32[]{:S(2)}) collective-permute-start(bf16[1,256,128]{2,1,0:T(8,128)(2,1)S(1)} %get-tuple-element.103), channel_id=1, source_target_pairs={{0,4},{1,5},{2,6},{3,7},{4,0},{5,1},{6,2},{7,3},{8,12},{9,13},{10,... | collective-permute-start | bytes 196616 | tf_op jit(solution)/shard_map/side_partial/ppermute | solution.py:407
  100.8 2.0 %collective-permute-start.25 = (bf16[1,256,128]{2,1,0:T(8,128)(2,1)S(1)}, bf16[1,256,128]{2,1,0:T(8,128)(2,1)S(1)}, u32[]{:S(2)}, u32[]{:S(2)}) collective-permute-start(bf16[1,256,128]{2,1,0:T(8,128)(2,1)S(1)} %get-tuple-element.105), channel_id=1, source_target_pairs={{0,6},{1,7},{2,0},{3,1},{4,2},{5,3},{6,4},{7,5},{8,14},{9,15},{10,... | collective-permute-start | bytes 196616 | tf_op jit(solution)/shard_map/side_partial/ppermute | solution.py:407
  102.9 1.1 collective-permute-done.23.refs_5_
  104.0 1.1 collective-permute-done.24.refs_6_
  105.1 0.1 collective-permute-done.25.refs_7_
  105.2 0.6 collect.5.t_ref
  105.8 0.1 collective-permute-start.26
  105.9 1.9 %collective-permute-done.26.other_ref = bf16[8,1,256,128]{3,2,1,0:T(8,128)(2,1)S(1)} collective-permute-done((bf16[8,1,256,128]{3,2,1,0:T(8,128)(2,1)S(1)}, bf16[8,1,256,128]{3,2,1,0:T(8,128)(2,1)S(1)}, u32[]{:S(2)}, u32[]{:S(2)}) %collective-permute-start.26) | collective-permute-done | bytes 524320 | tf_op jit(solution)/shard_map/side_partial/ppermute | solution.py:412
  107.8 5.0 %second_half_side.1 = (bf16[8,64,256]{2,1,0:T(8,128)(2,1)S(1)}, bf16[8,64,256]{2,1,0:T(8,128)(2,1)S(1)}) custom-call(s32[4]{0:T(128)S(1)} %pad_add_fusion.place, bf16[8,1,256,128]{3,2,1,0:T(8,128)(2,1)S(1)} %collect.5.t_ref, bf16[8,1,256,128]{3,2,1,0:T(8,128)(2,1)S(1)} %collective-permute-done.26.other_ref, bf16[2048,1024]{1,0:T(8,128)(2,1)} %get-tuple-element.87.c_hbm), custom_call_target="tpu_custom_call" | custom-call | tf_op jit(solution)/shard_map/side_partial/second_half_side/pallas_call | solution.py:304
  112.8 1.5 %collective-permute-start.27 = (bf16[8,64,256]{2,1,0:T(8,128)(2,1)S(1)}, bf16[8,64,256]{2,1,0:T(8,128)(2,1)S(1)}, u32[]{:S(2)}, u32[]{:S(2)}) collective-permute-start(bf16[8,64,256]{2,1,0:T(8,128)(2,1)S(1)} %get-tuple-element.108), channel_id=1, source_target_pairs={{0,16},{16,0},{1,17},{17,1},{2,18},{18,2},{3,19},{19,3},{4,20},{20... | collective-permute-start | bytes 786440 | tf_op jit(solution)/shard_map/ppermute | solution.py:412
  114.3 0.9 all-to-all-done.2.t_ref
  115.2 5.5 %second_half.1 = bf16[8,2,2,64,256]{4,3,2,1,0:T(8,128)(2,1)} custom-call(bf16[8,2,256,128]{3,2,1,0:T(8,128)(2,1)S(1)} %all-to-all-done.2.t_ref, bf16[2048,2048]{1,0:T(8,128)(2,1)} %c_hbm.3), custom_call_target="tpu_custom_call" | custom-call | tf_op jit(solution)/shard_map/second_half/pallas_call | solution.py:257
  120.7 0.5 collective-permute-done.27.got
  121.2 7.3 %all-to-all-start.3 = ((bf16[16,2,64,256]{3,2,1,0:T(8,128)(2,1)}), bf16[16,2,64,256]{3,2,1,0:T(8,128)(2,1)S(1)}, u32[]{:S(2)}, u32[]{:S(2)}) async-start(bf16[16,2,64,256]{3,2,1,0:T(8,128)(2,1)} %bitcast.13), calls=%async_computation.3 | async-start | bytes 2097152 | tf_op jit(solution)/shard_map/panels_out/all_to_all | solution.py:480
  128.6 0.6 join_and_spread.3
  129.2 5.5 %collective-permute-start.28 = (bf16[2,64,256]{2,1,0:T(8,128)(2,1)S(1)}, bf16[2,64,256]{2,1,0:T(8,128)(2,1)S(1)}, u32[]{:S(2)}, u32[]{:S(2)}) collective-permute-start(bf16[2,64,256]{2,1,0:T(8,128)(2,1)S(1)} %get-tuple-element.113), channel_id=1, source_target_pairs={{0,128},{32,160},{64,192},{96,224},{128,0},{160,32},{192,64},{224,... | collective-permute-start | bytes 196616 | tf_op jit(solution)/shard_map/side_out/ppermute | solution.py:407
  134.7 0.6 collective-permute-start.29
  135.3 4.5 %collective-permute-start.30 = (bf16[2,64,256]{2,1,0:T(8,128)(2,1)S(1)}, bf16[2,64,256]{2,1,0:T(8,128)(2,1)S(1)}, u32[]{:S(2)}, u32[]{:S(2)}) collective-permute-start(bf16[2,64,256]{2,1,0:T(8,128)(2,1)S(1)} %get-tuple-element.115), channel_id=1, source_target_pairs={{0,160},{32,192},{64,224},{96,0},{128,32},{160,64},{192,96},{224,1... | collective-permute-start | bytes 196616 | tf_op jit(solution)/shard_map/side_out/ppermute | solution.py:407
  139.7 0.6 collective-permute-start.31
  140.3 3.6 %collective-permute-start.32 = (bf16[2,64,256]{2,1,0:T(8,128)(2,1)S(1)}, bf16[2,64,256]{2,1,0:T(8,128)(2,1)S(1)}, u32[]{:S(2)}, u32[]{:S(2)}) collective-permute-start(bf16[2,64,256]{2,1,0:T(8,128)(2,1)S(1)} %get-tuple-element.117), channel_id=1, source_target_pairs={{0,192},{32,224},{64,0},{96,32},{128,64},{160,96},{192,128},{224,1... | collective-permute-start | bytes 196616 | tf_op jit(solution)/shard_map/side_out/ppermute | solution.py:407
  143.9 0.6 collective-permute-start.33
  144.5 2.6 %collective-permute-start.34 = (bf16[2,64,256]{2,1,0:T(8,128)(2,1)S(1)}, bf16[2,64,256]{2,1,0:T(8,128)(2,1)S(1)}, u32[]{:S(2)}, u32[]{:S(2)}) collective-permute-start(bf16[2,64,256]{2,1,0:T(8,128)(2,1)S(1)} %get-tuple-element.119), channel_id=1, source_target_pairs={{0,224},{32,0},{64,32},{96,64},{128,96},{160,128},{192,160},{224,1... | collective-permute-start | bytes 196616 | tf_op jit(solution)/shard_map/side_out/ppermute | solution.py:407
  147.2 2.2 %collective-permute-done.33.refs_6_ = bf16[2,64,256]{2,1,0:T(8,128)(2,1)S(1)} collective-permute-done((bf16[2,64,256]{2,1,0:T(8,128)(2,1)S(1)}, bf16[2,64,256]{2,1,0:T(8,128)(2,1)S(1)}, u32[]{:S(2)}, u32[]{:S(2)}) %collective-permute-start.33) | collective-permute-done | bytes 65568 | tf_op jit(solution)/shard_map/side_out/ppermute | solution.py:407
  149.4 1.8 %finish.1 = bf16[48,64,256]{2,1,0:T(8,128)(2,1)} custom-call(s32[4]{0:T(128)S(1)} %pad_add_fusion.place, bf16[2,64,256]{2,1,0:T(8,128)(2,1)S(1)} %get-tuple-element.112.refs_0_, bf16[2,64,256]{2,1,0:T(8,128)(2,1)S(1)} %collective-permute-done.28.refs_1_, bf16[2,64,256]{2,1,0:T(8,128)(2,1)S(1)} %collective-permute-done.29.refs_2_, ...), custom_call_target="tpu_custom_call" | custom-call | tf_op jit(solution)/shard_map/finish/pallas_call | solution.py:393
  (29 shorter events, 0.3 us)
Async XLA Ops:
  1.1 8.6 %collective-permute-start = (bf16[8,64,256]{2,1,0:T(8,128)(2,1)S(1)}, bf16[8,64,256]{2,1,0:T(8,128)(2,1)S(1)}, u32[]{:S(2)}, u32[]{:S(2)}) collective-permute-start(bf16[8,64,256]{2,1,0:T(8,128)(2,1)S(1)} %get-tuple-element.122), channel_id=1, source_target_pairs={{0,16},{16,0},{1,17},{17,1},{2,18},{18,2},{3,19},{19,3},{4,20},{20... | collective-permute-start | bytes 786440 | tf_op jit(solution)/shard_map/side_in/ppermute | solution.py:412
  9.8 30.3 %all-to-all-start = ((bf16[16,2,64,256]{3,2,1,0:T(8,128)(2,1)}), bf16[16,2,64,256]{3,2,1,0:T(8,128)(2,1)}, u32[]{:S(2)}, u32[]{:S(2)}) async-start(bf16[16,2,64,256]{3,2,1,0:T(8,128)(2,1)} %bitcast.23), calls=%async_computation | async-start | bytes 2097152 | tf_op jit(solution)/shard_map/panels_in/all_to_all | solution.py:439
  17.5 16.5 %collective-permute-start.1 = (bf16[2,64,256]{2,1,0:T(8,128)(2,1)S(1)}, bf16[2,64,256]{2,1,0:T(8,128)(2,1)S(1)}, u32[]{:S(2)}, u32[]{:S(2)}) collective-permute-start(bf16[2,64,256]{2,1,0:T(8,128)(2,1)S(1)} %get-tuple-element.69), channel_id=1, source_target_pairs={{0,128},{32,160},{64,192},{96,224},{128,0},{160,32},{192,64},{224,... | collective-permute-start | bytes 196616 | tf_op jit(solution)/shard_map/side_in/ppermute | solution.py:407
  24.8 10.3 %collective-permute-start.2 = (bf16[2,64,256]{2,1,0:T(8,128)(2,1)S(1)}, bf16[2,64,256]{2,1,0:T(8,128)(2,1)S(1)}, u32[]{:S(2)}, u32[]{:S(2)}) collective-permute-start(bf16[2,64,256]{2,1,0:T(8,128)(2,1)S(1)} %get-tuple-element.70), channel_id=1, source_target_pairs={{0,96},{32,128},{64,160},{96,192},{128,224},{160,0},{192,32},{224,... | collective-permute-start | bytes 196616 | tf_op jit(solution)/shard_map/side_in/ppermute | solution.py:407
  26.8 10.5 %collective-permute-start.3 = (bf16[2,64,256]{2,1,0:T(8,128)(2,1)S(1)}, bf16[2,64,256]{2,1,0:T(8,128)(2,1)S(1)}, u32[]{:S(2)}, u32[]{:S(2)}) collective-permute-start(bf16[2,64,256]{2,1,0:T(8,128)(2,1)S(1)} %get-tuple-element.71), channel_id=1, source_target_pairs={{0,160},{32,192},{64,224},{96,0},{128,32},{160,64},{192,96},{224,1... | collective-permute-start | bytes 196616 | tf_op jit(solution)/shard_map/side_in/ppermute | solution.py:407
  29.9 7.4 %collective-permute-start.4 = (bf16[2,64,256]{2,1,0:T(8,128)(2,1)S(1)}, bf16[2,64,256]{2,1,0:T(8,128)(2,1)S(1)}, u32[]{:S(2)}, u32[]{:S(2)}) collective-permute-start(bf16[2,64,256]{2,1,0:T(8,128)(2,1)S(1)} %get-tuple-element.72), channel_id=1, source_target_pairs={{0,64},{32,96},{64,128},{96,160},{128,192},{160,224},{192,0},{224,... | collective-permute-start | bytes 196616 | tf_op jit(solution)/shard_map/side_in/ppermute | solution.py:407
  31.3 6.6 %collective-permute-start.5 = (bf16[2,64,256]{2,1,0:T(8,128)(2,1)S(1)}, bf16[2,64,256]{2,1,0:T(8,128)(2,1)S(1)}, u32[]{:S(2)}, u32[]{:S(2)}) collective-permute-start(bf16[2,64,256]{2,1,0:T(8,128)(2,1)S(1)} %get-tuple-element.73), channel_id=1, source_target_pairs={{0,192},{32,224},{64,0},{96,32},{128,64},{160,96},{192,128},{224,1... | collective-permute-start | bytes 196616 | tf_op jit(solution)/shard_map/side_in/ppermute | solution.py:407
  34.0 5.5 %collective-permute-start.6 = (bf16[2,64,256]{2,1,0:T(8,128)(2,1)S(1)}, bf16[2,64,256]{2,1,0:T(8,128)(2,1)S(1)}, u32[]{:S(2)}, u32[]{:S(2)}) collective-permute-start(bf16[2,64,256]{2,1,0:T(8,128)(2,1)S(1)} %get-tuple-element.74), channel_id=1, source_target_pairs={{0,32},{32,64},{64,96},{96,128},{128,160},{160,192},{192,224},{224... | collective-permute-start | bytes 196616 | tf_op jit(solution)/shard_map/side_in/ppermute | solution.py:407
  35.1 4.4 %collective-permute-start.7 = (bf16[2,64,256]{2,1,0:T(8,128)(2,1)S(1)}, bf16[2,64,256]{2,1,0:T(8,128)(2,1)S(1)}, u32[]{:S(2)}, u32[]{:S(2)}) collective-permute-start(bf16[2,64,256]{2,1,0:T(8,128)(2,1)S(1)} %get-tuple-element.75), channel_id=1, source_target_pairs={{0,224},{32,0},{64,32},{96,64},{128,96},{160,128},{192,160},{224,1... | collective-permute-start | bytes 196616 | tf_op jit(solution)/shard_map/side_in/ppermute | solution.py:407
  40.1 31.3 %all-to-all-start.1 = ((bf16[8,2,2,64,256]{4,3,2,1,0:T(8,128)(2,1)}), bf16[8,2,2,64,256]{4,3,2,1,0:T(8,128)(2,1)S(1)}, u32[]{:S(2)}, u32[]{:S(2)}) async-start(bf16[8,2,2,64,256]{4,3,2,1,0:T(8,128)(2,1)} %bitcast.8.direct), calls=%async_computation.1 | async-start | bytes 2097152 | tf_op jit(solution)/shard_map/mirror/all_to_all | solution.py:447
  44.6 24.7 %collective-permute-start.8 = (bf16[8,2,2,64,256]{4,3,2,1,0:T(8,128)(2,1)}, bf16[8,2,2,64,256]{4,3,2,1,0:T(8,128)(2,1)S(1)}, u32[]{:S(2)}, u32[]{:S(2)}) collective-permute-start(bf16[8,2,2,64,256]{4,3,2,1,0:T(8,128)(2,1)} %bitcast.8.direct), channel_id=1, source_target_pairs={{0,8},{8,0},{1,9},{9,1},{2,10},{10,2},{3,11},{11,3},{4,12},{12,4},... | collective-permute-start | bytes 3145736 | tf_op jit(solution)/shard_map/ppermute | solution.py:412
  45.2 10.4 %collective-permute-start.9 = (bf16[2,64,256]{2,1,0:T(8,128)(2,1)S(1)}, bf16[2,64,256]{2,1,0:T(8,128)(2,1)S(1)}, u32[]{:S(2)}, u32[]{:S(2)}) collective-permute-start(bf16[2,64,256]{2,1,0:T(8,128)(2,1)S(1)} %get-tuple-element.80), channel_id=1, source_target_pairs={{0,3},{1,4},{2,5},{3,6},{4,7},{5,0},{6,1},{7,2},{8,11},{9,12},{10,... | collective-permute-start | bytes 196616 | tf_op jit(solution)/shard_map/side_mirror/ppermute | solution.py:407
  49.2 8.6 %collective-permute-start.10 = (bf16[2,64,256]{2,1,0:T(8,128)(2,1)S(1)}, bf16[2,64,256]{2,1,0:T(8,128)(2,1)S(1)}, u32[]{:S(2)}, u32[]{:S(2)}) collective-permute-start(bf16[2,64,256]{2,1,0:T(8,128)(2,1)S(1)} %get-tuple-element.81), channel_id=1, source_target_pairs={{0,5},{1,6},{2,7},{3,0},{4,1},{5,2},{6,3},{7,4},{8,13},{9,14},{10,... | collective-permute-start | bytes 196616 | tf_op jit(solution)/shard_map/side_mirror/ppermute | solution.py:407
  51.2 7.5 %collective-permute-start.11 = (bf16[2,64,256]{2,1,0:T(8,128)(2,1)S(1)}, bf16[2,64,256]{2,1,0:T(8,128)(2,1)S(1)}, u32[]{:S(2)}, u32[]{:S(2)}) collective-permute-start(bf16[2,64,256]{2,1,0:T(8,128)(2,1)S(1)} %get-tuple-element.82), channel_id=1, source_target_pairs={{0,1},{1,2},{2,3},{3,4},{4,5},{5,6},{6,7},{7,0},{8,9},{9,10},{10,1... | collective-permute-start | bytes 196616 | tf_op jit(solution)/shard_map/side_mirror/ppermute | solution.py:407
  52.7 7.1 %collective-permute-start.12 = (bf16[2,64,256]{2,1,0:T(8,128)(2,1)S(1)}, bf16[2,64,256]{2,1,0:T(8,128)(2,1)S(1)}, u32[]{:S(2)}, u32[]{:S(2)}) collective-permute-start(bf16[2,64,256]{2,1,0:T(8,128)(2,1)S(1)} %get-tuple-element.83), channel_id=1, source_target_pairs={{0,7},{1,0},{2,1},{3,2},{4,3},{5,4},{6,5},{7,6},{8,15},{9,8},{10,9... | collective-permute-start | bytes 196616 | tf_op jit(solution)/shard_map/side_mirror/ppermute | solution.py:407
  55.7 6.3 %collective-permute-start.13 = (bf16[2,64,256]{2,1,0:T(8,128)(2,1)S(1)}, bf16[2,64,256]{2,1,0:T(8,128)(2,1)S(1)}, u32[]{:S(2)}, u32[]{:S(2)}) collective-permute-start(bf16[2,64,256]{2,1,0:T(8,128)(2,1)S(1)} %get-tuple-element.84), channel_id=1, source_target_pairs={{0,4},{1,5},{2,6},{3,7},{4,0},{5,1},{6,2},{7,3},{8,12},{9,13},{10,... | collective-permute-start | bytes 196616 | tf_op jit(solution)/shard_map/side_mirror/ppermute | solution.py:407
  57.7 4.4 %collective-permute-start.14 = (bf16[2,64,256]{2,1,0:T(8,128)(2,1)S(1)}, bf16[2,64,256]{2,1,0:T(8,128)(2,1)S(1)}, u32[]{:S(2)}, u32[]{:S(2)}) collective-permute-start(bf16[2,64,256]{2,1,0:T(8,128)(2,1)S(1)} %get-tuple-element.85), channel_id=1, source_target_pairs={{0,2},{1,3},{2,4},{3,5},{4,6},{5,7},{6,0},{7,1},{8,10},{9,11},{10,... | collective-permute-start | bytes 196616 | tf_op jit(solution)/shard_map/side_mirror/ppermute | solution.py:407
  58.7 4.3 %collective-permute-start.15 = (bf16[2,64,256]{2,1,0:T(8,128)(2,1)S(1)}, bf16[2,64,256]{2,1,0:T(8,128)(2,1)S(1)}, u32[]{:S(2)}, u32[]{:S(2)}) collective-permute-start(bf16[2,64,256]{2,1,0:T(8,128)(2,1)S(1)} %get-tuple-element.86), channel_id=1, source_target_pairs={{0,6},{1,7},{2,0},{3,1},{4,2},{5,3},{6,4},{7,5},{8,14},{9,15},{10,... | collective-permute-start | bytes 196616 | tf_op jit(solution)/shard_map/side_mirror/ppermute | solution.py:407
  59.8 3.9 %collective-permute-start.17 = (bf16[8,2,64,256]{3,2,1,0:T(8,128)(2,1)S(1)}, bf16[8,2,64,256]{3,2,1,0:T(8,128)(2,1)S(1)}, u32[]{:S(2)}, u32[]{:S(2)}) collective-permute-start(bf16[8,2,64,256]{3,2,1,0:T(8,128)(2,1)S(1)} %collect.3.x_ref), channel_id=1, source_target_pairs={{0,8},{8,0},{1,9},{9,1},{2,10},{10,2},{3,11},{11,3},{4,12},{12,4},... | collective-permute-start | bytes 1572872 | tf_op jit(solution)/shard_map/side_mirror/ppermute | solution.py:412
  63.6 2.0 %collective-permute-start.16 = (bf16[8,2,64,256]{3,2,1,0:T(8,128)(2,1)S(1)}, bf16[8,2,64,256]{3,2,1,0:T(8,128)(2,1)S(1)}, u32[]{:S(2)}, u32[]{:S(2)}) collective-permute-start(bf16[8,2,64,256]{3,2,1,0:T(8,128)(2,1)S(1)} %collect.4), channel_id=1, source_target_pairs={{0,8},{8,0},{1,9},{9,1},{2,10},{10,2},{3,11},{11,3},{4,12},{12,4},... | collective-permute-start | bytes 1572872 | tf_op jit(solution)/shard_map/side_mirror/ppermute | solution.py:412
  71.4 2.7 %collective-permute-start.18 = (bf16[8,2,2,64,256]{4,3,2,1,0:T(8,128)(2,1)S(1)}, bf16[8,2,2,64,256]{4,3,2,1,0:T(8,128)(2,1)S(1)}, u32[]{:S(2)}, u32[]{:S(2)}) collective-permute-start(bf16[8,2,2,64,256]{4,3,2,1,0:T(8,128)(2,1)S(1)} %all-to-all-done.1.turned), channel_id=1, source_target_pairs={{0,8},{8,0},{1,9},{9,1},{2,10},{10,2},{3,11},{11,3},{4,12},{12,4},... | collective-permute-start | bytes 3145736 | tf_op jit(solution)/shard_map/ppermute | solution.py:412
  80.4 34.8 %all-to-all-start.2 = ((bf16[8,2,256,128]{3,2,1,0:T(8,128)(2,1)}), bf16[8,2,256,128]{3,2,1,0:T(8,128)(2,1)S(1)}, u32[]{:S(2)}, u32[]{:S(2)}) async-start(bf16[8,2,256,128]{3,2,1,0:T(8,128)(2,1)} %first_half.1), calls=%async_computation.2 | async-start | bytes 2097152 | tf_op jit(solution)/shard_map/partial/all_to_all | solution.py:466
  86.1 14.7 %collective-permute-start.19 = (bf16[1,256,128]{2,1,0:T(8,128)(2,1)S(1)}, bf16[1,256,128]{2,1,0:T(8,128)(2,1)S(1)}, u32[]{:S(2)}, u32[]{:S(2)}) collective-permute-start(bf16[1,256,128]{2,1,0:T(8,128)(2,1)S(1)} %get-tuple-element.99), channel_id=1, source_target_pairs={{0,3},{1,4},{2,5},{3,6},{4,7},{5,0},{6,1},{7,2},{8,11},{9,12},{10,... | collective-permute-start | bytes 196616 | tf_op jit(solution)/shard_map/side_partial/ppermute | solution.py:407
  87.9 12.9 %collective-permute-start.20 = (bf16[1,256,128]{2,1,0:T(8,128)(2,1)S(1)}, bf16[1,256,128]{2,1,0:T(8,128)(2,1)S(1)}, u32[]{:S(2)}, u32[]{:S(2)}) collective-permute-start(bf16[1,256,128]{2,1,0:T(8,128)(2,1)S(1)} %get-tuple-element.100), channel_id=1, source_target_pairs={{0,5},{1,6},{2,7},{3,0},{4,1},{5,2},{6,3},{7,4},{8,13},{9,14},{10,... | collective-permute-start | bytes 196616 | tf_op jit(solution)/shard_map/side_partial/ppermute | solution.py:407
  92.0 10.8 %collective-permute-start.21 = (bf16[1,256,128]{2,1,0:T(8,128)(2,1)S(1)}, bf16[1,256,128]{2,1,0:T(8,128)(2,1)S(1)}, u32[]{:S(2)}, u32[]{:S(2)}) collective-permute-start(bf16[1,256,128]{2,1,0:T(8,128)(2,1)S(1)} %get-tuple-element.101), channel_id=1, source_target_pairs={{0,1},{1,2},{2,3},{3,4},{4,5},{5,6},{6,7},{7,0},{8,9},{9,10},{10,1... | collective-permute-start | bytes 196616 | tf_op jit(solution)/shard_map/side_partial/ppermute | solution.py:407
  93.4 9.4 %collective-permute-start.22 = (bf16[1,256,128]{2,1,0:T(8,128)(2,1)S(1)}, bf16[1,256,128]{2,1,0:T(8,128)(2,1)S(1)}, u32[]{:S(2)}, u32[]{:S(2)}) collective-permute-start(bf16[1,256,128]{2,1,0:T(8,128)(2,1)S(1)} %get-tuple-element.102), channel_id=1, source_target_pairs={{0,7},{1,0},{2,1},{3,2},{4,3},{5,4},{6,5},{7,6},{8,15},{9,8},{10,9... | collective-permute-start | bytes 196616 | tf_op jit(solution)/shard_map/side_partial/ppermute | solution.py:407
  96.5 7.5 %collective-permute-start.23 = (bf16[1,256,128]{2,1,0:T(8,128)(2,1)S(1)}, bf16[1,256,128]{2,1,0:T(8,128)(2,1)S(1)}, u32[]{:S(2)}, u32[]{:S(2)}) collective-permute-start(bf16[1,256,128]{2,1,0:T(8,128)(2,1)S(1)} %get-tuple-element.103), channel_id=1, source_target_pairs={{0,4},{1,5},{2,6},{3,7},{4,0},{5,1},{6,2},{7,3},{8,12},{9,13},{10,... | collective-permute-start | bytes 196616 | tf_op jit(solution)/shard_map/side_partial/ppermute | solution.py:407
  100.8 4.3 %collective-permute-start.24 = (bf16[1,256,128]{2,1,0:T(8,128)(2,1)S(1)}, bf16[1,256,128]{2,1,0:T(8,128)(2,1)S(1)}, u32[]{:S(2)}, u32[]{:S(2)}) collective-permute-start(bf16[1,256,128]{2,1,0:T(8,128)(2,1)S(1)} %get-tuple-element.104), channel_id=1, source_target_pairs={{0,2},{1,3},{2,4},{3,5},{4,6},{5,7},{6,0},{7,1},{8,10},{9,11},{10,... | collective-permute-start | bytes 196616 | tf_op jit(solution)/shard_map/side_partial/ppermute | solution.py:407
  100.8 4.3 %collective-permute-start.25 = (bf16[1,256,128]{2,1,0:T(8,128)(2,1)S(1)}, bf16[1,256,128]{2,1,0:T(8,128)(2,1)S(1)}, u32[]{:S(2)}, u32[]{:S(2)}) collective-permute-start(bf16[1,256,128]{2,1,0:T(8,128)(2,1)S(1)} %get-tuple-element.105), channel_id=1, source_target_pairs={{0,6},{1,7},{2,0},{3,1},{4,2},{5,3},{6,4},{7,5},{8,14},{9,15},{10,... | collective-permute-start | bytes 196616 | tf_op jit(solution)/shard_map/side_partial/ppermute | solution.py:407
  105.8 2.0 %collective-permute-start.26 = (bf16[8,1,256,128]{3,2,1,0:T(8,128)(2,1)S(1)}, bf16[8,1,256,128]{3,2,1,0:T(8,128)(2,1)S(1)}, u32[]{:S(2)}, u32[]{:S(2)}) collective-permute-start(bf16[8,1,256,128]{3,2,1,0:T(8,128)(2,1)S(1)} %collect.5.t_ref), channel_id=1, source_target_pairs={{0,8},{8,0},{1,9},{9,1},{2,10},{10,2},{3,11},{11,3},{4,12},{12,4},... | collective-permute-start | bytes 1572872 | tf_op jit(solution)/shard_map/side_partial/ppermute | solution.py:412
  112.8 8.4 %collective-permute-start.27 = (bf16[8,64,256]{2,1,0:T(8,128)(2,1)S(1)}, bf16[8,64,256]{2,1,0:T(8,128)(2,1)S(1)}, u32[]{:S(2)}, u32[]{:S(2)}) collective-permute-start(bf16[8,64,256]{2,1,0:T(8,128)(2,1)S(1)} %get-tuple-element.108), channel_id=1, source_target_pairs={{0,16},{16,0},{1,17},{17,1},{2,18},{18,2},{3,19},{19,3},{4,20},{20... | collective-permute-start | bytes 786440 | tf_op jit(solution)/shard_map/ppermute | solution.py:412
  121.2 28.1 %all-to-all-start.3 = ((bf16[16,2,64,256]{3,2,1,0:T(8,128)(2,1)}), bf16[16,2,64,256]{3,2,1,0:T(8,128)(2,1)S(1)}, u32[]{:S(2)}, u32[]{:S(2)}) async-start(bf16[16,2,64,256]{3,2,1,0:T(8,128)(2,1)} %bitcast.13), calls=%async_computation.3 | async-start | bytes 2097152 | tf_op jit(solution)/shard_map/panels_out/all_to_all | solution.py:480
  129.2 14.7 %collective-permute-start.28 = (bf16[2,64,256]{2,1,0:T(8,128)(2,1)S(1)}, bf16[2,64,256]{2,1,0:T(8,128)(2,1)S(1)}, u32[]{:S(2)}, u32[]{:S(2)}) collective-permute-start(bf16[2,64,256]{2,1,0:T(8,128)(2,1)S(1)} %get-tuple-element.113), channel_id=1, source_target_pairs={{0,128},{32,160},{64,192},{96,224},{128,0},{160,32},{192,64},{224,... | collective-permute-start | bytes 196616 | tf_op jit(solution)/shard_map/side_out/ppermute | solution.py:407
  134.7 9.8 %collective-permute-start.29 = (bf16[2,64,256]{2,1,0:T(8,128)(2,1)S(1)}, bf16[2,64,256]{2,1,0:T(8,128)(2,1)S(1)}, u32[]{:S(2)}, u32[]{:S(2)}) collective-permute-start(bf16[2,64,256]{2,1,0:T(8,128)(2,1)S(1)} %get-tuple-element.114), channel_id=1, source_target_pairs={{0,96},{32,128},{64,160},{96,192},{128,224},{160,0},{192,32},{224,... | collective-permute-start | bytes 196616 | tf_op jit(solution)/shard_map/side_out/ppermute | solution.py:407
  135.3 11.9 %collective-permute-start.30 = (bf16[2,64,256]{2,1,0:T(8,128)(2,1)S(1)}, bf16[2,64,256]{2,1,0:T(8,128)(2,1)S(1)}, u32[]{:S(2)}, u32[]{:S(2)}) collective-permute-start(bf16[2,64,256]{2,1,0:T(8,128)(2,1)S(1)} %get-tuple-element.115), channel_id=1, source_target_pairs={{0,160},{32,192},{64,224},{96,0},{128,32},{160,64},{192,96},{224,1... | collective-permute-start | bytes 196616 | tf_op jit(solution)/shard_map/side_out/ppermute | solution.py:407
  139.7 7.4 %collective-permute-start.31 = (bf16[2,64,256]{2,1,0:T(8,128)(2,1)S(1)}, bf16[2,64,256]{2,1,0:T(8,128)(2,1)S(1)}, u32[]{:S(2)}, u32[]{:S(2)}) collective-permute-start(bf16[2,64,256]{2,1,0:T(8,128)(2,1)S(1)} %get-tuple-element.116), channel_id=1, source_target_pairs={{0,64},{32,96},{64,128},{96,160},{128,192},{160,224},{192,0},{224,... | collective-permute-start | bytes 196616 | tf_op jit(solution)/shard_map/side_out/ppermute | solution.py:407
  140.3 6.9 %collective-permute-start.32 = (bf16[2,64,256]{2,1,0:T(8,128)(2,1)S(1)}, bf16[2,64,256]{2,1,0:T(8,128)(2,1)S(1)}, u32[]{:S(2)}, u32[]{:S(2)}) collective-permute-start(bf16[2,64,256]{2,1,0:T(8,128)(2,1)S(1)} %get-tuple-element.117), channel_id=1, source_target_pairs={{0,192},{32,224},{64,0},{96,32},{128,64},{160,96},{192,128},{224,1... | collective-permute-start | bytes 196616 | tf_op jit(solution)/shard_map/side_out/ppermute | solution.py:407
  143.9 5.5 %collective-permute-start.33 = (bf16[2,64,256]{2,1,0:T(8,128)(2,1)S(1)}, bf16[2,64,256]{2,1,0:T(8,128)(2,1)S(1)}, u32[]{:S(2)}, u32[]{:S(2)}) collective-permute-start(bf16[2,64,256]{2,1,0:T(8,128)(2,1)S(1)} %get-tuple-element.118), channel_id=1, source_target_pairs={{0,32},{32,64},{64,96},{96,128},{128,160},{160,192},{192,224},{224... | collective-permute-start | bytes 196616 | tf_op jit(solution)/shard_map/side_out/ppermute | solution.py:407
  144.5 4.9 %collective-permute-start.34 = (bf16[2,64,256]{2,1,0:T(8,128)(2,1)S(1)}, bf16[2,64,256]{2,1,0:T(8,128)(2,1)S(1)}, u32[]{:S(2)}, u32[]{:S(2)}) collective-permute-start(bf16[2,64,256]{2,1,0:T(8,128)(2,1)S(1)} %get-tuple-element.119), channel_id=1, source_target_pairs={{0,224},{32,0},{64,32},{96,64},{128,96},{160,128},{192,160},{224,1... | collective-permute-start | bytes 196616 | tf_op jit(solution)/shard_map/side_out/ppermute | solution.py:407

commit v6 on v5

--- a/solution.py
+++ b/solution.py
@@ -19,7 +19,7 @@
 SMALL = pltpu.CompilerParams(vmem_limit_bytes=8 * 2**20)
 
 
-ORDER = {AT_Z: (0, 4, 3, 5, 2, 6, 1, 7), AT_C: (0, 3, 5, 1, 7, 4, 2, 6)}
+ORDER = {AT_Z: (0, 3, 5, 4, 2, 6, 1, 7), AT_C: (0, 3, 5, 1, 7, 4, 2, 6)}
 STEPS = 4
 HBM = pl.BlockSpec(memory_space=pltpu.HBM)
 

time: 152 us -> 153 us (level)
  no operation moved by 1% of the time
where the time goes in v6:
time: 153 us; the launch traced here: 152 us
  starting transfers between devices  98 us (64%)
  Pallas kernels  32.8 us (21%)
  waiting for transfers between devices  19.9 us (13%)
    ppermute x28, starting transfers between devices, rotate(): lax.ppermute(part, axes, [(i, (i + d) % BLOCKS) for i in range(BLOCKS)])  69.4 us
    ppermute x28, waiting for transfers between devices, rotate(): lax.ppermute(part, axes, [(i, (i + d) % BLOCKS) for i in range(BLOCKS)])  10.2 us
    pallas_call x2, Pallas kernels, first_half(): pl.pallas_call(functools.partial(first_kernel, index), out_shape=[jax.Sha...  10.1 us
    all_to_all x1, starting transfers between devices, per_device(): result = lax.all_to_all(result, PLANE, 0, 0, tiled=True)  7.36 us
    ppermute x7, waiting for transfers between devices, swap(): return lax.ppermute(value, axis, [(0, 1), (1, 0)])  7.3 us
    all_to_all x1, starting transfers between devices, per_device(): own = lax.all_to_all(own, PLANE, 0, 0, tiled=True)  7.2 us
    pallas_call x1, Pallas kernels, pick_columns(): pl.pallas_call(pick_kernel, out_shape=[pltpu.HBM((size, width), BF16), pl...  6.85 us
    all_to_all x1, starting transfers between devices, per_device(): partial_value = lax.all_to_all(partial_value, 'z', 0, 0, tiled=True)  6 us
  transfers between devices with their start and end apart: 39, of which 18 were waited for; matrix products, arithmetic and copies ran while one was open for 0% of the time, Pallas kernels for 16%

profile of v6, /device:TPU:2, one launch (start us, length us, event | category | flops | bytes accessed | tf_op | source)
XLA Modules:
  0.0 152.2 jit_solution(18051804652849799318)
XLA Ops:
  0.0 1.1 slice.3
  1.1 1.7 %collective-permute-start = (bf16[8,64,256]{2,1,0:T(8,128)(2,1)S(1)}, bf16[8,64,256]{2,1,0:T(8,128)(2,1)S(1)}, u32[]{:S(2)}, u32[]{:S(2)}) collective-permute-start(bf16[8,64,256]{2,1,0:T(8,128)(2,1)S(1)} %get-tuple-element.122), channel_id=1, source_target_pairs={{0,16},{16,0},{1,17},{17,1},{2,18},{18,2},{3,19},{19,3},{4,20},{20... | collective-permute-start | bytes 786440 | tf_op jit(solution)/shard_map/side_in/ppermute | solution.py:412
  2.9 6.9 %pick_columns.1 = (bf16[2048,1024]{1,0:T(8,128)(2,1)}, bf16[32,64,256]{2,1,0:T(8,128)(2,1)}) custom-call(s32[4]{0:T(128)S(1)} %pad_add_fusion.place, bf16[2048,2048]{1,0:T(8,128)(2,1)} %c_hbm.3, bf16[48,64,256]{2,1,0:T(8,128)(2,1)} %panel_hbm.1), custom_call_target="tpu_custom_call" | custom-call | tf_op jit(solution)/shard_map/pick_columns/pallas_call | solution.py:139
  9.8 7.2 %all-to-all-start = ((bf16[16,2,64,256]{3,2,1,0:T(8,128)(2,1)}), bf16[16,2,64,256]{3,2,1,0:T(8,128)(2,1)}, u32[]{:S(2)}, u32[]{:S(2)}) async-start(bf16[16,2,64,256]{3,2,1,0:T(8,128)(2,1)} %bitcast.23), calls=%async_computation | async-start | bytes 2097152 | tf_op jit(solution)/shard_map/panels_in/all_to_all | solution.py:439
  16.9 0.6 join_and_spread.2
  17.5 4.7 %collective-permute-start.1 = (bf16[2,64,256]{2,1,0:T(8,128)(2,1)S(1)}, bf16[2,64,256]{2,1,0:T(8,128)(2,1)S(1)}, u32[]{:S(2)}, u32[]{:S(2)}) collective-permute-start(bf16[2,64,256]{2,1,0:T(8,128)(2,1)S(1)} %get-tuple-element.69), channel_id=1, source_target_pairs={{0,96},{32,128},{64,160},{96,192},{128,224},{160,0},{192,32},{224,... | collective-permute-start | bytes 196616 | tf_op jit(solution)/shard_map/side_in/ppermute | solution.py:407
  22.2 2.2 %collective-permute-start.2 = (bf16[2,64,256]{2,1,0:T(8,128)(2,1)S(1)}, bf16[2,64,256]{2,1,0:T(8,128)(2,1)S(1)}, u32[]{:S(2)}, u32[]{:S(2)}) collective-permute-start(bf16[2,64,256]{2,1,0:T(8,128)(2,1)S(1)} %get-tuple-element.70), channel_id=1, source_target_pairs={{0,160},{32,192},{64,224},{96,0},{128,32},{160,64},{192,96},{224,1... | collective-permute-start | bytes 196616 | tf_op jit(solution)/shard_map/side_in/ppermute | solution.py:407
  24.5 5.4 %collective-permute-start.3 = (bf16[2,64,256]{2,1,0:T(8,128)(2,1)S(1)}, bf16[2,64,256]{2,1,0:T(8,128)(2,1)S(1)}, u32[]{:S(2)}, u32[]{:S(2)}) collective-permute-start(bf16[2,64,256]{2,1,0:T(8,128)(2,1)S(1)} %get-tuple-element.71), channel_id=1, source_target_pairs={{0,128},{32,160},{64,192},{96,224},{128,0},{160,32},{192,64},{224,... | collective-permute-start | bytes 196616 | tf_op jit(solution)/shard_map/side_in/ppermute | solution.py:407
  29.9 1.5 collective-permute-start.4
  31.3 2.7 %collective-permute-start.5 = (bf16[2,64,256]{2,1,0:T(8,128)(2,1)S(1)}, bf16[2,64,256]{2,1,0:T(8,128)(2,1)S(1)}, u32[]{:S(2)}, u32[]{:S(2)}) collective-permute-start(bf16[2,64,256]{2,1,0:T(8,128)(2,1)S(1)} %get-tuple-element.73), channel_id=1, source_target_pairs={{0,192},{32,224},{64,0},{96,32},{128,64},{160,96},{192,128},{224,1... | collective-permute-start | bytes 196616 | tf_op jit(solution)/shard_map/side_in/ppermute | solution.py:407
  34.0 1.0 collective-permute-start.6
  35.0 2.2 %collective-permute-start.7 = (bf16[2,64,256]{2,1,0:T(8,128)(2,1)S(1)}, bf16[2,64,256]{2,1,0:T(8,128)(2,1)S(1)}, u32[]{:S(2)}, u32[]{:S(2)}) collective-permute-start(bf16[2,64,256]{2,1,0:T(8,128)(2,1)S(1)} %get-tuple-element.75), channel_id=1, source_target_pairs={{0,224},{32,0},{64,32},{96,64},{128,96},{160,128},{192,160},{224,1... | collective-permute-start | bytes 196616 | tf_op jit(solution)/shard_map/side_in/ppermute | solution.py:407
  37.2 0.5 collective-permute-done.5.refs_5_
  37.8 1.7 %collective-permute-done.6.refs_6_ = bf16[2,64,256]{2,1,0:T(8,128)(2,1)S(1)} collective-permute-done((bf16[2,64,256]{2,1,0:T(8,128)(2,1)S(1)}, bf16[2,64,256]{2,1,0:T(8,128)(2,1)S(1)}, u32[]{:S(2)}, u32[]{:S(2)}) %collective-permute-start.6) | collective-permute-done | bytes 65568 | tf_op jit(solution)/shard_map/side_in/ppermute | solution.py:407
  39.5 0.2 collective-permute-done.7.refs_7_
  39.7 0.6 collect.3.x_ref
  40.3 4.6 %all-to-all-start.1 = ((bf16[8,2,2,64,256]{4,3,2,1,0:T(8,128)(2,1)}), bf16[8,2,2,64,256]{4,3,2,1,0:T(8,128)(2,1)S(1)}, u32[]{:S(2)}, u32[]{:S(2)}) async-start(bf16[8,2,2,64,256]{4,3,2,1,0:T(8,128)(2,1)} %bitcast.8.direct), calls=%async_computation.1 | async-start | bytes 2097152 | tf_op jit(solution)/shard_map/mirror/all_to_all | solution.py:447
  45.0 0.6 spread.1
  45.6 3.9 %collective-permute-start.9 = (bf16[2,64,256]{2,1,0:T(8,128)(2,1)S(1)}, bf16[2,64,256]{2,1,0:T(8,128)(2,1)S(1)}, u32[]{:S(2)}, u32[]{:S(2)}) collective-permute-start(bf16[2,64,256]{2,1,0:T(8,128)(2,1)S(1)} %get-tuple-element.80), channel_id=1, source_target_pairs={{0,3},{1,4},{2,5},{3,6},{4,7},{5,0},{6,1},{7,2},{8,11},{9,12},{10,... | collective-permute-start | bytes 196616 | tf_op jit(solution)/shard_map/side_mirror/ppermute | solution.py:407
  49.5 2.1 %collective-permute-start.10 = (bf16[2,64,256]{2,1,0:T(8,128)(2,1)S(1)}, bf16[2,64,256]{2,1,0:T(8,128)(2,1)S(1)}, u32[]{:S(2)}, u32[]{:S(2)}) collective-permute-start(bf16[2,64,256]{2,1,0:T(8,128)(2,1)S(1)} %get-tuple-element.81), channel_id=1, source_target_pairs={{0,5},{1,6},{2,7},{3,0},{4,1},{5,2},{6,3},{7,4},{8,13},{9,14},{10,... | collective-permute-start | bytes 196616 | tf_op jit(solution)/shard_map/side_mirror/ppermute | solution.py:407
  51.6 1.5 collective-permute-start.11
  53.0 3.0 %collective-permute-start.12 = (bf16[2,64,256]{2,1,0:T(8,128)(2,1)S(1)}, bf16[2,64,256]{2,1,0:T(8,128)(2,1)S(1)}, u32[]{:S(2)}, u32[]{:S(2)}) collective-permute-start(bf16[2,64,256]{2,1,0:T(8,128)(2,1)S(1)} %get-tuple-element.83), channel_id=1, source_target_pairs={{0,7},{1,0},{2,1},{3,2},{4,3},{5,4},{6,5},{7,6},{8,15},{9,8},{10,9... | collective-permute-start | bytes 196616 | tf_op jit(solution)/shard_map/side_mirror/ppermute | solution.py:407
  56.0 2.1 %collective-permute-start.13 = (bf16[2,64,256]{2,1,0:T(8,128)(2,1)S(1)}, bf16[2,64,256]{2,1,0:T(8,128)(2,1)S(1)}, u32[]{:S(2)}, u32[]{:S(2)}) collective-permute-start(bf16[2,64,256]{2,1,0:T(8,128)(2,1)S(1)} %get-tuple-element.84), channel_id=1, source_target_pairs={{0,4},{1,5},{2,6},{3,7},{4,0},{5,1},{6,2},{7,3},{8,12},{9,13},{10,... | collective-permute-start | bytes 196616 | tf_op jit(solution)/shard_map/side_mirror/ppermute | solution.py:407
  58.1 0.7 collective-permute-start.14
  58.8 1.3 collective-permute-start.15
  60.1 2.1 %collective-permute-done.13.refs_5_ = bf16[2,64,256]{2,1,0:T(8,128)(2,1)S(1)} collective-permute-done((bf16[2,64,256]{2,1,0:T(8,128)(2,1)S(1)}, bf16[2,64,256]{2,1,0:T(8,128)(2,1)S(1)}, u32[]{:S(2)}, u32[]{:S(2)}) %collective-permute-start.13) | collective-permute-done | bytes 65568 | tf_op jit(solution)/shard_map/side_mirror/ppermute | solution.py:407
  62.3 0.2 collective-permute-done.14.refs_6_
  62.5 0.6 collective-permute-done.15.refs_7_
  63.0 0.6 collect.4
  63.6 0.1 collective-permute-start.16
  63.7 1.9 %collective-permute-done.16 = bf16[8,2,64,256]{3,2,1,0:T(8,128)(2,1)S(1)} collective-permute-done((bf16[8,2,64,256]{3,2,1,0:T(8,128)(2,1)S(1)}, bf16[8,2,64,256]{3,2,1,0:T(8,128)(2,1)S(1)}, u32[]{:S(2)}, u32[]{:S(2)}) %collective-permute-start.16) | collective-permute-done | bytes 524320 | tf_op jit(solution)/shard_map/side_mirror/ppermute | solution.py:412
  65.6 3.8 %first_half_side.1 = (bf16[1,256,128]{2,1,0:T(8,128)(2,1)S(1)}, bf16[1,256,128]{2,1,0:T(8,128)(2,1)S(1)}, bf16[1,256,128]{2,1,0:T(8,128)(2,1)S(1)}, bf16[1,256,1...) custom-call(s32[4]{0:T(128)S(1)} %pad_add_fusion.place, ...), custom_call_target="tpu_custom_call" | custom-call | tf_op jit(solution)/shard_map/side_mirror/first_half_side/pallas_call | solution.py:215
  69.4 1.8 %all-to-all-done.1.turned = bf16[8,2,2,64,256]{4,3,2,1,0:T(8,128)(2,1)S(1)} async-done(((bf16[8,2,2,64,256]{4,3,2,1,0:T(8,128)(2,1)}), bf16[8,2,2,64,256]{4,3,2,1,0:T(8,128)(2,1)S(1)}, u32[]{:S(2)}, u32[]{:S(2)}) %all-to-all-start.1) | async-done | bytes 1048608 | tf_op jit(solution)/shard_map/mirror/all_to_all | solution.py:447
  71.2 2.7 %collective-permute-done.18.turned_other = bf16[8,2,2,64,256]{4,3,2,1,0:T(8,128)(2,1)S(1)} collective-permute-done((bf16[8,2,2,64,256]{4,3,2,1,0:T(8,128)(2,1)S(1)}, bf16[8,2,2,64,256]{4,3,2,1,0:T(8,128)(2,1)S(1)}, u32[]{:S(2)}, u32[]{:S(2)}) %collective-permute-start.18) | collective-permute-done | bytes 1048608 | tf_op jit(solution)/shard_map/ppermute | solution.py:412
  73.8 6.3 %first_half.1 = bf16[8,2,256,128]{3,2,1,0:T(8,128)(2,1)} custom-call(s32[4]{0:T(128)S(1)} %pad_add_fusion.place, bf16[8,2,2,64,256]{4,3,2,1,0:T(8,128)(2,1)} %bitcast.8.direct, bf16[8,2,2,64,256]{4,3,2,1,0:T(8,128)(2,1)S(1)} %collective-permute-done.8.direct_other, bf16[8,2,2,64,256]{4,3,2,1,0:T(8,128)(2,1)S(1)} %all-to-all-done.1.turned, ...), custom_call_target="tpu_custom_call" | custom-call | tf_op jit(solution)/shard_map/first_half/pallas_call | solution.py:215
  80.2 6.0 %all-to-all-start.2 = ((bf16[8,2,256,128]{3,2,1,0:T(8,128)(2,1)}), bf16[8,2,256,128]{3,2,1,0:T(8,128)(2,1)S(1)}, u32[]{:S(2)}, u32[]{:S(2)}) async-start(bf16[8,2,256,128]{3,2,1,0:T(8,128)(2,1)} %first_half.1), calls=%async_computation.2 | async-start | bytes 2097152 | tf_op jit(solution)/shard_map/partial/all_to_all | solution.py:466
  86.2 2.0 %collective-permute-start.19 = (bf16[1,256,128]{2,1,0:T(8,128)(2,1)S(1)}, bf16[1,256,128]{2,1,0:T(8,128)(2,1)S(1)}, u32[]{:S(2)}, u32[]{:S(2)}) collective-permute-start(bf16[1,256,128]{2,1,0:T(8,128)(2,1)S(1)} %get-tuple-element.99), channel_id=1, source_target_pairs={{0,3},{1,4},{2,5},{3,6},{4,7},{5,0},{6,1},{7,2},{8,11},{9,12},{10,... | collective-permute-start | bytes 196616 | tf_op jit(solution)/shard_map/side_partial/ppermute | solution.py:407
  88.2 3.9 %collective-permute-start.20 = (bf16[1,256,128]{2,1,0:T(8,128)(2,1)S(1)}, bf16[1,256,128]{2,1,0:T(8,128)(2,1)S(1)}, u32[]{:S(2)}, u32[]{:S(2)}) collective-permute-start(bf16[1,256,128]{2,1,0:T(8,128)(2,1)S(1)} %get-tuple-element.100), channel_id=1, source_target_pairs={{0,5},{1,6},{2,7},{3,0},{4,1},{5,2},{6,3},{7,4},{8,13},{9,14},{10,... | collective-permute-start | bytes 196616 | tf_op jit(solution)/shard_map/side_partial/ppermute | solution.py:407
  92.1 1.7 %collective-permute-start.21 = (bf16[1,256,128]{2,1,0:T(8,128)(2,1)S(1)}, bf16[1,256,128]{2,1,0:T(8,128)(2,1)S(1)}, u32[]{:S(2)}, u32[]{:S(2)}) collective-permute-start(bf16[1,256,128]{2,1,0:T(8,128)(2,1)S(1)} %get-tuple-element.101), channel_id=1, source_target_pairs={{0,1},{1,2},{2,3},{3,4},{4,5},{5,6},{6,7},{7,0},{8,9},{9,10},{10,1... | collective-permute-start | bytes 196616 | tf_op jit(solution)/shard_map/side_partial/ppermute | solution.py:407
  93.8 2.7 %collective-permute-start.22 = (bf16[1,256,128]{2,1,0:T(8,128)(2,1)S(1)}, bf16[1,256,128]{2,1,0:T(8,128)(2,1)S(1)}, u32[]{:S(2)}, u32[]{:S(2)}) collective-permute-start(bf16[1,256,128]{2,1,0:T(8,128)(2,1)S(1)} %get-tuple-element.102), channel_id=1, source_target_pairs={{0,7},{1,0},{2,1},{3,2},{4,3},{5,4},{6,5},{7,6},{8,15},{9,8},{10,9... | collective-permute-start | bytes 196616 | tf_op jit(solution)/shard_map/side_partial/ppermute | solution.py:407
  96.5 4.6 %collective-permute-start.23 = (bf16[1,256,128]{2,1,0:T(8,128)(2,1)S(1)}, bf16[1,256,128]{2,1,0:T(8,128)(2,1)S(1)}, u32[]{:S(2)}, u32[]{:S(2)}) collective-permute-start(bf16[1,256,128]{2,1,0:T(8,128)(2,1)S(1)} %get-tuple-element.103), channel_id=1, source_target_pairs={{0,4},{1,5},{2,6},{3,7},{4,0},{5,1},{6,2},{7,3},{8,12},{9,13},{10,... | collective-permute-start | bytes 196616 | tf_op jit(solution)/shard_map/side_partial/ppermute | solution.py:407
  101.2 2.0 %collective-permute-start.25 = (bf16[1,256,128]{2,1,0:T(8,128)(2,1)S(1)}, bf16[1,256,128]{2,1,0:T(8,128)(2,1)S(1)}, u32[]{:S(2)}, u32[]{:S(2)}) collective-permute-start(bf16[1,256,128]{2,1,0:T(8,128)(2,1)S(1)} %get-tuple-element.105), channel_id=1, source_target_pairs={{0,6},{1,7},{2,0},{3,1},{4,2},{5,3},{6,4},{7,5},{8,14},{9,15},{10,... | collective-permute-start | bytes 196616 | tf_op jit(solution)/shard_map/side_partial/ppermute | solution.py:407
  103.2 1.1 collective-permute-done.23.refs_5_
  104.3 1.1 collective-permute-done.24.refs_6_
  105.5 0.6 collect.5.t_ref
  106.2 1.9 %collective-permute-done.26.other_ref = bf16[8,1,256,128]{3,2,1,0:T(8,128)(2,1)S(1)} collective-permute-done((bf16[8,1,256,128]{3,2,1,0:T(8,128)(2,1)S(1)}, bf16[8,1,256,128]{3,2,1,0:T(8,128)(2,1)S(1)}, u32[]{:S(2)}, u32[]{:S(2)}) %collective-permute-start.26) | collective-permute-done | bytes 524320 | tf_op jit(solution)/shard_map/side_partial/ppermute | solution.py:412
  108.1 5.0 %second_half_side.1 = (bf16[8,64,256]{2,1,0:T(8,128)(2,1)S(1)}, bf16[8,64,256]{2,1,0:T(8,128)(2,1)S(1)}) custom-call(s32[4]{0:T(128)S(1)} %pad_add_fusion.place, bf16[8,1,256,128]{3,2,1,0:T(8,128)(2,1)S(1)} %collect.5.t_ref, bf16[8,1,256,128]{3,2,1,0:T(8,128)(2,1)S(1)} %collective-permute-done.26.other_ref, bf16[2048,1024]{1,0:T(8,128)(2,1)} %get-tuple-element.87.c_hbm), custom_call_target="tpu_custom_call" | custom-call | tf_op jit(solution)/shard_map/side_partial/second_half_side/pallas_call | solution.py:304
  113.1 1.5 %collective-permute-start.27 = (bf16[8,64,256]{2,1,0:T(8,128)(2,1)S(1)}, bf16[8,64,256]{2,1,0:T(8,128)(2,1)S(1)}, u32[]{:S(2)}, u32[]{:S(2)}) collective-permute-start(bf16[8,64,256]{2,1,0:T(8,128)(2,1)S(1)} %get-tuple-element.108), channel_id=1, source_target_pairs={{0,16},{16,0},{1,17},{17,1},{2,18},{18,2},{3,19},{19,3},{4,20},{20... | collective-permute-start | bytes 786440 | tf_op jit(solution)/shard_map/ppermute | solution.py:412
  114.7 0.6 all-to-all-done.2.t_ref
  115.2 5.5 %second_half.1 = bf16[8,2,2,64,256]{4,3,2,1,0:T(8,128)(2,1)} custom-call(bf16[8,2,256,128]{3,2,1,0:T(8,128)(2,1)S(1)} %all-to-all-done.2.t_ref, bf16[2048,2048]{1,0:T(8,128)(2,1)} %c_hbm.3), custom_call_target="tpu_custom_call" | custom-call | tf_op jit(solution)/shard_map/second_half/pallas_call | solution.py:257
  120.7 0.9 collective-permute-done.27.got
  121.6 7.4 %all-to-all-start.3 = ((bf16[16,2,64,256]{3,2,1,0:T(8,128)(2,1)}), bf16[16,2,64,256]{3,2,1,0:T(8,128)(2,1)S(1)}, u32[]{:S(2)}, u32[]{:S(2)}) async-start(bf16[16,2,64,256]{3,2,1,0:T(8,128)(2,1)} %bitcast.13), calls=%async_computation.3 | async-start | bytes 2097152 | tf_op jit(solution)/shard_map/panels_out/all_to_all | solution.py:480
  128.9 0.6 join_and_spread.3
  129.5 3.6 %collective-permute-start.28 = (bf16[2,64,256]{2,1,0:T(8,128)(2,1)S(1)}, bf16[2,64,256]{2,1,0:T(8,128)(2,1)S(1)}, u32[]{:S(2)}, u32[]{:S(2)}) collective-permute-start(bf16[2,64,256]{2,1,0:T(8,128)(2,1)S(1)} %get-tuple-element.113), channel_id=1, source_target_pairs={{0,96},{32,128},{64,160},{96,192},{128,224},{160,0},{192,32},{224,... | collective-permute-start | bytes 196616 | tf_op jit(solution)/shard_map/side_out/ppermute | solution.py:407
  133.2 1.7 %collective-permute-start.29 = (bf16[2,64,256]{2,1,0:T(8,128)(2,1)S(1)}, bf16[2,64,256]{2,1,0:T(8,128)(2,1)S(1)}, u32[]{:S(2)}, u32[]{:S(2)}) collective-permute-start(bf16[2,64,256]{2,1,0:T(8,128)(2,1)S(1)} %get-tuple-element.114), channel_id=1, source_target_pairs={{0,160},{32,192},{64,224},{96,0},{128,32},{160,64},{192,96},{224,1... | collective-permute-start | bytes 196616 | tf_op jit(solution)/shard_map/side_out/ppermute | solution.py:407
  134.9 5.4 %collective-permute-start.30 = (bf16[2,64,256]{2,1,0:T(8,128)(2,1)S(1)}, bf16[2,64,256]{2,1,0:T(8,128)(2,1)S(1)}, u32[]{:S(2)}, u32[]{:S(2)}) collective-permute-start(bf16[2,64,256]{2,1,0:T(8,128)(2,1)S(1)} %get-tuple-element.115), channel_id=1, source_target_pairs={{0,128},{32,160},{64,192},{96,224},{128,0},{160,32},{192,64},{224,... | collective-permute-start | bytes 196616 | tf_op jit(solution)/shard_map/side_out/ppermute | solution.py:407
  140.3 0.6 collective-permute-start.31
  140.9 3.6 %collective-permute-start.32 = (bf16[2,64,256]{2,1,0:T(8,128)(2,1)S(1)}, bf16[2,64,256]{2,1,0:T(8,128)(2,1)S(1)}, u32[]{:S(2)}, u32[]{:S(2)}) collective-permute-start(bf16[2,64,256]{2,1,0:T(8,128)(2,1)S(1)} %get-tuple-element.117), channel_id=1, source_target_pairs={{0,192},{32,224},{64,0},{96,32},{128,64},{160,96},{192,128},{224,1... | collective-permute-start | bytes 196616 | tf_op jit(solution)/shard_map/side_out/ppermute | solution.py:407
  144.4 0.6 collective-permute-start.33
  145.0 2.7 %collective-permute-start.34 = (bf16[2,64,256]{2,1,0:T(8,128)(2,1)S(1)}, bf16[2,64,256]{2,1,0:T(8,128)(2,1)S(1)}, u32[]{:S(2)}, u32[]{:S(2)}) collective-permute-start(bf16[2,64,256]{2,1,0:T(8,128)(2,1)S(1)} %get-tuple-element.119), channel_id=1, source_target_pairs={{0,224},{32,0},{64,32},{96,64},{128,96},{160,128},{192,160},{224,1... | collective-permute-start | bytes 196616 | tf_op jit(solution)/shard_map/side_out/ppermute | solution.py:407
  147.7 0.2 collective-permute-done.32.refs_5_
  147.8 2.1 %collective-permute-done.33.refs_6_ = bf16[2,64,256]{2,1,0:T(8,128)(2,1)S(1)} collective-permute-done((bf16[2,64,256]{2,1,0:T(8,128)(2,1)S(1)}, bf16[2,64,256]{2,1,0:T(8,128)(2,1)S(1)}, u32[]{:S(2)}, u32[]{:S(2)}) %collective-permute-start.33) | collective-permute-done | bytes 65568 | tf_op jit(solution)/shard_map/side_out/ppermute | solution.py:407
  149.9 0.2 collective-permute-done.34.refs_7_
  150.2 1.8 %finish.1 = bf16[48,64,256]{2,1,0:T(8,128)(2,1)} custom-call(s32[4]{0:T(128)S(1)} %pad_add_fusion.place, bf16[2,64,256]{2,1,0:T(8,128)(2,1)S(1)} %get-tuple-element.112.refs_0_, bf16[2,64,256]{2,1,0:T(8,128)(2,1)S(1)} %collective-permute-done.28.refs_1_, bf16[2,64,256]{2,1,0:T(8,128)(2,1)S(1)} %collective-permute-done.29.refs_2_, ...), custom_call_target="tpu_custom_call" | custom-call | tf_op jit(solution)/shard_map/finish/pallas_call | solution.py:393
  (29 shorter events, 0.4 us)
Async XLA Ops:
  1.1 8.6 %collective-permute-start = (bf16[8,64,256]{2,1,0:T(8,128)(2,1)S(1)}, bf16[8,64,256]{2,1,0:T(8,128)(2,1)S(1)}, u32[]{:S(2)}, u32[]{:S(2)}) collective-permute-start(bf16[8,64,256]{2,1,0:T(8,128)(2,1)S(1)} %get-tuple-element.122), channel_id=1, source_target_pairs={{0,16},{16,0},{1,17},{17,1},{2,18},{18,2},{3,19},{19,3},{4,20},{20... | collective-permute-start | bytes 786440 | tf_op jit(solution)/shard_map/side_in/ppermute | solution.py:412
  9.8 30.6 %all-to-all-start = ((bf16[16,2,64,256]{3,2,1,0:T(8,128)(2,1)}), bf16[16,2,64,256]{3,2,1,0:T(8,128)(2,1)}, u32[]{:S(2)}, u32[]{:S(2)}) async-start(bf16[16,2,64,256]{3,2,1,0:T(8,128)(2,1)} %bitcast.23), calls=%async_computation | async-start | bytes 2097152 | tf_op jit(solution)/shard_map/panels_in/all_to_all | solution.py:439
  17.5 16.4 %collective-permute-start.1 = (bf16[2,64,256]{2,1,0:T(8,128)(2,1)S(1)}, bf16[2,64,256]{2,1,0:T(8,128)(2,1)S(1)}, u32[]{:S(2)}, u32[]{:S(2)}) collective-permute-start(bf16[2,64,256]{2,1,0:T(8,128)(2,1)S(1)} %get-tuple-element.69), channel_id=1, source_target_pairs={{0,96},{32,128},{64,160},{96,192},{128,224},{160,0},{192,32},{224,... | collective-permute-start | bytes 196616 | tf_op jit(solution)/shard_map/side_in/ppermute | solution.py:407
  22.2 12.8 %collective-permute-start.2 = (bf16[2,64,256]{2,1,0:T(8,128)(2,1)S(1)}, bf16[2,64,256]{2,1,0:T(8,128)(2,1)S(1)}, u32[]{:S(2)}, u32[]{:S(2)}) collective-permute-start(bf16[2,64,256]{2,1,0:T(8,128)(2,1)S(1)} %get-tuple-element.70), channel_id=1, source_target_pairs={{0,160},{32,192},{64,224},{96,0},{128,32},{160,64},{192,96},{224,1... | collective-permute-start | bytes 196616 | tf_op jit(solution)/shard_map/side_in/ppermute | solution.py:407
  24.5 12.8 %collective-permute-start.3 = (bf16[2,64,256]{2,1,0:T(8,128)(2,1)S(1)}, bf16[2,64,256]{2,1,0:T(8,128)(2,1)S(1)}, u32[]{:S(2)}, u32[]{:S(2)}) collective-permute-start(bf16[2,64,256]{2,1,0:T(8,128)(2,1)S(1)} %get-tuple-element.71), channel_id=1, source_target_pairs={{0,128},{32,160},{64,192},{96,224},{128,0},{160,32},{192,64},{224,... | collective-permute-start | bytes 196616 | tf_op jit(solution)/shard_map/side_in/ppermute | solution.py:407
  29.9 7.4 %collective-permute-start.4 = (bf16[2,64,256]{2,1,0:T(8,128)(2,1)S(1)}, bf16[2,64,256]{2,1,0:T(8,128)(2,1)S(1)}, u32[]{:S(2)}, u32[]{:S(2)}) collective-permute-start(bf16[2,64,256]{2,1,0:T(8,128)(2,1)S(1)} %get-tuple-element.72), channel_id=1, source_target_pairs={{0,64},{32,96},{64,128},{96,160},{128,192},{160,224},{192,0},{224,... | collective-permute-start | bytes 196616 | tf_op jit(solution)/shard_map/side_in/ppermute | solution.py:407
  31.3 6.4 %collective-permute-start.5 = (bf16[2,64,256]{2,1,0:T(8,128)(2,1)S(1)}, bf16[2,64,256]{2,1,0:T(8,128)(2,1)S(1)}, u32[]{:S(2)}, u32[]{:S(2)}) collective-permute-start(bf16[2,64,256]{2,1,0:T(8,128)(2,1)S(1)} %get-tuple-element.73), channel_id=1, source_target_pairs={{0,192},{32,224},{64,0},{96,32},{128,64},{160,96},{192,128},{224,1... | collective-permute-start | bytes 196616 | tf_op jit(solution)/shard_map/side_in/ppermute | solution.py:407
  34.0 5.5 %collective-permute-start.6 = (bf16[2,64,256]{2,1,0:T(8,128)(2,1)S(1)}, bf16[2,64,256]{2,1,0:T(8,128)(2,1)S(1)}, u32[]{:S(2)}, u32[]{:S(2)}) collective-permute-start(bf16[2,64,256]{2,1,0:T(8,128)(2,1)S(1)} %get-tuple-element.74), channel_id=1, source_target_pairs={{0,32},{32,64},{64,96},{96,128},{128,160},{160,192},{192,224},{224... | collective-permute-start | bytes 196616 | tf_op jit(solution)/shard_map/side_in/ppermute | solution.py:407
  35.0 4.7 %collective-permute-start.7 = (bf16[2,64,256]{2,1,0:T(8,128)(2,1)S(1)}, bf16[2,64,256]{2,1,0:T(8,128)(2,1)S(1)}, u32[]{:S(2)}, u32[]{:S(2)}) collective-permute-start(bf16[2,64,256]{2,1,0:T(8,128)(2,1)S(1)} %get-tuple-element.75), channel_id=1, source_target_pairs={{0,224},{32,0},{64,32},{96,64},{128,96},{160,128},{192,160},{224,1... | collective-permute-start | bytes 196616 | tf_op jit(solution)/shard_map/side_in/ppermute | solution.py:407
  40.3 30.8 %all-to-all-start.1 = ((bf16[8,2,2,64,256]{4,3,2,1,0:T(8,128)(2,1)}), bf16[8,2,2,64,256]{4,3,2,1,0:T(8,128)(2,1)S(1)}, u32[]{:S(2)}, u32[]{:S(2)}) async-start(bf16[8,2,2,64,256]{4,3,2,1,0:T(8,128)(2,1)} %bitcast.8.direct), calls=%async_computation.1 | async-start | bytes 2097152 | tf_op jit(solution)/shard_map/mirror/all_to_all | solution.py:447
  44.9 24.4 %collective-permute-start.8 = (bf16[8,2,2,64,256]{4,3,2,1,0:T(8,128)(2,1)}, bf16[8,2,2,64,256]{4,3,2,1,0:T(8,128)(2,1)S(1)}, u32[]{:S(2)}, u32[]{:S(2)}) collective-permute-start(bf16[8,2,2,64,256]{4,3,2,1,0:T(8,128)(2,1)} %bitcast.8.direct), channel_id=1, source_target_pairs={{0,8},{8,0},{1,9},{9,1},{2,10},{10,2},{3,11},{11,3},{4,12},{12,4},... | collective-permute-start | bytes 3145736 | tf_op jit(solution)/shard_map/ppermute | solution.py:412
  45.6 10.4 %collective-permute-start.9 = (bf16[2,64,256]{2,1,0:T(8,128)(2,1)S(1)}, bf16[2,64,256]{2,1,0:T(8,128)(2,1)S(1)}, u32[]{:S(2)}, u32[]{:S(2)}) collective-permute-start(bf16[2,64,256]{2,1,0:T(8,128)(2,1)S(1)} %get-tuple-element.80), channel_id=1, source_target_pairs={{0,3},{1,4},{2,5},{3,6},{4,7},{5,0},{6,1},{7,2},{8,11},{9,12},{10,... | collective-permute-start | bytes 196616 | tf_op jit(solution)/shard_map/side_mirror/ppermute | solution.py:407
  49.5 8.6 %collective-permute-start.10 = (bf16[2,64,256]{2,1,0:T(8,128)(2,1)S(1)}, bf16[2,64,256]{2,1,0:T(8,128)(2,1)S(1)}, u32[]{:S(2)}, u32[]{:S(2)}) collective-permute-start(bf16[2,64,256]{2,1,0:T(8,128)(2,1)S(1)} %get-tuple-element.81), channel_id=1, source_target_pairs={{0,5},{1,6},{2,7},{3,0},{4,1},{5,2},{6,3},{7,4},{8,13},{9,14},{10,... | collective-permute-start | bytes 196616 | tf_op jit(solution)/shard_map/side_mirror/ppermute | solution.py:407
  51.6 7.2 %collective-permute-start.11 = (bf16[2,64,256]{2,1,0:T(8,128)(2,1)S(1)}, bf16[2,64,256]{2,1,0:T(8,128)(2,1)S(1)}, u32[]{:S(2)}, u32[]{:S(2)}) collective-permute-start(bf16[2,64,256]{2,1,0:T(8,128)(2,1)S(1)} %get-tuple-element.82), channel_id=1, source_target_pairs={{0,1},{1,2},{2,3},{3,4},{4,5},{5,6},{6,7},{7,0},{8,9},{9,10},{10,1... | collective-permute-start | bytes 196616 | tf_op jit(solution)/shard_map/side_mirror/ppermute | solution.py:407
  53.0 7.1 %collective-permute-start.12 = (bf16[2,64,256]{2,1,0:T(8,128)(2,1)S(1)}, bf16[2,64,256]{2,1,0:T(8,128)(2,1)S(1)}, u32[]{:S(2)}, u32[]{:S(2)}) collective-permute-start(bf16[2,64,256]{2,1,0:T(8,128)(2,1)S(1)} %get-tuple-element.83), channel_id=1, source_target_pairs={{0,7},{1,0},{2,1},{3,2},{4,3},{5,4},{6,5},{7,6},{8,15},{9,8},{10,9... | collective-permute-start | bytes 196616 | tf_op jit(solution)/shard_map/side_mirror/ppermute | solution.py:407
  56.0 6.3 %collective-permute-start.13 = (bf16[2,64,256]{2,1,0:T(8,128)(2,1)S(1)}, bf16[2,64,256]{2,1,0:T(8,128)(2,1)S(1)}, u32[]{:S(2)}, u32[]{:S(2)}) collective-permute-start(bf16[2,64,256]{2,1,0:T(8,128)(2,1)S(1)} %get-tuple-element.84), channel_id=1, source_target_pairs={{0,4},{1,5},{2,6},{3,7},{4,0},{5,1},{6,2},{7,3},{8,12},{9,13},{10,... | collective-permute-start | bytes 196616 | tf_op jit(solution)/shard_map/side_mirror/ppermute | solution.py:407
  58.1 4.4 %collective-permute-start.14 = (bf16[2,64,256]{2,1,0:T(8,128)(2,1)S(1)}, bf16[2,64,256]{2,1,0:T(8,128)(2,1)S(1)}, u32[]{:S(2)}, u32[]{:S(2)}) collective-permute-start(bf16[2,64,256]{2,1,0:T(8,128)(2,1)S(1)} %get-tuple-element.85), channel_id=1, source_target_pairs={{0,2},{1,3},{2,4},{3,5},{4,6},{5,7},{6,0},{7,1},{8,10},{9,11},{10,... | collective-permute-start | bytes 196616 | tf_op jit(solution)/shard_map/side_mirror/ppermute | solution.py:407
  58.8 4.3 %collective-permute-start.15 = (bf16[2,64,256]{2,1,0:T(8,128)(2,1)S(1)}, bf16[2,64,256]{2,1,0:T(8,128)(2,1)S(1)}, u32[]{:S(2)}, u32[]{:S(2)}) collective-permute-start(bf16[2,64,256]{2,1,0:T(8,128)(2,1)S(1)} %get-tuple-element.86), channel_id=1, source_target_pairs={{0,6},{1,7},{2,0},{3,1},{4,2},{5,3},{6,4},{7,5},{8,14},{9,15},{10,... | collective-permute-start | bytes 196616 | tf_op jit(solution)/shard_map/side_mirror/ppermute | solution.py:407
  60.1 3.6 %collective-permute-start.17 = (bf16[8,2,64,256]{3,2,1,0:T(8,128)(2,1)S(1)}, bf16[8,2,64,256]{3,2,1,0:T(8,128)(2,1)S(1)}, u32[]{:S(2)}, u32[]{:S(2)}) collective-permute-start(bf16[8,2,64,256]{3,2,1,0:T(8,128)(2,1)S(1)} %collect.3.x_ref), channel_id=1, source_target_pairs={{0,8},{8,0},{1,9},{9,1},{2,10},{10,2},{3,11},{11,3},{4,12},{12,4},... | collective-permute-start | bytes 1572872 | tf_op jit(solution)/shard_map/side_mirror/ppermute | solution.py:412
  63.6 2.0 %collective-permute-start.16 = (bf16[8,2,64,256]{3,2,1,0:T(8,128)(2,1)S(1)}, bf16[8,2,64,256]{3,2,1,0:T(8,128)(2,1)S(1)}, u32[]{:S(2)}, u32[]{:S(2)}) collective-permute-start(bf16[8,2,64,256]{3,2,1,0:T(8,128)(2,1)S(1)} %collect.4), channel_id=1, source_target_pairs={{0,8},{8,0},{1,9},{9,1},{2,10},{10,2},{3,11},{11,3},{4,12},{12,4},... | collective-permute-start | bytes 1572872 | tf_op jit(solution)/shard_map/side_mirror/ppermute | solution.py:412
  71.2 2.7 %collective-permute-start.18 = (bf16[8,2,2,64,256]{4,3,2,1,0:T(8,128)(2,1)S(1)}, bf16[8,2,2,64,256]{4,3,2,1,0:T(8,128)(2,1)S(1)}, u32[]{:S(2)}, u32[]{:S(2)}) collective-permute-start(bf16[8,2,2,64,256]{4,3,2,1,0:T(8,128)(2,1)S(1)} %all-to-all-done.1.turned), channel_id=1, source_target_pairs={{0,8},{8,0},{1,9},{9,1},{2,10},{10,2},{3,11},{11,3},{4,12},{12,4},... | collective-permute-start | bytes 3145736 | tf_op jit(solution)/shard_map/ppermute | solution.py:412
  80.2 35.1 %all-to-all-start.2 = ((bf16[8,2,256,128]{3,2,1,0:T(8,128)(2,1)}), bf16[8,2,256,128]{3,2,1,0:T(8,128)(2,1)S(1)}, u32[]{:S(2)}, u32[]{:S(2)}) async-start(bf16[8,2,256,128]{3,2,1,0:T(8,128)(2,1)} %first_half.1), calls=%async_computation.2 | async-start | bytes 2097152 | tf_op jit(solution)/shard_map/partial/all_to_all | solution.py:466
  86.2 15.0 %collective-permute-start.19 = (bf16[1,256,128]{2,1,0:T(8,128)(2,1)S(1)}, bf16[1,256,128]{2,1,0:T(8,128)(2,1)S(1)}, u32[]{:S(2)}, u32[]{:S(2)}) collective-permute-start(bf16[1,256,128]{2,1,0:T(8,128)(2,1)S(1)} %get-tuple-element.99), channel_id=1, source_target_pairs={{0,3},{1,4},{2,5},{3,6},{4,7},{5,0},{6,1},{7,2},{8,11},{9,12},{10,... | collective-permute-start | bytes 196616 | tf_op jit(solution)/shard_map/side_partial/ppermute | solution.py:407
  88.2 13.0 %collective-permute-start.20 = (bf16[1,256,128]{2,1,0:T(8,128)(2,1)S(1)}, bf16[1,256,128]{2,1,0:T(8,128)(2,1)S(1)}, u32[]{:S(2)}, u32[]{:S(2)}) collective-permute-start(bf16[1,256,128]{2,1,0:T(8,128)(2,1)S(1)} %get-tuple-element.100), channel_id=1, source_target_pairs={{0,5},{1,6},{2,7},{3,0},{4,1},{5,2},{6,3},{7,4},{8,13},{9,14},{10,... | collective-permute-start | bytes 196616 | tf_op jit(solution)/shard_map/side_partial/ppermute | solution.py:407
  92.1 11.1 %collective-permute-start.21 = (bf16[1,256,128]{2,1,0:T(8,128)(2,1)S(1)}, bf16[1,256,128]{2,1,0:T(8,128)(2,1)S(1)}, u32[]{:S(2)}, u32[]{:S(2)}) collective-permute-start(bf16[1,256,128]{2,1,0:T(8,128)(2,1)S(1)} %get-tuple-element.101), channel_id=1, source_target_pairs={{0,1},{1,2},{2,3},{3,4},{4,5},{5,6},{6,7},{7,0},{8,9},{9,10},{10,1... | collective-permute-start | bytes 196616 | tf_op jit(solution)/shard_map/side_partial/ppermute | solution.py:407
  93.8 9.4 %collective-permute-start.22 = (bf16[1,256,128]{2,1,0:T(8,128)(2,1)S(1)}, bf16[1,256,128]{2,1,0:T(8,128)(2,1)S(1)}, u32[]{:S(2)}, u32[]{:S(2)}) collective-permute-start(bf16[1,256,128]{2,1,0:T(8,128)(2,1)S(1)} %get-tuple-element.102), channel_id=1, source_target_pairs={{0,7},{1,0},{2,1},{3,2},{4,3},{5,4},{6,5},{7,6},{8,15},{9,8},{10,9... | collective-permute-start | bytes 196616 | tf_op jit(solution)/shard_map/side_partial/ppermute | solution.py:407
  96.5 7.8 %collective-permute-start.23 = (bf16[1,256,128]{2,1,0:T(8,128)(2,1)S(1)}, bf16[1,256,128]{2,1,0:T(8,128)(2,1)S(1)}, u32[]{:S(2)}, u32[]{:S(2)}) collective-permute-start(bf16[1,256,128]{2,1,0:T(8,128)(2,1)S(1)} %get-tuple-element.103), channel_id=1, source_target_pairs={{0,4},{1,5},{2,6},{3,7},{4,0},{5,1},{6,2},{7,3},{8,12},{9,13},{10,... | collective-permute-start | bytes 196616 | tf_op jit(solution)/shard_map/side_partial/ppermute | solution.py:407
  101.2 4.3 %collective-permute-start.24 = (bf16[1,256,128]{2,1,0:T(8,128)(2,1)S(1)}, bf16[1,256,128]{2,1,0:T(8,128)(2,1)S(1)}, u32[]{:S(2)}, u32[]{:S(2)}) collective-permute-start(bf16[1,256,128]{2,1,0:T(8,128)(2,1)S(1)} %get-tuple-element.104), channel_id=1, source_target_pairs={{0,2},{1,3},{2,4},{3,5},{4,6},{5,7},{6,0},{7,1},{8,10},{9,11},{10,... | collective-permute-start | bytes 196616 | tf_op jit(solution)/shard_map/side_partial/ppermute | solution.py:407
  101.2 4.3 %collective-permute-start.25 = (bf16[1,256,128]{2,1,0:T(8,128)(2,1)S(1)}, bf16[1,256,128]{2,1,0:T(8,128)(2,1)S(1)}, u32[]{:S(2)}, u32[]{:S(2)}) collective-permute-start(bf16[1,256,128]{2,1,0:T(8,128)(2,1)S(1)} %get-tuple-element.105), channel_id=1, source_target_pairs={{0,6},{1,7},{2,0},{3,1},{4,2},{5,3},{6,4},{7,5},{8,14},{9,15},{10,... | collective-permute-start | bytes 196616 | tf_op jit(solution)/shard_map/side_partial/ppermute | solution.py:407
  106.1 2.0 %collective-permute-start.26 = (bf16[8,1,256,128]{3,2,1,0:T(8,128)(2,1)S(1)}, bf16[8,1,256,128]{3,2,1,0:T(8,128)(2,1)S(1)}, u32[]{:S(2)}, u32[]{:S(2)}) collective-permute-start(bf16[8,1,256,128]{3,2,1,0:T(8,128)(2,1)S(1)} %collect.5.t_ref), channel_id=1, source_target_pairs={{0,8},{8,0},{1,9},{9,1},{2,10},{10,2},{3,11},{11,3},{4,12},{12,4},... | collective-permute-start | bytes 1572872 | tf_op jit(solution)/shard_map/side_partial/ppermute | solution.py:412
  113.1 8.4 %collective-permute-start.27 = (bf16[8,64,256]{2,1,0:T(8,128)(2,1)S(1)}, bf16[8,64,256]{2,1,0:T(8,128)(2,1)S(1)}, u32[]{:S(2)}, u32[]{:S(2)}) collective-permute-start(bf16[8,64,256]{2,1,0:T(8,128)(2,1)S(1)} %get-tuple-element.108), channel_id=1, source_target_pairs={{0,16},{16,0},{1,17},{17,1},{2,18},{18,2},{3,19},{19,3},{4,20},{20... | collective-permute-start | bytes 786440 | tf_op jit(solution)/shard_map/ppermute | solution.py:412
  121.6 28.6 %all-to-all-start.3 = ((bf16[16,2,64,256]{3,2,1,0:T(8,128)(2,1)}), bf16[16,2,64,256]{3,2,1,0:T(8,128)(2,1)S(1)}, u32[]{:S(2)}, u32[]{:S(2)}) async-start(bf16[16,2,64,256]{3,2,1,0:T(8,128)(2,1)} %bitcast.13), calls=%async_computation.3 | async-start | bytes 2097152 | tf_op jit(solution)/shard_map/panels_out/all_to_all | solution.py:480
  129.5 14.9 %collective-permute-start.28 = (bf16[2,64,256]{2,1,0:T(8,128)(2,1)S(1)}, bf16[2,64,256]{2,1,0:T(8,128)(2,1)S(1)}, u32[]{:S(2)}, u32[]{:S(2)}) collective-permute-start(bf16[2,64,256]{2,1,0:T(8,128)(2,1)S(1)} %get-tuple-element.113), channel_id=1, source_target_pairs={{0,96},{32,128},{64,160},{96,192},{128,224},{160,0},{192,32},{224,... | collective-permute-start | bytes 196616 | tf_op jit(solution)/shard_map/side_out/ppermute | solution.py:407
  133.2 11.9 %collective-permute-start.29 = (bf16[2,64,256]{2,1,0:T(8,128)(2,1)S(1)}, bf16[2,64,256]{2,1,0:T(8,128)(2,1)S(1)}, u32[]{:S(2)}, u32[]{:S(2)}) collective-permute-start(bf16[2,64,256]{2,1,0:T(8,128)(2,1)S(1)} %get-tuple-element.114), channel_id=1, source_target_pairs={{0,160},{32,192},{64,224},{96,0},{128,32},{160,64},{192,96},{224,1... | collective-permute-start | bytes 196616 | tf_op jit(solution)/shard_map/side_out/ppermute | solution.py:407
  134.9 12.8 %collective-permute-start.30 = (bf16[2,64,256]{2,1,0:T(8,128)(2,1)S(1)}, bf16[2,64,256]{2,1,0:T(8,128)(2,1)S(1)}, u32[]{:S(2)}, u32[]{:S(2)}) collective-permute-start(bf16[2,64,256]{2,1,0:T(8,128)(2,1)S(1)} %get-tuple-element.115), channel_id=1, source_target_pairs={{0,128},{32,160},{64,192},{96,224},{128,0},{160,32},{192,64},{224,... | collective-permute-start | bytes 196616 | tf_op jit(solution)/shard_map/side_out/ppermute | solution.py:407
  140.3 7.4 %collective-permute-start.31 = (bf16[2,64,256]{2,1,0:T(8,128)(2,1)S(1)}, bf16[2,64,256]{2,1,0:T(8,128)(2,1)S(1)}, u32[]{:S(2)}, u32[]{:S(2)}) collective-permute-start(bf16[2,64,256]{2,1,0:T(8,128)(2,1)S(1)} %get-tuple-element.116), channel_id=1, source_target_pairs={{0,64},{32,96},{64,128},{96,160},{128,192},{160,224},{192,0},{224,... | collective-permute-start | bytes 196616 | tf_op jit(solution)/shard_map/side_out/ppermute | solution.py:407
  140.9 7.0 %collective-permute-start.32 = (bf16[2,64,256]{2,1,0:T(8,128)(2,1)S(1)}, bf16[2,64,256]{2,1,0:T(8,128)(2,1)S(1)}, u32[]{:S(2)}, u32[]{:S(2)}) collective-permute-start(bf16[2,64,256]{2,1,0:T(8,128)(2,1)S(1)} %get-tuple-element.117), channel_id=1, source_target_pairs={{0,192},{32,224},{64,0},{96,32},{128,64},{160,96},{192,128},{224,1... | collective-permute-start | bytes 196616 | tf_op jit(solution)/shard_map/side_out/ppermute | solution.py:407
  144.4 5.5 %collective-permute-start.33 = (bf16[2,64,256]{2,1,0:T(8,128)(2,1)S(1)}, bf16[2,64,256]{2,1,0:T(8,128)(2,1)S(1)}, u32[]{:S(2)}, u32[]{:S(2)}) collective-permute-start(bf16[2,64,256]{2,1,0:T(8,128)(2,1)S(1)} %get-tuple-element.118), channel_id=1, source_target_pairs={{0,32},{32,64},{64,96},{96,128},{128,160},{160,192},{192,224},{224... | collective-permute-start | bytes 196616 | tf_op jit(solution)/shard_map/side_out/ppermute | solution.py:407
  145.0 5.2 %collective-permute-start.34 = (bf16[2,64,256]{2,1,0:T(8,128)(2,1)S(1)}, bf16[2,64,256]{2,1,0:T(8,128)(2,1)S(1)}, u32[]{:S(2)}, u32[]{:S(2)}) collective-permute-start(bf16[2,64,256]{2,1,0:T(8,128)(2,1)S(1)} %get-tuple-element.119), channel_id=1, source_target_pairs={{0,224},{32,0},{64,32},{96,64},{128,96},{160,128},{192,160},{224,1... | collective-permute-start | bytes 196616 | tf_op jit(solution)/shard_map/side_out/ppermute | solution.py:407
